TPU v7x, 32 devices: a whole 2x2x4 slice. The times are simulated.
32 devices in a mesh: group: 2 (over x), frame: 4 (over y, core), strip: 4 (over z).
Axes of the slice: x: 2, y: 2, z: 4, core: 2. Of those that a mesh axis runs over, the one named last changes fastest.
Arguments:
- spatial_queries: bfloat16 [32, 1024, 576], P(('group', 'frame'), 'strip'), parts along dimension 0, may hold values from -6 to 6
- spatial_keys: bfloat16 [32, 1024, 576], P(('group', 'frame'), 'strip'), parts along dimension 0, may hold values from -6 to 6
- spatial_values: bfloat16 [32, 1024, 576], P(('group', 'frame'), 'strip'), parts along dimension 0, may hold values from -6 to 6
- hidden: bfloat16 [32, 1024, 1152], P(('group', 'frame'), 'strip'), parts along dimension 0, may hold values from -6 to 6
- spatial_out_weight: bfloat16 [576, 1152], replicated, may hold values from -0.25 to 0.25
- spatial_gain: float32 [1152], replicated, may hold values from 0.5 to 1.5
- temporal_qkv_weight: bfloat16 [1152, 1728], replicated, may hold values from -0.1875 to 0.1875
- temporal_out_weight: bfloat16 [576, 1152], replicated, may hold values from -0.25 to 0.25
- temporal_gain: float32 [1152], replicated, may hold values from 0.5 to 1.5
- tile_list: int32 [32, 8, 3], P(('group', 'frame'), 'strip'), parts along dimension 0, may hold values from 0 to 7, as said below
- tile_count: int32 [32, 8], P(('group', 'frame'), 'strip'), parts along dimension 0, may hold values from 1 to 3, as said below
Outputs:
- block_out: bfloat16 [32, 1024, 1152], P(('group', 'frame'), 'strip'), parts along dimension 0
There are 2 independent parts, one for each index of `group`. A program takes and returns all parts, laid end to end along the dimension named above; an argument that names none is the same for every part. Nothing has to cross between parts.
Inputs may be any that keep to these rules, and one draw needn't show every extreme that they name: `tile_list`: entry 0 of a query tile's row is the query tile itself; the 3 entries of a row are distinct tiles, each in the query tile's own strip of 2 tiles or the nearest tile of an adjacent strip of the same frame. In frame 0, the first tile of every strip but the first attends the tile just below it, and the last tile of every strip but the last attends the tile just above it. `tile_count`: some query tile has 3 in every draw.
All inputs are finite; a program needn't handle non-finite values.
Results may differ from a plain program's by a relative error of at most 0.0083.
Values may be sent and summed in bfloat16 or wider, within the bound.
No kernel may reach another device: no remote copies, remote signals or barrier semaphores. Data moves between devices by JAX's collectives and lax.ppermute only.
A program may use at most 128 MiB of HBM per device.

v0:
```python
import functools
import math

import jax
import jax.numpy as jnp
from jax import lax
from jax.experimental import pallas as pl
from jax.experimental.pallas import tpu as pltpu
from jax.sharding import PartitionSpec as P


HEAD_DIM = 72
TILE = 128
MAXT = 3
SUB = 16
EPS = 1e-06
EXP2_SCALE = HEAD_DIM ** -0.5 * math.log2(math.e)

BF = jnp.bfloat16
F32 = jnp.float32


def peer(i, j, n):
    return i ^ j if n & (n - 1) == 0 else (i + j) % n


def vmem(limit):
    return pltpu.CompilerParams(vmem_limit_bytes=limit << 20)


def whole(shape):
    return pl.BlockSpec(shape, lambda *_: (0,) * len(shape))


def contract(a, b, da, db):
    return lax.dot_general(a, b, (((da,), (db,)), ((), ())), preferred_element_type=F32)


def head_scale(x):
    return lax.rsqrt(jnp.mean(x * x, axis=0, keepdims=True) + EPS)


def head(h, base=0):
    return slice(base + h * HEAD_DIM, base + (h + 1) * HEAD_DIM)


def pipeline(steps, scores, weigh, gather):
    ahead, behind = scores(*steps[0]), None
    for n, step in enumerate(steps):
        now = ahead
        if n + 1 < len(steps):
            ahead = scores(*steps[n + 1])
        weighed = weigh(now)
        if behind is not None:
            gather(*steps[n - 1], *behind)
        behind = weighed
    gather(*steps[-1], *behind)


def prep_kernel(place, *refs):
    n = len(refs) // 4
    width = refs[0].shape[1]
    even = place[1] % 2 == 0
    for f in range(n):
        k_ref, v_ref = refs[2 * f:2 * f + 2]
        a_ref, b_ref = refs[2 * n + 2 * f:2 * n + 2 * f + 2]

        def fill(first, second):
            for h in range(width // HEAD_DIM):
                x = k_ref[0, head(h), :].astype(F32)
                y = (x * head_scale(x)).astype(BF)
                first[head(h), :] = y[:, :TILE]
                second[head(h), :] = y[:, TILE:]
            first[width:, :] = v_ref[0, :, :TILE]
            second[width:, :] = v_ref[0, :, TILE:]

        pl.when(even)(functools.partial(fill, b_ref, a_ref))
        pl.when(jnp.logical_not(even))(functools.partial(fill, a_ref, b_ref))


def spatial_kernel(frame, n_groups, place, counts, lists, q_ref, a_ref, b_ref, ra_ref, rb_ref, h_ref, w_ref, g_ref, *rest):
    outs, (att, mix) = rest[:n_groups], rest[n_groups:]
    width, tokens = q_ref.shape[1], q_ref.shape[2]
    tiles = tokens // TILE
    share = tokens // n_groups
    keys = ((a_ref, b_ref), (ra_ref, rb_ref))
    strip = place[1]
    odd = strip % 2
    first = strip * tiles
    places = (first + 1 - odd, first + odd, first + 2 - 3 * odd, first - 1 + 3 * odd)
    masks = []
    for t in range(tiles):
        live = counts[t, frame]
        cells = []
        for spot in places:
            hit = jnp.bool_(False)
            for j in range(MAXT):
                hit = hit | ((lists[j, t, frame] == spot) & (j < live))
            cells.append(jnp.where(hit, 1.0, 0.0).astype(F32))
        masks.append(cells)

    def scores(h):
        q = q_ref[0, head(h), :].astype(F32)
        qn = (q * head_scale(q)).astype(BF)
        return [[contract(keys[i][u][head(h), :], qn, 0, 0) for u in range(2)] for i in range(2)]

    def weigh(pair):
        partial, halves = [], []
        for i in range(2):
            packed = []
            for u in range(2):
                p = jnp.exp2(pair[i][u] * EXP2_SCALE)
                p = jnp.concatenate(
                    [p[:, t * TILE:(t + 1) * TILE] * masks[t][2 * i + u] for t in range(tiles)], axis=1
                )
                partial.append(jnp.sum(p.reshape(TILE // 8, 8, tokens), axis=0))
                packed.append(p.astype(BF))
            halves.append(jnp.concatenate(packed, axis=0))
        return jnp.sum(sum(partial), axis=0, keepdims=True), halves

    def gather(h, total, halves):
        o = 0
        for i in range(2):
            v = jnp.concatenate([r[head(h, width), :] for r in keys[i]], axis=1)
            o += contract(v, halves[i], 1, 0)
        att[head(h), :] = (o / total).astype(BF)

    pipeline([(h,) for h in range(width // HEAD_DIM)], scores, weigh, gather)
    proj = contract(att[...], w_ref[...], 0, 0)
    scale = lax.rsqrt(jnp.mean(proj * proj, axis=-1, keepdims=True) + EPS)
    mix[...] = (h_ref[0].astype(F32) + proj * scale * g_ref[...]).astype(BF)
    for j, out in enumerate(outs):
        group = peer(place[0], j, n_groups)
        out[...] = mix[pl.ds(pl.multiple_of(group * share, SUB), share), :]


def paired(chunks, lanes, frames):
    return chunks % 2 == 0 and frames % 2 == 0 and 2 * lanes == TILE


def project_kernel(frame, frames, *refs):
    pieces, w_ref, out, x = refs[:-3], refs[-3], refs[-2], refs[-1]
    n_groups = len(pieces)
    chunks = pieces[0].shape[0] // SUB
    swap = frame & 1 if paired(chunks, n_groups * SUB, frames) else 0
    for c in range(chunks):
        for j, piece in enumerate(pieces):
            at = ((c ^ swap) * n_groups + j) * SUB
            x[at:at + SUB, :] = piece[c * SUB:(c + 1) * SUB, :]
    width = w_ref.shape[0] // 3
    cut = w_ref.shape[0] // 2
    heads = width // HEAD_DIM
    parts = [contract(w_ref[i * cut:(i + 1) * cut, :], x[...], 1, 1) for i in range(2)]
    for h in range(3 * heads):
        i, at = divmod(h * HEAD_DIM, cut)
        y = parts[i][at:at + HEAD_DIM, :]
        if h < 2 * heads:
            y = y * head_scale(y)
        out[head(h), :] = y.astype(BF)


def temporal_kernel(n_groups, *refs):
    frames = len(refs) - n_groups - 1
    ins, outs, att = refs[:frames], refs[frames:frames + n_groups], refs[-1]
    lanes = n_groups * SUB
    chunks = ins[0].shape[1] // lanes
    width = ins[0].shape[0] // 3
    rows = frames * lanes
    pair = paired(chunks, lanes, frames)
    row_pos = lax.broadcasted_iota(jnp.int32, (rows, rows), 0) % SUB
    col_pos = lax.broadcasted_iota(jnp.int32, (rows, rows), 1) % SUB
    same = jnp.where(row_pos == col_pos, 1.0, 0.0).astype(F32)
    low = lax.broadcasted_iota(jnp.int32, (HEAD_DIM, TILE), 1) < lanes

    def take(c, where):
        if not pair:
            return jnp.concatenate([r[where, c * lanes:(c + 1) * lanes] for r in ins], axis=1)
        tile = slice(c // 2 * TILE, (c // 2 + 1) * TILE)
        got = [r[where, tile] for r in ins]
        return jnp.concatenate(
            [
                jnp.where(low, got[m + (c & 1)], got[m + 1 - (c & 1)])
                for m in range(0, frames, 2)
            ],
            axis=1,
        )

    def scores(c, h):
        return contract(take(c, head(h, width)), take(c, head(h)), 0, 0)

    def weigh(s):
        p = jnp.exp2(s * EXP2_SCALE) * same
        return jnp.sum(p, axis=0, keepdims=True), p.astype(BF)

    def gather(c, h, total, p):
        att[c, head(h), :] = contract(take(c, head(h, 2 * width)), p, 1, 0) / total

    steps = [(c, h) for c in range(chunks) for h in range(width // HEAD_DIM)]
    pipeline(steps, scores, weigh, gather)
    turned = [att[c].T.astype(BF) for c in range(chunks)]
    for j, out in enumerate(outs):
        for c in range(chunks):
            for f in range(frames):
                slot = f ^ (c & 1) if pair else f
                at = slot * lanes + j * SUB
                out[c * SUB:(c + 1) * SUB, f * width:(f + 1) * width] = turned[c][at:at + SUB, :]


def output_kernel(n_groups, frames, half, halves, aliased, place, *refs):
    n_in = n_groups * frames
    atts, pieces = refs[:n_groups], refs[n_groups:n_groups + n_in]
    w_ref, g_ref = refs[n_groups + n_in:n_groups + n_in + 2]
    out, buf, sems = refs[n_groups + n_in + 2 + aliased:]
    rows = pieces[0].shape[0]
    width = w_ref.shape[0]
    copies = []
    for j in range(n_groups):
        x = jnp.concatenate([atts[j][:, f * width:(f + 1) * width] for f in range(frames)], axis=0)
        proj = contract(x, w_ref[...], 1, 0)
        scale = lax.rsqrt(jnp.mean(proj * proj, axis=-1, keepdims=True) + EPS)
        res = proj * scale * g_ref[...]
        for f in range(frames):
            mine = pieces[j * frames + f][...].astype(F32)
            buf[j, f] = (mine + res[f * rows:(f + 1) * rows, :]).astype(BF)
        group = peer(place[0], j, n_groups)
        start = pl.multiple_of((group * halves + half) * rows, SUB)
        copy = pltpu.make_async_copy(buf.at[j], out.at[:, pl.ds(start, rows), :], sems.at[j])
        copy.start()
        copies.append(copy)
    for copy in copies:
        copy.wait()


def shards(
    spatial_queries,
    spatial_keys,
    spatial_values,
    hidden,
    spatial_out_weight,
    spatial_gain,
    temporal_qkv_weight,
    temporal_out_weight,
    temporal_gain,
    tile_list,
    tile_count,
):
    frames, tokens, width = spatial_queries.shape
    model = hidden.shape[2]
    groups = lax.axis_size("frame")
    strips = lax.axis_size("strip")
    share = tokens // groups
    halves = 2 if share % (4 * SUB) == 0 else 1
    rows = share // halves
    queries = jnp.transpose(spatial_queries, (0, 2, 1))
    keys = pltpu.with_memory_space_constraint(jnp.transpose(spatial_keys, (0, 2, 1)), pltpu.HBM)
    values = pltpu.with_memory_space_constraint(jnp.transpose(spatial_values, (0, 2, 1)), pltpu.HBM)
    lists = jnp.transpose(tile_list, (2, 1, 0))
    counts = tile_count.T
    qkv_weight = temporal_qkv_weight.T
    gain_one = spatial_gain.reshape(1, model)
    gain_two = temporal_gain.reshape(1, model)
    place = jnp.stack([lax.axis_index("frame"), lax.axis_index("strip")]).astype(jnp.int32)
    near = [(i, i ^ 1) for i in range(strips) if i ^ 1 < strips]
    far = [e for i in range(1, strips - 1, 2) for e in ((i, i + 1), (i + 1, i))]
    edge = jax.ShapeDtypeStruct((2 * width, TILE), BF)
    smem = pl.BlockSpec(memory_space=pltpu.SMEM)

    def call(kernel, in_specs, out_specs, out_shape, scratch=(), limit=32, prefetch=0, alias=None):
        return pl.pallas_call(
            kernel,
            grid_spec=pltpu.PrefetchScalarGridSpec(
                num_scalar_prefetch=prefetch,
                grid=(1,),
                in_specs=in_specs,
                out_specs=out_specs,
                scratch_shapes=list(scratch),
            ),
            out_shape=out_shape,
            input_output_aliases=alias or {},
            compiler_params=vmem(limit),
        )

    def frame_block(f):
        return pl.BlockSpec((1, width, tokens), lambda *_: (f, 0, 0))

    edges, halos = [], []
    for some in [[0], list(range(1, frames))]:
        got = call(
            prep_kernel,
            [smem] + [frame_block(f) for f in some for _ in range(2)],
            [whole(edge.shape)] * (2 * len(some)),
            [edge] * (2 * len(some)),
            limit=16,
        )(place, *[keys, values] * len(some))
        edges += [got[2 * i:2 * i + 2] for i in range(len(some))]
    for a, b in edges:
        halos.append((lax.ppermute(a, "strip", near), lax.ppermute(b, "strip", far)))

    mixed = [[None] * frames for _ in range(groups)]
    projected = []
    for f in range(frames):
        parts = call(
            functools.partial(spatial_kernel, f, groups),
            [smem, smem, smem, frame_block(f)]
            + [whole(edge.shape)] * 4
            + [
                pl.BlockSpec((1, tokens, model), lambda *_, f=f: (f, 0, 0)),
                whole((width, model)),
                whole((1, model)),
            ],
            [whole((share, model))] * groups,
            [jax.ShapeDtypeStruct((share, model), BF)] * groups,
            [pltpu.VMEM((width, tokens), BF), pltpu.VMEM((tokens, model), BF)],
        )(place, counts, lists, queries, *edges[f], *halos[f], hidden, spatial_out_weight, gain_one)
        arrived = []
        for j in range(groups):
            mixed[j][f] = parts[j]
            pairs = [(i, peer(i, j, groups)) for i in range(groups)]
            arrived.append(parts[j] if j == 0 else lax.ppermute(parts[j], "frame", pairs))
        projected.append(
            call(
                functools.partial(project_kernel, f, frames),
                [whole((share, model))] * groups + [whole((3 * width, model))],
                whole((3 * width, tokens)),
                jax.ShapeDtypeStruct((3 * width, tokens), BF),
                [pltpu.VMEM((tokens, model), BF)],
            )(*arrived, qkv_weight)
        )

    returned = []
    back_shape = (rows, frames * width)
    for half in range(halves):
        part = pl.BlockSpec((3 * width, tokens // halves), lambda *_, half=half: (0, half))
        back = call(
            functools.partial(temporal_kernel, groups),
            [part] * frames,
            [whole(back_shape)] * groups,
            [jax.ShapeDtypeStruct(back_shape, BF)] * groups,
            [pltpu.VMEM((rows // SUB, width, groups * frames * SUB), F32)],
        )(*projected)
        got = []
        for j in range(groups):
            pairs = [(peer(i, j, groups), i) for i in range(groups)]
            got.append(back[j] if j == 0 else lax.ppermute(back[j], "frame", pairs))
        returned.append(got)

    out = None
    mine = [mixed[j][f] for j in range(groups) for f in range(frames)]
    any_spec = pl.BlockSpec(memory_space=pl.ANY)
    for half in range(halves):
        piece = pl.BlockSpec((rows, model), lambda *_, half=half: (half, 0))
        extra = [] if out is None else [out]
        out = call(
            functools.partial(output_kernel, groups, frames, half, halves, len(extra)),
            [smem]
            + [whole(back_shape)] * groups
            + [piece] * len(mine)
            + [whole((width, model)), whole((1, model))]
            + [any_spec] * len(extra),
            any_spec,
            jax.ShapeDtypeStruct((frames, tokens, model), BF),
            [
                pltpu.VMEM((groups, frames, rows, model), BF),
                pltpu.SemaphoreType.DMA((groups,)),
            ],
            alias={1 + groups + len(mine) + 2: 0} if extra else None,
        )(place, *returned[half], *mine, temporal_out_weight, gain_two, *extra)
    return out


def solution(mesh):
    rows = P(("group", "frame"), "strip", None)
    placed = (rows, rows, rows, rows, P(), P(), P(), P(), P(), rows, P(("group", "frame"), "strip"))

    return jax.shard_map(shards, mesh=mesh, in_specs=placed, out_specs=rows, check_vma=False)
```

profile of v0, /device:TPU:0, one launch (start us, length us, event | category | flops | bytes accessed | tf_op | source)
XLA Modules:
  0.0 78.4 jit_solution(13472205819874208008)
XLA Ops:
  0.0 0.1 pad_add_fusion.place
  0.1 1.2 %shard_map.109 = (bf16[1152,128]{1,0:T(8,128)(2,1)S(1)}, bf16[1152,128]{1,0:T(8,128)(2,1)S(1)}) custom-call(s32[2]{0:T(128)S(1)} %pad_add_fusion.place, bf16[4,576,256]{2,1,0:T(8,128)(2,1)} %bitcast.24, bf16[4,576,256]{2,1,0:T(8,128)(2,1)} %bitcast.28), custom_call_target="tpu_custom_call" | custom-call | tf_op jit(solution)/shard_map/pallas_call | solution.py:288
  1.3 3.1 %collective-permute-start = (bf16[1152,128]{1,0:T(8,128)(2,1)S(1)}, bf16[1152,128]{1,0:T(8,128)(2,1)S(1)}, u32[]{:S(2)}, u32[]{:S(2)}) collective-permute-start(bf16[1152,128]{1,0:T(8,128)(2,1)S(1)} %get-tuple-element.37.a_ref), channel_id=1, source_target_pairs={{0,1},{1,0},{2,3},{3,2},{4,5},{5,4},{6,7},{7,6},{8,9},{9,8},{10,11... | collective-permute-start | bytes 884744 | tf_op jit(solution)/shard_map/ppermute | solution.py:297
  4.4 0.0 copy-start.6
  4.4 0.8 %collective-permute-start.1 = (bf16[1152,128]{1,0:T(8,128)(2,1)S(1)}, bf16[1152,128]{1,0:T(8,128)(2,1)S(1)}, u32[]{:S(2)}, u32[]{:S(2)}) collective-permute-start(bf16[1152,128]{1,0:T(8,128)(2,1)S(1)} %get-tuple-element.38.b_ref), channel_id=1, source_target_pairs={{1,2},{2,1},{5,6},{6,5},{9,10},{10,9},{13,14},{14,13},{17,18},{18,... | collective-permute-start | bytes 884744 | tf_op jit(solution)/shard_map/ppermute | solution.py:297
  5.2 0.0 copy-start.1
  5.2 2.0 %shard_map.112 = (bf16[1152,128]{1,0:T(8,128)(2,1)S(1)}, bf16[1152,128]{1,0:T(8,128)(2,1)S(1)}, bf16[1152,128]{1,0:T(8,128)(2,1)S(1)}, bf16[1152,128]{1,0:T(8,12...) custom-call(s32[2]{0:T(128)S(1)} %pad_add_fusion.place, bf16[4,576,256]{2,1,0:T(8,128)(2,1)} %bitcast.25, ...), custom_call_target="tpu_custom_call" | custom-call | tf_op jit(solution)/shard_map/pallas_call | solution.py:288
  7.2 4.4 %collective-permute-start.10 = (bf16[1152,128]{1,0:T(8,128)(2,1)S(1)}, bf16[1152,128]{1,0:T(8,128)(2,1)S(1)}, u32[]{:S(2)}, u32[]{:S(2)}) collective-permute-start(bf16[1152,128]{1,0:T(8,128)(2,1)S(1)} %get-tuple-element.49.a_ref), channel_id=1, source_target_pairs={{0,1},{1,0},{2,3},{3,2},{4,5},{5,4},{6,7},{7,6},{8,9},{9,8},{10,11... | collective-permute-start | bytes 884744 | tf_op jit(solution)/shard_map/ppermute | solution.py:297
  11.7 0.7 collective-permute-start.11
  12.3 1.3 %collective-permute-start.15 = (bf16[1152,128]{1,0:T(8,128)(2,1)S(1)}, bf16[1152,128]{1,0:T(8,128)(2,1)S(1)}, u32[]{:S(2)}, u32[]{:S(2)}) collective-permute-start(bf16[1152,128]{1,0:T(8,128)(2,1)S(1)} %get-tuple-element.55.a_ref), channel_id=1, source_target_pairs={{0,1},{1,0},{2,3},{3,2},{4,5},{5,4},{6,7},{7,6},{8,9},{9,8},{10,11... | collective-permute-start | bytes 884744 | tf_op jit(solution)/shard_map/ppermute | solution.py:297
  13.7 0.0 collective-permute-done.ra_ref
  13.7 0.7 collective-permute-start.16
  14.3 0.0 collective-permute-done.1.rb_ref
  14.3 3.3 %collective-permute-start.5 = (bf16[1152,128]{1,0:T(8,128)(2,1)S(1)}, bf16[1152,128]{1,0:T(8,128)(2,1)S(1)}, u32[]{:S(2)}, u32[]{:S(2)}) collective-permute-start(bf16[1152,128]{1,0:T(8,128)(2,1)S(1)} %get-tuple-element.43.a_ref), channel_id=1, source_target_pairs={{0,1},{1,0},{2,3},{3,2},{4,5},{5,4},{6,7},{7,6},{8,9},{9,8},{10,11... | collective-permute-start | bytes 884744 | tf_op jit(solution)/shard_map/ppermute | solution.py:297
  17.7 1.8 %collective-permute-done.10.ra_ref = bf16[1152,128]{1,0:T(8,128)(2,1)S(1)} collective-permute-done((bf16[1152,128]{1,0:T(8,128)(2,1)S(1)}, bf16[1152,128]{1,0:T(8,128)(2,1)S(1)}, u32[]{:S(2)}, u32[]{:S(2)}) %collective-permute-start.10) | collective-permute-done | bytes 294944 | tf_op jit(solution)/shard_map/ppermute | solution.py:297
  19.5 0.7 collective-permute-start.6
  20.3 2.7 %shard_map.110 = (bf16[64,1152]{1,0:T(8,128)(2,1)S(1)}, bf16[64,1152]{1,0:T(8,128)(2,1)S(1)}, bf16[64,1152]{1,0:T(8,128)(2,1)S(1)}, bf16[64,1152]{1,0:T(8,128)(2,1)S(1)}) custom-call(s32[2]{0:T(128)S(1)} %pad_add_fusion.place, s32[2,4]{1,0:T(2,128)S(1)} %bitcast.20, s32[3,2,4]{2,1,0:T(2,128)S(1)} %bitcast.16, bf16[4,576,256]{2,1,0:T(8,128)(2,1)S(1)} %bitcast.12, ...), custom_call_target="tpu_custom_call" | custom-call | tf_op jit(solution)/shard_map/pallas_call | solution.py:302
  23.0 0.1 collective-permute-start.2
  23.1 2.8 %collective-permute-done.15.ra_ref = bf16[1152,128]{1,0:T(8,128)(2,1)S(1)} collective-permute-done((bf16[1152,128]{1,0:T(8,128)(2,1)S(1)}, bf16[1152,128]{1,0:T(8,128)(2,1)S(1)}, u32[]{:S(2)}, u32[]{:S(2)}) %collective-permute-start.15) | collective-permute-done | bytes 294944 | tf_op jit(solution)/shard_map/ppermute | solution.py:297
  25.8 1.5 %collective-permute-start.3 = (bf16[64,1152]{1,0:T(8,128)(2,1)S(1)}, bf16[64,1152]{1,0:T(8,128)(2,1)S(1)}, u32[]{:S(2)}, u32[]{:S(2)}) collective-permute-start(bf16[64,1152]{1,0:T(8,128)(2,1)S(1)} %get-tuple-element.41.refs_12_), channel_id=1, source_target_pairs={{0,8},{4,12},{8,0},{12,4},{1,9},{5,13},{9,1},{13,5},{2,10},{6,14},... | collective-permute-start | bytes 442376 | tf_op jit(solution)/shard_map/ppermute | solution.py:319
  27.4 2.7 %shard_map.115 = (bf16[64,1152]{1,0:T(8,128)(2,1)S(1)}, bf16[64,1152]{1,0:T(8,128)(2,1)S(1)}, bf16[64,1152]{1,0:T(8,128)(2,1)S(1)}, bf16[64,1152]{1,0:T(8,128)(2,1)S(1)}) custom-call(s32[2]{0:T(128)S(1)} %pad_add_fusion.place, s32[2,4]{1,0:T(2,128)S(1)} %bitcast.21, s32[3,2,4]{2,1,0:T(2,128)S(1)} %bitcast.17, bf16[4,576,256]{2,1,0:T(8,128)(2,1)S(1)} %bitcast.13, ...), custom_call_target="tpu_custom_call" | custom-call | tf_op jit(solution)/shard_map/pallas_call | solution.py:302
  30.1 0.1 collective-permute-start.4
  30.1 2.7 %shard_map.117 = (bf16[64,1152]{1,0:T(8,128)(2,1)S(1)}, bf16[64,1152]{1,0:T(8,128)(2,1)S(1)}, bf16[64,1152]{1,0:T(8,128)(2,1)S(1)}, bf16[64,1152]{1,0:T(8,128)(2,1)S(1)}) custom-call(s32[2]{0:T(128)S(1)} %pad_add_fusion.place, s32[2,4]{1,0:T(2,128)S(1)} %bitcast.22, s32[3,2,4]{2,1,0:T(2,128)S(1)} %bitcast.18, bf16[4,576,256]{2,1,0:T(8,128)(2,1)S(1)} %bitcast.14, ...), custom_call_target="tpu_custom_call" | custom-call | tf_op jit(solution)/shard_map/pallas_call | solution.py:302
  32.9 0.0 collective-permute-done.5.ra_ref
  32.9 0.7 collective-permute-start.12
  33.5 0.1 collective-permute-start.17
  33.6 0.0 collective-permute-done.2.refs_1_
  33.6 1.5 %collective-permute-start.18 = (bf16[64,1152]{1,0:T(8,128)(2,1)S(1)}, bf16[64,1152]{1,0:T(8,128)(2,1)S(1)}, u32[]{:S(2)}, u32[]{:S(2)}) collective-permute-start(bf16[64,1152]{1,0:T(8,128)(2,1)S(1)} %get-tuple-element.59.refs_15_), channel_id=1, source_target_pairs={{0,8},{4,12},{8,0},{12,4},{1,9},{5,13},{9,1},{13,5},{2,10},{6,14},... | collective-permute-start | bytes 442376 | tf_op jit(solution)/shard_map/ppermute | solution.py:319
  35.1 0.3 collective-permute-start.19
  35.4 2.7 %shard_map.113 = (bf16[64,1152]{1,0:T(8,128)(2,1)S(1)}, bf16[64,1152]{1,0:T(8,128)(2,1)S(1)}, bf16[64,1152]{1,0:T(8,128)(2,1)S(1)}, bf16[64,1152]{1,0:T(8,128)(2,1)S(1)}) custom-call(s32[2]{0:T(128)S(1)} %pad_add_fusion.place, s32[2,4]{1,0:T(2,128)S(1)} %bitcast.23, s32[3,2,4]{2,1,0:T(2,128)S(1)} %bitcast.19, bf16[4,576,256]{2,1,0:T(8,128)(2,1)S(1)} %bitcast.15, ...), custom_call_target="tpu_custom_call" | custom-call | tf_op jit(solution)/shard_map/pallas_call | solution.py:302
  38.1 0.4 collective-permute-start.7
  38.5 1.5 %collective-permute-start.13 = (bf16[64,1152]{1,0:T(8,128)(2,1)S(1)}, bf16[64,1152]{1,0:T(8,128)(2,1)S(1)}, u32[]{:S(2)}, u32[]{:S(2)}) collective-permute-start(bf16[64,1152]{1,0:T(8,128)(2,1)S(1)} %get-tuple-element.53.refs_14_), channel_id=1, source_target_pairs={{0,8},{4,12},{8,0},{12,4},{1,9},{5,13},{9,1},{13,5},{2,10},{6,14},... | collective-permute-start | bytes 442376 | tf_op jit(solution)/shard_map/ppermute | solution.py:319
  40.1 0.0 collective-permute-done.17.refs_1_
  40.1 0.0 collective-permute-start.14
  40.1 0.3 collective-permute-done.18.refs_2_
  40.3 1.5 %collective-permute-start.8 = (bf16[64,1152]{1,0:T(8,128)(2,1)S(1)}, bf16[64,1152]{1,0:T(8,128)(2,1)S(1)}, u32[]{:S(2)}, u32[]{:S(2)}) collective-permute-start(bf16[64,1152]{1,0:T(8,128)(2,1)S(1)} %get-tuple-element.47.refs_13_), channel_id=1, source_target_pairs={{0,8},{4,12},{8,0},{12,4},{1,9},{5,13},{9,1},{13,5},{2,10},{6,14},... | collective-permute-start | bytes 442376 | tf_op jit(solution)/shard_map/ppermute | solution.py:319
  41.9 0.7 collective-permute-done.19.refs_3_
  42.5 1.9 %collective-permute-start.9 = (bf16[64,1152]{1,0:T(8,128)(2,1)S(1)}, bf16[64,1152]{1,0:T(8,128)(2,1)S(1)}, u32[]{:S(2)}, u32[]{:S(2)}) collective-permute-start(bf16[64,1152]{1,0:T(8,128)(2,1)S(1)} %get-tuple-element.48.refs_17_), channel_id=1, source_target_pairs={{0,12},{4,8},{8,4},{12,0},{1,13},{5,9},{9,5},{13,1},{2,14},{6,10},... | collective-permute-start | bytes 442376 | tf_op jit(solution)/shard_map/ppermute | solution.py:319
  44.4 1.4 %shard_map.111.refs_0_ = bf16[1728,256]{1,0:T(8,128)(2,1)S(1)} custom-call(bf16[64,1152]{1,0:T(8,128)(2,1)S(1)} %get-tuple-element.39.refs_0_.refs_4_, bf16[64,1152]{1,0:T(8,128)(2,1)S(1)} %collective-permute-done.2.refs_1_, bf16[64,1152]{1,0:T(8,128)(2,1)S(1)} %collective-permute-done.3.refs_2_, bf16[64,1152]{1,0:T(8,128)(2,1)S(1)} %collective-permute-done.4.refs_3_, ...), custom_call_target="tpu_custom_call" | custom-call | tf_op jit(solution)/shard_map/pallas_call | solution.py:321
  45.8 1.4 %shard_map.118.refs_3_ = bf16[1728,256]{1,0:T(8,128)(2,1)S(1)} custom-call(bf16[64,1152]{1,0:T(8,128)(2,1)S(1)} %get-tuple-element.57.refs_0_.refs_7_, bf16[64,1152]{1,0:T(8,128)(2,1)S(1)} %collective-permute-done.17.refs_1_, bf16[64,1152]{1,0:T(8,128)(2,1)S(1)} %collective-permute-done.18.refs_2_, bf16[64,1152]{1,0:T(8,128)(2,1)S(1)} %collective-permute-done.19.refs_3_, ...), custom_call_target="tpu_custom_call" | custom-call | tf_op jit(solution)/shard_map/pallas_call | solution.py:321
  47.2 0.0 collective-permute-done.13.refs_2_
  47.2 1.6 %collective-permute-done.14.refs_3_ = bf16[64,1152]{1,0:T(8,128)(2,1)S(1)} collective-permute-done((bf16[64,1152]{1,0:T(8,128)(2,1)S(1)}, bf16[64,1152]{1,0:T(8,128)(2,1)S(1)}, u32[]{:S(2)}, u32[]{:S(2)}) %collective-permute-start.14) | collective-permute-done | bytes 147488 | tf_op jit(solution)/shard_map/ppermute | solution.py:319
  48.9 1.4 %shard_map.116.refs_2_ = bf16[1728,256]{1,0:T(8,128)(2,1)S(1)} custom-call(bf16[64,1152]{1,0:T(8,128)(2,1)S(1)} %get-tuple-element.51.refs_0_.refs_6_, bf16[64,1152]{1,0:T(8,128)(2,1)S(1)} %collective-permute-done.12.refs_1_, bf16[64,1152]{1,0:T(8,128)(2,1)S(1)} %collective-permute-done.13.refs_2_, bf16[64,1152]{1,0:T(8,128)(2,1)S(1)} %collective-permute-done.14.refs_3_, ...), custom_call_target="tpu_custom_call" | custom-call | tf_op jit(solution)/shard_map/pallas_call | solution.py:321
  50.2 0.0 collective-permute-done.7.refs_1_
  50.3 2.7 %collective-permute-done.8.refs_2_ = bf16[64,1152]{1,0:T(8,128)(2,1)S(1)} collective-permute-done((bf16[64,1152]{1,0:T(8,128)(2,1)S(1)}, bf16[64,1152]{1,0:T(8,128)(2,1)S(1)}, u32[]{:S(2)}, u32[]{:S(2)}) %collective-permute-start.8) | collective-permute-done | bytes 147488 | tf_op jit(solution)/shard_map/ppermute | solution.py:319
  53.0 2.1 %collective-permute-done.9.refs_3_ = bf16[64,1152]{1,0:T(8,128)(2,1)S(1)} collective-permute-done((bf16[64,1152]{1,0:T(8,128)(2,1)S(1)}, bf16[64,1152]{1,0:T(8,128)(2,1)S(1)}, u32[]{:S(2)}, u32[]{:S(2)}) %collective-permute-start.9) | collective-permute-done | bytes 147488 | tf_op jit(solution)/shard_map/ppermute | solution.py:319
  55.1 1.4 %shard_map.114.refs_1_ = bf16[1728,256]{1,0:T(8,128)(2,1)S(1)} custom-call(bf16[64,1152]{1,0:T(8,128)(2,1)S(1)} %get-tuple-element.45.refs_0_.refs_5_, bf16[64,1152]{1,0:T(8,128)(2,1)S(1)} %collective-permute-done.7.refs_1_, bf16[64,1152]{1,0:T(8,128)(2,1)S(1)} %collective-permute-done.8.refs_2_, bf16[64,1152]{1,0:T(8,128)(2,1)S(1)} %collective-permute-done.9.refs_3_, ...), custom_call_target="tpu_custom_call" | custom-call | tf_op jit(solution)/shard_map/pallas_call | solution.py:321
  56.4 2.1 %shard_map.120 = (bf16[32,2304]{1,0:T(8,128)(2,1)S(1)}, bf16[32,2304]{1,0:T(8,128)(2,1)S(1)}, bf16[32,2304]{1,0:T(8,128)(2,1)S(1)}, bf16[32,2304]{1,0:T(8,128)(2,1)S(1)}) custom-call(bf16[1728,256]{1,0:T(8,128)(2,1)S(1)} %shard_map.111.refs_0_, bf16[1728,256]{1,0:T(8,128)(2,1)S(1)} %shard_map.114.refs_1_, bf16[1728,256]{1,0:T(8,128)(2,1)S(1)} %shard_map.116.refs_2_, ...), custom_call_target="tpu_custom_call" | custom-call | tf_op jit(solution)/shard_map/pallas_call | solution.py:334
  58.5 0.0 copy-start.8
  58.5 0.0 copy-start.4
  58.5 0.4 collective-permute-start.23
  59.0 1.9 %shard_map.119 = (bf16[32,2304]{1,0:T(8,128)(2,1)S(1)}, bf16[32,2304]{1,0:T(8,128)(2,1)S(1)}, bf16[32,2304]{1,0:T(8,128)(2,1)S(1)}, bf16[32,2304]{1,0:T(8,128)(2,1)S(1)}) custom-call(bf16[1728,256]{1,0:T(8,128)(2,1)S(1)} %shard_map.111.refs_0_, bf16[1728,256]{1,0:T(8,128)(2,1)S(1)} %shard_map.114.refs_1_, bf16[1728,256]{1,0:T(8,128)(2,1)S(1)} %shard_map.116.refs_2_, ...), custom_call_target="tpu_custom_call" | custom-call | tf_op jit(solution)/shard_map/pallas_call | solution.py:334
  60.9 1.6 %collective-permute-start.24 = (bf16[32,2304]{1,0:T(8,128)(2,1)S(1)}, bf16[32,2304]{1,0:T(8,128)(2,1)S(1)}, u32[]{:S(2)}, u32[]{:S(2)}) collective-permute-start(bf16[32,2304]{1,0:T(8,128)(2,1)S(1)} %get-tuple-element.67), channel_id=1, source_target_pairs={{8,0},{12,4},{0,8},{4,12},{9,1},{13,5},{1,9},{5,13},{10,2},{14,6},... | collective-permute-start | bytes 442376 | tf_op jit(solution)/shard_map/ppermute | solution.py:344
  62.4 0.6 collective-permute-start.20
  63.1 1.5 %collective-permute-start.21 = (bf16[32,2304]{1,0:T(8,128)(2,1)S(1)}, bf16[32,2304]{1,0:T(8,128)(2,1)S(1)}, u32[]{:S(2)}, u32[]{:S(2)}) collective-permute-start(bf16[32,2304]{1,0:T(8,128)(2,1)S(1)} %get-tuple-element.63), channel_id=1, source_target_pairs={{8,0},{12,4},{0,8},{4,12},{9,1},{13,5},{1,9},{5,13},{10,2},{14,6},... | collective-permute-start | bytes 442376 | tf_op jit(solution)/shard_map/ppermute | solution.py:344
  64.6 0.0 collective-permute-done.23.refs_1_
  64.6 0.0 collective-permute-start.22
  64.6 3.0 %collective-permute-done.24.refs_2_ = bf16[32,2304]{1,0:T(8,128)(2,1)S(1)} collective-permute-done((bf16[32,2304]{1,0:T(8,128)(2,1)S(1)}, bf16[32,2304]{1,0:T(8,128)(2,1)S(1)}, u32[]{:S(2)}, u32[]{:S(2)}) %collective-permute-start.24) | collective-permute-done | bytes 147488 | tf_op jit(solution)/shard_map/ppermute | solution.py:344
  67.6 2.2 %collective-permute-done.25.refs_3_ = bf16[32,2304]{1,0:T(8,128)(2,1)S(1)} collective-permute-done((bf16[32,2304]{1,0:T(8,128)(2,1)S(1)}, bf16[32,2304]{1,0:T(8,128)(2,1)S(1)}, u32[]{:S(2)}, u32[]{:S(2)}) %collective-permute-start.25) | collective-permute-done | bytes 147488 | tf_op jit(solution)/shard_map/ppermute | solution.py:344
  69.8 2.8 %shard_map.121.refs_22_ = bf16[4,256,1152]{2,1,0:T(8,128)(2,1)} custom-call(s32[2]{0:T(128)S(1)} %pad_add_fusion.place, bf16[32,2304]{1,0:T(8,128)(2,1)S(1)} %get-tuple-element.65.refs_0_, bf16[32,2304]{1,0:T(8,128)(2,1)S(1)} %collective-permute-done.23.refs_1_, bf16[32,2304]{1,0:T(8,128)(2,1)S(1)} %collective-permute-done.24.refs_2_, ...), custom_call_target="tpu_custom_call" | custom-call | tf_op jit(solution)/shard_map/pallas_call | solution.py:353
  72.6 0.0 collective-permute-done.20.refs_1_
  72.6 1.3 %collective-permute-done.21.refs_2_ = bf16[32,2304]{1,0:T(8,128)(2,1)S(1)} collective-permute-done((bf16[32,2304]{1,0:T(8,128)(2,1)S(1)}, bf16[32,2304]{1,0:T(8,128)(2,1)S(1)}, u32[]{:S(2)}, u32[]{:S(2)}) %collective-permute-start.21) | collective-permute-done | bytes 147488 | tf_op jit(solution)/shard_map/ppermute | solution.py:344
  74.0 1.5 %collective-permute-done.22.refs_3_ = bf16[32,2304]{1,0:T(8,128)(2,1)S(1)} collective-permute-done((bf16[32,2304]{1,0:T(8,128)(2,1)S(1)}, bf16[32,2304]{1,0:T(8,128)(2,1)S(1)}, u32[]{:S(2)}, u32[]{:S(2)}) %collective-permute-start.22) | collective-permute-done | bytes 147488 | tf_op jit(solution)/shard_map/ppermute | solution.py:344
  75.4 2.8 %shard_map.122 = bf16[4,256,1152]{2,1,0:T(8,128)(2,1)} custom-call(s32[2]{0:T(128)S(1)} %pad_add_fusion.place, bf16[32,2304]{1,0:T(8,128)(2,1)S(1)} %get-tuple-element.61.refs_0_, bf16[32,2304]{1,0:T(8,128)(2,1)S(1)} %collective-permute-done.20.refs_1_, bf16[32,2304]{1,0:T(8,128)(2,1)S(1)} %collective-permute-done.21.refs_2_, ...), custom_call_target="tpu_custom_call", output_to_operand_aliasing={{}: (23, {})} | custom-call | tf_op jit(solution)/shard_map/pallas_call | solution.py:353
  (23 shorter events, 0.1 us)
Async XLA Ops:
  1.3 12.4 %collective-permute-start = (bf16[1152,128]{1,0:T(8,128)(2,1)S(1)}, bf16[1152,128]{1,0:T(8,128)(2,1)S(1)}, u32[]{:S(2)}, u32[]{:S(2)}) collective-permute-start(bf16[1152,128]{1,0:T(8,128)(2,1)S(1)} %get-tuple-element.37.a_ref), channel_id=1, source_target_pairs={{0,1},{1,0},{2,3},{3,2},{4,5},{5,4},{6,7},{7,6},{8,9},{9,8},{10,11... | collective-permute-start | bytes 884744 | tf_op jit(solution)/shard_map/ppermute | solution.py:297
  4.4 15.8 %copy-start.7 = (f32[1152]{0:T(1024)S(1)}, f32[1152]{0:T(1024)}, u32[]{:S(2)}) copy-start(f32[1152]{0:T(1024)} %param.16) | copy-start | bytes 13828
  4.4 15.8 %copy-start.2 = (bf16[576,1152]{1,0:T(8,128)(2,1)S(1)}, bf16[576,1152]{1,0:T(8,128)(2,1)}, u32[]{:S(2)}) copy-start(bf16[576,1152]{1,0:T(8,128)(2,1)} %w_ref.7) | copy-start | bytes 3981316
  4.4 15.8 %copy-start.3 = (bf16[4,256,576]{1,2,0:T(8,128)(2,1)S(1)}, bf16[4,256,576]{1,2,0:T(8,128)(2,1)}, u32[]{:S(2)}) copy-start(bf16[4,256,576]{1,2,0:T(8,128)(2,1)} %param.11) | copy-start | bytes 3538948
  4.4 15.8 %copy-start.5 = (s32[4,2,3]{0,1,2:T(2,128)S(1)}, s32[4,2,3]{0,1,2:T(2,128)}, u32[]{:S(2)}) copy-start(s32[4,2,3]{0,1,2:T(2,128)} %param.20) | copy-start | bytes 292
  4.4 15.8 %copy-start.6 = (s32[4,2]{0,1:T(2,128)S(1)}, s32[4,2]{0,1:T(2,128)}, u32[]{:S(2)}) copy-start(s32[4,2]{0,1:T(2,128)} %param.21) | copy-start | bytes 100
  4.4 9.9 %collective-permute-start.1 = (bf16[1152,128]{1,0:T(8,128)(2,1)S(1)}, bf16[1152,128]{1,0:T(8,128)(2,1)S(1)}, u32[]{:S(2)}, u32[]{:S(2)}) collective-permute-start(bf16[1152,128]{1,0:T(8,128)(2,1)S(1)} %get-tuple-element.38.b_ref), channel_id=1, source_target_pairs={{1,2},{2,1},{5,6},{6,5},{9,10},{10,9},{13,14},{14,13},{17,18},{18,... | collective-permute-start | bytes 884744 | tf_op jit(solution)/shard_map/ppermute | solution.py:297
  5.2 15.0 %copy-start.1 = (bf16[4,256,1152]{2,1,0:T(8,128)(2,1)S(1)}, bf16[4,256,1152]{2,1,0:T(8,128)(2,1)}, u32[]{:S(2)}) copy-start(bf16[4,256,1152]{2,1,0:T(8,128)(2,1)} %h_ref.7) | copy-start | bytes 7077892
  7.2 12.3 %collective-permute-start.10 = (bf16[1152,128]{1,0:T(8,128)(2,1)S(1)}, bf16[1152,128]{1,0:T(8,128)(2,1)S(1)}, u32[]{:S(2)}, u32[]{:S(2)}) collective-permute-start(bf16[1152,128]{1,0:T(8,128)(2,1)S(1)} %get-tuple-element.49.a_ref), channel_id=1, source_target_pairs={{0,1},{1,0},{2,3},{3,2},{4,5},{5,4},{6,7},{7,6},{8,9},{9,8},{10,11... | collective-permute-start | bytes 884744 | tf_op jit(solution)/shard_map/ppermute | solution.py:297
  11.7 11.3 %collective-permute-start.11 = (bf16[1152,128]{1,0:T(8,128)(2,1)S(1)}, bf16[1152,128]{1,0:T(8,128)(2,1)S(1)}, u32[]{:S(2)}, u32[]{:S(2)}) collective-permute-start(bf16[1152,128]{1,0:T(8,128)(2,1)S(1)} %get-tuple-element.50.b_ref), channel_id=1, source_target_pairs={{1,2},{2,1},{5,6},{6,5},{9,10},{10,9},{13,14},{14,13},{17,18},{18,... | collective-permute-start | bytes 884744 | tf_op jit(solution)/shard_map/ppermute | solution.py:297
  12.3 13.5 %collective-permute-start.15 = (bf16[1152,128]{1,0:T(8,128)(2,1)S(1)}, bf16[1152,128]{1,0:T(8,128)(2,1)S(1)}, u32[]{:S(2)}, u32[]{:S(2)}) collective-permute-start(bf16[1152,128]{1,0:T(8,128)(2,1)S(1)} %get-tuple-element.55.a_ref), channel_id=1, source_target_pairs={{0,1},{1,0},{2,3},{3,2},{4,5},{5,4},{6,7},{7,6},{8,9},{9,8},{10,11... | collective-permute-start | bytes 884744 | tf_op jit(solution)/shard_map/ppermute | solution.py:297
  13.7 16.4 %collective-permute-start.16 = (bf16[1152,128]{1,0:T(8,128)(2,1)S(1)}, bf16[1152,128]{1,0:T(8,128)(2,1)S(1)}, u32[]{:S(2)}, u32[]{:S(2)}) collective-permute-start(bf16[1152,128]{1,0:T(8,128)(2,1)S(1)} %get-tuple-element.56.b_ref), channel_id=1, source_target_pairs={{1,2},{2,1},{5,6},{6,5},{9,10},{10,9},{13,14},{14,13},{17,18},{18,... | collective-permute-start | bytes 884744 | tf_op jit(solution)/shard_map/ppermute | solution.py:297
  14.3 18.5 %collective-permute-start.5 = (bf16[1152,128]{1,0:T(8,128)(2,1)S(1)}, bf16[1152,128]{1,0:T(8,128)(2,1)S(1)}, u32[]{:S(2)}, u32[]{:S(2)}) collective-permute-start(bf16[1152,128]{1,0:T(8,128)(2,1)S(1)} %get-tuple-element.43.a_ref), channel_id=1, source_target_pairs={{0,1},{1,0},{2,3},{3,2},{4,5},{5,4},{6,7},{7,6},{8,9},{9,8},{10,11... | collective-permute-start | bytes 884744 | tf_op jit(solution)/shard_map/ppermute | solution.py:297
  19.5 14.0 %collective-permute-start.6 = (bf16[1152,128]{1,0:T(8,128)(2,1)S(1)}, bf16[1152,128]{1,0:T(8,128)(2,1)S(1)}, u32[]{:S(2)}, u32[]{:S(2)}) collective-permute-start(bf16[1152,128]{1,0:T(8,128)(2,1)S(1)} %get-tuple-element.44.b_ref), channel_id=1, source_target_pairs={{1,2},{2,1},{5,6},{6,5},{9,10},{10,9},{13,14},{14,13},{17,18},{18,... | collective-permute-start | bytes 884744 | tf_op jit(solution)/shard_map/ppermute | solution.py:297
  23.0 10.6 %collective-permute-start.2 = (bf16[64,1152]{1,0:T(8,128)(2,1)S(1)}, bf16[64,1152]{1,0:T(8,128)(2,1)S(1)}, u32[]{:S(2)}, u32[]{:S(2)}) collective-permute-start(bf16[64,1152]{1,0:T(8,128)(2,1)S(1)} %get-tuple-element.40.refs_8_), channel_id=1, source_target_pairs={{0,4},{4,0},{8,12},{12,8},{1,5},{5,1},{9,13},{13,9},{2,6},{6,2},{1... | collective-permute-start | bytes 442376 | tf_op jit(solution)/shard_map/ppermute | solution.py:319
  25.8 9.3 %collective-permute-start.3 = (bf16[64,1152]{1,0:T(8,128)(2,1)S(1)}, bf16[64,1152]{1,0:T(8,128)(2,1)S(1)}, u32[]{:S(2)}, u32[]{:S(2)}) collective-permute-start(bf16[64,1152]{1,0:T(8,128)(2,1)S(1)} %get-tuple-element.41.refs_12_), channel_id=1, source_target_pairs={{0,8},{4,12},{8,0},{12,4},{1,9},{5,13},{9,1},{13,5},{2,10},{6,14},... | collective-permute-start | bytes 442376 | tf_op jit(solution)/shard_map/ppermute | solution.py:319
  30.1 8.0 %collective-permute-start.4 = (bf16[64,1152]{1,0:T(8,128)(2,1)S(1)}, bf16[64,1152]{1,0:T(8,128)(2,1)S(1)}, u32[]{:S(2)}, u32[]{:S(2)}) collective-permute-start(bf16[64,1152]{1,0:T(8,128)(2,1)S(1)} %get-tuple-element.42.refs_16_), channel_id=1, source_target_pairs={{0,12},{4,8},{8,4},{12,0},{1,13},{5,9},{9,5},{13,1},{2,14},{6,10},... | collective-permute-start | bytes 442376 | tf_op jit(solution)/shard_map/ppermute | solution.py:319
  32.9 5.7 %collective-permute-start.12 = (bf16[64,1152]{1,0:T(8,128)(2,1)S(1)}, bf16[64,1152]{1,0:T(8,128)(2,1)S(1)}, u32[]{:S(2)}, u32[]{:S(2)}) collective-permute-start(bf16[64,1152]{1,0:T(8,128)(2,1)S(1)} %get-tuple-element.52.refs_10_), channel_id=1, source_target_pairs={{0,4},{4,0},{8,12},{12,8},{1,5},{5,1},{9,13},{13,9},{2,6},{6,2},{1... | collective-permute-start | bytes 442376 | tf_op jit(solution)/shard_map/ppermute | solution.py:319
  33.5 6.5 %collective-permute-start.17 = (bf16[64,1152]{1,0:T(8,128)(2,1)S(1)}, bf16[64,1152]{1,0:T(8,128)(2,1)S(1)}, u32[]{:S(2)}, u32[]{:S(2)}) collective-permute-start(bf16[64,1152]{1,0:T(8,128)(2,1)S(1)} %get-tuple-element.58.refs_11_), channel_id=1, source_target_pairs={{0,4},{4,0},{8,12},{12,8},{1,5},{5,1},{9,13},{13,9},{2,6},{6,2},{1... | collective-permute-start | bytes 442376 | tf_op jit(solution)/shard_map/ppermute | solution.py:319
  33.6 6.7 %collective-permute-start.18 = (bf16[64,1152]{1,0:T(8,128)(2,1)S(1)}, bf16[64,1152]{1,0:T(8,128)(2,1)S(1)}, u32[]{:S(2)}, u32[]{:S(2)}) collective-permute-start(bf16[64,1152]{1,0:T(8,128)(2,1)S(1)} %get-tuple-element.59.refs_15_), channel_id=1, source_target_pairs={{0,8},{4,12},{8,0},{12,4},{1,9},{5,13},{9,1},{13,5},{2,10},{6,14},... | collective-permute-start | bytes 442376 | tf_op jit(solution)/shard_map/ppermute | solution.py:319
  35.1 7.4 %collective-permute-start.19 = (bf16[64,1152]{1,0:T(8,128)(2,1)S(1)}, bf16[64,1152]{1,0:T(8,128)(2,1)S(1)}, u32[]{:S(2)}, u32[]{:S(2)}) collective-permute-start(bf16[64,1152]{1,0:T(8,128)(2,1)S(1)} %get-tuple-element.60.refs_19_), channel_id=1, source_target_pairs={{0,12},{4,8},{8,4},{12,0},{1,13},{5,9},{9,5},{13,1},{2,14},{6,10},... | collective-permute-start | bytes 442376 | tf_op jit(solution)/shard_map/ppermute | solution.py:319
  35.4 9.0 %copy-start = (bf16[1152,1728]{0,1:T(8,128)(2,1)S(1)}, bf16[1152,1728]{0,1:T(8,128)(2,1)}, u32[]{:S(2)}) copy-start(bf16[1152,1728]{0,1:T(8,128)(2,1)} %param.17) | copy-start | bytes 11943940
  38.1 12.1 %collective-permute-start.7 = (bf16[64,1152]{1,0:T(8,128)(2,1)S(1)}, bf16[64,1152]{1,0:T(8,128)(2,1)S(1)}, u32[]{:S(2)}, u32[]{:S(2)}) collective-permute-start(bf16[64,1152]{1,0:T(8,128)(2,1)S(1)} %get-tuple-element.46.refs_9_), channel_id=1, source_target_pairs={{0,4},{4,0},{8,12},{12,8},{1,5},{5,1},{9,13},{13,9},{2,6},{6,2},{1... | collective-permute-start | bytes 442376 | tf_op jit(solution)/shard_map/ppermute | solution.py:319
  38.5 8.7 %collective-permute-start.13 = (bf16[64,1152]{1,0:T(8,128)(2,1)S(1)}, bf16[64,1152]{1,0:T(8,128)(2,1)S(1)}, u32[]{:S(2)}, u32[]{:S(2)}) collective-permute-start(bf16[64,1152]{1,0:T(8,128)(2,1)S(1)} %get-tuple-element.53.refs_14_), channel_id=1, source_target_pairs={{0,8},{4,12},{8,0},{12,4},{1,9},{5,13},{9,1},{13,5},{2,10},{6,14},... | collective-permute-start | bytes 442376 | tf_op jit(solution)/shard_map/ppermute | solution.py:319
  40.1 8.8 %collective-permute-start.14 = (bf16[64,1152]{1,0:T(8,128)(2,1)S(1)}, bf16[64,1152]{1,0:T(8,128)(2,1)S(1)}, u32[]{:S(2)}, u32[]{:S(2)}) collective-permute-start(bf16[64,1152]{1,0:T(8,128)(2,1)S(1)} %get-tuple-element.54.refs_18_), channel_id=1, source_target_pairs={{0,12},{4,8},{8,4},{12,0},{1,13},{5,9},{9,5},{13,1},{2,14},{6,10},... | collective-permute-start | bytes 442376 | tf_op jit(solution)/shard_map/ppermute | solution.py:319
  40.3 12.6 %collective-permute-start.8 = (bf16[64,1152]{1,0:T(8,128)(2,1)S(1)}, bf16[64,1152]{1,0:T(8,128)(2,1)S(1)}, u32[]{:S(2)}, u32[]{:S(2)}) collective-permute-start(bf16[64,1152]{1,0:T(8,128)(2,1)S(1)} %get-tuple-element.47.refs_13_), channel_id=1, source_target_pairs={{0,8},{4,12},{8,0},{12,4},{1,9},{5,13},{9,1},{13,5},{2,10},{6,14},... | collective-permute-start | bytes 442376 | tf_op jit(solution)/shard_map/ppermute | solution.py:319
  42.5 12.5 %collective-permute-start.9 = (bf16[64,1152]{1,0:T(8,128)(2,1)S(1)}, bf16[64,1152]{1,0:T(8,128)(2,1)S(1)}, u32[]{:S(2)}, u32[]{:S(2)}) collective-permute-start(bf16[64,1152]{1,0:T(8,128)(2,1)S(1)} %get-tuple-element.48.refs_17_), channel_id=1, source_target_pairs={{0,12},{4,8},{8,4},{12,0},{1,13},{5,9},{9,5},{13,1},{2,14},{6,10},... | collective-permute-start | bytes 442376 | tf_op jit(solution)/shard_map/ppermute | solution.py:319
  58.5 6.1 %copy-start.8 = (f32[1152]{0:T(1024)S(1)}, f32[1152]{0:T(1024)}, u32[]{:S(2)}) copy-start(f32[1152]{0:T(1024)} %param.19) | copy-start | bytes 13828
  58.5 11.3 %copy-start.4 = (bf16[576,1152]{1,0:T(8,128)(2,1)S(1)}, bf16[576,1152]{1,0:T(8,128)(2,1)}, u32[]{:S(2)}) copy-start(bf16[576,1152]{1,0:T(8,128)(2,1)} %refs_20_.3) | copy-start | bytes 3981316
  58.5 6.0 %collective-permute-start.23 = (bf16[32,2304]{1,0:T(8,128)(2,1)S(1)}, bf16[32,2304]{1,0:T(8,128)(2,1)S(1)}, u32[]{:S(2)}, u32[]{:S(2)}) collective-permute-start(bf16[32,2304]{1,0:T(8,128)(2,1)S(1)} %get-tuple-element.66), channel_id=1, source_target_pairs={{4,0},{0,4},{12,8},{8,12},{5,1},{1,5},{13,9},{9,13},{6,2},{2,6},{1... | collective-permute-start | bytes 442376 | tf_op jit(solution)/shard_map/ppermute | solution.py:344
  60.9 6.8 %collective-permute-start.24 = (bf16[32,2304]{1,0:T(8,128)(2,1)S(1)}, bf16[32,2304]{1,0:T(8,128)(2,1)S(1)}, u32[]{:S(2)}, u32[]{:S(2)}) collective-permute-start(bf16[32,2304]{1,0:T(8,128)(2,1)S(1)} %get-tuple-element.67), channel_id=1, source_target_pairs={{8,0},{12,4},{0,8},{4,12},{9,1},{13,5},{1,9},{5,13},{10,2},{14,6},... | collective-permute-start | bytes 442376 | tf_op jit(solution)/shard_map/ppermute | solution.py:344
  62.4 7.4 %collective-permute-start.25 = (bf16[32,2304]{1,0:T(8,128)(2,1)S(1)}, bf16[32,2304]{1,0:T(8,128)(2,1)S(1)}, u32[]{:S(2)}, u32[]{:S(2)}) collective-permute-start(bf16[32,2304]{1,0:T(8,128)(2,1)S(1)} %get-tuple-element.68), channel_id=1, source_target_pairs={{12,0},{8,4},{4,8},{0,12},{13,1},{9,5},{5,9},{1,13},{14,2},{10,6},... | collective-permute-start | bytes 442376 | tf_op jit(solution)/shard_map/ppermute | solution.py:344
  62.4 10.2 %collective-permute-start.20 = (bf16[32,2304]{1,0:T(8,128)(2,1)S(1)}, bf16[32,2304]{1,0:T(8,128)(2,1)S(1)}, u32[]{:S(2)}, u32[]{:S(2)}) collective-permute-start(bf16[32,2304]{1,0:T(8,128)(2,1)S(1)} %get-tuple-element.62), channel_id=1, source_target_pairs={{4,0},{0,4},{12,8},{8,12},{5,1},{1,5},{13,9},{9,13},{6,2},{2,6},{1... | collective-permute-start | bytes 442376 | tf_op jit(solution)/shard_map/ppermute | solution.py:344
  63.1 10.9 %collective-permute-start.21 = (bf16[32,2304]{1,0:T(8,128)(2,1)S(1)}, bf16[32,2304]{1,0:T(8,128)(2,1)S(1)}, u32[]{:S(2)}, u32[]{:S(2)}) collective-permute-start(bf16[32,2304]{1,0:T(8,128)(2,1)S(1)} %get-tuple-element.63), channel_id=1, source_target_pairs={{8,0},{12,4},{0,8},{4,12},{9,1},{13,5},{1,9},{5,13},{10,2},{14,6},... | collective-permute-start | bytes 442376 | tf_op jit(solution)/shard_map/ppermute | solution.py:344
  64.6 10.9 %collective-permute-start.22 = (bf16[32,2304]{1,0:T(8,128)(2,1)S(1)}, bf16[32,2304]{1,0:T(8,128)(2,1)S(1)}, u32[]{:S(2)}, u32[]{:S(2)}) collective-permute-start(bf16[32,2304]{1,0:T(8,128)(2,1)S(1)} %get-tuple-element.64), channel_id=1, source_target_pairs={{12,0},{8,4},{4,8},{0,12},{13,1},{9,5},{5,9},{1,13},{14,2},{10,6},... | collective-permute-start | bytes 442376 | tf_op jit(solution)/shard_map/ppermute | solution.py:344
where the time goes:
time: 78.8 us; the launch traced here: 78.4 us
  Pallas kernels  29 us (37%)
  starting transfers between devices  28.8 us (37%)
  waiting for transfers between devices  20 us (25%)
    ppermute x4, starting transfers between devices, shards(): lax.ppermute(a, 'strip', near)  12.2 us
    pallas_call x4, Pallas kernels, shards(): call(functools.partial(spatial_kernel, f, groups), [smem, smem, smem, fra...  10.8 us
    ppermute x12, starting transfers between devices, shards(): lax.ppermute(parts[j], 'frame', pairs)  9.57 us
    ppermute x6, waiting for transfers between devices, shards(): got.append(back[j] if j == 0 else lax.ppermute(back[j], 'frame', pairs))  8.04 us
    ppermute x12, waiting for transfers between devices, shards(): lax.ppermute(parts[j], 'frame', pairs)  7.4 us
    pallas_call x2, Pallas kernels, shards(): call(functools.partial(output_kernel, groups, frames, half, halves, len(e...  5.59 us
    pallas_call x4, Pallas kernels, shards(): call(functools.partial(project_kernel, f, frames), [whole((share, model))...  5.49 us
    ppermute x4, waiting for transfers between devices, shards(): lax.ppermute(a, 'strip', near)  4.59 us
  transfers between devices with their start and end apart: 26, of which 11 were waited for; matrix products, arithmetic and copies ran while one was open for 0% of the time, Pallas kernels for 27%

commit v1 on v0

v1 whole, which is shorter than its diff:
```python
import functools
import math

import jax
import jax.numpy as jnp
from jax import lax
from jax.experimental import pallas as pl
from jax.experimental.pallas import tpu as pltpu
from jax.sharding import PartitionSpec as P


HEAD_DIM = 72
TILE = 128
MAXT = 3
SUB = 16
EPS = 1e-06
EXP2_SCALE = HEAD_DIM ** -0.5 * math.log2(math.e)

BF = jnp.bfloat16
F32 = jnp.float32


def peer(i, j, n):
    return i ^ j if n & (n - 1) == 0 else (i + j) % n


def vmem(limit):
    return pltpu.CompilerParams(vmem_limit_bytes=limit << 20)


def whole(shape):
    return pl.BlockSpec(shape, lambda *_: (0,) * len(shape))


def contract(a, b, da, db):
    return lax.dot_general(a, b, (((da,), (db,)), ((), ())), preferred_element_type=F32)


def head_scale(x):
    return lax.rsqrt(jnp.mean(x * x, axis=0, keepdims=True) + EPS)


def head(h, base=0):
    return slice(base + h * HEAD_DIM, base + (h + 1) * HEAD_DIM)


def pipeline(steps, scores, weigh, gather):
    ahead, behind = scores(*steps[0]), None
    for n, step in enumerate(steps):
        now = ahead
        if n + 1 < len(steps):
            ahead = scores(*steps[n + 1])
        weighed = weigh(now)
        if behind is not None:
            gather(*steps[n - 1], *behind)
        behind = weighed
    gather(*steps[-1], *behind)


def prep_kernel(place, k_ref, v_ref, a_ref, b_ref):
    n, width, _ = k_ref.shape
    even = place[1] % 2 == 0

    def fill(first, second):
        for f in range(n):
            for h in range(width // HEAD_DIM):
                x = k_ref[f, head(h), :].astype(F32)
                y = (x * head_scale(x)).astype(BF)
                first[f, head(h), :] = y[:, :TILE]
                second[f, head(h), :] = y[:, TILE:]
            first[f, width:, :] = v_ref[f, :, :TILE]
            second[f, width:, :] = v_ref[f, :, TILE:]

    pl.when(even)(functools.partial(fill, b_ref, a_ref))
    pl.when(jnp.logical_not(even))(functools.partial(fill, a_ref, b_ref))


def split_kernel(place, *refs):
    n = len(refs) // 2
    for src, dst in zip(refs[:n], refs[n:]):
        dst[...] = src[...]


def attend(frame, place, counts, lists, q_ref, keys, att):
    n, width, tokens = q_ref.shape
    tiles = tokens // TILE
    strip = place[1]
    odd = strip % 2
    first = strip * tiles
    places = (first + 1 - odd, first + odd, first + 2 - 3 * odd, first - 1 + 3 * odd)
    masks = []
    for f in range(n):
        table = []
        for t in range(tiles):
            live = counts[t, frame + f]
            cells = []
            for spot in places:
                hit = jnp.bool_(False)
                for j in range(MAXT):
                    hit = hit | ((lists[j, t, frame + f] == spot) & (j < live))
                cells.append(jnp.where(hit, 1.0, 0.0).astype(F32))
            table.append(cells)
        masks.append(table)

    def scores(f, h):
        q = q_ref[f, head(h), :].astype(F32)
        qn = (q * head_scale(q)).astype(BF)
        return f, [contract(ref[f, head(h), :], qn, 0, 0) for ref in keys]

    def weigh(scored):
        f, s = scored
        partial, packed = [], []
        for i, x in enumerate(s):
            p = jnp.exp2(x * EXP2_SCALE)
            p = jnp.concatenate(
                [p[:, t * TILE:(t + 1) * TILE] * masks[f][t][i] for t in range(tiles)], axis=1
            )
            partial.append(jnp.sum(p.reshape(TILE // 8, 8, tokens), axis=0))
            packed.append(p.astype(BF))
        halves = [jnp.concatenate(packed[i:i + 2], axis=0) for i in (0, 2)]
        return jnp.sum(sum(partial), axis=0, keepdims=True), halves

    def gather(f, h, total, halves):
        o = 0
        for i in range(2):
            v = jnp.concatenate([r[f, head(h, width), :] for r in keys[2 * i:2 * i + 2]], axis=1)
            o += contract(v, halves[i], 1, 0)
        att[f, head(h), :] = (o / total).astype(att.dtype)

    pipeline([(f, h) for f in range(n) for h in range(width // HEAD_DIM)], scores, weigh, gather)


def add_normed(base, proj, gain):
    scale = lax.rsqrt(jnp.mean(proj * proj, axis=-1, keepdims=True) + EPS)
    return (base.astype(F32) + proj * scale * gain).astype(BF)


def spatial_kernel(frame, n_groups, place, counts, lists, q_ref, a_ref, b_ref, ra_ref, rb_ref, h_ref, w_ref, g_ref, *rest):
    outs, (att, mix) = rest[:n_groups], rest[n_groups:]
    attend(frame, place, counts, lists, q_ref, (a_ref, b_ref, ra_ref, rb_ref), att)
    mix[...] = add_normed(h_ref[0], contract(att[0], w_ref[...], 0, 0), g_ref[...])
    share = mix.shape[0] // n_groups
    for j, out in enumerate(outs):
        group = peer(place[0], j, n_groups)
        out[...] = mix[pl.ds(pl.multiple_of(group * share, SUB), share), :]


def late_kernel(frame, n_groups, halves, place, counts, lists, q_ref, a_ref, b_ref, ra_ref, rb_ref, *rest):
    outs, (att, rows) = rest[:n_groups * halves], rest[n_groups * halves:]
    n, width, tokens = q_ref.shape
    attend(frame, place, counts, lists, q_ref, (a_ref, b_ref, ra_ref, rb_ref), att)
    for f in range(n):
        rows[:, f * width:(f + 1) * width] = att[f].T.astype(BF)
    size = tokens // n_groups // halves
    for half in range(halves):
        for j in range(n_groups):
            start = (peer(place[0], j, n_groups) * halves + half) * size
            outs[half * n_groups + j][...] = rows[pl.ds(pl.multiple_of(start, SUB), size), :]


def mix_kernel(*refs):
    atts, hids = refs[:len(refs) // 2 - 1], refs[len(refs) // 2 - 1:-3]
    w_ref, g_ref, out = refs[-3:]
    width = w_ref.shape[0]
    n, rows, _ = hids[0].shape
    for j, (att, hid) in enumerate(zip(atts, hids)):
        x = jnp.concatenate([att[:, f * width:(f + 1) * width] for f in range(n)], axis=0)
        proj = contract(x, w_ref[...], 1, 0)
        for f in range(n):
            out[j, f] = add_normed(hid[f], proj[f * rows:(f + 1) * rows, :], g_ref[...])


def paired(chunks, lanes, frames):
    return chunks % 2 == 0 and frames % 2 == 0 and 2 * lanes == TILE


def slot(c, frame, chunks, n_groups, frames):
    return c ^ (frame & 1) if paired(chunks, n_groups * SUB, frames) else c


def project(w_ref, x, out):
    width = w_ref.shape[0] // 3
    cut = w_ref.shape[0] // 2
    heads = width // HEAD_DIM
    parts = [contract(w_ref[i * cut:(i + 1) * cut, :], x[...], 1, 1) for i in range(2)]
    for h in range(3 * heads):
        i, at = divmod(h * HEAD_DIM, cut)
        y = parts[i][at:at + HEAD_DIM, :]
        if h < 2 * heads:
            y = y * head_scale(y)
        out[head(h), :] = y.astype(BF)


def project_kernel(frame, frames, *refs):
    pieces, w_ref, out, x = refs[:-3], refs[-3], refs[-2], refs[-1]
    n_groups = len(pieces)
    chunks = pieces[0].shape[0] // SUB
    for c in range(chunks):
        for j, piece in enumerate(pieces):
            at = (slot(c, frame, chunks, n_groups, frames) * n_groups + j) * SUB
            x[at:at + SUB, :] = piece[c * SUB:(c + 1) * SUB, :]
    project(w_ref, x, out)


def late_project_kernel(frame, frames, *refs):
    n_groups = (len(refs) - 7) // 2
    atts, hids = refs[:n_groups], refs[n_groups:2 * n_groups]
    w_ref, g_ref, qkv_ref, out, a, b, x = refs[2 * n_groups:]
    width = w_ref.shape[0]
    n, rows, _ = hids[0].shape
    chunks = rows // SUB
    for f in range(n):
        for c in range(chunks):
            for j in range(n_groups):
                at = ((f * chunks + slot(c, frame + f, chunks, n_groups, frames)) * n_groups + j) * SUB
                piece = slice(c * SUB, (c + 1) * SUB)
                a[at:at + SUB, :] = atts[j][piece, f * width:(f + 1) * width]
                b[at:at + SUB, :] = hids[j][f, piece, :]
    x[...] = add_normed(b[...], contract(a[...], w_ref[...], 1, 0), g_ref[...])
    project(qkv_ref, x, out)


def temporal_kernel(n_groups, *refs):
    frames = len(refs) - n_groups - 1
    ins, outs, att = refs[:frames], refs[frames:frames + n_groups], refs[-1]
    lanes = n_groups * SUB
    chunks = ins[0].shape[1] // lanes
    width = ins[0].shape[0] // 3
    rows = frames * lanes
    pair = paired(chunks, lanes, frames)
    row_pos = lax.broadcasted_iota(jnp.int32, (rows, rows), 0) % SUB
    col_pos = lax.broadcasted_iota(jnp.int32, (rows, rows), 1) % SUB
    same = jnp.where(row_pos == col_pos, 1.0, 0.0).astype(F32)
    low = lax.broadcasted_iota(jnp.int32, (HEAD_DIM, TILE), 1) < lanes

    def take(c, where):
        if not pair:
            return jnp.concatenate([r[where, c * lanes:(c + 1) * lanes] for r in ins], axis=1)
        tile = slice(c // 2 * TILE, (c // 2 + 1) * TILE)
        got = [r[where, tile] for r in ins]
        return jnp.concatenate(
            [
                jnp.where(low, got[m + (c & 1)], got[m + 1 - (c & 1)])
                for m in range(0, frames, 2)
            ],
            axis=1,
        )

    def scores(c, h):
        return contract(take(c, head(h, width)), take(c, head(h)), 0, 0)

    def weigh(s):
        p = jnp.exp2(s * EXP2_SCALE) * same
        return jnp.sum(p, axis=0, keepdims=True), p.astype(BF)

    def gather(c, h, total, p):
        att[c, head(h), :] = contract(take(c, head(h, 2 * width)), p, 1, 0) / total

    steps = [(c, h) for c in range(chunks) for h in range(width // HEAD_DIM)]
    pipeline(steps, scores, weigh, gather)
    turned = [att[c].T.astype(BF) for c in range(chunks)]
    for j, out in enumerate(outs):
        for c in range(chunks):
            for f in range(frames):
                at = (f ^ (c & 1) if pair else f) * lanes + j * SUB
                out[c * SUB:(c + 1) * SUB, f * width:(f + 1) * width] = turned[c][at:at + SUB, :]


def output_kernel(n_groups, js, early, half, halves, aliased, place, *refs):
    n = len(js)
    atts, pieces = refs[:n], refs[n:n * (1 + early)]
    late_ref, w_ref, g_ref = refs[n * (1 + early):n * (1 + early) + 3]
    out, buf, sems = refs[n * (1 + early) + 3 + aliased:]
    _, late, rows, _ = late_ref.shape
    width = w_ref.shape[0]
    frames = early + late
    copies = []
    for i, j in enumerate(js):
        x = jnp.concatenate([atts[i][:, f * width:(f + 1) * width] for f in range(frames)], axis=0)
        proj = contract(x, w_ref[...], 1, 0)
        for f in range(frames):
            mine = pieces[i * early + f][...] if f < early else late_ref[j, f - early]
            buf[i, f] = add_normed(mine, proj[f * rows:(f + 1) * rows, :], g_ref[...])
        group = peer(place[0], j, n_groups)
        start = pl.multiple_of((group * halves + half) * rows, SUB)
        copy = pltpu.make_async_copy(buf.at[i], out.at[:, pl.ds(start, rows), :], sems.at[i])
        copy.start()
        copies.append(copy)
    for copy in copies:
        copy.wait()


def shards(
    spatial_queries,
    spatial_keys,
    spatial_values,
    hidden,
    spatial_out_weight,
    spatial_gain,
    temporal_qkv_weight,
    temporal_out_weight,
    temporal_gain,
    tile_list,
    tile_count,
):
    frames, tokens, width = spatial_queries.shape
    model = hidden.shape[2]
    groups = lax.axis_size("frame")
    strips = lax.axis_size("strip")
    share = tokens // groups
    halves = 2 if share % (4 * SUB) == 0 else 1
    rows = share // halves
    queries = jnp.transpose(spatial_queries, (0, 2, 1))
    keys = pltpu.with_memory_space_constraint(jnp.transpose(spatial_keys, (0, 2, 1)), pltpu.HBM)
    values = pltpu.with_memory_space_constraint(jnp.transpose(spatial_values, (0, 2, 1)), pltpu.HBM)
    hidden_far = pltpu.with_memory_space_constraint(hidden, pltpu.HBM)
    lists = jnp.transpose(tile_list, (2, 1, 0))
    counts = tile_count.T
    qkv_weight = temporal_qkv_weight.T
    gain_one = spatial_gain.reshape(1, model)
    gain_two = temporal_gain.reshape(1, model)
    place = jnp.stack([lax.axis_index("frame"), lax.axis_index("strip")]).astype(jnp.int32)
    near = [(i, i ^ 1) for i in range(strips) if i ^ 1 < strips]
    far = [e for i in range(1, strips - 1, 2) for e in ((i, i + 1), (i + 1, i))]
    edge = jax.ShapeDtypeStruct((2 * width, TILE), BF)
    smem = pl.BlockSpec(memory_space=pltpu.SMEM)

    def call(kernel, in_specs, out_specs, out_shape, scratch=(), limit=32, prefetch=0, alias=None):
        return pl.pallas_call(
            kernel,
            grid_spec=pltpu.PrefetchScalarGridSpec(
                num_scalar_prefetch=prefetch,
                grid=(1,),
                in_specs=in_specs,
                out_specs=out_specs,
                scratch_shapes=list(scratch),
            ),
            out_shape=out_shape,
            input_output_aliases=alias or {},
            compiler_params=vmem(limit),
        )

    def frame_block(f):
        return pl.BlockSpec((1, width, tokens), lambda *_: (f, 0, 0))

    late = frames // 2
    early = frames - late

    halos = []
    for some in range(2):
        block = pl.BlockSpec((late, width, tokens), lambda *_, some=some: (some, 0, 0))
        a, b = call(
            prep_kernel,
            [smem, block, block],
            [whole((late,) + edge.shape)] * 2,
            [jax.ShapeDtypeStruct((late,) + edge.shape, BF)] * 2,
            limit=16,
        )(place, keys, values)
        halos.append((a, b, lax.ppermute(a, "strip", near), lax.ppermute(b, "strip", far)))

    def out_pairs(j):
        return [(i, peer(i, j, groups)) for i in range(groups)]

    def send(x, j):
        return x if j == 0 else lax.ppermute(x, "frame", out_pairs(j))

    own_hidden = call(
        split_kernel,
        [
            pl.BlockSpec((late, share, model), lambda _, at, j=j: (1, peer(at[0], j, groups), 0))
            for j in range(groups)
        ],
        [whole((late, share, model))] * groups,
        [jax.ShapeDtypeStruct((late, share, model), BF)] * groups,
        prefetch=1,
        limit=16,
    )(place, *[hidden_far] * groups)
    far_hidden = [send(x, j) for j, x in enumerate(own_hidden)]

    mixed = [[None] * early for _ in range(groups)]
    projected = []
    for f in range(early):
        edge_block = pl.BlockSpec((1,) + edge.shape, lambda *_, f=f: (f, 0, 0))
        parts = call(
            functools.partial(spatial_kernel, f, groups),
            [smem, smem, smem, frame_block(f)]
            + [edge_block] * 4
            + [
                pl.BlockSpec((1, tokens, model), lambda *_, f=f: (f, 0, 0)),
                whole((width, model)),
                whole((1, model)),
            ],
            [whole((share, model))] * groups,
            [jax.ShapeDtypeStruct((share, model), BF)] * groups,
            [pltpu.VMEM((1, width, tokens), BF), pltpu.VMEM((tokens, model), BF)],
        )(place, counts, lists, queries, *halos[0], hidden, spatial_out_weight, gain_one)
        for j in range(groups):
            mixed[j][f] = parts[j]
        projected.append(
            call(
                functools.partial(project_kernel, f, frames),
                [whole((share, model))] * groups + [whole((3 * width, model))],
                whole((3 * width, tokens)),
                jax.ShapeDtypeStruct((3 * width, tokens), BF),
                [pltpu.VMEM((tokens, model), BF)],
            )(*[send(x, j) for j, x in enumerate(parts)], qkv_weight)
        )

    late_shape = (rows, late * width)
    own_late = call(
        functools.partial(late_kernel, early, groups, halves),
        [smem, smem, smem, pl.BlockSpec((late, width, tokens), lambda *_: (1, 0, 0))]
        + [whole((late,) + edge.shape)] * 4,
        [whole(late_shape)] * (groups * halves),
        [jax.ShapeDtypeStruct(late_shape, BF)] * (groups * halves),
        [pltpu.VMEM((late, width, tokens), F32), pltpu.VMEM((tokens, late * width), BF)],
    )(place, counts, lists, queries, *halos[1])
    own_late = [own_late[half * groups:(half + 1) * groups] for half in range(halves)]
    far_late = [[send(x, j) for j, x in enumerate(some)] for some in own_late]

    returned, late_mixed = [], []
    back_shape = (rows, frames * width)
    lanes = tokens // halves
    for half in range(halves):
        hid_block = pl.BlockSpec((late, rows, model), lambda *_, half=half: (0, half, 0))
        late_specs = [whole(late_shape)] * groups + [hid_block] * groups
        late_specs += [whole((width, model)), whole((1, model))]
        late_projected = call(
            functools.partial(late_project_kernel, early, frames),
            late_specs + [whole((3 * width, model))],
            whole((3 * width, late * lanes)),
            jax.ShapeDtypeStruct((3 * width, late * lanes), BF),
            [
                pltpu.VMEM((late * lanes, width), BF),
                pltpu.VMEM((late * lanes, model), BF),
                pltpu.VMEM((late * lanes, model), BF),
            ],
        )(*far_late[half], *far_hidden, spatial_out_weight, gain_one, qkv_weight)
        back = call(
            functools.partial(temporal_kernel, groups),
            [pl.BlockSpec((3 * width, lanes), lambda *_, half=half: (0, half))] * early
            + [pl.BlockSpec((3 * width, lanes), lambda *_, f=f: (0, f)) for f in range(late)],
            [whole(back_shape)] * groups,
            [jax.ShapeDtypeStruct(back_shape, BF)] * groups,
            [pltpu.VMEM((rows // SUB, width, groups * frames * SUB), F32)],
        )(*projected, *[late_projected] * late)
        got = []
        for j in range(groups):
            pairs = [(b, a) for a, b in out_pairs(j)]
            got.append(back[j] if j == 0 else lax.ppermute(back[j], "frame", pairs))
        returned.append(got)
        late_mixed.append(
            call(
                mix_kernel,
                late_specs,
                whole((groups, late, rows, model)),
                jax.ShapeDtypeStruct((groups, late, rows, model), BF),
            )(*own_late[half], *own_hidden, spatial_out_weight, gain_one)
        )

    out = None
    any_spec = pl.BlockSpec(memory_space=pl.ANY)
    for half in range(halves):
        piece = pl.BlockSpec((rows, model), lambda *_, half=half: (half, 0))
        cuts = [groups] if half + 1 < halves else [groups // 2, groups * 3 // 4, groups]
        for lo, hi in zip([0] + cuts, cuts):
            js = range(lo, hi)
            if not js:
                continue
            extra = [] if out is None else [out]
            out = call(
                functools.partial(output_kernel, groups, tuple(js), early, half, halves, len(extra)),
                [smem]
                + [whole(back_shape)] * len(js)
                + [piece] * (len(js) * early)
                + [whole((groups, late, rows, model)), whole((width, model)), whole((1, model))]
                + [any_spec] * len(extra),
                any_spec,
                jax.ShapeDtypeStruct((frames, tokens, model), BF),
                [
                    pltpu.VMEM((len(js), frames, rows, model), BF),
                    pltpu.SemaphoreType.DMA((len(js),)),
                ],
                alias={4 + len(js) * (1 + early): 0} if extra else None,
            )(
                place,
                *[returned[half][j] for j in js],
                *[mixed[j][f] for j in js for f in range(early)],
                late_mixed[half],
                temporal_out_weight,
                gain_two,
                *extra,
            )
    return out


def solution(mesh):
    rows = P(("group", "frame"), "strip", None)
    placed = (rows, rows, rows, rows, P(), P(), P(), P(), P(), rows, P(("group", "frame"), "strip"))

    return jax.shard_map(shards, mesh=mesh, in_specs=placed, out_specs=rows, check_vma=False)
```

time: 78.8 us -> 84.1 us (1.067)
  the two profiles are of different devices: /device:TPU:0 before, /device:TPU:21 now
where the time goes in v1:
time: 84.1 us; the launch traced here: 83.8 us
  Pallas kernels  35.4 us (42%)
  starting transfers between devices  27.2 us (32%)
  waiting for transfers between devices  20.6 us (24%)
    ppermute x15, starting transfers between devices, send(): return x if j == 0 else lax.ppermute(x, 'frame', out_pairs(j))  16.2 us
    ppermute x15, waiting for transfers between devices, send(): return x if j == 0 else lax.ppermute(x, 'frame', out_pairs(j))  10.6 us
    pallas_call x4, Pallas kernels, shards(): call(functools.partial(output_kernel, groups, tuple(js), early, half, hal...  8.8 us
    ppermute x2, waiting for transfers between devices, shards(): lax.ppermute(a, 'strip', near)  5.89 us
    ppermute x2, starting transfers between devices, shards(): lax.ppermute(b, 'strip', far)  5.53 us
    pallas_call x2, Pallas kernels, shards(): call(functools.partial(spatial_kernel, f, groups), [smem, smem, smem, fra...  5.4 us
    pallas_call x2, Pallas kernels, shards(): call(functools.partial(late_project_kernel, early, frames), late_specs +...  4.31 us
    ppermute x6, starting transfers between devices, shards(): got.append(back[j] if j == 0 else lax.ppermute(back[j], 'frame', pairs))  4.05 us
  transfers between devices with their start and end apart: 25, of which 9 were waited for; matrix products, arithmetic and copies ran while one was open for 0% of the time, Pallas kernels for 34%

profile of v1, /device:TPU:21, one launch (start us, length us, event | category | flops | bytes accessed | tf_op | source)
XLA Modules:
  0.0 83.8 jit_solution(280974853133927374)
XLA Ops:
  0.0 0.1 pad_add_fusion.place
  0.1 1.5 %shard_map.109 = (bf16[2,1152,128]{2,1,0:T(8,128)(2,1)S(1)}, bf16[2,1152,128]{2,1,0:T(8,128)(2,1)S(1)}) custom-call(s32[2]{0:T(128)S(1)} %pad_add_fusion.place, bf16[4,576,256]{2,1,0:T(8,128)(2,1)} %bitcast.21, bf16[4,576,256]{2,1,0:T(8,128)(2,1)} %bitcast.23), custom_call_target="tpu_custom_call" | custom-call | tf_op jit(solution)/shard_map/pallas_call | solution.py:352
  1.6 1.4 %collective-permute-start = (bf16[2,1152,128]{2,1,0:T(8,128)(2,1)S(1)}, bf16[2,1152,128]{2,1,0:T(8,128)(2,1)S(1)}, u32[]{:S(2)}, u32[]{:S(2)}) collective-permute-start(bf16[2,1152,128]{2,1,0:T(8,128)(2,1)S(1)} %get-tuple-element.37.a_ref), channel_id=1, source_target_pairs={{0,1},{1,0},{2,3},{3,2},{4,5},{5,4},{6,7},{7,6},{8,9},{9,8},{10,11... | collective-permute-start | bytes 1769480 | tf_op jit(solution)/shard_map/ppermute | solution.py:359
  2.9 1.9 %collective-permute-start.1 = (bf16[2,1152,128]{2,1,0:T(8,128)(2,1)S(1)}, bf16[2,1152,128]{2,1,0:T(8,128)(2,1)S(1)}, u32[]{:S(2)}, u32[]{:S(2)}) collective-permute-start(bf16[2,1152,128]{2,1,0:T(8,128)(2,1)S(1)} %get-tuple-element.38.b_ref), channel_id=1, source_target_pairs={{1,2},{2,1},{5,6},{6,5},{9,10},{10,9},{13,14},{14,13},{17,18},{18,... | collective-permute-start | bytes 1769480 | tf_op jit(solution)/shard_map/ppermute | solution.py:359
  4.9 1.5 %shard_map.114 = (bf16[2,1152,128]{2,1,0:T(8,128)(2,1)S(1)}, bf16[2,1152,128]{2,1,0:T(8,128)(2,1)S(1)}) custom-call(s32[2]{0:T(128)S(1)} %pad_add_fusion.place, bf16[4,576,256]{2,1,0:T(8,128)(2,1)} %bitcast.22, bf16[4,576,256]{2,1,0:T(8,128)(2,1)} %bitcast.24), custom_call_target="tpu_custom_call" | custom-call | tf_op jit(solution)/shard_map/pallas_call | solution.py:352
  6.4 0.1 collective-permute-start.8
  6.4 0.0 copy-start.7
  6.5 0.0 copy-start
  6.5 0.0 copy-start.2
  6.5 0.0 copy-start.4
  6.5 0.0 copy-start.5
  6.5 0.0 copy-start.6
  6.5 3.6 %collective-permute-start.9 = (bf16[2,1152,128]{2,1,0:T(8,128)(2,1)S(1)}, bf16[2,1152,128]{2,1,0:T(8,128)(2,1)S(1)}, u32[]{:S(2)}, u32[]{:S(2)}) collective-permute-start(bf16[2,1152,128]{2,1,0:T(8,128)(2,1)S(1)} %get-tuple-element.48.b_ref), channel_id=1, source_target_pairs={{1,2},{2,1},{5,6},{6,5},{9,10},{10,9},{13,14},{14,13},{17,18},{18,... | collective-permute-start | bytes 1769480 | tf_op jit(solution)/shard_map/ppermute | solution.py:359
  10.1 1.9 %shard_map.116 = (bf16[2,64,1152]{2,1,0:T(8,128)(2,1)S(1)}, bf16[2,64,1152]{2,1,0:T(8,128)(2,1)S(1)}, bf16[2,64,1152]{2,1,0:T(8,128)(2,1)S(1)}, bf16[2,64,1152]{2,1,0:T(8,128)(2,1)S(1)}) custom-call(s32[2]{0:T(128)S(1)} %pad_add_fusion.place, bf16[4,256,1152]{2,1,0:T(8,128)(2,1)} %refs_3_.1, bf16[4,256,1152]{2,1,0:T(8,128)(2,1)} %refs_3_.1, ...), custom_call_target="tpu_custom_call" | custom-call | tf_op jit(solution)/shard_map/pallas_call | solution.py:367
  12.0 1.6 %collective-permute-start.13 = (bf16[2,64,1152]{2,1,0:T(8,128)(2,1)S(1)}, bf16[2,64,1152]{2,1,0:T(8,128)(2,1)S(1)}, u32[]{:S(2)}, u32[]{:S(2)}) collective-permute-start(bf16[2,64,1152]{2,1,0:T(8,128)(2,1)S(1)} %get-tuple-element.54.refs_5_), channel_id=1, source_target_pairs={{0,4},{4,0},{8,12},{12,8},{1,5},{5,1},{9,13},{13,9},{2,6},{6,2},{1... | collective-permute-start | bytes 884744 | tf_op jit(solution)/shard_map/ppermute | solution.py:365
  13.6 2.3 %collective-permute-done.ra_ref = bf16[2,1152,128]{2,1,0:T(8,128)(2,1)S(1)} collective-permute-done((bf16[2,1152,128]{2,1,0:T(8,128)(2,1)S(1)}, bf16[2,1152,128]{2,1,0:T(8,128)(2,1)S(1)}, u32[]{:S(2)}, u32[]{:S(2)}) %collective-permute-start) | collective-permute-done | bytes 589856 | tf_op jit(solution)/shard_map/ppermute | solution.py:359
  15.9 0.2 collective-permute-start.14
  16.1 2.7 %collective-permute-done.1.rb_ref = bf16[2,1152,128]{2,1,0:T(8,128)(2,1)S(1)} collective-permute-done((bf16[2,1152,128]{2,1,0:T(8,128)(2,1)S(1)}, bf16[2,1152,128]{2,1,0:T(8,128)(2,1)S(1)}, u32[]{:S(2)}, u32[]{:S(2)}) %collective-permute-start.1) | collective-permute-done | bytes 589856 | tf_op jit(solution)/shard_map/ppermute | solution.py:359
  18.8 3.3 %collective-permute-start.15 = (bf16[2,64,1152]{2,1,0:T(8,128)(2,1)S(1)}, bf16[2,64,1152]{2,1,0:T(8,128)(2,1)S(1)}, u32[]{:S(2)}, u32[]{:S(2)}) collective-permute-start(bf16[2,64,1152]{2,1,0:T(8,128)(2,1)S(1)} %get-tuple-element.56.refs_7_), channel_id=1, source_target_pairs={{0,12},{4,8},{8,4},{12,0},{1,13},{5,9},{9,5},{13,1},{2,14},{6,10},... | collective-permute-start | bytes 884744 | tf_op jit(solution)/shard_map/ppermute | solution.py:365
  22.1 2.7 %shard_map.110 = (bf16[64,1152]{1,0:T(8,128)(2,1)S(1)}, bf16[64,1152]{1,0:T(8,128)(2,1)S(1)}, bf16[64,1152]{1,0:T(8,128)(2,1)S(1)}, bf16[64,1152]{1,0:T(8,128)(2,1)S(1)}) custom-call(s32[2]{0:T(128)S(1)} %pad_add_fusion.place, s32[2,4]{1,0:T(2,128)S(1)} %bitcast.18, s32[3,2,4]{2,1,0:T(2,128)S(1)} %bitcast.15, bf16[4,576,256]{2,1,0:T(8,128)(2,1)S(1)} %bitcast.12, ...), custom_call_target="tpu_custom_call" | custom-call | tf_op jit(solution)/shard_map/pallas_call | solution.py:384
  24.9 3.6 %collective-permute-done.8.ra_ref = bf16[2,1152,128]{2,1,0:T(8,128)(2,1)S(1)} collective-permute-done((bf16[2,1152,128]{2,1,0:T(8,128)(2,1)S(1)}, bf16[2,1152,128]{2,1,0:T(8,128)(2,1)S(1)}, u32[]{:S(2)}, u32[]{:S(2)}) %collective-permute-start.8) | collective-permute-done | bytes 589856 | tf_op jit(solution)/shard_map/ppermute | solution.py:359
  28.5 1.5 %collective-permute-start.2 = (bf16[64,1152]{1,0:T(8,128)(2,1)S(1)}, bf16[64,1152]{1,0:T(8,128)(2,1)S(1)}, u32[]{:S(2)}, u32[]{:S(2)}) collective-permute-start(bf16[64,1152]{1,0:T(8,128)(2,1)S(1)} %get-tuple-element.40.refs_6_.refs_4_), channel_id=1, source_target_pairs={{0,4},{4,0},{8,12},{12,8},{1,5},{5,1},{9,13},{13,9},{2,6},{6,2},{1... | collective-permute-start | bytes 442376 | tf_op jit(solution)/shard_map/ppermute | solution.py:365
  30.0 1.4 %collective-permute-done.9.rb_ref = bf16[2,1152,128]{2,1,0:T(8,128)(2,1)S(1)} collective-permute-done((bf16[2,1152,128]{2,1,0:T(8,128)(2,1)S(1)}, bf16[2,1152,128]{2,1,0:T(8,128)(2,1)S(1)}, u32[]{:S(2)}, u32[]{:S(2)}) %collective-permute-start.9) | collective-permute-done | bytes 589856 | tf_op jit(solution)/shard_map/ppermute | solution.py:359
  31.4 3.0 %shard_map.115 = (bf16[32,1152]{1,0:T(8,128)(2,1)S(1)}, bf16[32,1152]{1,0:T(8,128)(2,1)S(1)}, bf16[32,1152]{1,0:T(8,128)(2,1)S(1)}, bf16[32,1152]{1,0:T(8,128)(2...) custom-call(s32[2]{0:T(128)S(1)} %pad_add_fusion.place, ...), custom_call_target="tpu_custom_call" | custom-call | tf_op jit(solution)/shard_map/pallas_call | solution.py:410
  34.4 1.9 %collective-permute-start.19 = (bf16[32,1152]{1,0:T(8,128)(2,1)S(1)}, bf16[32,1152]{1,0:T(8,128)(2,1)S(1)}, u32[]{:S(2)}, u32[]{:S(2)}) collective-permute-start(bf16[32,1152]{1,0:T(8,128)(2,1)S(1)} %get-tuple-element.62.refs_1_), channel_id=1, source_target_pairs={{0,4},{4,0},{8,12},{12,8},{1,5},{5,1},{9,13},{13,9},{2,6},{6,2},{1... | collective-permute-start | bytes 221192 | tf_op jit(solution)/shard_map/ppermute | solution.py:365
  36.3 0.2 collective-permute-start.20
  36.5 1.5 %collective-permute-start.21 = (bf16[32,1152]{1,0:T(8,128)(2,1)S(1)}, bf16[32,1152]{1,0:T(8,128)(2,1)S(1)}, u32[]{:S(2)}, u32[]{:S(2)}) collective-permute-start(bf16[32,1152]{1,0:T(8,128)(2,1)S(1)} %get-tuple-element.64.refs_3_), channel_id=1, source_target_pairs={{0,12},{4,8},{8,4},{12,0},{1,13},{5,9},{9,5},{13,1},{2,14},{6,10},... | collective-permute-start | bytes 221192 | tf_op jit(solution)/shard_map/ppermute | solution.py:365
  38.0 2.7 %shard_map.112 = (bf16[64,1152]{1,0:T(8,128)(2,1)S(1)}, bf16[64,1152]{1,0:T(8,128)(2,1)S(1)}, bf16[64,1152]{1,0:T(8,128)(2,1)S(1)}, bf16[64,1152]{1,0:T(8,128)(2,1)S(1)}) custom-call(s32[2]{0:T(128)S(1)} %pad_add_fusion.place, s32[2,4]{1,0:T(2,128)S(1)} %bitcast.20, s32[3,2,4]{2,1,0:T(2,128)S(1)} %bitcast.17, bf16[4,576,256]{2,1,0:T(8,128)(2,1)S(1)} %bitcast.14, ...), custom_call_target="tpu_custom_call" | custom-call | tf_op jit(solution)/shard_map/pallas_call | solution.py:384
  40.7 0.0 collective-permute-done.15.refs_7_
  40.7 0.2 collective-permute-start.5
  40.9 0.0 collective-permute-done.19.refs_1_
  40.9 0.2 collective-permute-start.3
  41.2 1.8 %collective-permute-start.4 = (bf16[64,1152]{1,0:T(8,128)(2,1)S(1)}, bf16[64,1152]{1,0:T(8,128)(2,1)S(1)}, u32[]{:S(2)}, u32[]{:S(2)}) collective-permute-start(bf16[64,1152]{1,0:T(8,128)(2,1)S(1)} %get-tuple-element.42.refs_10_.refs_1_), channel_id=1, source_target_pairs={{0,12},{4,8},{8,4},{12,0},{1,13},{5,9},{9,5},{13,1},{2,14},{6,10},... | collective-permute-start | bytes 442376 | tf_op jit(solution)/shard_map/ppermute | solution.py:365
  42.9 0.2 collective-permute-start.6
  43.2 1.3 %collective-permute-start.7 = (bf16[64,1152]{1,0:T(8,128)(2,1)S(1)}, bf16[64,1152]{1,0:T(8,128)(2,1)S(1)}, u32[]{:S(2)}, u32[]{:S(2)}) collective-permute-start(bf16[64,1152]{1,0:T(8,128)(2,1)S(1)} %get-tuple-element.46.refs_11_.refs_2_), channel_id=1, source_target_pairs={{0,12},{4,8},{8,4},{12,0},{1,13},{5,9},{9,5},{13,1},{2,14},{6,10},... | collective-permute-start | bytes 442376 | tf_op jit(solution)/shard_map/ppermute | solution.py:365
  44.4 2.2 %shard_map.120.refs_2_.refs_3_ = bf16[1728,256]{1,0:T(8,128)(2,1)S(1)} custom-call(bf16[32,1152]{1,0:T(8,128)(2,1)S(1)} %get-tuple-element.61.refs_0_, bf16[32,1152]{1,0:T(8,128)(2,1)S(1)} %collective-permute-done.19.refs_1_, bf16[32,1152]{1,0:T(8,128)(2,1)S(1)} %collective-permute-done.20.refs_2_, bf16[32,1152]{1,0:T(8,128)(2,1)S(1)} %collective-permute-done.21.refs_3_, ...), custom_call_target="tpu_custom_call" | custom-call | tf_op jit(solution)/shard_map/pallas_call | solution.py:428
  46.6 3.9 %collective-permute-done.4.refs_3_ = bf16[64,1152]{1,0:T(8,128)(2,1)S(1)} collective-permute-done((bf16[64,1152]{1,0:T(8,128)(2,1)S(1)}, bf16[64,1152]{1,0:T(8,128)(2,1)S(1)}, u32[]{:S(2)}, u32[]{:S(2)}) %collective-permute-start.4) | collective-permute-done | bytes 147488 | tf_op jit(solution)/shard_map/ppermute | solution.py:365
  50.5 1.4 %shard_map.111.refs_0_ = bf16[1728,256]{1,0:T(8,128)(2,1)S(1)} custom-call(bf16[64,1152]{1,0:T(8,128)(2,1)S(1)} %get-tuple-element.39.refs_0_.refs_4_.refs_2_, bf16[64,1152]{1,0:T(8,128)(2,1)S(1)} %collective-permute-done.2.refs_1_, bf16[64,1152]{1,0:T(8,128)(2,1)S(1)} %collective-permute-done.3.refs_2_, ...), custom_call_target="tpu_custom_call" | custom-call | tf_op jit(solution)/shard_map/pallas_call | solution.py:400
  51.9 0.4 collective-permute-done.6.refs_2_
  52.3 3.7 %collective-permute-done.7.refs_3_ = bf16[64,1152]{1,0:T(8,128)(2,1)S(1)} collective-permute-done((bf16[64,1152]{1,0:T(8,128)(2,1)S(1)}, bf16[64,1152]{1,0:T(8,128)(2,1)S(1)}, u32[]{:S(2)}, u32[]{:S(2)}) %collective-permute-start.7) | collective-permute-done | bytes 147488 | tf_op jit(solution)/shard_map/ppermute | solution.py:365
  56.0 1.4 %shard_map.113.refs_1_ = bf16[1728,256]{1,0:T(8,128)(2,1)S(1)} custom-call(bf16[64,1152]{1,0:T(8,128)(2,1)S(1)} %get-tuple-element.43.refs_0_.refs_5_.refs_3_, bf16[64,1152]{1,0:T(8,128)(2,1)S(1)} %collective-permute-done.5.refs_1_, bf16[64,1152]{1,0:T(8,128)(2,1)S(1)} %collective-permute-done.6.refs_2_, ...), custom_call_target="tpu_custom_call" | custom-call | tf_op jit(solution)/shard_map/pallas_call | solution.py:400
  57.4 1.9 %shard_map.121 = (bf16[32,2304]{1,0:T(8,128)(2,1)S(1)}, bf16[32,2304]{1,0:T(8,128)(2,1)S(1)}, bf16[32,2304]{1,0:T(8,128)(2,1)S(1)}, bf16[32,2304]{1,0:T(8,128)(2,1)S(1)}) custom-call(bf16[1728,256]{1,0:T(8,128)(2,1)S(1)} %shard_map.111.refs_0_, bf16[1728,256]{1,0:T(8,128)(2,1)S(1)} %shard_map.113.refs_1_, bf16[1728,256]{1,0:T(8,128)(2,1)S(1)} %shard_map.120.refs_2_.refs_3_, ...), custom_call_target="tpu_custom_call" | custom-call | tf_op jit(solution)/shard_map/pallas_call | solution.py:439
  59.3 0.1 collective-permute-start.22
  59.3 0.5 collective-permute-start.10
  59.8 0.2 collective-permute-start.11
  60.1 1.5 %collective-permute-start.12 = (bf16[32,1152]{1,0:T(8,128)(2,1)S(1)}, bf16[32,1152]{1,0:T(8,128)(2,1)S(1)}, u32[]{:S(2)}, u32[]{:S(2)}) collective-permute-start(bf16[32,1152]{1,0:T(8,128)(2,1)S(1)} %get-tuple-element.52.refs_3_), channel_id=1, source_target_pairs={{0,12},{4,8},{8,4},{12,0},{1,13},{5,9},{9,5},{13,1},{2,14},{6,10},... | collective-permute-start | bytes 221192 | tf_op jit(solution)/shard_map/ppermute | solution.py:365
  61.6 0.2 collective-permute-start.23
  61.8 1.6 %collective-permute-start.24 = (bf16[32,2304]{1,0:T(8,128)(2,1)S(1)}, bf16[32,2304]{1,0:T(8,128)(2,1)S(1)}, u32[]{:S(2)}, u32[]{:S(2)}) collective-permute-start(bf16[32,2304]{1,0:T(8,128)(2,1)S(1)} %get-tuple-element.68), channel_id=1, source_target_pairs={{12,0},{8,4},{4,8},{0,12},{13,1},{9,5},{5,9},{1,13},{14,2},{10,6},... | collective-permute-start | bytes 442376 | tf_op jit(solution)/shard_map/ppermute | solution.py:450
  63.3 0.2 collective-permute-done.11.refs_2_
  63.6 2.4 %collective-permute-done.12.refs_3_ = bf16[32,1152]{1,0:T(8,128)(2,1)S(1)} collective-permute-done((bf16[32,1152]{1,0:T(8,128)(2,1)S(1)}, bf16[32,1152]{1,0:T(8,128)(2,1)S(1)}, u32[]{:S(2)}, u32[]{:S(2)}) %collective-permute-start.12) | collective-permute-done | bytes 73760 | tf_op jit(solution)/shard_map/ppermute | solution.py:365
  66.0 2.2 %shard_map.117.refs_2_.refs_3_ = bf16[1728,256]{1,0:T(8,128)(2,1)S(1)} custom-call(bf16[32,1152]{1,0:T(8,128)(2,1)S(1)} %get-tuple-element.49.refs_0_, bf16[32,1152]{1,0:T(8,128)(2,1)S(1)} %collective-permute-done.10.refs_1_, bf16[32,1152]{1,0:T(8,128)(2,1)S(1)} %collective-permute-done.11.refs_2_, bf16[32,1152]{1,0:T(8,128)(2,1)S(1)} %collective-permute-done.12.refs_3_, ...), custom_call_target="tpu_custom_call" | custom-call | tf_op jit(solution)/shard_map/pallas_call | solution.py:428
  68.1 0.0 copy-start.8
  68.1 1.9 %shard_map.118 = (bf16[32,2304]{1,0:T(8,128)(2,1)S(1)}, bf16[32,2304]{1,0:T(8,128)(2,1)S(1)}, bf16[32,2304]{1,0:T(8,128)(2,1)S(1)}, bf16[32,2304]{1,0:T(8,128)(2,1)S(1)}) custom-call(bf16[1728,256]{1,0:T(8,128)(2,1)S(1)} %shard_map.111.refs_0_, bf16[1728,256]{1,0:T(8,128)(2,1)S(1)} %shard_map.113.refs_1_, bf16[1728,256]{1,0:T(8,128)(2,1)S(1)} %shard_map.117.refs_2_.refs_3_, ...), custom_call_target="tpu_custom_call" | custom-call | tf_op jit(solution)/shard_map/pallas_call | solution.py:439
  70.0 0.1 collective-permute-start.18
  70.1 0.1 collective-permute-start.17
  70.2 2.0 %collective-permute-start.16 = (bf16[32,2304]{1,0:T(8,128)(2,1)S(1)}, bf16[32,2304]{1,0:T(8,128)(2,1)S(1)}, u32[]{:S(2)}, u32[]{:S(2)}) collective-permute-start(bf16[32,2304]{1,0:T(8,128)(2,1)S(1)} %get-tuple-element.57), channel_id=1, source_target_pairs={{12,0},{8,4},{4,8},{0,12},{13,1},{9,5},{5,9},{1,13},{14,2},{10,6},... | collective-permute-start | bytes 442376 | tf_op jit(solution)/shard_map/ppermute | solution.py:450
  72.2 1.3 %shard_map.119.refs_6_.refs_3_ = bf16[4,2,32,1152]{3,2,1,0:T(8,128)(2,1)S(1)} custom-call(bf16[32,1152]{1,0:T(8,128)(2,1)S(1)} %get-tuple-element.49.refs_0_, bf16[32,1152]{1,0:T(8,128)(2,1)S(1)} %get-tuple-element.50.refs_1_, bf16[32,1152]{1,0:T(8,128)(2,1)S(1)} %get-tuple-element.51.refs_2_, bf16[32,1152]{1,0:T(8,128)(2,1)S(1)} %get-tuple-element.52.refs_3_, ...), custom_call_target="tpu_custom_call" | custom-call | tf_op jit(solution)/shard_map/pallas_call | solution.py:453
  73.5 0.0 copy-start.3
  73.5 1.2 %shard_map.122.refs_12_ = bf16[4,2,32,1152]{3,2,1,0:T(8,128)(2,1)S(1)} custom-call(bf16[32,1152]{1,0:T(8,128)(2,1)S(1)} %get-tuple-element.61.refs_0_, bf16[32,1152]{1,0:T(8,128)(2,1)S(1)} %get-tuple-element.62.refs_1_, bf16[32,1152]{1,0:T(8,128)(2,1)S(1)} %get-tuple-element.63.refs_2_, bf16[32,1152]{1,0:T(8,128)(2,1)S(1)} %get-tuple-element.64.refs_3_, ...), custom_call_target="tpu_custom_call" | custom-call | tf_op jit(solution)/shard_map/pallas_call | solution.py:453
  74.8 0.0 copy-done.3
  74.8 2.9 %shard_map.123.refs_9_ = bf16[4,256,1152]{2,1,0:T(8,128)(2,1)} custom-call(s32[2]{0:T(128)S(1)} %pad_add_fusion.place, bf16[32,2304]{1,0:T(8,128)(2,1)S(1)} %get-tuple-element.65.refs_0_, bf16[32,2304]{1,0:T(8,128)(2,1)S(1)} %collective-permute-done.22.refs_1_, bf16[32,2304]{1,0:T(8,128)(2,1)S(1)} %collective-permute-done.23.refs_2_, ...), custom_call_target="tpu_custom_call" | custom-call | tf_op jit(solution)/shard_map/pallas_call | solution.py:471
  77.7 2.2 %shard_map.124.refs_6_ = bf16[4,256,1152]{2,1,0:T(8,128)(2,1)} custom-call(s32[2]{0:T(128)S(1)} %pad_add_fusion.place, bf16[32,2304]{1,0:T(8,128)(2,1)S(1)} %get-tuple-element.59.refs_0_, bf16[32,2304]{1,0:T(8,128)(2,1)S(1)} %collective-permute-done.18.refs_1_, ...), custom_call_target="tpu_custom_call", output_to_operand_aliasing={{}: (10, {})} | custom-call | tf_op jit(solution)/shard_map/pallas_call | solution.py:471
  79.9 1.9 %shard_map.125.refs_6_ = bf16[4,256,1152]{2,1,0:T(8,128)(2,1)} custom-call(s32[2]{0:T(128)S(1)} %pad_add_fusion.place, bf16[32,2304]{1,0:T(8,128)(2,1)S(1)} %collective-permute-done.17.refs_0_, bf16[64,1152]{1,0:T(8,128)(2,1)S(1)} %get-tuple-element.41.refs_8_.refs_1_, ...), custom_call_target="tpu_custom_call", output_to_operand_aliasing={{}: (7, {})} | custom-call | tf_op jit(solution)/shard_map/pallas_call | solution.py:471
  81.8 1.9 %shard_map.126 = bf16[4,256,1152]{2,1,0:T(8,128)(2,1)} custom-call(s32[2]{0:T(128)S(1)} %pad_add_fusion.place, bf16[32,2304]{1,0:T(8,128)(2,1)S(1)} %collective-permute-done.16.refs_0_, bf16[64,1152]{1,0:T(8,128)(2,1)S(1)} %get-tuple-element.42.refs_10_.refs_1_, ...), custom_call_target="tpu_custom_call", output_to_operand_aliasing={{}: (7, {})} | custom-call | tf_op jit(solution)/shard_map/pallas_call | solution.py:471
  (25 shorter events, 0.1 us)
Async XLA Ops:
  1.6 14.3 %collective-permute-start = (bf16[2,1152,128]{2,1,0:T(8,128)(2,1)S(1)}, bf16[2,1152,128]{2,1,0:T(8,128)(2,1)S(1)}, u32[]{:S(2)}, u32[]{:S(2)}) collective-permute-start(bf16[2,1152,128]{2,1,0:T(8,128)(2,1)S(1)} %get-tuple-element.37.a_ref), channel_id=1, source_target_pairs={{0,1},{1,0},{2,3},{3,2},{4,5},{5,4},{6,7},{7,6},{8,9},{9,8},{10,11... | collective-permute-start | bytes 1769480 | tf_op jit(solution)/shard_map/ppermute | solution.py:359
  2.9 15.8 %collective-permute-start.1 = (bf16[2,1152,128]{2,1,0:T(8,128)(2,1)S(1)}, bf16[2,1152,128]{2,1,0:T(8,128)(2,1)S(1)}, u32[]{:S(2)}, u32[]{:S(2)}) collective-permute-start(bf16[2,1152,128]{2,1,0:T(8,128)(2,1)S(1)} %get-tuple-element.38.b_ref), channel_id=1, source_target_pairs={{1,2},{2,1},{5,6},{6,5},{9,10},{10,9},{13,14},{14,13},{17,18},{18,... | collective-permute-start | bytes 1769480 | tf_op jit(solution)/shard_map/ppermute | solution.py:359
  6.4 22.1 %collective-permute-start.8 = (bf16[2,1152,128]{2,1,0:T(8,128)(2,1)S(1)}, bf16[2,1152,128]{2,1,0:T(8,128)(2,1)S(1)}, u32[]{:S(2)}, u32[]{:S(2)}) collective-permute-start(bf16[2,1152,128]{2,1,0:T(8,128)(2,1)S(1)} %get-tuple-element.47.a_ref), channel_id=1, source_target_pairs={{0,1},{1,0},{2,3},{3,2},{4,5},{5,4},{6,7},{7,6},{8,9},{9,8},{10,11... | collective-permute-start | bytes 1769480 | tf_op jit(solution)/shard_map/ppermute | solution.py:359
  6.4 15.6 %copy-start.7 = (f32[1152]{0:T(1024)S(1)}, f32[1152]{0:T(1024)}, u32[]{:S(2)}) copy-start(f32[1152]{0:T(1024)} %param.16) | copy-start | bytes 13828
  6.5 15.6 %copy-start = (bf16[4,256,1152]{2,1,0:T(8,128)(2,1)S(1)}, bf16[4,256,1152]{2,1,0:T(8,128)(2,1)}, u32[]{:S(2)}) copy-start(bf16[4,256,1152]{2,1,0:T(8,128)(2,1)} %refs_3_.1) | copy-start | bytes 7077892
  6.5 15.6 %copy-start.2 = (bf16[576,1152]{1,0:T(8,128)(2,1)S(1)}, bf16[576,1152]{1,0:T(8,128)(2,1)}, u32[]{:S(2)}) copy-start(bf16[576,1152]{1,0:T(8,128)(2,1)} %refs_8_.7) | copy-start | bytes 3981316
  6.5 15.6 %copy-start.4 = (bf16[4,256,576]{1,2,0:T(8,128)(2,1)S(1)}, bf16[4,256,576]{1,2,0:T(8,128)(2,1)}, u32[]{:S(2)}) copy-start(bf16[4,256,576]{1,2,0:T(8,128)(2,1)} %param.11) | copy-start | bytes 3538948
  6.5 15.6 %copy-start.5 = (s32[4,2,3]{0,1,2:T(2,128)S(1)}, s32[4,2,3]{0,1,2:T(2,128)}, u32[]{:S(2)}) copy-start(s32[4,2,3]{0,1,2:T(2,128)} %param.20) | copy-start | bytes 292
  6.5 15.6 %copy-start.6 = (s32[4,2]{0,1:T(2,128)S(1)}, s32[4,2]{0,1:T(2,128)}, u32[]{:S(2)}) copy-start(s32[4,2]{0,1:T(2,128)} %param.21) | copy-start | bytes 100
  6.5 24.9 %collective-permute-start.9 = (bf16[2,1152,128]{2,1,0:T(8,128)(2,1)S(1)}, bf16[2,1152,128]{2,1,0:T(8,128)(2,1)S(1)}, u32[]{:S(2)}, u32[]{:S(2)}) collective-permute-start(bf16[2,1152,128]{2,1,0:T(8,128)(2,1)S(1)} %get-tuple-element.48.b_ref), channel_id=1, source_target_pairs={{1,2},{2,1},{5,6},{6,5},{9,10},{10,9},{13,14},{14,13},{17,18},{18,... | collective-permute-start | bytes 1769480 | tf_op jit(solution)/shard_map/ppermute | solution.py:359
  12.0 24.3 %collective-permute-start.13 = (bf16[2,64,1152]{2,1,0:T(8,128)(2,1)S(1)}, bf16[2,64,1152]{2,1,0:T(8,128)(2,1)S(1)}, u32[]{:S(2)}, u32[]{:S(2)}) collective-permute-start(bf16[2,64,1152]{2,1,0:T(8,128)(2,1)S(1)} %get-tuple-element.54.refs_5_), channel_id=1, source_target_pairs={{0,4},{4,0},{8,12},{12,8},{1,5},{5,1},{9,13},{13,9},{2,6},{6,2},{1... | collective-permute-start | bytes 884744 | tf_op jit(solution)/shard_map/ppermute | solution.py:365
  15.9 20.7 %collective-permute-start.14 = (bf16[2,64,1152]{2,1,0:T(8,128)(2,1)S(1)}, bf16[2,64,1152]{2,1,0:T(8,128)(2,1)S(1)}, u32[]{:S(2)}, u32[]{:S(2)}) collective-permute-start(bf16[2,64,1152]{2,1,0:T(8,128)(2,1)S(1)} %get-tuple-element.55.refs_6_), channel_id=1, source_target_pairs={{0,8},{4,12},{8,0},{12,4},{1,9},{5,13},{9,1},{13,5},{2,10},{6,14},... | collective-permute-start | bytes 884744 | tf_op jit(solution)/shard_map/ppermute | solution.py:365
  18.8 22.0 %collective-permute-start.15 = (bf16[2,64,1152]{2,1,0:T(8,128)(2,1)S(1)}, bf16[2,64,1152]{2,1,0:T(8,128)(2,1)S(1)}, u32[]{:S(2)}, u32[]{:S(2)}) collective-permute-start(bf16[2,64,1152]{2,1,0:T(8,128)(2,1)S(1)} %get-tuple-element.56.refs_7_), channel_id=1, source_target_pairs={{0,12},{4,8},{8,4},{12,0},{1,13},{5,9},{9,5},{13,1},{2,14},{6,10},... | collective-permute-start | bytes 884744 | tf_op jit(solution)/shard_map/ppermute | solution.py:365
  28.5 14.7 %collective-permute-start.2 = (bf16[64,1152]{1,0:T(8,128)(2,1)S(1)}, bf16[64,1152]{1,0:T(8,128)(2,1)S(1)}, u32[]{:S(2)}, u32[]{:S(2)}) collective-permute-start(bf16[64,1152]{1,0:T(8,128)(2,1)S(1)} %get-tuple-element.40.refs_6_.refs_4_), channel_id=1, source_target_pairs={{0,4},{4,0},{8,12},{12,8},{1,5},{5,1},{9,13},{13,9},{2,6},{6,2},{1... | collective-permute-start | bytes 442376 | tf_op jit(solution)/shard_map/ppermute | solution.py:365
  34.4 6.5 %collective-permute-start.19 = (bf16[32,1152]{1,0:T(8,128)(2,1)S(1)}, bf16[32,1152]{1,0:T(8,128)(2,1)S(1)}, u32[]{:S(2)}, u32[]{:S(2)}) collective-permute-start(bf16[32,1152]{1,0:T(8,128)(2,1)S(1)} %get-tuple-element.62.refs_1_), channel_id=1, source_target_pairs={{0,4},{4,0},{8,12},{12,8},{1,5},{5,1},{9,13},{13,9},{2,6},{6,2},{1... | collective-permute-start | bytes 221192 | tf_op jit(solution)/shard_map/ppermute | solution.py:365
  36.3 4.9 %collective-permute-start.20 = (bf16[32,1152]{1,0:T(8,128)(2,1)S(1)}, bf16[32,1152]{1,0:T(8,128)(2,1)S(1)}, u32[]{:S(2)}, u32[]{:S(2)}) collective-permute-start(bf16[32,1152]{1,0:T(8,128)(2,1)S(1)} %get-tuple-element.63.refs_2_), channel_id=1, source_target_pairs={{0,8},{4,12},{8,0},{12,4},{1,9},{5,13},{9,1},{13,5},{2,10},{6,14},... | collective-permute-start | bytes 221192 | tf_op jit(solution)/shard_map/ppermute | solution.py:365
  36.5 7.9 %copy-start.1 = (bf16[1152,1728]{0,1:T(8,128)(2,1)S(1)}, bf16[1152,1728]{0,1:T(8,128)(2,1)}, u32[]{:S(2)}) copy-start(bf16[1152,1728]{0,1:T(8,128)(2,1)} %param.17) | copy-start | bytes 11943940
  36.5 6.4 %collective-permute-start.21 = (bf16[32,1152]{1,0:T(8,128)(2,1)S(1)}, bf16[32,1152]{1,0:T(8,128)(2,1)S(1)}, u32[]{:S(2)}, u32[]{:S(2)}) collective-permute-start(bf16[32,1152]{1,0:T(8,128)(2,1)S(1)} %get-tuple-element.64.refs_3_), channel_id=1, source_target_pairs={{0,12},{4,8},{8,4},{12,0},{1,13},{5,9},{9,5},{13,1},{2,14},{6,10},... | collective-permute-start | bytes 221192 | tf_op jit(solution)/shard_map/ppermute | solution.py:365
  40.7 11.2 %collective-permute-start.5 = (bf16[64,1152]{1,0:T(8,128)(2,1)S(1)}, bf16[64,1152]{1,0:T(8,128)(2,1)S(1)}, u32[]{:S(2)}, u32[]{:S(2)}) collective-permute-start(bf16[64,1152]{1,0:T(8,128)(2,1)S(1)} %get-tuple-element.44.refs_7_.refs_5_), channel_id=1, source_target_pairs={{0,4},{4,0},{8,12},{12,8},{1,5},{5,1},{9,13},{13,9},{2,6},{6,2},{1... | collective-permute-start | bytes 442376 | tf_op jit(solution)/shard_map/ppermute | solution.py:365
  40.9 5.7 %collective-permute-start.3 = (bf16[64,1152]{1,0:T(8,128)(2,1)S(1)}, bf16[64,1152]{1,0:T(8,128)(2,1)S(1)}, u32[]{:S(2)}, u32[]{:S(2)}) collective-permute-start(bf16[64,1152]{1,0:T(8,128)(2,1)S(1)} %get-tuple-element.41.refs_8_.refs_1_), channel_id=1, source_target_pairs={{0,8},{4,12},{8,0},{12,4},{1,9},{5,13},{9,1},{13,5},{2,10},{6,14},... | collective-permute-start | bytes 442376 | tf_op jit(solution)/shard_map/ppermute | solution.py:365
  41.2 9.3 %collective-permute-start.4 = (bf16[64,1152]{1,0:T(8,128)(2,1)S(1)}, bf16[64,1152]{1,0:T(8,128)(2,1)S(1)}, u32[]{:S(2)}, u32[]{:S(2)}) collective-permute-start(bf16[64,1152]{1,0:T(8,128)(2,1)S(1)} %get-tuple-element.42.refs_10_.refs_1_), channel_id=1, source_target_pairs={{0,12},{4,8},{8,4},{12,0},{1,13},{5,9},{9,5},{13,1},{2,14},{6,10},... | collective-permute-start | bytes 442376 | tf_op jit(solution)/shard_map/ppermute | solution.py:365
  42.9 9.4 %collective-permute-start.6 = (bf16[64,1152]{1,0:T(8,128)(2,1)S(1)}, bf16[64,1152]{1,0:T(8,128)(2,1)S(1)}, u32[]{:S(2)}, u32[]{:S(2)}) collective-permute-start(bf16[64,1152]{1,0:T(8,128)(2,1)S(1)} %get-tuple-element.45.refs_9_.refs_2_), channel_id=1, source_target_pairs={{0,8},{4,12},{8,0},{12,4},{1,9},{5,13},{9,1},{13,5},{2,10},{6,14},... | collective-permute-start | bytes 442376 | tf_op jit(solution)/shard_map/ppermute | solution.py:365
  43.2 12.8 %collective-permute-start.7 = (bf16[64,1152]{1,0:T(8,128)(2,1)S(1)}, bf16[64,1152]{1,0:T(8,128)(2,1)S(1)}, u32[]{:S(2)}, u32[]{:S(2)}) collective-permute-start(bf16[64,1152]{1,0:T(8,128)(2,1)S(1)} %get-tuple-element.46.refs_11_.refs_2_), channel_id=1, source_target_pairs={{0,12},{4,8},{8,4},{12,0},{1,13},{5,9},{9,5},{13,1},{2,14},{6,10},... | collective-permute-start | bytes 442376 | tf_op jit(solution)/shard_map/ppermute | solution.py:365
  59.3 11.0 %collective-permute-start.22 = (bf16[32,2304]{1,0:T(8,128)(2,1)S(1)}, bf16[32,2304]{1,0:T(8,128)(2,1)S(1)}, u32[]{:S(2)}, u32[]{:S(2)}) collective-permute-start(bf16[32,2304]{1,0:T(8,128)(2,1)S(1)} %get-tuple-element.66), channel_id=1, source_target_pairs={{4,0},{0,4},{12,8},{8,12},{5,1},{1,5},{13,9},{9,13},{6,2},{2,6},{1... | collective-permute-start | bytes 442376 | tf_op jit(solution)/shard_map/ppermute | solution.py:450
  59.3 2.4 %collective-permute-start.10 = (bf16[32,1152]{1,0:T(8,128)(2,1)S(1)}, bf16[32,1152]{1,0:T(8,128)(2,1)S(1)}, u32[]{:S(2)}, u32[]{:S(2)}) collective-permute-start(bf16[32,1152]{1,0:T(8,128)(2,1)S(1)} %get-tuple-element.50.refs_1_), channel_id=1, source_target_pairs={{0,4},{4,0},{8,12},{12,8},{1,5},{5,1},{9,13},{13,9},{2,6},{6,2},{1... | collective-permute-start | bytes 221192 | tf_op jit(solution)/shard_map/ppermute | solution.py:365
  59.8 3.7 %collective-permute-start.11 = (bf16[32,1152]{1,0:T(8,128)(2,1)S(1)}, bf16[32,1152]{1,0:T(8,128)(2,1)S(1)}, u32[]{:S(2)}, u32[]{:S(2)}) collective-permute-start(bf16[32,1152]{1,0:T(8,128)(2,1)S(1)} %get-tuple-element.51.refs_2_), channel_id=1, source_target_pairs={{0,8},{4,12},{8,0},{12,4},{1,9},{5,13},{9,1},{13,5},{2,10},{6,14},... | collective-permute-start | bytes 221192 | tf_op jit(solution)/shard_map/ppermute | solution.py:365
  60.1 5.9 %collective-permute-start.12 = (bf16[32,1152]{1,0:T(8,128)(2,1)S(1)}, bf16[32,1152]{1,0:T(8,128)(2,1)S(1)}, u32[]{:S(2)}, u32[]{:S(2)}) collective-permute-start(bf16[32,1152]{1,0:T(8,128)(2,1)S(1)} %get-tuple-element.52.refs_3_), channel_id=1, source_target_pairs={{0,12},{4,8},{8,4},{12,0},{1,13},{5,9},{9,5},{13,1},{2,14},{6,10},... | collective-permute-start | bytes 221192 | tf_op jit(solution)/shard_map/ppermute | solution.py:365
  61.6 13.2 %collective-permute-start.23 = (bf16[32,2304]{1,0:T(8,128)(2,1)S(1)}, bf16[32,2304]{1,0:T(8,128)(2,1)S(1)}, u32[]{:S(2)}, u32[]{:S(2)}) collective-permute-start(bf16[32,2304]{1,0:T(8,128)(2,1)S(1)} %get-tuple-element.67), channel_id=1, source_target_pairs={{8,0},{12,4},{0,8},{4,12},{9,1},{13,5},{1,9},{5,13},{10,2},{14,6},... | collective-permute-start | bytes 442376 | tf_op jit(solution)/shard_map/ppermute | solution.py:450
  61.8 13.0 %collective-permute-start.24 = (bf16[32,2304]{1,0:T(8,128)(2,1)S(1)}, bf16[32,2304]{1,0:T(8,128)(2,1)S(1)}, u32[]{:S(2)}, u32[]{:S(2)}) collective-permute-start(bf16[32,2304]{1,0:T(8,128)(2,1)S(1)} %get-tuple-element.68), channel_id=1, source_target_pairs={{12,0},{8,4},{4,8},{0,12},{13,1},{9,5},{5,9},{1,13},{14,2},{10,6},... | collective-permute-start | bytes 442376 | tf_op jit(solution)/shard_map/ppermute | solution.py:450
  68.1 4.1 %copy-start.8 = (f32[1152]{0:T(1024)S(1)}, f32[1152]{0:T(1024)}, u32[]{:S(2)}) copy-start(f32[1152]{0:T(1024)} %param.19) | copy-start | bytes 13828
  70.0 7.7 %collective-permute-start.18 = (bf16[32,2304]{1,0:T(8,128)(2,1)S(1)}, bf16[32,2304]{1,0:T(8,128)(2,1)S(1)}, u32[]{:S(2)}, u32[]{:S(2)}) collective-permute-start(bf16[32,2304]{1,0:T(8,128)(2,1)S(1)} %get-tuple-element.60), channel_id=1, source_target_pairs={{4,0},{0,4},{12,8},{8,12},{5,1},{1,5},{13,9},{9,13},{6,2},{2,6},{1... | collective-permute-start | bytes 442376 | tf_op jit(solution)/shard_map/ppermute | solution.py:450
  70.1 9.8 %collective-permute-start.17 = (bf16[32,2304]{1,0:T(8,128)(2,1)S(1)}, bf16[32,2304]{1,0:T(8,128)(2,1)S(1)}, u32[]{:S(2)}, u32[]{:S(2)}) collective-permute-start(bf16[32,2304]{1,0:T(8,128)(2,1)S(1)} %get-tuple-element.58), channel_id=1, source_target_pairs={{8,0},{12,4},{0,8},{4,12},{9,1},{13,5},{1,9},{5,13},{10,2},{14,6},... | collective-permute-start | bytes 442376 | tf_op jit(solution)/shard_map/ppermute | solution.py:450
  70.2 11.6 %collective-permute-start.16 = (bf16[32,2304]{1,0:T(8,128)(2,1)S(1)}, bf16[32,2304]{1,0:T(8,128)(2,1)S(1)}, u32[]{:S(2)}, u32[]{:S(2)}) collective-permute-start(bf16[32,2304]{1,0:T(8,128)(2,1)S(1)} %get-tuple-element.57), channel_id=1, source_target_pairs={{12,0},{8,4},{4,8},{0,12},{13,1},{9,5},{5,9},{1,13},{14,2},{10,6},... | collective-permute-start | bytes 442376 | tf_op jit(solution)/shard_map/ppermute | solution.py:450
  73.5 1.3 %copy-start.3 = (bf16[576,1152]{1,0:T(8,128)(2,1)S(1)}, bf16[576,1152]{1,0:T(8,128)(2,1)}, u32[]{:S(2)}) copy-start(bf16[576,1152]{1,0:T(8,128)(2,1)} %refs_4_.3) | copy-start | bytes 3981316

commit v2 on v1

--- a/solution.py
+++ b/solution.py
@@ -75,10 +75,17 @@
     pl.when(jnp.logical_not(even))(functools.partial(fill, a_ref, b_ref))
 
 
-def split_kernel(place, *refs):
-    n = len(refs) // 2
-    for src, dst in zip(refs[:n], refs[n:]):
-        dst[...] = src[...]
+def split_kernel(place, src, *refs):
+    outs, sems = refs[:-1], refs[-1]
+    late, share, _ = outs[0].shape
+    copies = []
+    for j, dst in enumerate(outs):
+        start = pl.multiple_of(peer(place[0], j, len(outs)) * share, SUB)
+        part = src.at[pl.ds(src.shape[0] - late, late), pl.ds(start, share), :]
+        copies.append(pltpu.make_async_copy(part, dst, sems.at[j]))
+        copies[-1].start()
+    for copy in copies:
+        copy.wait()
 
 
 def attend(frame, place, counts, lists, q_ref, keys, att):
@@ -130,15 +137,29 @@
     pipeline([(f, h) for f in range(n) for h in range(width // HEAD_DIM)], scores, weigh, gather)
 
 
-def add_normed(base, proj, gain):
-    scale = lax.rsqrt(jnp.mean(proj * proj, axis=-1, keepdims=True) + EPS)
-    return (base.astype(F32) + proj * scale * gain).astype(BF)
+def add_normed(blocks):
+    ahead = blocks[0][0]()
+    for n, (_, finish) in enumerate(blocks):
+        proj = ahead
+        if n + 1 < len(blocks):
+            ahead = blocks[n + 1][0]()
+        scale = lax.rsqrt(jnp.mean(proj * proj, axis=-1, keepdims=True) + EPS)
+        finish(proj * scale)
 
 
 def spatial_kernel(frame, n_groups, place, counts, lists, q_ref, a_ref, b_ref, ra_ref, rb_ref, h_ref, w_ref, g_ref, *rest):
     outs, (att, mix) = rest[:n_groups], rest[n_groups:]
     attend(frame, place, counts, lists, q_ref, (a_ref, b_ref, ra_ref, rb_ref), att)
-    mix[...] = add_normed(h_ref[0], contract(att[0], w_ref[...], 0, 0), g_ref[...])
+
+    def block(at):
+        rows = slice(at, at + TILE)
+
+        def finish(normed):
+            mix[rows, :] = (h_ref[0, rows, :].astype(F32) + normed * g_ref[...]).astype(BF)
+
+        return lambda: contract(att[0, :, rows], w_ref[...], 0, 0), finish
+
+    add_normed([block(at) for at in range(0, mix.shape[0], TILE)])
     share = mix.shape[0] // n_groups
     for j, out in enumerate(outs):
         group = peer(place[0], j, n_groups)
@@ -162,12 +183,15 @@
     atts, hids = refs[:len(refs) // 2 - 1], refs[len(refs) // 2 - 1:-3]
     w_ref, g_ref, out = refs[-3:]
     width = w_ref.shape[0]
-    n, rows, _ = hids[0].shape
-    for j, (att, hid) in enumerate(zip(atts, hids)):
-        x = jnp.concatenate([att[:, f * width:(f + 1) * width] for f in range(n)], axis=0)
-        proj = contract(x, w_ref[...], 1, 0)
-        for f in range(n):
-            out[j, f] = add_normed(hid[f], proj[f * rows:(f + 1) * rows, :], g_ref[...])
+    n, _, _ = hids[0].shape
+
+    def block(j, f):
+        def finish(normed):
+            out[j, f] = (hids[j][f].astype(F32) + normed * g_ref[...]).astype(BF)
+
+        return lambda: contract(atts[j][:, f * width:(f + 1) * width], w_ref[...], 1, 0), finish
+
+    add_normed([block(j, f) for j in range(len(atts)) for f in range(n)])
 
 
 def paired(chunks, lanes, frames):
@@ -216,7 +240,16 @@
                 piece = slice(c * SUB, (c + 1) * SUB)
                 a[at:at + SUB, :] = atts[j][piece, f * width:(f + 1) * width]
                 b[at:at + SUB, :] = hids[j][f, piece, :]
-    x[...] = add_normed(b[...], contract(a[...], w_ref[...], 1, 0), g_ref[...])
+
+    def block(at):
+        cut = slice(at, at + TILE)
+
+        def finish(normed):
+            x[cut, :] = (b[cut, :].astype(F32) + normed * g_ref[...]).astype(BF)
+
+        return lambda: contract(a[cut, :], w_ref[...], 1, 0), finish
+
+    add_normed([block(at) for at in range(0, x.shape[0], TILE)])
     project(qkv_ref, x, out)
 
 
@@ -275,17 +308,26 @@
     width = w_ref.shape[0]
     frames = early + late
     copies = []
-    for i, j in enumerate(js):
-        x = jnp.concatenate([atts[i][:, f * width:(f + 1) * width] for f in range(frames)], axis=0)
-        proj = contract(x, w_ref[...], 1, 0)
-        for f in range(frames):
-            mine = pieces[i * early + f][...] if f < early else late_ref[j, f - early]
-            buf[i, f] = add_normed(mine, proj[f * rows:(f + 1) * rows, :], g_ref[...])
-        group = peer(place[0], j, n_groups)
-        start = pl.multiple_of((group * halves + half) * rows, SUB)
-        copy = pltpu.make_async_copy(buf.at[i], out.at[:, pl.ds(start, rows), :], sems.at[i])
-        copy.start()
-        copies.append(copy)
+
+    def block(i, j):
+        def start():
+            x = jnp.concatenate([atts[i][:, f * width:(f + 1) * width] for f in range(frames)], axis=0)
+            return contract(x, w_ref[...], 1, 0)
+
+        def finish(normed):
+            for f in range(frames):
+                mine = pieces[i * early + f][...] if f < early else late_ref[j, f - early]
+                part = normed[f * rows:(f + 1) * rows, :] * g_ref[...]
+                buf[i, f] = (mine.astype(F32) + part).astype(BF)
+            group = peer(place[0], j, n_groups)
+            at = pl.multiple_of((group * halves + half) * rows, SUB)
+            copy = pltpu.make_async_copy(buf.at[i], out.at[:, pl.ds(at, rows), :], sems.at[i])
+            copy.start()
+            copies.append(copy)
+
+        return start, finish
+
+    add_normed([block(i, j) for i, j in enumerate(js)])
     for copy in copies:
         copy.wait()
 
@@ -324,6 +366,7 @@
     far = [e for i in range(1, strips - 1, 2) for e in ((i, i + 1), (i + 1, i))]
     edge = jax.ShapeDtypeStruct((2 * width, TILE), BF)
     smem = pl.BlockSpec(memory_space=pltpu.SMEM)
+    any_spec = pl.BlockSpec(memory_space=pl.ANY)
 
     def call(kernel, in_specs, out_specs, out_shape, scratch=(), limit=32, prefetch=0, alias=None):
         return pl.pallas_call(
@@ -366,15 +409,12 @@
 
     own_hidden = call(
         split_kernel,
-        [
-            pl.BlockSpec((late, share, model), lambda _, at, j=j: (1, peer(at[0], j, groups), 0))
-            for j in range(groups)
-        ],
-        [whole((late, share, model))] * groups,
+        [smem, any_spec],
+        [any_spec] * groups,
         [jax.ShapeDtypeStruct((late, share, model), BF)] * groups,
-        prefetch=1,
+        [pltpu.SemaphoreType.DMA((groups,))],
         limit=16,
-    )(place, *[hidden_far] * groups)
+    )(place, hidden_far)
     far_hidden = [send(x, j) for j, x in enumerate(own_hidden)]
 
     mixed = [[None] * early for _ in range(groups)]
@@ -396,6 +436,7 @@
         )(place, counts, lists, queries, *halos[0], hidden, spatial_out_weight, gain_one)
         for j in range(groups):
             mixed[j][f] = parts[j]
+        arrived = [send(x, j) for j, x in enumerate(parts)]
         projected.append(
             call(
                 functools.partial(project_kernel, f, frames),
@@ -403,7 +444,7 @@
                 whole((3 * width, tokens)),
                 jax.ShapeDtypeStruct((3 * width, tokens), BF),
                 [pltpu.VMEM((tokens, model), BF)],
-            )(*[send(x, j) for j, x in enumerate(parts)], qkv_weight)
+            )(*arrived, qkv_weight)
         )
 
     late_shape = (rows, late * width)
@@ -416,7 +457,9 @@
         [pltpu.VMEM((late, width, tokens), F32), pltpu.VMEM((tokens, late * width), BF)],
     )(place, counts, lists, queries, *halos[1])
     own_late = [own_late[half * groups:(half + 1) * groups] for half in range(halves)]
-    far_late = [[send(x, j) for j, x in enumerate(some)] for some in own_late]
+    far_late = []
+    for half in range(halves):
+        far_late.append([send(x, j) for j, x in enumerate(own_late[half])])
 
     returned, late_mixed = [], []
     back_shape = (rows, frames * width)
@@ -459,10 +502,9 @@
         )
 
     out = None
-    any_spec = pl.BlockSpec(memory_space=pl.ANY)
     for half in range(halves):
         piece = pl.BlockSpec((rows, model), lambda *_, half=half: (half, 0))
-        cuts = [groups] if half + 1 < halves else [groups // 2, groups * 3 // 4, groups]
+        cuts = [groups]
         for lo, hi in zip([0] + cuts, cuts):
             js = range(lo, hi)
             if not js:

time: 84.1 us -> 88.2 us (1.049)
  the two profiles are of different devices: /device:TPU:21 before, /device:TPU:17 now
where the time goes in v2:
time: 88.2 us; the launch traced here: 88 us
  Pallas kernels  34.2 us (39%)
  starting transfers between devices  29.4 us (33%)
  waiting for transfers between devices  23.8 us (27%)
    ppermute x15, starting transfers between devices, send(): return x if j == 0 else lax.ppermute(x, 'frame', out_pairs(j))  18.3 us
    ppermute x15, waiting for transfers between devices, send(): return x if j == 0 else lax.ppermute(x, 'frame', out_pairs(j))  11.9 us
    pallas_call x2, Pallas kernels, shards(): call(functools.partial(output_kernel, groups, tuple(js), early, half, hal...  5.77 us
    pallas_call x2, Pallas kernels, shards(): call(functools.partial(spatial_kernel, f, groups), [smem, smem, smem, fra...  5.45 us
    ppermute x2, starting transfers between devices, shards(): lax.ppermute(b, 'strip', far)  5.4 us
    ppermute x2, waiting for transfers between devices, shards(): lax.ppermute(a, 'strip', near)  4.91 us
    pallas_call x2, Pallas kernels, shards(): call(functools.partial(late_project_kernel, early, frames), late_specs +...  4.48 us
    ppermute x6, starting transfers between devices, shards(): got.append(back[j] if j == 0 else lax.ppermute(back[j], 'frame', pairs))  4.3 us
  transfers between devices with their start and end apart: 25, of which 11 were waited for; matrix products, arithmetic and copies ran while one was open for 0% of the time, Pallas kernels for 30%

profile of v2, /device:TPU:17, one launch (start us, length us, event | category | flops | bytes accessed | tf_op | source)
XLA Modules:
  0.0 88.0 jit_solution(5390632362348890717)
XLA Ops:
  0.0 0.1 pad_add_fusion.place
  0.1 1.6 %shard_map.109 = (bf16[2,1152,128]{2,1,0:T(8,128)(2,1)S(1)}, bf16[2,1152,128]{2,1,0:T(8,128)(2,1)S(1)}) custom-call(s32[2]{0:T(128)S(1)} %pad_add_fusion.place, bf16[4,576,256]{2,1,0:T(8,128)(2,1)} %bitcast.21, bf16[4,576,256]{2,1,0:T(8,128)(2,1)} %bitcast.23), custom_call_target="tpu_custom_call" | custom-call | tf_op jit(solution)/shard_map/pallas_call | solution.py:395
  1.7 1.4 %collective-permute-start = (bf16[2,1152,128]{2,1,0:T(8,128)(2,1)S(1)}, bf16[2,1152,128]{2,1,0:T(8,128)(2,1)S(1)}, u32[]{:S(2)}, u32[]{:S(2)}) collective-permute-start(bf16[2,1152,128]{2,1,0:T(8,128)(2,1)S(1)} %get-tuple-element.37.a_ref), channel_id=1, source_target_pairs={{0,1},{1,0},{2,3},{3,2},{4,5},{5,4},{6,7},{7,6},{8,9},{9,8},{10,11... | collective-permute-start | bytes 1769480 | tf_op jit(solution)/shard_map/ppermute | solution.py:402
  3.0 1.9 %collective-permute-start.1 = (bf16[2,1152,128]{2,1,0:T(8,128)(2,1)S(1)}, bf16[2,1152,128]{2,1,0:T(8,128)(2,1)S(1)}, u32[]{:S(2)}, u32[]{:S(2)}) collective-permute-start(bf16[2,1152,128]{2,1,0:T(8,128)(2,1)S(1)} %get-tuple-element.38.b_ref), channel_id=1, source_target_pairs={{1,2},{2,1},{5,6},{6,5},{9,10},{10,9},{13,14},{14,13},{17,18},{18,... | collective-permute-start | bytes 1769480 | tf_op jit(solution)/shard_map/ppermute | solution.py:402
  5.0 0.0 copy-start.2
  5.0 1.6 %shard_map.114 = (bf16[2,1152,128]{2,1,0:T(8,128)(2,1)S(1)}, bf16[2,1152,128]{2,1,0:T(8,128)(2,1)S(1)}) custom-call(s32[2]{0:T(128)S(1)} %pad_add_fusion.place, bf16[4,576,256]{2,1,0:T(8,128)(2,1)} %bitcast.22, bf16[4,576,256]{2,1,0:T(8,128)(2,1)} %bitcast.24), custom_call_target="tpu_custom_call" | custom-call | tf_op jit(solution)/shard_map/pallas_call | solution.py:395
  6.6 0.0 copy-start.7
  6.6 0.0 copy-start.1
  6.6 0.0 copy-start.5
  6.7 0.0 copy-start.6
  6.7 0.1 collective-permute-start.8
  6.8 3.5 %collective-permute-start.9 = (bf16[2,1152,128]{2,1,0:T(8,128)(2,1)S(1)}, bf16[2,1152,128]{2,1,0:T(8,128)(2,1)S(1)}, u32[]{:S(2)}, u32[]{:S(2)}) collective-permute-start(bf16[2,1152,128]{2,1,0:T(8,128)(2,1)S(1)} %get-tuple-element.48.b_ref), channel_id=1, source_target_pairs={{1,2},{2,1},{5,6},{6,5},{9,10},{10,9},{13,14},{14,13},{17,18},{18,... | collective-permute-start | bytes 1769480 | tf_op jit(solution)/shard_map/ppermute | solution.py:402
  10.3 1.8 %shard_map.116 = (bf16[2,64,1152]{2,1,0:T(8,128)(2,1)S(1)}, bf16[2,64,1152]{2,1,0:T(8,128)(2,1)S(1)}, bf16[2,64,1152]{2,1,0:T(8,128)(2,1)S(1)}, bf16[2,64,1152]{2,1,0:T(8,128)(2,1)S(1)}) custom-call(s32[2]{0:T(128)S(1)} %pad_add_fusion.place, bf16[4,256,1152]{2,1,0:T(8,128)(2,1)} %src.1), custom_call_target="tpu_custom_call" | custom-call | tf_op jit(solution)/shard_map/pallas_call | solution.py:410
  12.1 1.6 %collective-permute-start.13 = (bf16[2,64,1152]{2,1,0:T(8,128)(2,1)S(1)}, bf16[2,64,1152]{2,1,0:T(8,128)(2,1)S(1)}, u32[]{:S(2)}, u32[]{:S(2)}) collective-permute-start(bf16[2,64,1152]{2,1,0:T(8,128)(2,1)S(1)} %get-tuple-element.54.refs_5_), channel_id=1, source_target_pairs={{0,4},{4,0},{8,12},{12,8},{1,5},{5,1},{9,13},{13,9},{2,6},{6,2},{1... | collective-permute-start | bytes 884744 | tf_op jit(solution)/shard_map/ppermute | solution.py:408
  13.7 2.3 %collective-permute-done.ra_ref = bf16[2,1152,128]{2,1,0:T(8,128)(2,1)S(1)} collective-permute-done((bf16[2,1152,128]{2,1,0:T(8,128)(2,1)S(1)}, bf16[2,1152,128]{2,1,0:T(8,128)(2,1)S(1)}, u32[]{:S(2)}, u32[]{:S(2)}) %collective-permute-start) | collective-permute-done | bytes 589856 | tf_op jit(solution)/shard_map/ppermute | solution.py:402
  16.0 1.2 %collective-permute-start.14 = (bf16[2,64,1152]{2,1,0:T(8,128)(2,1)S(1)}, bf16[2,64,1152]{2,1,0:T(8,128)(2,1)S(1)}, u32[]{:S(2)}, u32[]{:S(2)}) collective-permute-start(bf16[2,64,1152]{2,1,0:T(8,128)(2,1)S(1)} %get-tuple-element.55.refs_6_), channel_id=1, source_target_pairs={{0,8},{4,12},{8,0},{12,4},{1,9},{5,13},{9,1},{13,5},{2,10},{6,14},... | collective-permute-start | bytes 884744 | tf_op jit(solution)/shard_map/ppermute | solution.py:408
  17.2 1.7 %collective-permute-done.1.rb_ref = bf16[2,1152,128]{2,1,0:T(8,128)(2,1)S(1)} collective-permute-done((bf16[2,1152,128]{2,1,0:T(8,128)(2,1)S(1)}, bf16[2,1152,128]{2,1,0:T(8,128)(2,1)S(1)}, u32[]{:S(2)}, u32[]{:S(2)}) %collective-permute-start.1) | collective-permute-done | bytes 589856 | tf_op jit(solution)/shard_map/ppermute | solution.py:402
  18.9 4.3 %collective-permute-start.15 = (bf16[2,64,1152]{2,1,0:T(8,128)(2,1)S(1)}, bf16[2,64,1152]{2,1,0:T(8,128)(2,1)S(1)}, u32[]{:S(2)}, u32[]{:S(2)}) collective-permute-start(bf16[2,64,1152]{2,1,0:T(8,128)(2,1)S(1)} %get-tuple-element.56.refs_7_), channel_id=1, source_target_pairs={{0,12},{4,8},{8,4},{12,0},{1,13},{5,9},{9,5},{13,1},{2,14},{6,10},... | collective-permute-start | bytes 884744 | tf_op jit(solution)/shard_map/ppermute | solution.py:408
  23.3 2.7 %shard_map.110 = (bf16[64,1152]{1,0:T(8,128)(2,1)S(1)}, bf16[64,1152]{1,0:T(8,128)(2,1)S(1)}, bf16[64,1152]{1,0:T(8,128)(2,1)S(1)}, bf16[64,1152]{1,0:T(8,128)(2,1)S(1)}) custom-call(s32[2]{0:T(128)S(1)} %pad_add_fusion.place, s32[2,4]{1,0:T(2,128)S(1)} %bitcast.18, s32[3,2,4]{2,1,0:T(2,128)S(1)} %bitcast.15, bf16[4,576,256]{2,1,0:T(8,128)(2,1)S(1)} %bitcast.12, ...), custom_call_target="tpu_custom_call" | custom-call | tf_op jit(solution)/shard_map/pallas_call | solution.py:424
  26.0 2.6 %collective-permute-done.8.ra_ref = bf16[2,1152,128]{2,1,0:T(8,128)(2,1)S(1)} collective-permute-done((bf16[2,1152,128]{2,1,0:T(8,128)(2,1)S(1)}, bf16[2,1152,128]{2,1,0:T(8,128)(2,1)S(1)}, u32[]{:S(2)}, u32[]{:S(2)}) %collective-permute-start.8) | collective-permute-done | bytes 589856 | tf_op jit(solution)/shard_map/ppermute | solution.py:402
  28.6 1.5 %collective-permute-start.2 = (bf16[64,1152]{1,0:T(8,128)(2,1)S(1)}, bf16[64,1152]{1,0:T(8,128)(2,1)S(1)}, u32[]{:S(2)}, u32[]{:S(2)}) collective-permute-start(bf16[64,1152]{1,0:T(8,128)(2,1)S(1)} %get-tuple-element.40.refs_6_), channel_id=1, source_target_pairs={{0,4},{4,0},{8,12},{12,8},{1,5},{5,1},{9,13},{13,9},{2,6},{6,2},{1... | collective-permute-start | bytes 442376 | tf_op jit(solution)/shard_map/ppermute | solution.py:408
  30.1 1.4 %collective-permute-done.9.rb_ref = bf16[2,1152,128]{2,1,0:T(8,128)(2,1)S(1)} collective-permute-done((bf16[2,1152,128]{2,1,0:T(8,128)(2,1)S(1)}, bf16[2,1152,128]{2,1,0:T(8,128)(2,1)S(1)}, u32[]{:S(2)}, u32[]{:S(2)}) %collective-permute-start.9) | collective-permute-done | bytes 589856 | tf_op jit(solution)/shard_map/ppermute | solution.py:402
  31.5 3.0 %shard_map.115 = (bf16[32,1152]{1,0:T(8,128)(2,1)S(1)}, bf16[32,1152]{1,0:T(8,128)(2,1)S(1)}, bf16[32,1152]{1,0:T(8,128)(2,1)S(1)}, bf16[32,1152]{1,0:T(8,128)(2...) custom-call(s32[2]{0:T(128)S(1)} %pad_add_fusion.place, ...), custom_call_target="tpu_custom_call" | custom-call | tf_op jit(solution)/shard_map/pallas_call | solution.py:451
  34.5 1.9 %collective-permute-start.19 = (bf16[32,1152]{1,0:T(8,128)(2,1)S(1)}, bf16[32,1152]{1,0:T(8,128)(2,1)S(1)}, u32[]{:S(2)}, u32[]{:S(2)}) collective-permute-start(bf16[32,1152]{1,0:T(8,128)(2,1)S(1)} %get-tuple-element.62.refs_1_), channel_id=1, source_target_pairs={{0,4},{4,0},{8,12},{12,8},{1,5},{5,1},{9,13},{13,9},{2,6},{6,2},{1... | collective-permute-start | bytes 221192 | tf_op jit(solution)/shard_map/ppermute | solution.py:408
  36.4 1.2 %collective-permute-start.20 = (bf16[32,1152]{1,0:T(8,128)(2,1)S(1)}, bf16[32,1152]{1,0:T(8,128)(2,1)S(1)}, u32[]{:S(2)}, u32[]{:S(2)}) collective-permute-start(bf16[32,1152]{1,0:T(8,128)(2,1)S(1)} %get-tuple-element.63.refs_2_), channel_id=1, source_target_pairs={{0,8},{4,12},{8,0},{12,4},{1,9},{5,13},{9,1},{13,5},{2,10},{6,14},... | collective-permute-start | bytes 221192 | tf_op jit(solution)/shard_map/ppermute | solution.py:408
  37.6 0.5 collective-permute-start.21
  38.1 2.7 %shard_map.112 = (bf16[64,1152]{1,0:T(8,128)(2,1)S(1)}, bf16[64,1152]{1,0:T(8,128)(2,1)S(1)}, bf16[64,1152]{1,0:T(8,128)(2,1)S(1)}, bf16[64,1152]{1,0:T(8,128)(2,1)S(1)}) custom-call(s32[2]{0:T(128)S(1)} %pad_add_fusion.place, s32[2,4]{1,0:T(2,128)S(1)} %bitcast.20, s32[3,2,4]{2,1,0:T(2,128)S(1)} %bitcast.17, bf16[4,576,256]{2,1,0:T(8,128)(2,1)S(1)} %bitcast.14, ...), custom_call_target="tpu_custom_call" | custom-call | tf_op jit(solution)/shard_map/pallas_call | solution.py:424
  40.8 0.0 collective-permute-done.15.refs_7_
  40.9 0.2 collective-permute-start.5
  41.1 0.0 collective-permute-done.19.refs_1_
  41.1 1.2 %collective-permute-start.3 = (bf16[64,1152]{1,0:T(8,128)(2,1)S(1)}, bf16[64,1152]{1,0:T(8,128)(2,1)S(1)}, u32[]{:S(2)}, u32[]{:S(2)}) collective-permute-start(bf16[64,1152]{1,0:T(8,128)(2,1)S(1)} %get-tuple-element.41.refs_8_), channel_id=1, source_target_pairs={{0,8},{4,12},{8,0},{12,4},{1,9},{5,13},{9,1},{13,5},{2,10},{6,14},... | collective-permute-start | bytes 442376 | tf_op jit(solution)/shard_map/ppermute | solution.py:408
  42.3 0.0 collective-permute-done.20.refs_2_
  42.3 0.8 collective-permute-start.4
  43.1 0.0 collective-permute-done.21.refs_3_
  43.1 1.2 %collective-permute-start.6 = (bf16[64,1152]{1,0:T(8,128)(2,1)S(1)}, bf16[64,1152]{1,0:T(8,128)(2,1)S(1)}, u32[]{:S(2)}, u32[]{:S(2)}) collective-permute-start(bf16[64,1152]{1,0:T(8,128)(2,1)S(1)} %get-tuple-element.45.refs_9_), channel_id=1, source_target_pairs={{0,8},{4,12},{8,0},{12,4},{1,9},{5,13},{9,1},{13,5},{2,10},{6,14},... | collective-permute-start | bytes 442376 | tf_op jit(solution)/shard_map/ppermute | solution.py:408
  44.3 0.3 collective-permute-start.7
  44.7 2.1 %shard_map.120.refs_2_.refs_3_ = bf16[1728,256]{1,0:T(8,128)(2,1)S(1)} custom-call(bf16[32,1152]{1,0:T(8,128)(2,1)S(1)} %get-tuple-element.61.refs_0_, bf16[32,1152]{1,0:T(8,128)(2,1)S(1)} %collective-permute-done.19.refs_1_, bf16[32,1152]{1,0:T(8,128)(2,1)S(1)} %collective-permute-done.20.refs_2_, bf16[32,1152]{1,0:T(8,128)(2,1)S(1)} %collective-permute-done.21.refs_3_, ...), custom_call_target="tpu_custom_call" | custom-call | tf_op jit(solution)/shard_map/pallas_call | solution.py:471
  46.8 0.0 collective-permute-done.3.refs_2_
  46.8 3.8 %collective-permute-done.4.refs_3_ = bf16[64,1152]{1,0:T(8,128)(2,1)S(1)} collective-permute-done((bf16[64,1152]{1,0:T(8,128)(2,1)S(1)}, bf16[64,1152]{1,0:T(8,128)(2,1)S(1)}, u32[]{:S(2)}, u32[]{:S(2)}) %collective-permute-start.4) | collective-permute-done | bytes 147488 | tf_op jit(solution)/shard_map/ppermute | solution.py:408
  50.6 1.4 %shard_map.111.refs_0_ = bf16[1728,256]{1,0:T(8,128)(2,1)S(1)} custom-call(bf16[64,1152]{1,0:T(8,128)(2,1)S(1)} %get-tuple-element.39.refs_0_.refs_4_, bf16[64,1152]{1,0:T(8,128)(2,1)S(1)} %collective-permute-done.2.refs_1_, bf16[64,1152]{1,0:T(8,128)(2,1)S(1)} %collective-permute-done.3.refs_2_, bf16[64,1152]{1,0:T(8,128)(2,1)S(1)} %collective-permute-done.4.refs_3_, ...), custom_call_target="tpu_custom_call" | custom-call | tf_op jit(solution)/shard_map/pallas_call | solution.py:441
  52.0 0.4 collective-permute-done.6.refs_2_
  52.4 3.7 %collective-permute-done.7.refs_3_ = bf16[64,1152]{1,0:T(8,128)(2,1)S(1)} collective-permute-done((bf16[64,1152]{1,0:T(8,128)(2,1)S(1)}, bf16[64,1152]{1,0:T(8,128)(2,1)S(1)}, u32[]{:S(2)}, u32[]{:S(2)}) %collective-permute-start.7) | collective-permute-done | bytes 147488 | tf_op jit(solution)/shard_map/ppermute | solution.py:408
  56.1 1.4 %shard_map.113.refs_1_ = bf16[1728,256]{1,0:T(8,128)(2,1)S(1)} custom-call(bf16[64,1152]{1,0:T(8,128)(2,1)S(1)} %get-tuple-element.43.refs_0_.refs_5_, bf16[64,1152]{1,0:T(8,128)(2,1)S(1)} %collective-permute-done.5.refs_1_, bf16[64,1152]{1,0:T(8,128)(2,1)S(1)} %collective-permute-done.6.refs_2_, bf16[64,1152]{1,0:T(8,128)(2,1)S(1)} %collective-permute-done.7.refs_3_, ...), custom_call_target="tpu_custom_call" | custom-call | tf_op jit(solution)/shard_map/pallas_call | solution.py:441
  57.5 1.9 %shard_map.121 = (bf16[32,2304]{1,0:T(8,128)(2,1)S(1)}, bf16[32,2304]{1,0:T(8,128)(2,1)S(1)}, bf16[32,2304]{1,0:T(8,128)(2,1)S(1)}, bf16[32,2304]{1,0:T(8,128)(2,1)S(1)}) custom-call(bf16[1728,256]{1,0:T(8,128)(2,1)S(1)} %shard_map.111.refs_0_, bf16[1728,256]{1,0:T(8,128)(2,1)S(1)} %shard_map.113.refs_1_, bf16[1728,256]{1,0:T(8,128)(2,1)S(1)} %shard_map.120.refs_2_.refs_3_, ...), custom_call_target="tpu_custom_call" | custom-call | tf_op jit(solution)/shard_map/pallas_call | solution.py:482
  59.4 0.1 collective-permute-start.22
  59.5 0.5 collective-permute-start.10
  60.0 1.2 %collective-permute-start.11 = (bf16[32,1152]{1,0:T(8,128)(2,1)S(1)}, bf16[32,1152]{1,0:T(8,128)(2,1)S(1)}, u32[]{:S(2)}, u32[]{:S(2)}) collective-permute-start(bf16[32,1152]{1,0:T(8,128)(2,1)S(1)} %get-tuple-element.51.refs_2_), channel_id=1, source_target_pairs={{0,8},{4,12},{8,0},{12,4},{1,9},{5,13},{9,1},{13,5},{2,10},{6,14},... | collective-permute-start | bytes 221192 | tf_op jit(solution)/shard_map/ppermute | solution.py:408
  61.2 0.5 collective-permute-start.12
  61.7 2.0 %collective-permute-done.11.refs_2_ = bf16[32,1152]{1,0:T(8,128)(2,1)S(1)} collective-permute-done((bf16[32,1152]{1,0:T(8,128)(2,1)S(1)}, bf16[32,1152]{1,0:T(8,128)(2,1)S(1)}, u32[]{:S(2)}, u32[]{:S(2)}) %collective-permute-start.11) | collective-permute-done | bytes 73760 | tf_op jit(solution)/shard_map/ppermute | solution.py:408
  63.7 1.9 %collective-permute-done.12.refs_3_ = bf16[32,1152]{1,0:T(8,128)(2,1)S(1)} collective-permute-done((bf16[32,1152]{1,0:T(8,128)(2,1)S(1)}, bf16[32,1152]{1,0:T(8,128)(2,1)S(1)}, u32[]{:S(2)}, u32[]{:S(2)}) %collective-permute-start.12) | collective-permute-done | bytes 73760 | tf_op jit(solution)/shard_map/ppermute | solution.py:408
  65.6 2.3 %shard_map.117.refs_2_.refs_3_ = bf16[1728,256]{1,0:T(8,128)(2,1)S(1)} custom-call(bf16[32,1152]{1,0:T(8,128)(2,1)S(1)} %get-tuple-element.49.refs_0_, bf16[32,1152]{1,0:T(8,128)(2,1)S(1)} %collective-permute-done.10.refs_1_, bf16[32,1152]{1,0:T(8,128)(2,1)S(1)} %collective-permute-done.11.refs_2_, bf16[32,1152]{1,0:T(8,128)(2,1)S(1)} %collective-permute-done.12.refs_3_, ...), custom_call_target="tpu_custom_call" | custom-call | tf_op jit(solution)/shard_map/pallas_call | solution.py:471
  68.0 0.0 copy-start.8
  68.0 1.9 %shard_map.118 = (bf16[32,2304]{1,0:T(8,128)(2,1)S(1)}, bf16[32,2304]{1,0:T(8,128)(2,1)S(1)}, bf16[32,2304]{1,0:T(8,128)(2,1)S(1)}, bf16[32,2304]{1,0:T(8,128)(2,1)S(1)}) custom-call(bf16[1728,256]{1,0:T(8,128)(2,1)S(1)} %shard_map.111.refs_0_, bf16[1728,256]{1,0:T(8,128)(2,1)S(1)} %shard_map.113.refs_1_, bf16[1728,256]{1,0:T(8,128)(2,1)S(1)} %shard_map.117.refs_2_.refs_3_, ...), custom_call_target="tpu_custom_call" | custom-call | tf_op jit(solution)/shard_map/pallas_call | solution.py:482
  69.9 1.2 %collective-permute-start.23 = (bf16[32,2304]{1,0:T(8,128)(2,1)S(1)}, bf16[32,2304]{1,0:T(8,128)(2,1)S(1)}, u32[]{:S(2)}, u32[]{:S(2)}) collective-permute-start(bf16[32,2304]{1,0:T(8,128)(2,1)S(1)} %get-tuple-element.67), channel_id=1, source_target_pairs={{8,0},{12,4},{0,8},{4,12},{9,1},{13,5},{1,9},{5,13},{10,2},{14,6},... | collective-permute-start | bytes 442376 | tf_op jit(solution)/shard_map/ppermute | solution.py:493
  71.1 0.9 collective-permute-start.24
  72.0 1.0 %collective-permute-start.17 = (bf16[32,2304]{1,0:T(8,128)(2,1)S(1)}, bf16[32,2304]{1,0:T(8,128)(2,1)S(1)}, u32[]{:S(2)}, u32[]{:S(2)}) collective-permute-start(bf16[32,2304]{1,0:T(8,128)(2,1)S(1)} %get-tuple-element.59), channel_id=1, source_target_pairs={{8,0},{12,4},{0,8},{4,12},{9,1},{13,5},{1,9},{5,13},{10,2},{14,6},... | collective-permute-start | bytes 442376 | tf_op jit(solution)/shard_map/ppermute | solution.py:493
  73.0 1.1 %collective-permute-start.18 = (bf16[32,2304]{1,0:T(8,128)(2,1)S(1)}, bf16[32,2304]{1,0:T(8,128)(2,1)S(1)}, u32[]{:S(2)}, u32[]{:S(2)}) collective-permute-start(bf16[32,2304]{1,0:T(8,128)(2,1)S(1)} %get-tuple-element.60), channel_id=1, source_target_pairs={{12,0},{8,4},{4,8},{0,12},{13,1},{9,5},{5,9},{1,13},{14,2},{10,6},... | collective-permute-start | bytes 442376 | tf_op jit(solution)/shard_map/ppermute | solution.py:493
  74.1 1.9 %shard_map.119.refs_12_ = bf16[4,2,32,1152]{3,2,1,0:T(8,128)(2,1)S(1)} custom-call(bf16[32,1152]{1,0:T(8,128)(2,1)S(1)} %get-tuple-element.49.refs_0_, bf16[32,1152]{1,0:T(8,128)(2,1)S(1)} %get-tuple-element.50.refs_1_, bf16[32,1152]{1,0:T(8,128)(2,1)S(1)} %get-tuple-element.51.refs_2_, bf16[32,1152]{1,0:T(8,128)(2,1)S(1)} %get-tuple-element.52.refs_3_, ...), custom_call_target="tpu_custom_call" | custom-call | tf_op jit(solution)/shard_map/pallas_call | solution.py:496
  76.1 0.0 copy-start.4
  76.1 1.9 %shard_map.122.refs_12_ = bf16[4,2,32,1152]{3,2,1,0:T(8,128)(2,1)S(1)} custom-call(bf16[32,1152]{1,0:T(8,128)(2,1)S(1)} %get-tuple-element.61.refs_0_, bf16[32,1152]{1,0:T(8,128)(2,1)S(1)} %get-tuple-element.62.refs_1_, bf16[32,1152]{1,0:T(8,128)(2,1)S(1)} %get-tuple-element.63.refs_2_, bf16[32,1152]{1,0:T(8,128)(2,1)S(1)} %get-tuple-element.64.refs_3_, ...), custom_call_target="tpu_custom_call" | custom-call | tf_op jit(solution)/shard_map/pallas_call | solution.py:496
  78.0 1.5 %collective-permute-done.24.refs_3_ = bf16[32,2304]{1,0:T(8,128)(2,1)S(1)} collective-permute-done((bf16[32,2304]{1,0:T(8,128)(2,1)S(1)}, bf16[32,2304]{1,0:T(8,128)(2,1)S(1)}, u32[]{:S(2)}, u32[]{:S(2)}) %collective-permute-start.24) | collective-permute-done | bytes 147488 | tf_op jit(solution)/shard_map/ppermute | solution.py:493
  79.5 2.9 %shard_map.123.refs_15_ = bf16[4,256,1152]{2,1,0:T(8,128)(2,1)} custom-call(s32[2]{0:T(128)S(1)} %pad_add_fusion.place, bf16[32,2304]{1,0:T(8,128)(2,1)S(1)} %get-tuple-element.65.refs_0_, bf16[32,2304]{1,0:T(8,128)(2,1)S(1)} %collective-permute-done.22.refs_1_, bf16[32,2304]{1,0:T(8,128)(2,1)S(1)} %collective-permute-done.23.refs_2_, ...), custom_call_target="tpu_custom_call" | custom-call | tf_op jit(solution)/shard_map/pallas_call | solution.py:513
  82.4 2.6 %collective-permute-done.18.refs_3_ = bf16[32,2304]{1,0:T(8,128)(2,1)S(1)} collective-permute-done((bf16[32,2304]{1,0:T(8,128)(2,1)S(1)}, bf16[32,2304]{1,0:T(8,128)(2,1)S(1)}, u32[]{:S(2)}, u32[]{:S(2)}) %collective-permute-start.18) | collective-permute-done | bytes 147488 | tf_op jit(solution)/shard_map/ppermute | solution.py:493
  85.0 2.9 %shard_map.124 = bf16[4,256,1152]{2,1,0:T(8,128)(2,1)} custom-call(s32[2]{0:T(128)S(1)} %pad_add_fusion.place, bf16[32,2304]{1,0:T(8,128)(2,1)S(1)} %get-tuple-element.57.refs_0_, bf16[32,2304]{1,0:T(8,128)(2,1)S(1)} %collective-permute-done.16.refs_1_, bf16[32,2304]{1,0:T(8,128)(2,1)S(1)} %collective-permute-done.17.refs_2_, ...), custom_call_target="tpu_custom_call", output_to_operand_aliasing={{}: (16, {})} | custom-call | tf_op jit(solution)/shard_map/pallas_call | solution.py:513
  (23 shorter events, 0.1 us)
Async XLA Ops:
  0.1 23.1 %copy-start.3 = (bf16[4,256,576]{1,2,0:T(8,128)(2,1)S(1)}, bf16[4,256,576]{1,2,0:T(8,128)(2,1)}, u32[]{:S(2)}) copy-start(bf16[4,256,576]{1,2,0:T(8,128)(2,1)} %param.11) | copy-start | bytes 3538948
  1.7 14.3 %collective-permute-start = (bf16[2,1152,128]{2,1,0:T(8,128)(2,1)S(1)}, bf16[2,1152,128]{2,1,0:T(8,128)(2,1)S(1)}, u32[]{:S(2)}, u32[]{:S(2)}) collective-permute-start(bf16[2,1152,128]{2,1,0:T(8,128)(2,1)S(1)} %get-tuple-element.37.a_ref), channel_id=1, source_target_pairs={{0,1},{1,0},{2,3},{3,2},{4,5},{5,4},{6,7},{7,6},{8,9},{9,8},{10,11... | collective-permute-start | bytes 1769480 | tf_op jit(solution)/shard_map/ppermute | solution.py:402
  3.0 15.8 %collective-permute-start.1 = (bf16[2,1152,128]{2,1,0:T(8,128)(2,1)S(1)}, bf16[2,1152,128]{2,1,0:T(8,128)(2,1)S(1)}, u32[]{:S(2)}, u32[]{:S(2)}) collective-permute-start(bf16[2,1152,128]{2,1,0:T(8,128)(2,1)S(1)} %get-tuple-element.38.b_ref), channel_id=1, source_target_pairs={{1,2},{2,1},{5,6},{6,5},{9,10},{10,9},{13,14},{14,13},{17,18},{18,... | collective-permute-start | bytes 1769480 | tf_op jit(solution)/shard_map/ppermute | solution.py:402
  5.0 18.3 %copy-start.2 = (bf16[4,256,1152]{2,1,0:T(8,128)(2,1)S(1)}, bf16[4,256,1152]{2,1,0:T(8,128)(2,1)}, u32[]{:S(2)}) copy-start(bf16[4,256,1152]{2,1,0:T(8,128)(2,1)} %src.1) | copy-start | bytes 7077892
  6.6 16.6 %copy-start.7 = (f32[1152]{0:T(1024)S(1)}, f32[1152]{0:T(1024)}, u32[]{:S(2)}) copy-start(f32[1152]{0:T(1024)} %param.16) | copy-start | bytes 13828
  6.6 16.6 %copy-start.1 = (bf16[576,1152]{1,0:T(8,128)(2,1)S(1)}, bf16[576,1152]{1,0:T(8,128)(2,1)}, u32[]{:S(2)}) copy-start(bf16[576,1152]{1,0:T(8,128)(2,1)} %refs_8_.7) | copy-start | bytes 3981316
  6.6 16.6 %copy-start.5 = (s32[4,2,3]{0,1,2:T(2,128)S(1)}, s32[4,2,3]{0,1,2:T(2,128)}, u32[]{:S(2)}) copy-start(s32[4,2,3]{0,1,2:T(2,128)} %param.20) | copy-start | bytes 292
  6.7 16.6 %copy-start.6 = (s32[4,2]{0,1:T(2,128)S(1)}, s32[4,2]{0,1:T(2,128)}, u32[]{:S(2)}) copy-start(s32[4,2]{0,1:T(2,128)} %param.21) | copy-start | bytes 100
  6.7 21.9 %collective-permute-start.8 = (bf16[2,1152,128]{2,1,0:T(8,128)(2,1)S(1)}, bf16[2,1152,128]{2,1,0:T(8,128)(2,1)S(1)}, u32[]{:S(2)}, u32[]{:S(2)}) collective-permute-start(bf16[2,1152,128]{2,1,0:T(8,128)(2,1)S(1)} %get-tuple-element.47.a_ref), channel_id=1, source_target_pairs={{0,1},{1,0},{2,3},{3,2},{4,5},{5,4},{6,7},{7,6},{8,9},{9,8},{10,11... | collective-permute-start | bytes 1769480 | tf_op jit(solution)/shard_map/ppermute | solution.py:402
  6.8 24.7 %collective-permute-start.9 = (bf16[2,1152,128]{2,1,0:T(8,128)(2,1)S(1)}, bf16[2,1152,128]{2,1,0:T(8,128)(2,1)S(1)}, u32[]{:S(2)}, u32[]{:S(2)}) collective-permute-start(bf16[2,1152,128]{2,1,0:T(8,128)(2,1)S(1)} %get-tuple-element.48.b_ref), channel_id=1, source_target_pairs={{1,2},{2,1},{5,6},{6,5},{9,10},{10,9},{13,14},{14,13},{17,18},{18,... | collective-permute-start | bytes 1769480 | tf_op jit(solution)/shard_map/ppermute | solution.py:402
  12.1 24.3 %collective-permute-start.13 = (bf16[2,64,1152]{2,1,0:T(8,128)(2,1)S(1)}, bf16[2,64,1152]{2,1,0:T(8,128)(2,1)S(1)}, u32[]{:S(2)}, u32[]{:S(2)}) collective-permute-start(bf16[2,64,1152]{2,1,0:T(8,128)(2,1)S(1)} %get-tuple-element.54.refs_5_), channel_id=1, source_target_pairs={{0,4},{4,0},{8,12},{12,8},{1,5},{5,1},{9,13},{13,9},{2,6},{6,2},{1... | collective-permute-start | bytes 884744 | tf_op jit(solution)/shard_map/ppermute | solution.py:408
  16.0 21.7 %collective-permute-start.14 = (bf16[2,64,1152]{2,1,0:T(8,128)(2,1)S(1)}, bf16[2,64,1152]{2,1,0:T(8,128)(2,1)S(1)}, u32[]{:S(2)}, u32[]{:S(2)}) collective-permute-start(bf16[2,64,1152]{2,1,0:T(8,128)(2,1)S(1)} %get-tuple-element.55.refs_6_), channel_id=1, source_target_pairs={{0,8},{4,12},{8,0},{12,4},{1,9},{5,13},{9,1},{13,5},{2,10},{6,14},... | collective-permute-start | bytes 884744 | tf_op jit(solution)/shard_map/ppermute | solution.py:408
  18.9 22.0 %collective-permute-start.15 = (bf16[2,64,1152]{2,1,0:T(8,128)(2,1)S(1)}, bf16[2,64,1152]{2,1,0:T(8,128)(2,1)S(1)}, u32[]{:S(2)}, u32[]{:S(2)}) collective-permute-start(bf16[2,64,1152]{2,1,0:T(8,128)(2,1)S(1)} %get-tuple-element.56.refs_7_), channel_id=1, source_target_pairs={{0,12},{4,8},{8,4},{12,0},{1,13},{5,9},{9,5},{13,1},{2,14},{6,10},... | collective-permute-start | bytes 884744 | tf_op jit(solution)/shard_map/ppermute | solution.py:408
  28.6 15.7 %collective-permute-start.2 = (bf16[64,1152]{1,0:T(8,128)(2,1)S(1)}, bf16[64,1152]{1,0:T(8,128)(2,1)S(1)}, u32[]{:S(2)}, u32[]{:S(2)}) collective-permute-start(bf16[64,1152]{1,0:T(8,128)(2,1)S(1)} %get-tuple-element.40.refs_6_), channel_id=1, source_target_pairs={{0,4},{4,0},{8,12},{12,8},{1,5},{5,1},{9,13},{13,9},{2,6},{6,2},{1... | collective-permute-start | bytes 442376 | tf_op jit(solution)/shard_map/ppermute | solution.py:408
  34.5 6.6 %collective-permute-start.19 = (bf16[32,1152]{1,0:T(8,128)(2,1)S(1)}, bf16[32,1152]{1,0:T(8,128)(2,1)S(1)}, u32[]{:S(2)}, u32[]{:S(2)}) collective-permute-start(bf16[32,1152]{1,0:T(8,128)(2,1)S(1)} %get-tuple-element.62.refs_1_), channel_id=1, source_target_pairs={{0,4},{4,0},{8,12},{12,8},{1,5},{5,1},{9,13},{13,9},{2,6},{6,2},{1... | collective-permute-start | bytes 221192 | tf_op jit(solution)/shard_map/ppermute | solution.py:408
  36.4 5.9 %collective-permute-start.20 = (bf16[32,1152]{1,0:T(8,128)(2,1)S(1)}, bf16[32,1152]{1,0:T(8,128)(2,1)S(1)}, u32[]{:S(2)}, u32[]{:S(2)}) collective-permute-start(bf16[32,1152]{1,0:T(8,128)(2,1)S(1)} %get-tuple-element.63.refs_2_), channel_id=1, source_target_pairs={{0,8},{4,12},{8,0},{12,4},{1,9},{5,13},{9,1},{13,5},{2,10},{6,14},... | collective-permute-start | bytes 221192 | tf_op jit(solution)/shard_map/ppermute | solution.py:408
  37.6 5.4 %collective-permute-start.21 = (bf16[32,1152]{1,0:T(8,128)(2,1)S(1)}, bf16[32,1152]{1,0:T(8,128)(2,1)S(1)}, u32[]{:S(2)}, u32[]{:S(2)}) collective-permute-start(bf16[32,1152]{1,0:T(8,128)(2,1)S(1)} %get-tuple-element.64.refs_3_), channel_id=1, source_target_pairs={{0,12},{4,8},{8,4},{12,0},{1,13},{5,9},{9,5},{13,1},{2,14},{6,10},... | collective-permute-start | bytes 221192 | tf_op jit(solution)/shard_map/ppermute | solution.py:408
  38.1 6.6 %copy-start = (bf16[1152,1728]{0,1:T(8,128)(2,1)S(1)}, bf16[1152,1728]{0,1:T(8,128)(2,1)}, u32[]{:S(2)}) copy-start(bf16[1152,1728]{0,1:T(8,128)(2,1)} %param.17) | copy-start | bytes 11943940
  40.9 11.2 %collective-permute-start.5 = (bf16[64,1152]{1,0:T(8,128)(2,1)S(1)}, bf16[64,1152]{1,0:T(8,128)(2,1)S(1)}, u32[]{:S(2)}, u32[]{:S(2)}) collective-permute-start(bf16[64,1152]{1,0:T(8,128)(2,1)S(1)} %get-tuple-element.44.refs_7_), channel_id=1, source_target_pairs={{0,4},{4,0},{8,12},{12,8},{1,5},{5,1},{9,13},{13,9},{2,6},{6,2},{1... | collective-permute-start | bytes 442376 | tf_op jit(solution)/shard_map/ppermute | solution.py:408
  41.1 5.7 %collective-permute-start.3 = (bf16[64,1152]{1,0:T(8,128)(2,1)S(1)}, bf16[64,1152]{1,0:T(8,128)(2,1)S(1)}, u32[]{:S(2)}, u32[]{:S(2)}) collective-permute-start(bf16[64,1152]{1,0:T(8,128)(2,1)S(1)} %get-tuple-element.41.refs_8_), channel_id=1, source_target_pairs={{0,8},{4,12},{8,0},{12,4},{1,9},{5,13},{9,1},{13,5},{2,10},{6,14},... | collective-permute-start | bytes 442376 | tf_op jit(solution)/shard_map/ppermute | solution.py:408
  42.3 8.3 %collective-permute-start.4 = (bf16[64,1152]{1,0:T(8,128)(2,1)S(1)}, bf16[64,1152]{1,0:T(8,128)(2,1)S(1)}, u32[]{:S(2)}, u32[]{:S(2)}) collective-permute-start(bf16[64,1152]{1,0:T(8,128)(2,1)S(1)} %get-tuple-element.42.refs_10_), channel_id=1, source_target_pairs={{0,12},{4,8},{8,4},{12,0},{1,13},{5,9},{9,5},{13,1},{2,14},{6,10},... | collective-permute-start | bytes 442376 | tf_op jit(solution)/shard_map/ppermute | solution.py:408
  43.1 9.4 %collective-permute-start.6 = (bf16[64,1152]{1,0:T(8,128)(2,1)S(1)}, bf16[64,1152]{1,0:T(8,128)(2,1)S(1)}, u32[]{:S(2)}, u32[]{:S(2)}) collective-permute-start(bf16[64,1152]{1,0:T(8,128)(2,1)S(1)} %get-tuple-element.45.refs_9_), channel_id=1, source_target_pairs={{0,8},{4,12},{8,0},{12,4},{1,9},{5,13},{9,1},{13,5},{2,10},{6,14},... | collective-permute-start | bytes 442376 | tf_op jit(solution)/shard_map/ppermute | solution.py:408
  44.3 11.8 %collective-permute-start.7 = (bf16[64,1152]{1,0:T(8,128)(2,1)S(1)}, bf16[64,1152]{1,0:T(8,128)(2,1)S(1)}, u32[]{:S(2)}, u32[]{:S(2)}) collective-permute-start(bf16[64,1152]{1,0:T(8,128)(2,1)S(1)} %get-tuple-element.46.refs_11_), channel_id=1, source_target_pairs={{0,12},{4,8},{8,4},{12,0},{1,13},{5,9},{9,5},{13,1},{2,14},{6,10},... | collective-permute-start | bytes 442376 | tf_op jit(solution)/shard_map/ppermute | solution.py:408
  59.4 13.6 %collective-permute-start.22 = (bf16[32,2304]{1,0:T(8,128)(2,1)S(1)}, bf16[32,2304]{1,0:T(8,128)(2,1)S(1)}, u32[]{:S(2)}, u32[]{:S(2)}) collective-permute-start(bf16[32,2304]{1,0:T(8,128)(2,1)S(1)} %get-tuple-element.66), channel_id=1, source_target_pairs={{4,0},{0,4},{12,8},{8,12},{5,1},{1,5},{13,9},{9,13},{6,2},{2,6},{1... | collective-permute-start | bytes 442376 | tf_op jit(solution)/shard_map/ppermute | solution.py:493
  59.5 2.2 %collective-permute-start.10 = (bf16[32,1152]{1,0:T(8,128)(2,1)S(1)}, bf16[32,1152]{1,0:T(8,128)(2,1)S(1)}, u32[]{:S(2)}, u32[]{:S(2)}) collective-permute-start(bf16[32,1152]{1,0:T(8,128)(2,1)S(1)} %get-tuple-element.50.refs_1_), channel_id=1, source_target_pairs={{0,4},{4,0},{8,12},{12,8},{1,5},{5,1},{9,13},{13,9},{2,6},{6,2},{1... | collective-permute-start | bytes 221192 | tf_op jit(solution)/shard_map/ppermute | solution.py:408
  60.0 3.7 %collective-permute-start.11 = (bf16[32,1152]{1,0:T(8,128)(2,1)S(1)}, bf16[32,1152]{1,0:T(8,128)(2,1)S(1)}, u32[]{:S(2)}, u32[]{:S(2)}) collective-permute-start(bf16[32,1152]{1,0:T(8,128)(2,1)S(1)} %get-tuple-element.51.refs_2_), channel_id=1, source_target_pairs={{0,8},{4,12},{8,0},{12,4},{1,9},{5,13},{9,1},{13,5},{2,10},{6,14},... | collective-permute-start | bytes 221192 | tf_op jit(solution)/shard_map/ppermute | solution.py:408
  61.2 4.4 %collective-permute-start.12 = (bf16[32,1152]{1,0:T(8,128)(2,1)S(1)}, bf16[32,1152]{1,0:T(8,128)(2,1)S(1)}, u32[]{:S(2)}, u32[]{:S(2)}) collective-permute-start(bf16[32,1152]{1,0:T(8,128)(2,1)S(1)} %get-tuple-element.52.refs_3_), channel_id=1, source_target_pairs={{0,12},{4,8},{8,4},{12,0},{1,13},{5,9},{9,5},{13,1},{2,14},{6,10},... | collective-permute-start | bytes 221192 | tf_op jit(solution)/shard_map/ppermute | solution.py:408
  68.0 6.1 %copy-start.8 = (f32[1152]{0:T(1024)S(1)}, f32[1152]{0:T(1024)}, u32[]{:S(2)}) copy-start(f32[1152]{0:T(1024)} %param.19) | copy-start | bytes 13828
  69.9 8.2 %collective-permute-start.23 = (bf16[32,2304]{1,0:T(8,128)(2,1)S(1)}, bf16[32,2304]{1,0:T(8,128)(2,1)S(1)}, u32[]{:S(2)}, u32[]{:S(2)}) collective-permute-start(bf16[32,2304]{1,0:T(8,128)(2,1)S(1)} %get-tuple-element.67), channel_id=1, source_target_pairs={{8,0},{12,4},{0,8},{4,12},{9,1},{13,5},{1,9},{5,13},{10,2},{14,6},... | collective-permute-start | bytes 442376 | tf_op jit(solution)/shard_map/ppermute | solution.py:493
  71.1 8.4 %collective-permute-start.24 = (bf16[32,2304]{1,0:T(8,128)(2,1)S(1)}, bf16[32,2304]{1,0:T(8,128)(2,1)S(1)}, u32[]{:S(2)}, u32[]{:S(2)}) collective-permute-start(bf16[32,2304]{1,0:T(8,128)(2,1)S(1)} %get-tuple-element.68), channel_id=1, source_target_pairs={{12,0},{8,4},{4,8},{0,12},{13,1},{9,5},{5,9},{1,13},{14,2},{10,6},... | collective-permute-start | bytes 442376 | tf_op jit(solution)/shard_map/ppermute | solution.py:493
  72.0 10.4 %collective-permute-start.16 = (bf16[32,2304]{1,0:T(8,128)(2,1)S(1)}, bf16[32,2304]{1,0:T(8,128)(2,1)S(1)}, u32[]{:S(2)}, u32[]{:S(2)}) collective-permute-start(bf16[32,2304]{1,0:T(8,128)(2,1)S(1)} %get-tuple-element.58), channel_id=1, source_target_pairs={{4,0},{0,4},{12,8},{8,12},{5,1},{1,5},{13,9},{9,13},{6,2},{2,6},{1... | collective-permute-start | bytes 442376 | tf_op jit(solution)/shard_map/ppermute | solution.py:493
  72.0 10.5 %collective-permute-start.17 = (bf16[32,2304]{1,0:T(8,128)(2,1)S(1)}, bf16[32,2304]{1,0:T(8,128)(2,1)S(1)}, u32[]{:S(2)}, u32[]{:S(2)}) collective-permute-start(bf16[32,2304]{1,0:T(8,128)(2,1)S(1)} %get-tuple-element.59), channel_id=1, source_target_pairs={{8,0},{12,4},{0,8},{4,12},{9,1},{13,5},{1,9},{5,13},{10,2},{14,6},... | collective-permute-start | bytes 442376 | tf_op jit(solution)/shard_map/ppermute | solution.py:493
  73.0 12.0 %collective-permute-start.18 = (bf16[32,2304]{1,0:T(8,128)(2,1)S(1)}, bf16[32,2304]{1,0:T(8,128)(2,1)S(1)}, u32[]{:S(2)}, u32[]{:S(2)}) collective-permute-start(bf16[32,2304]{1,0:T(8,128)(2,1)S(1)} %get-tuple-element.60), channel_id=1, source_target_pairs={{12,0},{8,4},{4,8},{0,12},{13,1},{9,5},{5,9},{1,13},{14,2},{10,6},... | collective-permute-start | bytes 442376 | tf_op jit(solution)/shard_map/ppermute | solution.py:493
  76.1 3.5 %copy-start.4 = (bf16[576,1152]{1,0:T(8,128)(2,1)S(1)}, bf16[576,1152]{1,0:T(8,128)(2,1)}, u32[]{:S(2)}) copy-start(bf16[576,1152]{1,0:T(8,128)(2,1)} %refs_13_.3) | copy-start | bytes 3981316

commit v3 on v2

--- a/solution.py
+++ b/solution.py
@@ -42,6 +42,14 @@
 
 def head(h, base=0):
     return slice(base + h * HEAD_DIM, base + (h + 1) * HEAD_DIM)
+
+
+def with_ones(v):
+    return jnp.concatenate([v, jnp.ones((8, v.shape[1]), v.dtype)], axis=0)
+
+
+def averaged(o):
+    return o[:HEAD_DIM, :] / o[HEAD_DIM:HEAD_DIM + 1, :]
 
 
 def pipeline(steps, scores, weigh, gather):
@@ -52,14 +60,25 @@
             ahead = scores(*steps[n + 1])
         weighed = weigh(now)
         if behind is not None:
-            gather(*steps[n - 1], *behind)
+            gather(*steps[n - 1], behind)
         behind = weighed
-    gather(*steps[-1], *behind)
-
-
-def prep_kernel(place, k_ref, v_ref, a_ref, b_ref):
+    gather(*steps[-1], behind)
+
+
+def prep_kernel(place, k_ref, v_ref, *refs):
     n, width, _ = k_ref.shape
     even = place[1] % 2 == 0
+    copies = []
+    if len(refs) > 2:
+        src, (a_ref, b_ref), pieces, sems = refs[0], refs[1:3], refs[3:-1], refs[-1]
+        late, share, _ = pieces[0].shape
+        for j in reversed(range(len(pieces))):
+            start = pl.multiple_of(peer(place[0], j, len(pieces)) * share, SUB)
+            part = src.at[pl.ds(src.shape[0] - late, late), pl.ds(start, share), :]
+            copies.append(pltpu.make_async_copy(part, pieces[j], sems.at[j]))
+            copies[-1].start()
+    else:
+        a_ref, b_ref = refs
 
     def fill(first, second):
         for f in range(n):
@@ -73,17 +92,6 @@
 
     pl.when(even)(functools.partial(fill, b_ref, a_ref))
     pl.when(jnp.logical_not(even))(functools.partial(fill, a_ref, b_ref))
-
-
-def split_kernel(place, src, *refs):
-    outs, sems = refs[:-1], refs[-1]
-    late, share, _ = outs[0].shape
-    copies = []
-    for j, dst in enumerate(outs):
-        start = pl.multiple_of(peer(place[0], j, len(outs)) * share, SUB)
-        part = src.at[pl.ds(src.shape[0] - late, late), pl.ds(start, share), :]
-        copies.append(pltpu.make_async_copy(part, dst, sems.at[j]))
-        copies[-1].start()
     for copy in copies:
         copy.wait()
 
@@ -105,9 +113,9 @@
                 hit = jnp.bool_(False)
                 for j in range(MAXT):
                     hit = hit | ((lists[j, t, frame + f] == spot) & (j < live))
-                cells.append(jnp.where(hit, 1.0, 0.0).astype(F32))
+                cells.append(jnp.full((SUB, TILE), jnp.where(hit, 1.0, 0.0), F32))
             table.append(cells)
-        masks.append(table)
+        masks.append([jnp.concatenate(row, axis=1).astype(BF) for row in zip(*table)])
 
     def scores(f, h):
         q = q_ref[f, head(h), :].astype(F32)
@@ -116,23 +124,18 @@
 
     def weigh(scored):
         f, s = scored
-        partial, packed = [], []
+        packed = []
         for i, x in enumerate(s):
-            p = jnp.exp2(x * EXP2_SCALE)
-            p = jnp.concatenate(
-                [p[:, t * TILE:(t + 1) * TILE] * masks[f][t][i] for t in range(tiles)], axis=1
-            )
-            partial.append(jnp.sum(p.reshape(TILE // 8, 8, tokens), axis=0))
-            packed.append(p.astype(BF))
-        halves = [jnp.concatenate(packed[i:i + 2], axis=0) for i in (0, 2)]
-        return jnp.sum(sum(partial), axis=0, keepdims=True), halves
-
-    def gather(f, h, total, halves):
+            p = jnp.exp2(x * EXP2_SCALE).astype(BF).reshape(TILE // SUB, SUB, tokens)
+            packed.append((p * masks[f][i]).reshape(TILE, tokens))
+        return [jnp.concatenate(packed[i:i + 2], axis=0) for i in (0, 2)]
+
+    def gather(f, h, halves):
         o = 0
         for i in range(2):
             v = jnp.concatenate([r[f, head(h, width), :] for r in keys[2 * i:2 * i + 2]], axis=1)
-            o += contract(v, halves[i], 1, 0)
-        att[f, head(h), :] = (o / total).astype(att.dtype)
+            o += contract(with_ones(v), halves[i], 1, 0)
+        att[f, head(h), :] = averaged(o).astype(att.dtype)
 
     pipeline([(f, h) for f in range(n) for h in range(width // HEAD_DIM)], scores, weigh, gather)
 
@@ -151,15 +154,10 @@
     outs, (att, mix) = rest[:n_groups], rest[n_groups:]
     attend(frame, place, counts, lists, q_ref, (a_ref, b_ref, ra_ref, rb_ref), att)
 
-    def block(at):
-        rows = slice(at, at + TILE)
-
-        def finish(normed):
-            mix[rows, :] = (h_ref[0, rows, :].astype(F32) + normed * g_ref[...]).astype(BF)
-
-        return lambda: contract(att[0, :, rows], w_ref[...], 0, 0), finish
-
-    add_normed([block(at) for at in range(0, mix.shape[0], TILE)])
+    def finish(normed):
+        mix[...] = (h_ref[0].astype(F32) + normed * g_ref[...]).astype(BF)
+
+    add_normed([(lambda: contract(att[0], w_ref[...], 0, 0), finish)])
     share = mix.shape[0] // n_groups
     for j, out in enumerate(outs):
         group = peer(place[0], j, n_groups)
@@ -180,18 +178,38 @@
 
 
 def mix_kernel(*refs):
-    atts, hids = refs[:len(refs) // 2 - 1], refs[len(refs) // 2 - 1:-3]
     w_ref, g_ref, out = refs[-3:]
+    n_groups, n, share, _ = out.shape
+    atts, hids = refs[:-3 - n_groups], refs[-3 - n_groups:-3]
     width = w_ref.shape[0]
-    n, _, _ = hids[0].shape
-
-    def block(j, f):
+    rows = atts[0].shape[0]
+    halves = share // rows
+
+    def block(js):
+        def start():
+            x = [
+                atts[half * n_groups + j][:, f * width:(f + 1) * width]
+                for j in js
+                for f in range(n)
+                for half in range(halves)
+            ]
+            return contract(jnp.concatenate(x, axis=0), w_ref[...], 1, 0)
+
         def finish(normed):
-            out[j, f] = (hids[j][f].astype(F32) + normed * g_ref[...]).astype(BF)
-
-        return lambda: contract(atts[j][:, f * width:(f + 1) * width], w_ref[...], 1, 0), finish
-
-    add_normed([block(j, f) for j in range(len(atts)) for f in range(n)])
+            for i, j in enumerate(js):
+                for f in range(n):
+                    at = (i * n + f) * share
+                    part = normed[at:at + share, :] * g_ref[...]
+                    out[j, f] = (hids[j][f].astype(F32) + part).astype(BF)
+
+        return start, finish
+
+    add_normed([block(js) for js in blocks_of(n_groups, n * share)])
+
+
+def blocks_of(n_groups, rows):
+    size = max(1, min(n_groups, 2 * TILE // rows))
+    return [range(at, min(at + size, n_groups)) for at in range(0, n_groups, size)]
 
 
 def paired(chunks, lanes, frames):
@@ -241,15 +259,10 @@
                 a[at:at + SUB, :] = atts[j][piece, f * width:(f + 1) * width]
                 b[at:at + SUB, :] = hids[j][f, piece, :]
 
-    def block(at):
-        cut = slice(at, at + TILE)
-
-        def finish(normed):
-            x[cut, :] = (b[cut, :].astype(F32) + normed * g_ref[...]).astype(BF)
-
-        return lambda: contract(a[cut, :], w_ref[...], 1, 0), finish
-
-    add_normed([block(at) for at in range(0, x.shape[0], TILE)])
+    def finish(normed):
+        x[...] = (b[...].astype(F32) + normed * g_ref[...]).astype(BF)
+
+    add_normed([(lambda: contract(a[...], w_ref[...], 1, 0), finish)])
     project(qkv_ref, x, out)
 
 
@@ -263,7 +276,7 @@
     pair = paired(chunks, lanes, frames)
     row_pos = lax.broadcasted_iota(jnp.int32, (rows, rows), 0) % SUB
     col_pos = lax.broadcasted_iota(jnp.int32, (rows, rows), 1) % SUB
-    same = jnp.where(row_pos == col_pos, 1.0, 0.0).astype(F32)
+    same = jnp.where(row_pos == col_pos, 1.0, 0.0).astype(BF)
     low = lax.broadcasted_iota(jnp.int32, (HEAD_DIM, TILE), 1) < lanes
 
     def take(c, where):
@@ -283,11 +296,10 @@
         return contract(take(c, head(h, width)), take(c, head(h)), 0, 0)
 
     def weigh(s):
-        p = jnp.exp2(s * EXP2_SCALE) * same
-        return jnp.sum(p, axis=0, keepdims=True), p.astype(BF)
-
-    def gather(c, h, total, p):
-        att[c, head(h), :] = contract(take(c, head(h, 2 * width)), p, 1, 0) / total
+        return jnp.exp2(s * EXP2_SCALE).astype(BF) * same
+
+    def gather(c, h, p):
+        att[c, head(h), :] = averaged(contract(with_ones(take(c, head(h, 2 * width))), p, 1, 0))
 
     steps = [(c, h) for c in range(chunks) for h in range(width // HEAD_DIM)]
     pipeline(steps, scores, weigh, gather)
@@ -309,25 +321,28 @@
     frames = early + late
     copies = []
 
-    def block(i, j):
+    def block(some):
         def start():
-            x = jnp.concatenate([atts[i][:, f * width:(f + 1) * width] for f in range(frames)], axis=0)
-            return contract(x, w_ref[...], 1, 0)
+            x = [atts[i][:, f * width:(f + 1) * width] for i in some for f in range(frames)]
+            return contract(jnp.concatenate(x, axis=0), w_ref[...], 1, 0)
 
         def finish(normed):
-            for f in range(frames):
-                mine = pieces[i * early + f][...] if f < early else late_ref[j, f - early]
-                part = normed[f * rows:(f + 1) * rows, :] * g_ref[...]
-                buf[i, f] = (mine.astype(F32) + part).astype(BF)
-            group = peer(place[0], j, n_groups)
-            at = pl.multiple_of((group * halves + half) * rows, SUB)
-            copy = pltpu.make_async_copy(buf.at[i], out.at[:, pl.ds(at, rows), :], sems.at[i])
-            copy.start()
-            copies.append(copy)
+            for k, i in enumerate(some):
+                j = js[i]
+                for f in range(frames):
+                    mine = pieces[i * early + f][...] if f < early else late_ref[j, f - early]
+                    at = (k * frames + f) * rows
+                    part = normed[at:at + rows, :] * g_ref[...]
+                    buf[i, f] = (mine.astype(F32) + part).astype(BF)
+                group = peer(place[0], j, n_groups)
+                at = pl.multiple_of((group * halves + half) * rows, SUB)
+                copy = pltpu.make_async_copy(buf.at[i], out.at[:, pl.ds(at, rows), :], sems.at[i])
+                copy.start()
+                copies.append(copy)
 
         return start, finish
 
-    add_normed([block(i, j) for i, j in enumerate(js)])
+    add_normed([block(some) for some in blocks_of(len(js), frames * rows)])
     for copy in copies:
         copy.wait()
 
@@ -389,33 +404,30 @@
     late = frames // 2
     early = frames - late
 
+    def out_pairs(j):
+        return [(i, peer(i, j, groups)) for i in range(groups)]
+
+    def send(parts):
+        sent = {j: lax.ppermute(parts[j], "frame", out_pairs(j)) for j in reversed(range(1, groups))}
+        return [parts[0]] + [sent[j] for j in range(1, groups)]
+
     halos = []
     for some in range(2):
         block = pl.BlockSpec((late, width, tokens), lambda *_, some=some: (some, 0, 0))
-        a, b = call(
+        split = groups if some == 0 else 0
+        a, b, *pieces = call(
             prep_kernel,
-            [smem, block, block],
-            [whole((late,) + edge.shape)] * 2,
-            [jax.ShapeDtypeStruct((late,) + edge.shape, BF)] * 2,
+            [smem, block, block] + [any_spec] * bool(split),
+            [whole((late,) + edge.shape)] * 2 + [any_spec] * split,
+            [jax.ShapeDtypeStruct((late,) + edge.shape, BF)] * 2
+            + [jax.ShapeDtypeStruct((late, share, model), BF)] * split,
+            [pltpu.SemaphoreType.DMA((groups,))] * bool(split),
             limit=16,
-        )(place, keys, values)
+        )(place, keys, values, *[hidden_far] * bool(split))
+        if split:
+            own_hidden = pieces
         halos.append((a, b, lax.ppermute(a, "strip", near), lax.ppermute(b, "strip", far)))
-
-    def out_pairs(j):
-        return [(i, peer(i, j, groups)) for i in range(groups)]
-
-    def send(x, j):
-        return x if j == 0 else lax.ppermute(x, "frame", out_pairs(j))
-
-    own_hidden = call(
-        split_kernel,
-        [smem, any_spec],
-        [any_spec] * groups,
-        [jax.ShapeDtypeStruct((late, share, model), BF)] * groups,
-        [pltpu.SemaphoreType.DMA((groups,))],
-        limit=16,
-    )(place, hidden_far)
-    far_hidden = [send(x, j) for j, x in enumerate(own_hidden)]
+    far_hidden = send(own_hidden)
 
     mixed = [[None] * early for _ in range(groups)]
     projected = []
@@ -436,7 +448,7 @@
         )(place, counts, lists, queries, *halos[0], hidden, spatial_out_weight, gain_one)
         for j in range(groups):
             mixed[j][f] = parts[j]
-        arrived = [send(x, j) for j, x in enumerate(parts)]
+        arrived = send(parts)
         projected.append(
             call(
                 functools.partial(project_kernel, f, frames),
@@ -459,9 +471,9 @@
     own_late = [own_late[half * groups:(half + 1) * groups] for half in range(halves)]
     far_late = []
     for half in range(halves):
-        far_late.append([send(x, j) for j, x in enumerate(own_late[half])])
-
-    returned, late_mixed = [], []
+        far_late.append(send(own_late[half]))
+
+    returned = []
     back_shape = (rows, frames * width)
     lanes = tokens // halves
     for half in range(halves):
@@ -487,19 +499,20 @@
             [jax.ShapeDtypeStruct(back_shape, BF)] * groups,
             [pltpu.VMEM((rows // SUB, width, groups * frames * SUB), F32)],
         )(*projected, *[late_projected] * late)
-        got = []
-        for j in range(groups):
-            pairs = [(b, a) for a, b in out_pairs(j)]
-            got.append(back[j] if j == 0 else lax.ppermute(back[j], "frame", pairs))
-        returned.append(got)
-        late_mixed.append(
-            call(
-                mix_kernel,
-                late_specs,
-                whole((groups, late, rows, model)),
-                jax.ShapeDtypeStruct((groups, late, rows, model), BF),
-            )(*own_late[half], *own_hidden, spatial_out_weight, gain_one)
-        )
+        home = {
+            j: lax.ppermute(back[j], "frame", [(b, a) for a, b in out_pairs(j)])
+            for j in reversed(range(1, groups))
+        }
+        returned.append([back[0]] + [home[j] for j in range(1, groups)])
+
+    late_mixed = call(
+        mix_kernel,
+        [whole(late_shape)] * (groups * halves)
+        + [whole((late, share, model))] * groups
+        + [whole((width, model)), whole((1, model))],
+        whole((groups, late, share, model)),
+        jax.ShapeDtypeStruct((groups, late, share, model), BF),
+    )(*[x for some in own_late for x in some], *own_hidden, spatial_out_weight, gain_one)
 
     out = None
     for half in range(halves):
@@ -515,7 +528,8 @@
                 [smem]
                 + [whole(back_shape)] * len(js)
                 + [piece] * (len(js) * early)
-                + [whole((groups, late, rows, model)), whole((width, model)), whole((1, model))]
+                + [pl.BlockSpec((groups, late, rows, model), lambda *_, half=half: (0, 0, half, 0))]
+                + [whole((width, model)), whole((1, model))]
                 + [any_spec] * len(extra),
                 any_spec,
                 jax.ShapeDtypeStruct((frames, tokens, model), BF),
@@ -528,7 +542,7 @@
                 place,
                 *[returned[half][j] for j in js],
                 *[mixed[j][f] for j in js for f in range(early)],
-                late_mixed[half],
+                late_mixed,
                 temporal_out_weight,
                 gain_two,
                 *extra,

time: 88.2 us -> 89.2 us (1.011)
  the two profiles are of different devices: /device:TPU:17 before, /device:TPU:19 now
where the time goes in v3:
time: 89.2 us; the launch traced here: 89 us
  Pallas kernels  30.8 us (35%)
  starting transfers between devices  29.3 us (33%)
  waiting for transfers between devices  28.4 us (32%)
    ppermute x15, starting transfers between devices, send(): lax.ppermute(parts[j], 'frame', out_pairs(j))  18.3 us
    ppermute x15, waiting for transfers between devices, send(): lax.ppermute(parts[j], 'frame', out_pairs(j))  11.8 us
    ppermute x2, waiting for transfers between devices, shards(): lax.ppermute(a, 'strip', near)  7.09 us
    ppermute x6, waiting for transfers between devices, shards(): lax.ppermute(back[j], 'frame', [(b, a) for a, b in out_pairs(j)])  6.46 us
    pallas_call x2, Pallas kernels, shards(): call(functools.partial(output_kernel, groups, tuple(js), early, half, hal...  5.66 us
    pallas_call x2, Pallas kernels, shards(): call(functools.partial(spatial_kernel, f, groups), [smem, smem, smem, fra...  5.41 us
    ppermute x2, starting transfers between devices, shards(): lax.ppermute(b, 'strip', far)  5.27 us
    pallas_call x2, Pallas kernels, shards(): call(functools.partial(late_project_kernel, early, frames), late_specs +...  4.51 us
  transfers between devices with their start and end apart: 25, of which 11 were waited for; matrix products, arithmetic and copies ran while one was open for 0% of the time, Pallas kernels for 25%

profile of v3, /device:TPU:19, one launch (start us, length us, event | category | flops | bytes accessed | tf_op | source)
XLA Modules:
  0.0 89.0 jit_solution(5071179169295846185)
XLA Ops:
  0.0 0.1 pad_add_fusion.place
  0.1 2.7 %shard_map.109 = (bf16[2,1152,128]{2,1,0:T(8,128)(2,1)S(1)}, bf16[2,1152,128]{2,1,0:T(8,128)(2,1)S(1)}, bf16[2,64,1152]{2,1,0:T(8,128)(2,1)S(1)}, bf16[2,64,1152...) custom-call(s32[2]{0:T(128)S(1)} %pad_add_fusion.place, ...), custom_call_target="tpu_custom_call" | custom-call | tf_op jit(solution)/shard_map/pallas_call | solution.py:418
  2.8 0.0 copy-start.7
  2.8 0.0 copy-start.1
  2.8 0.0 copy-start.5
  2.8 0.0 copy-start.6
  2.8 1.4 %collective-permute-start = (bf16[2,1152,128]{2,1,0:T(8,128)(2,1)S(1)}, bf16[2,1152,128]{2,1,0:T(8,128)(2,1)S(1)}, u32[]{:S(2)}, u32[]{:S(2)}) collective-permute-start(bf16[2,1152,128]{2,1,0:T(8,128)(2,1)S(1)} %get-tuple-element.37.a_ref), channel_id=1, source_target_pairs={{0,1},{1,0},{2,3},{3,2},{4,5},{5,4},{6,7},{7,6},{8,9},{9,8},{10,11... | collective-permute-start | bytes 1769480 | tf_op jit(solution)/shard_map/ppermute | solution.py:429
  4.2 1.9 %collective-permute-start.1 = (bf16[2,1152,128]{2,1,0:T(8,128)(2,1)S(1)}, bf16[2,1152,128]{2,1,0:T(8,128)(2,1)S(1)}, u32[]{:S(2)}, u32[]{:S(2)}) collective-permute-start(bf16[2,1152,128]{2,1,0:T(8,128)(2,1)S(1)} %get-tuple-element.38.b_ref), channel_id=1, source_target_pairs={{1,2},{2,1},{5,6},{6,5},{9,10},{10,9},{13,14},{14,13},{17,18},{18,... | collective-permute-start | bytes 1769480 | tf_op jit(solution)/shard_map/ppermute | solution.py:429
  6.1 1.5 %shard_map.114 = (bf16[2,1152,128]{2,1,0:T(8,128)(2,1)S(1)}, bf16[2,1152,128]{2,1,0:T(8,128)(2,1)S(1)}) custom-call(s32[2]{0:T(128)S(1)} %pad_add_fusion.place, bf16[4,576,256]{2,1,0:T(8,128)(2,1)} %bitcast.22, bf16[4,576,256]{2,1,0:T(8,128)(2,1)} %bitcast.24), custom_call_target="tpu_custom_call" | custom-call | tf_op jit(solution)/shard_map/pallas_call | solution.py:418
  7.6 0.1 collective-permute-start.8
  7.7 3.4 %collective-permute-start.9 = (bf16[2,1152,128]{2,1,0:T(8,128)(2,1)S(1)}, bf16[2,1152,128]{2,1,0:T(8,128)(2,1)S(1)}, u32[]{:S(2)}, u32[]{:S(2)}) collective-permute-start(bf16[2,1152,128]{2,1,0:T(8,128)(2,1)S(1)} %get-tuple-element.48.b_ref), channel_id=1, source_target_pairs={{1,2},{2,1},{5,6},{6,5},{9,10},{10,9},{13,14},{14,13},{17,18},{18,... | collective-permute-start | bytes 1769480 | tf_op jit(solution)/shard_map/ppermute | solution.py:429
  11.0 1.6 %collective-permute-start.13 = (bf16[2,64,1152]{2,1,0:T(8,128)(2,1)S(1)}, bf16[2,64,1152]{2,1,0:T(8,128)(2,1)S(1)}, u32[]{:S(2)}, u32[]{:S(2)}) collective-permute-start(bf16[2,64,1152]{2,1,0:T(8,128)(2,1)S(1)} %get-tuple-element.54.refs_9_), channel_id=1, source_target_pairs={{0,4},{4,0},{8,12},{12,8},{1,5},{5,1},{9,13},{13,9},{2,6},{6,2},{1... | collective-permute-start | bytes 884744 | tf_op jit(solution)/shard_map/ppermute | solution.py:411
  12.6 4.5 %collective-permute-done.ra_ref = bf16[2,1152,128]{2,1,0:T(8,128)(2,1)S(1)} collective-permute-done((bf16[2,1152,128]{2,1,0:T(8,128)(2,1)S(1)}, bf16[2,1152,128]{2,1,0:T(8,128)(2,1)S(1)}, u32[]{:S(2)}, u32[]{:S(2)}) %collective-permute-start) | collective-permute-done | bytes 589856 | tf_op jit(solution)/shard_map/ppermute | solution.py:429
  17.1 1.2 %collective-permute-start.14 = (bf16[2,64,1152]{2,1,0:T(8,128)(2,1)S(1)}, bf16[2,64,1152]{2,1,0:T(8,128)(2,1)S(1)}, u32[]{:S(2)}, u32[]{:S(2)}) collective-permute-start(bf16[2,64,1152]{2,1,0:T(8,128)(2,1)S(1)} %get-tuple-element.55.refs_10_), channel_id=1, source_target_pairs={{0,8},{4,12},{8,0},{12,4},{1,9},{5,13},{9,1},{13,5},{2,10},{6,14},... | collective-permute-start | bytes 884744 | tf_op jit(solution)/shard_map/ppermute | solution.py:411
  18.3 1.7 %collective-permute-done.1.rb_ref = bf16[2,1152,128]{2,1,0:T(8,128)(2,1)S(1)} collective-permute-done((bf16[2,1152,128]{2,1,0:T(8,128)(2,1)S(1)}, bf16[2,1152,128]{2,1,0:T(8,128)(2,1)S(1)}, u32[]{:S(2)}, u32[]{:S(2)}) %collective-permute-start.1) | collective-permute-done | bytes 589856 | tf_op jit(solution)/shard_map/ppermute | solution.py:429
  20.0 4.3 %collective-permute-start.15 = (bf16[2,64,1152]{2,1,0:T(8,128)(2,1)S(1)}, bf16[2,64,1152]{2,1,0:T(8,128)(2,1)S(1)}, u32[]{:S(2)}, u32[]{:S(2)}) collective-permute-start(bf16[2,64,1152]{2,1,0:T(8,128)(2,1)S(1)} %get-tuple-element.56.refs_11_), channel_id=1, source_target_pairs={{0,12},{4,8},{8,4},{12,0},{1,13},{5,9},{9,5},{13,1},{2,14},{6,10},... | collective-permute-start | bytes 884744 | tf_op jit(solution)/shard_map/ppermute | solution.py:411
  24.4 2.7 %shard_map.110 = (bf16[64,1152]{1,0:T(8,128)(2,1)S(1)}, bf16[64,1152]{1,0:T(8,128)(2,1)S(1)}, bf16[64,1152]{1,0:T(8,128)(2,1)S(1)}, bf16[64,1152]{1,0:T(8,128)(2,1)S(1)}) custom-call(s32[2]{0:T(128)S(1)} %pad_add_fusion.place, s32[2,4]{1,0:T(2,128)S(1)} %bitcast.18, s32[3,2,4]{2,1,0:T(2,128)S(1)} %bitcast.15, bf16[4,576,256]{2,1,0:T(8,128)(2,1)S(1)} %bitcast.12, ...), custom_call_target="tpu_custom_call" | custom-call | tf_op jit(solution)/shard_map/pallas_call | solution.py:436
  27.1 2.6 %collective-permute-done.8.ra_ref = bf16[2,1152,128]{2,1,0:T(8,128)(2,1)S(1)} collective-permute-done((bf16[2,1152,128]{2,1,0:T(8,128)(2,1)S(1)}, bf16[2,1152,128]{2,1,0:T(8,128)(2,1)S(1)}, u32[]{:S(2)}, u32[]{:S(2)}) %collective-permute-start.8) | collective-permute-done | bytes 589856 | tf_op jit(solution)/shard_map/ppermute | solution.py:429
  29.7 1.5 %collective-permute-start.2 = (bf16[64,1152]{1,0:T(8,128)(2,1)S(1)}, bf16[64,1152]{1,0:T(8,128)(2,1)S(1)}, u32[]{:S(2)}, u32[]{:S(2)}) collective-permute-start(bf16[64,1152]{1,0:T(8,128)(2,1)S(1)} %get-tuple-element.40.refs_6_), channel_id=1, source_target_pairs={{0,4},{4,0},{8,12},{12,8},{1,5},{5,1},{9,13},{13,9},{2,6},{6,2},{1... | collective-permute-start | bytes 442376 | tf_op jit(solution)/shard_map/ppermute | solution.py:411
  31.3 1.4 %collective-permute-done.9.rb_ref = bf16[2,1152,128]{2,1,0:T(8,128)(2,1)S(1)} collective-permute-done((bf16[2,1152,128]{2,1,0:T(8,128)(2,1)S(1)}, bf16[2,1152,128]{2,1,0:T(8,128)(2,1)S(1)}, u32[]{:S(2)}, u32[]{:S(2)}) %collective-permute-start.9) | collective-permute-done | bytes 589856 | tf_op jit(solution)/shard_map/ppermute | solution.py:429
  32.6 3.0 %shard_map.115 = (bf16[32,1152]{1,0:T(8,128)(2,1)S(1)}, bf16[32,1152]{1,0:T(8,128)(2,1)S(1)}, bf16[32,1152]{1,0:T(8,128)(2,1)S(1)}, bf16[32,1152]{1,0:T(8,128)(2...) custom-call(s32[2]{0:T(128)S(1)} %pad_add_fusion.place, ...), custom_call_target="tpu_custom_call" | custom-call | tf_op jit(solution)/shard_map/pallas_call | solution.py:463
  35.6 1.9 %collective-permute-start.19 = (bf16[32,1152]{1,0:T(8,128)(2,1)S(1)}, bf16[32,1152]{1,0:T(8,128)(2,1)S(1)}, u32[]{:S(2)}, u32[]{:S(2)}) collective-permute-start(bf16[32,1152]{1,0:T(8,128)(2,1)S(1)} %get-tuple-element.62.refs_1_), channel_id=1, source_target_pairs={{0,4},{4,0},{8,12},{12,8},{1,5},{5,1},{9,13},{13,9},{2,6},{6,2},{1... | collective-permute-start | bytes 221192 | tf_op jit(solution)/shard_map/ppermute | solution.py:411
  37.5 0.0 collective-permute-done.13.refs_5_
  37.5 1.2 %collective-permute-start.20 = (bf16[32,1152]{1,0:T(8,128)(2,1)S(1)}, bf16[32,1152]{1,0:T(8,128)(2,1)S(1)}, u32[]{:S(2)}, u32[]{:S(2)}) collective-permute-start(bf16[32,1152]{1,0:T(8,128)(2,1)S(1)} %get-tuple-element.63.refs_2_), channel_id=1, source_target_pairs={{0,8},{4,12},{8,0},{12,4},{1,9},{5,13},{9,1},{13,5},{2,10},{6,14},... | collective-permute-start | bytes 221192 | tf_op jit(solution)/shard_map/ppermute | solution.py:411
  38.8 0.0 collective-permute-done.14.refs_6_
  38.8 0.5 collective-permute-start.21
  39.2 2.7 %shard_map.112 = (bf16[64,1152]{1,0:T(8,128)(2,1)S(1)}, bf16[64,1152]{1,0:T(8,128)(2,1)S(1)}, bf16[64,1152]{1,0:T(8,128)(2,1)S(1)}, bf16[64,1152]{1,0:T(8,128)(2,1)S(1)}) custom-call(s32[2]{0:T(128)S(1)} %pad_add_fusion.place, s32[2,4]{1,0:T(2,128)S(1)} %bitcast.20, s32[3,2,4]{2,1,0:T(2,128)S(1)} %bitcast.17, bf16[4,576,256]{2,1,0:T(8,128)(2,1)S(1)} %bitcast.14, ...), custom_call_target="tpu_custom_call" | custom-call | tf_op jit(solution)/shard_map/pallas_call | solution.py:436
  41.9 0.0 collective-permute-done.15.refs_7_
  42.0 0.2 collective-permute-start.5
  42.2 1.2 %collective-permute-start.3 = (bf16[64,1152]{1,0:T(8,128)(2,1)S(1)}, bf16[64,1152]{1,0:T(8,128)(2,1)S(1)}, u32[]{:S(2)}, u32[]{:S(2)}) collective-permute-start(bf16[64,1152]{1,0:T(8,128)(2,1)S(1)} %get-tuple-element.41.refs_8_), channel_id=1, source_target_pairs={{0,8},{4,12},{8,0},{12,4},{1,9},{5,13},{9,1},{13,5},{2,10},{6,14},... | collective-permute-start | bytes 442376 | tf_op jit(solution)/shard_map/ppermute | solution.py:411
  43.4 0.8 collective-permute-start.4
  44.2 0.0 collective-permute-done.21.refs_3_
  44.2 1.2 %collective-permute-start.6 = (bf16[64,1152]{1,0:T(8,128)(2,1)S(1)}, bf16[64,1152]{1,0:T(8,128)(2,1)S(1)}, u32[]{:S(2)}, u32[]{:S(2)}) collective-permute-start(bf16[64,1152]{1,0:T(8,128)(2,1)S(1)} %get-tuple-element.45.refs_9_), channel_id=1, source_target_pairs={{0,8},{4,12},{8,0},{12,4},{1,9},{5,13},{9,1},{13,5},{2,10},{6,14},... | collective-permute-start | bytes 442376 | tf_op jit(solution)/shard_map/ppermute | solution.py:411
  45.4 0.0 collective-permute-done.2.refs_1_
  45.4 0.3 collective-permute-start.7
  45.8 2.2 %shard_map.119.refs_2_.refs_3_ = bf16[1728,256]{1,0:T(8,128)(2,1)S(1)} custom-call(bf16[32,1152]{1,0:T(8,128)(2,1)S(1)} %get-tuple-element.61.refs_0_, bf16[32,1152]{1,0:T(8,128)(2,1)S(1)} %collective-permute-done.19.refs_1_, bf16[32,1152]{1,0:T(8,128)(2,1)S(1)} %collective-permute-done.20.refs_2_, bf16[32,1152]{1,0:T(8,128)(2,1)S(1)} %collective-permute-done.21.refs_3_, ...), custom_call_target="tpu_custom_call" | custom-call | tf_op jit(solution)/shard_map/pallas_call | solution.py:483
  48.0 3.8 %collective-permute-done.4.refs_3_ = bf16[64,1152]{1,0:T(8,128)(2,1)S(1)} collective-permute-done((bf16[64,1152]{1,0:T(8,128)(2,1)S(1)}, bf16[64,1152]{1,0:T(8,128)(2,1)S(1)}, u32[]{:S(2)}, u32[]{:S(2)}) %collective-permute-start.4) | collective-permute-done | bytes 147488 | tf_op jit(solution)/shard_map/ppermute | solution.py:411
  51.7 1.4 %shard_map.111.refs_0_ = bf16[1728,256]{1,0:T(8,128)(2,1)S(1)} custom-call(bf16[64,1152]{1,0:T(8,128)(2,1)S(1)} %get-tuple-element.39.refs_0_.refs_4_, bf16[64,1152]{1,0:T(8,128)(2,1)S(1)} %collective-permute-done.2.refs_1_, bf16[64,1152]{1,0:T(8,128)(2,1)S(1)} %collective-permute-done.3.refs_2_, bf16[64,1152]{1,0:T(8,128)(2,1)S(1)} %collective-permute-done.4.refs_3_, ...), custom_call_target="tpu_custom_call" | custom-call | tf_op jit(solution)/shard_map/pallas_call | solution.py:453
  53.1 0.4 collective-permute-done.6.refs_2_
  53.5 3.7 %collective-permute-done.7.refs_3_ = bf16[64,1152]{1,0:T(8,128)(2,1)S(1)} collective-permute-done((bf16[64,1152]{1,0:T(8,128)(2,1)S(1)}, bf16[64,1152]{1,0:T(8,128)(2,1)S(1)}, u32[]{:S(2)}, u32[]{:S(2)}) %collective-permute-start.7) | collective-permute-done | bytes 147488 | tf_op jit(solution)/shard_map/ppermute | solution.py:411
  57.2 1.4 %shard_map.113.refs_1_ = bf16[1728,256]{1,0:T(8,128)(2,1)S(1)} custom-call(bf16[64,1152]{1,0:T(8,128)(2,1)S(1)} %get-tuple-element.43.refs_0_.refs_5_, bf16[64,1152]{1,0:T(8,128)(2,1)S(1)} %collective-permute-done.5.refs_1_, bf16[64,1152]{1,0:T(8,128)(2,1)S(1)} %collective-permute-done.6.refs_2_, bf16[64,1152]{1,0:T(8,128)(2,1)S(1)} %collective-permute-done.7.refs_3_, ...), custom_call_target="tpu_custom_call" | custom-call | tf_op jit(solution)/shard_map/pallas_call | solution.py:453
  58.6 1.9 %shard_map.120 = (bf16[32,2304]{1,0:T(8,128)(2,1)S(1)}, bf16[32,2304]{1,0:T(8,128)(2,1)S(1)}, bf16[32,2304]{1,0:T(8,128)(2,1)S(1)}, bf16[32,2304]{1,0:T(8,128)(2,1)S(1)}) custom-call(bf16[1728,256]{1,0:T(8,128)(2,1)S(1)} %shard_map.111.refs_0_, bf16[1728,256]{1,0:T(8,128)(2,1)S(1)} %shard_map.113.refs_1_, bf16[1728,256]{1,0:T(8,128)(2,1)S(1)} %shard_map.119.refs_2_.refs_3_, ...), custom_call_target="tpu_custom_call" | custom-call | tf_op jit(solution)/shard_map/pallas_call | solution.py:494
  60.5 0.1 collective-permute-start.22
  60.6 0.5 collective-permute-start.10
  61.1 1.2 %collective-permute-start.11 = (bf16[32,1152]{1,0:T(8,128)(2,1)S(1)}, bf16[32,1152]{1,0:T(8,128)(2,1)S(1)}, u32[]{:S(2)}, u32[]{:S(2)}) collective-permute-start(bf16[32,1152]{1,0:T(8,128)(2,1)S(1)} %get-tuple-element.51.refs_6_), channel_id=1, source_target_pairs={{0,8},{4,12},{8,0},{12,4},{1,9},{5,13},{9,1},{13,5},{2,10},{6,14},... | collective-permute-start | bytes 221192 | tf_op jit(solution)/shard_map/ppermute | solution.py:411
  62.3 0.5 collective-permute-start.12
  62.8 0.0 collective-permute-done.10.refs_1_
  62.8 2.0 %collective-permute-done.11.refs_2_ = bf16[32,1152]{1,0:T(8,128)(2,1)S(1)} collective-permute-done((bf16[32,1152]{1,0:T(8,128)(2,1)S(1)}, bf16[32,1152]{1,0:T(8,128)(2,1)S(1)}, u32[]{:S(2)}, u32[]{:S(2)}) %collective-permute-start.11) | collective-permute-done | bytes 73760 | tf_op jit(solution)/shard_map/ppermute | solution.py:411
  64.8 1.9 %collective-permute-done.12.refs_3_ = bf16[32,1152]{1,0:T(8,128)(2,1)S(1)} collective-permute-done((bf16[32,1152]{1,0:T(8,128)(2,1)S(1)}, bf16[32,1152]{1,0:T(8,128)(2,1)S(1)}, u32[]{:S(2)}, u32[]{:S(2)}) %collective-permute-start.12) | collective-permute-done | bytes 73760 | tf_op jit(solution)/shard_map/ppermute | solution.py:411
  66.7 2.3 %shard_map.116.refs_2_.refs_3_ = bf16[1728,256]{1,0:T(8,128)(2,1)S(1)} custom-call(bf16[32,1152]{1,0:T(8,128)(2,1)S(1)} %get-tuple-element.49.refs_0_.refs_4_, bf16[32,1152]{1,0:T(8,128)(2,1)S(1)} %collective-permute-done.10.refs_1_, bf16[32,1152]{1,0:T(8,128)(2,1)S(1)} %collective-permute-done.11.refs_2_, ...), custom_call_target="tpu_custom_call" | custom-call | tf_op jit(solution)/shard_map/pallas_call | solution.py:483
  69.0 0.0 copy-start.8
  69.1 1.9 %shard_map.117 = (bf16[32,2304]{1,0:T(8,128)(2,1)S(1)}, bf16[32,2304]{1,0:T(8,128)(2,1)S(1)}, bf16[32,2304]{1,0:T(8,128)(2,1)S(1)}, bf16[32,2304]{1,0:T(8,128)(2,1)S(1)}) custom-call(bf16[1728,256]{1,0:T(8,128)(2,1)S(1)} %shard_map.111.refs_0_, bf16[1728,256]{1,0:T(8,128)(2,1)S(1)} %shard_map.113.refs_1_, bf16[1728,256]{1,0:T(8,128)(2,1)S(1)} %shard_map.116.refs_2_.refs_3_, ...), custom_call_target="tpu_custom_call" | custom-call | tf_op jit(solution)/shard_map/pallas_call | solution.py:494
  70.9 1.2 %collective-permute-start.23 = (bf16[32,2304]{1,0:T(8,128)(2,1)S(1)}, bf16[32,2304]{1,0:T(8,128)(2,1)S(1)}, u32[]{:S(2)}, u32[]{:S(2)}) collective-permute-start(bf16[32,2304]{1,0:T(8,128)(2,1)S(1)} %get-tuple-element.67), channel_id=1, source_target_pairs={{8,0},{12,4},{0,8},{4,12},{9,1},{13,5},{1,9},{5,13},{10,2},{14,6},... | collective-permute-start | bytes 442376 | tf_op jit(solution)/shard_map/ppermute | solution.py:503
  72.2 0.9 collective-permute-start.24
  73.0 1.0 %collective-permute-start.17 = (bf16[32,2304]{1,0:T(8,128)(2,1)S(1)}, bf16[32,2304]{1,0:T(8,128)(2,1)S(1)}, u32[]{:S(2)}, u32[]{:S(2)}) collective-permute-start(bf16[32,2304]{1,0:T(8,128)(2,1)S(1)} %get-tuple-element.59), channel_id=1, source_target_pairs={{8,0},{12,4},{0,8},{4,12},{9,1},{13,5},{1,9},{5,13},{10,2},{14,6},... | collective-permute-start | bytes 442376 | tf_op jit(solution)/shard_map/ppermute | solution.py:503
  74.0 0.0 collective-permute-done.22.refs_1_
  74.0 1.1 %collective-permute-start.18 = (bf16[32,2304]{1,0:T(8,128)(2,1)S(1)}, bf16[32,2304]{1,0:T(8,128)(2,1)S(1)}, u32[]{:S(2)}, u32[]{:S(2)}) collective-permute-start(bf16[32,2304]{1,0:T(8,128)(2,1)S(1)} %get-tuple-element.60), channel_id=1, source_target_pairs={{12,0},{8,4},{4,8},{0,12},{13,1},{9,5},{5,9},{1,13},{14,2},{10,6},... | collective-permute-start | bytes 442376 | tf_op jit(solution)/shard_map/ppermute | solution.py:503
  75.2 1.5 %shard_map.118.refs_12_ = bf16[4,2,64,1152]{3,2,1,0:T(8,128)(2,1)S(1)} custom-call(bf16[32,1152]{1,0:T(8,128)(2,1)S(1)} %get-tuple-element.61.refs_0_, bf16[32,1152]{1,0:T(8,128)(2,1)S(1)} %get-tuple-element.62.refs_1_, bf16[32,1152]{1,0:T(8,128)(2,1)S(1)} %get-tuple-element.63.refs_2_, bf16[32,1152]{1,0:T(8,128)(2,1)S(1)} %get-tuple-element.64.refs_3_, ...), custom_call_target="tpu_custom_call" | custom-call | tf_op jit(solution)/shard_map/pallas_call | solution.py:508
  76.7 0.0 collective-permute-done.23.refs_2_
  76.7 3.8 %collective-permute-done.24.refs_3_ = bf16[32,2304]{1,0:T(8,128)(2,1)S(1)} collective-permute-done((bf16[32,2304]{1,0:T(8,128)(2,1)S(1)}, bf16[32,2304]{1,0:T(8,128)(2,1)S(1)}, u32[]{:S(2)}, u32[]{:S(2)}) %collective-permute-start.24) | collective-permute-done | bytes 147488 | tf_op jit(solution)/shard_map/ppermute | solution.py:503
  80.6 2.8 %shard_map.121.refs_15_ = bf16[4,256,1152]{2,1,0:T(8,128)(2,1)} custom-call(s32[2]{0:T(128)S(1)} %pad_add_fusion.place, bf16[32,2304]{1,0:T(8,128)(2,1)S(1)} %get-tuple-element.65.refs_0_, bf16[32,2304]{1,0:T(8,128)(2,1)S(1)} %collective-permute-done.22.refs_1_, bf16[32,2304]{1,0:T(8,128)(2,1)S(1)} %collective-permute-done.23.refs_2_, ...), custom_call_target="tpu_custom_call" | custom-call | tf_op jit(solution)/shard_map/pallas_call | solution.py:526
  83.4 0.0 collective-permute-done.17.refs_2_
  83.4 2.6 %collective-permute-done.18.refs_3_ = bf16[32,2304]{1,0:T(8,128)(2,1)S(1)} collective-permute-done((bf16[32,2304]{1,0:T(8,128)(2,1)S(1)}, bf16[32,2304]{1,0:T(8,128)(2,1)S(1)}, u32[]{:S(2)}, u32[]{:S(2)}) %collective-permute-start.18) | collective-permute-done | bytes 147488 | tf_op jit(solution)/shard_map/ppermute | solution.py:503
  86.0 2.8 %shard_map.122 = bf16[4,256,1152]{2,1,0:T(8,128)(2,1)} custom-call(s32[2]{0:T(128)S(1)} %pad_add_fusion.place, bf16[32,2304]{1,0:T(8,128)(2,1)S(1)} %get-tuple-element.57.refs_0_, bf16[32,2304]{1,0:T(8,128)(2,1)S(1)} %collective-permute-done.16.refs_1_, bf16[32,2304]{1,0:T(8,128)(2,1)S(1)} %collective-permute-done.17.refs_2_, ...), custom_call_target="tpu_custom_call", output_to_operand_aliasing={{}: (16, {})} | custom-call | tf_op jit(solution)/shard_map/pallas_call | solution.py:526
  (21 shorter events, 0.0 us)
Async XLA Ops:
  0.1 24.3 %copy-start.2 = (bf16[4,256,1152]{2,1,0:T(8,128)(2,1)S(1)}, bf16[4,256,1152]{2,1,0:T(8,128)(2,1)}, u32[]{:S(2)}) copy-start(bf16[4,256,1152]{2,1,0:T(8,128)(2,1)} %h_ref.3) | copy-start | bytes 7077892
  0.1 24.3 %copy-start.3 = (bf16[4,256,576]{1,2,0:T(8,128)(2,1)S(1)}, bf16[4,256,576]{1,2,0:T(8,128)(2,1)}, u32[]{:S(2)}) copy-start(bf16[4,256,576]{1,2,0:T(8,128)(2,1)} %param.11) | copy-start | bytes 3538948
  2.8 21.6 %copy-start.7 = (f32[1152]{0:T(1024)S(1)}, f32[1152]{0:T(1024)}, u32[]{:S(2)}) copy-start(f32[1152]{0:T(1024)} %param.16) | copy-start | bytes 13828
  2.8 21.6 %copy-start.1 = (bf16[576,1152]{1,0:T(8,128)(2,1)S(1)}, bf16[576,1152]{1,0:T(8,128)(2,1)}, u32[]{:S(2)}) copy-start(bf16[576,1152]{1,0:T(8,128)(2,1)} %refs_8_.3) | copy-start | bytes 3981316
  2.8 21.6 %copy-start.5 = (s32[4,2,3]{0,1,2:T(2,128)S(1)}, s32[4,2,3]{0,1,2:T(2,128)}, u32[]{:S(2)}) copy-start(s32[4,2,3]{0,1,2:T(2,128)} %param.20) | copy-start | bytes 292
  2.8 21.6 %copy-start.6 = (s32[4,2]{0,1:T(2,128)S(1)}, s32[4,2]{0,1:T(2,128)}, u32[]{:S(2)}) copy-start(s32[4,2]{0,1:T(2,128)} %param.21) | copy-start | bytes 100
  2.8 14.3 %collective-permute-start = (bf16[2,1152,128]{2,1,0:T(8,128)(2,1)S(1)}, bf16[2,1152,128]{2,1,0:T(8,128)(2,1)S(1)}, u32[]{:S(2)}, u32[]{:S(2)}) collective-permute-start(bf16[2,1152,128]{2,1,0:T(8,128)(2,1)S(1)} %get-tuple-element.37.a_ref), channel_id=1, source_target_pairs={{0,1},{1,0},{2,3},{3,2},{4,5},{5,4},{6,7},{7,6},{8,9},{9,8},{10,11... | collective-permute-start | bytes 1769480 | tf_op jit(solution)/shard_map/ppermute | solution.py:429
  4.2 15.8 %collective-permute-start.1 = (bf16[2,1152,128]{2,1,0:T(8,128)(2,1)S(1)}, bf16[2,1152,128]{2,1,0:T(8,128)(2,1)S(1)}, u32[]{:S(2)}, u32[]{:S(2)}) collective-permute-start(bf16[2,1152,128]{2,1,0:T(8,128)(2,1)S(1)} %get-tuple-element.38.b_ref), channel_id=1, source_target_pairs={{1,2},{2,1},{5,6},{6,5},{9,10},{10,9},{13,14},{14,13},{17,18},{18,... | collective-permute-start | bytes 1769480 | tf_op jit(solution)/shard_map/ppermute | solution.py:429
  7.6 22.1 %collective-permute-start.8 = (bf16[2,1152,128]{2,1,0:T(8,128)(2,1)S(1)}, bf16[2,1152,128]{2,1,0:T(8,128)(2,1)S(1)}, u32[]{:S(2)}, u32[]{:S(2)}) collective-permute-start(bf16[2,1152,128]{2,1,0:T(8,128)(2,1)S(1)} %get-tuple-element.47.a_ref), channel_id=1, source_target_pairs={{0,1},{1,0},{2,3},{3,2},{4,5},{5,4},{6,7},{7,6},{8,9},{9,8},{10,11... | collective-permute-start | bytes 1769480 | tf_op jit(solution)/shard_map/ppermute | solution.py:429
  7.7 25.0 %collective-permute-start.9 = (bf16[2,1152,128]{2,1,0:T(8,128)(2,1)S(1)}, bf16[2,1152,128]{2,1,0:T(8,128)(2,1)S(1)}, u32[]{:S(2)}, u32[]{:S(2)}) collective-permute-start(bf16[2,1152,128]{2,1,0:T(8,128)(2,1)S(1)} %get-tuple-element.48.b_ref), channel_id=1, source_target_pairs={{1,2},{2,1},{5,6},{6,5},{9,10},{10,9},{13,14},{14,13},{17,18},{18,... | collective-permute-start | bytes 1769480 | tf_op jit(solution)/shard_map/ppermute | solution.py:429
  11.0 26.5 %collective-permute-start.13 = (bf16[2,64,1152]{2,1,0:T(8,128)(2,1)S(1)}, bf16[2,64,1152]{2,1,0:T(8,128)(2,1)S(1)}, u32[]{:S(2)}, u32[]{:S(2)}) collective-permute-start(bf16[2,64,1152]{2,1,0:T(8,128)(2,1)S(1)} %get-tuple-element.54.refs_9_), channel_id=1, source_target_pairs={{0,4},{4,0},{8,12},{12,8},{1,5},{5,1},{9,13},{13,9},{2,6},{6,2},{1... | collective-permute-start | bytes 884744 | tf_op jit(solution)/shard_map/ppermute | solution.py:411
  17.1 21.7 %collective-permute-start.14 = (bf16[2,64,1152]{2,1,0:T(8,128)(2,1)S(1)}, bf16[2,64,1152]{2,1,0:T(8,128)(2,1)S(1)}, u32[]{:S(2)}, u32[]{:S(2)}) collective-permute-start(bf16[2,64,1152]{2,1,0:T(8,128)(2,1)S(1)} %get-tuple-element.55.refs_10_), channel_id=1, source_target_pairs={{0,8},{4,12},{8,0},{12,4},{1,9},{5,13},{9,1},{13,5},{2,10},{6,14},... | collective-permute-start | bytes 884744 | tf_op jit(solution)/shard_map/ppermute | solution.py:411
  20.0 22.0 %collective-permute-start.15 = (bf16[2,64,1152]{2,1,0:T(8,128)(2,1)S(1)}, bf16[2,64,1152]{2,1,0:T(8,128)(2,1)S(1)}, u32[]{:S(2)}, u32[]{:S(2)}) collective-permute-start(bf16[2,64,1152]{2,1,0:T(8,128)(2,1)S(1)} %get-tuple-element.56.refs_11_), channel_id=1, source_target_pairs={{0,12},{4,8},{8,4},{12,0},{1,13},{5,9},{9,5},{13,1},{2,14},{6,10},... | collective-permute-start | bytes 884744 | tf_op jit(solution)/shard_map/ppermute | solution.py:411
  29.7 15.7 %collective-permute-start.2 = (bf16[64,1152]{1,0:T(8,128)(2,1)S(1)}, bf16[64,1152]{1,0:T(8,128)(2,1)S(1)}, u32[]{:S(2)}, u32[]{:S(2)}) collective-permute-start(bf16[64,1152]{1,0:T(8,128)(2,1)S(1)} %get-tuple-element.40.refs_6_), channel_id=1, source_target_pairs={{0,4},{4,0},{8,12},{12,8},{1,5},{5,1},{9,13},{13,9},{2,6},{6,2},{1... | collective-permute-start | bytes 442376 | tf_op jit(solution)/shard_map/ppermute | solution.py:411
  35.6 6.5 %collective-permute-start.19 = (bf16[32,1152]{1,0:T(8,128)(2,1)S(1)}, bf16[32,1152]{1,0:T(8,128)(2,1)S(1)}, u32[]{:S(2)}, u32[]{:S(2)}) collective-permute-start(bf16[32,1152]{1,0:T(8,128)(2,1)S(1)} %get-tuple-element.62.refs_1_), channel_id=1, source_target_pairs={{0,4},{4,0},{8,12},{12,8},{1,5},{5,1},{9,13},{13,9},{2,6},{6,2},{1... | collective-permute-start | bytes 221192 | tf_op jit(solution)/shard_map/ppermute | solution.py:411
  37.5 5.9 %collective-permute-start.20 = (bf16[32,1152]{1,0:T(8,128)(2,1)S(1)}, bf16[32,1152]{1,0:T(8,128)(2,1)S(1)}, u32[]{:S(2)}, u32[]{:S(2)}) collective-permute-start(bf16[32,1152]{1,0:T(8,128)(2,1)S(1)} %get-tuple-element.63.refs_2_), channel_id=1, source_target_pairs={{0,8},{4,12},{8,0},{12,4},{1,9},{5,13},{9,1},{13,5},{2,10},{6,14},... | collective-permute-start | bytes 221192 | tf_op jit(solution)/shard_map/ppermute | solution.py:411
  38.8 5.4 %collective-permute-start.21 = (bf16[32,1152]{1,0:T(8,128)(2,1)S(1)}, bf16[32,1152]{1,0:T(8,128)(2,1)S(1)}, u32[]{:S(2)}, u32[]{:S(2)}) collective-permute-start(bf16[32,1152]{1,0:T(8,128)(2,1)S(1)} %get-tuple-element.64.refs_3_), channel_id=1, source_target_pairs={{0,12},{4,8},{8,4},{12,0},{1,13},{5,9},{9,5},{13,1},{2,14},{6,10},... | collective-permute-start | bytes 221192 | tf_op jit(solution)/shard_map/ppermute | solution.py:411
  39.2 6.5 %copy-start = (bf16[1152,1728]{0,1:T(8,128)(2,1)S(1)}, bf16[1152,1728]{0,1:T(8,128)(2,1)}, u32[]{:S(2)}) copy-start(bf16[1152,1728]{0,1:T(8,128)(2,1)} %param.17) | copy-start | bytes 11943940
  42.0 11.2 %collective-permute-start.5 = (bf16[64,1152]{1,0:T(8,128)(2,1)S(1)}, bf16[64,1152]{1,0:T(8,128)(2,1)S(1)}, u32[]{:S(2)}, u32[]{:S(2)}) collective-permute-start(bf16[64,1152]{1,0:T(8,128)(2,1)S(1)} %get-tuple-element.44.refs_7_), channel_id=1, source_target_pairs={{0,4},{4,0},{8,12},{12,8},{1,5},{5,1},{9,13},{13,9},{2,6},{6,2},{1... | collective-permute-start | bytes 442376 | tf_op jit(solution)/shard_map/ppermute | solution.py:411
  42.2 5.8 %collective-permute-start.3 = (bf16[64,1152]{1,0:T(8,128)(2,1)S(1)}, bf16[64,1152]{1,0:T(8,128)(2,1)S(1)}, u32[]{:S(2)}, u32[]{:S(2)}) collective-permute-start(bf16[64,1152]{1,0:T(8,128)(2,1)S(1)} %get-tuple-element.41.refs_8_), channel_id=1, source_target_pairs={{0,8},{4,12},{8,0},{12,4},{1,9},{5,13},{9,1},{13,5},{2,10},{6,14},... | collective-permute-start | bytes 442376 | tf_op jit(solution)/shard_map/ppermute | solution.py:411
  43.4 8.3 %collective-permute-start.4 = (bf16[64,1152]{1,0:T(8,128)(2,1)S(1)}, bf16[64,1152]{1,0:T(8,128)(2,1)S(1)}, u32[]{:S(2)}, u32[]{:S(2)}) collective-permute-start(bf16[64,1152]{1,0:T(8,128)(2,1)S(1)} %get-tuple-element.42.refs_10_), channel_id=1, source_target_pairs={{0,12},{4,8},{8,4},{12,0},{1,13},{5,9},{9,5},{13,1},{2,14},{6,10},... | collective-permute-start | bytes 442376 | tf_op jit(solution)/shard_map/ppermute | solution.py:411
  44.2 9.4 %collective-permute-start.6 = (bf16[64,1152]{1,0:T(8,128)(2,1)S(1)}, bf16[64,1152]{1,0:T(8,128)(2,1)S(1)}, u32[]{:S(2)}, u32[]{:S(2)}) collective-permute-start(bf16[64,1152]{1,0:T(8,128)(2,1)S(1)} %get-tuple-element.45.refs_9_), channel_id=1, source_target_pairs={{0,8},{4,12},{8,0},{12,4},{1,9},{5,13},{9,1},{13,5},{2,10},{6,14},... | collective-permute-start | bytes 442376 | tf_op jit(solution)/shard_map/ppermute | solution.py:411
  45.4 11.8 %collective-permute-start.7 = (bf16[64,1152]{1,0:T(8,128)(2,1)S(1)}, bf16[64,1152]{1,0:T(8,128)(2,1)S(1)}, u32[]{:S(2)}, u32[]{:S(2)}) collective-permute-start(bf16[64,1152]{1,0:T(8,128)(2,1)S(1)} %get-tuple-element.46.refs_11_), channel_id=1, source_target_pairs={{0,12},{4,8},{8,4},{12,0},{1,13},{5,9},{9,5},{13,1},{2,14},{6,10},... | collective-permute-start | bytes 442376 | tf_op jit(solution)/shard_map/ppermute | solution.py:411
  60.5 13.5 %collective-permute-start.22 = (bf16[32,2304]{1,0:T(8,128)(2,1)S(1)}, bf16[32,2304]{1,0:T(8,128)(2,1)S(1)}, u32[]{:S(2)}, u32[]{:S(2)}) collective-permute-start(bf16[32,2304]{1,0:T(8,128)(2,1)S(1)} %get-tuple-element.66), channel_id=1, source_target_pairs={{4,0},{0,4},{12,8},{8,12},{5,1},{1,5},{13,9},{9,13},{6,2},{2,6},{1... | collective-permute-start | bytes 442376 | tf_op jit(solution)/shard_map/ppermute | solution.py:503
  60.6 2.2 %collective-permute-start.10 = (bf16[32,1152]{1,0:T(8,128)(2,1)S(1)}, bf16[32,1152]{1,0:T(8,128)(2,1)S(1)}, u32[]{:S(2)}, u32[]{:S(2)}) collective-permute-start(bf16[32,1152]{1,0:T(8,128)(2,1)S(1)} %get-tuple-element.50.refs_5_), channel_id=1, source_target_pairs={{0,4},{4,0},{8,12},{12,8},{1,5},{5,1},{9,13},{13,9},{2,6},{6,2},{1... | collective-permute-start | bytes 221192 | tf_op jit(solution)/shard_map/ppermute | solution.py:411
  61.1 3.7 %collective-permute-start.11 = (bf16[32,1152]{1,0:T(8,128)(2,1)S(1)}, bf16[32,1152]{1,0:T(8,128)(2,1)S(1)}, u32[]{:S(2)}, u32[]{:S(2)}) collective-permute-start(bf16[32,1152]{1,0:T(8,128)(2,1)S(1)} %get-tuple-element.51.refs_6_), channel_id=1, source_target_pairs={{0,8},{4,12},{8,0},{12,4},{1,9},{5,13},{9,1},{13,5},{2,10},{6,14},... | collective-permute-start | bytes 221192 | tf_op jit(solution)/shard_map/ppermute | solution.py:411
  62.3 4.4 %collective-permute-start.12 = (bf16[32,1152]{1,0:T(8,128)(2,1)S(1)}, bf16[32,1152]{1,0:T(8,128)(2,1)S(1)}, u32[]{:S(2)}, u32[]{:S(2)}) collective-permute-start(bf16[32,1152]{1,0:T(8,128)(2,1)S(1)} %get-tuple-element.52.refs_7_), channel_id=1, source_target_pairs={{0,12},{4,8},{8,4},{12,0},{1,13},{5,9},{9,5},{13,1},{2,14},{6,10},... | collective-permute-start | bytes 221192 | tf_op jit(solution)/shard_map/ppermute | solution.py:411
  69.0 6.1 %copy-start.8 = (f32[1152]{0:T(1024)S(1)}, f32[1152]{0:T(1024)}, u32[]{:S(2)}) copy-start(f32[1152]{0:T(1024)} %param.19) | copy-start | bytes 13828
  70.9 5.8 %collective-permute-start.23 = (bf16[32,2304]{1,0:T(8,128)(2,1)S(1)}, bf16[32,2304]{1,0:T(8,128)(2,1)S(1)}, u32[]{:S(2)}, u32[]{:S(2)}) collective-permute-start(bf16[32,2304]{1,0:T(8,128)(2,1)S(1)} %get-tuple-element.67), channel_id=1, source_target_pairs={{8,0},{12,4},{0,8},{4,12},{9,1},{13,5},{1,9},{5,13},{10,2},{14,6},... | collective-permute-start | bytes 442376 | tf_op jit(solution)/shard_map/ppermute | solution.py:503
  72.2 8.4 %collective-permute-start.24 = (bf16[32,2304]{1,0:T(8,128)(2,1)S(1)}, bf16[32,2304]{1,0:T(8,128)(2,1)S(1)}, u32[]{:S(2)}, u32[]{:S(2)}) collective-permute-start(bf16[32,2304]{1,0:T(8,128)(2,1)S(1)} %get-tuple-element.68), channel_id=1, source_target_pairs={{12,0},{8,4},{4,8},{0,12},{13,1},{9,5},{5,9},{1,13},{14,2},{10,6},... | collective-permute-start | bytes 442376 | tf_op jit(solution)/shard_map/ppermute | solution.py:503
  73.0 10.4 %collective-permute-start.16 = (bf16[32,2304]{1,0:T(8,128)(2,1)S(1)}, bf16[32,2304]{1,0:T(8,128)(2,1)S(1)}, u32[]{:S(2)}, u32[]{:S(2)}) collective-permute-start(bf16[32,2304]{1,0:T(8,128)(2,1)S(1)} %get-tuple-element.58), channel_id=1, source_target_pairs={{4,0},{0,4},{12,8},{8,12},{5,1},{1,5},{13,9},{9,13},{6,2},{2,6},{1... | collective-permute-start | bytes 442376 | tf_op jit(solution)/shard_map/ppermute | solution.py:503
  73.0 10.4 %collective-permute-start.17 = (bf16[32,2304]{1,0:T(8,128)(2,1)S(1)}, bf16[32,2304]{1,0:T(8,128)(2,1)S(1)}, u32[]{:S(2)}, u32[]{:S(2)}) collective-permute-start(bf16[32,2304]{1,0:T(8,128)(2,1)S(1)} %get-tuple-element.59), channel_id=1, source_target_pairs={{8,0},{12,4},{0,8},{4,12},{9,1},{13,5},{1,9},{5,13},{10,2},{14,6},... | collective-permute-start | bytes 442376 | tf_op jit(solution)/shard_map/ppermute | solution.py:503
  74.0 12.0 %collective-permute-start.18 = (bf16[32,2304]{1,0:T(8,128)(2,1)S(1)}, bf16[32,2304]{1,0:T(8,128)(2,1)S(1)}, u32[]{:S(2)}, u32[]{:S(2)}) collective-permute-start(bf16[32,2304]{1,0:T(8,128)(2,1)S(1)} %get-tuple-element.60), channel_id=1, source_target_pairs={{12,0},{8,4},{4,8},{0,12},{13,1},{9,5},{5,9},{1,13},{14,2},{10,6},... | collective-permute-start | bytes 442376 | tf_op jit(solution)/shard_map/ppermute | solution.py:503
  75.2 5.4 %copy-start.4 = (bf16[576,1152]{1,0:T(8,128)(2,1)S(1)}, bf16[576,1152]{1,0:T(8,128)(2,1)}, u32[]{:S(2)}) copy-start(bf16[576,1152]{1,0:T(8,128)(2,1)} %refs_13_.3) | copy-start | bytes 3981316

commit v4 on v3

--- a/solution.py
+++ b/solution.py
@@ -96,48 +96,83 @@
         copy.wait()
 
 
-def attend(frame, place, counts, lists, q_ref, keys, att):
-    n, width, tokens = q_ref.shape
-    tiles = tokens // TILE
+def tile_masks(frame, n, tiles, local, place, counts, lists):
     strip = place[1]
     odd = strip % 2
     first = strip * tiles
-    places = (first + 1 - odd, first + odd, first + 2 - 3 * odd, first - 1 + 3 * odd)
+    if local:
+        spots = (first + 1 - odd, first + odd)
+    else:
+        spots = (first + 2 - 3 * odd, first - 1 + 3 * odd)
     masks = []
     for f in range(n):
-        table = []
-        for t in range(tiles):
-            live = counts[t, frame + f]
+        rows = []
+        for spot in spots:
             cells = []
-            for spot in places:
+            for t in range(tiles):
                 hit = jnp.bool_(False)
                 for j in range(MAXT):
-                    hit = hit | ((lists[j, t, frame + f] == spot) & (j < live))
+                    hit = hit | ((lists[j, t, frame + f] == spot) & (j < counts[t, frame + f]))
                 cells.append(jnp.full((SUB, TILE), jnp.where(hit, 1.0, 0.0), F32))
-            table.append(cells)
-        masks.append([jnp.concatenate(row, axis=1).astype(BF) for row in zip(*table)])
+            rows.append(jnp.concatenate(cells, axis=1).astype(BF))
+        masks.append(rows)
+    return masks
+
+
+def attend(masks, keys, query, finish):
+    n = keys[0].shape[0]
+    width = keys[0].shape[1] // 2
 
     def scores(f, h):
-        q = q_ref[f, head(h), :].astype(F32)
-        qn = (q * head_scale(q)).astype(BF)
+        qn = query(f, h)
         return f, [contract(ref[f, head(h), :], qn, 0, 0) for ref in keys]
 
     def weigh(scored):
         f, s = scored
         packed = []
-        for i, x in enumerate(s):
-            p = jnp.exp2(x * EXP2_SCALE).astype(BF).reshape(TILE // SUB, SUB, tokens)
-            packed.append((p * masks[f][i]).reshape(TILE, tokens))
-        return [jnp.concatenate(packed[i:i + 2], axis=0) for i in (0, 2)]
-
-    def gather(f, h, halves):
-        o = 0
-        for i in range(2):
-            v = jnp.concatenate([r[f, head(h, width), :] for r in keys[2 * i:2 * i + 2]], axis=1)
-            o += contract(with_ones(v), halves[i], 1, 0)
-        att[f, head(h), :] = averaged(o).astype(att.dtype)
+        for mask, x in zip(masks[f], s):
+            p = jnp.exp2(x * EXP2_SCALE).astype(BF).reshape(TILE // SUB, SUB, x.shape[1])
+            packed.append((p * mask).reshape(x.shape))
+        return jnp.concatenate(packed, axis=0)
+
+    def gather(f, h, weights):
+        v = jnp.concatenate([ref[f, head(h, width), :] for ref in keys], axis=1)
+        finish(f, h, contract(with_ones(v), weights, 1, 0))
 
     pipeline([(f, h) for f in range(n) for h in range(width // HEAD_DIM)], scores, weigh, gather)
+
+
+def sums(h):
+    return slice(h * (HEAD_DIM + 8), (h + 1) * (HEAD_DIM + 8))
+
+
+def local_kernel(frame, place, counts, lists, q_ref, a_ref, b_ref, qn_ref, sum_ref):
+    n, _, tokens = q_ref.shape
+
+    def query(f, h):
+        q = q_ref[f, head(h), :].astype(F32)
+        qn = (q * head_scale(q)).astype(BF)
+        qn_ref[f, head(h), :] = qn
+        return qn
+
+    def finish(f, h, o):
+        sum_ref[f, sums(h), :] = o
+
+    masks = tile_masks(frame, n, tokens // TILE, True, place, counts, lists)
+    attend(masks, (a_ref, b_ref), query, finish)
+
+
+def remote_attend(frame, place, counts, lists, qn_ref, sum_ref, ra_ref, rb_ref, att):
+    n, _, tokens = qn_ref.shape
+
+    def query(f, h):
+        return qn_ref[f, head(h), :]
+
+    def finish(f, h, o):
+        att[f, head(h), :] = averaged(o + sum_ref[f, sums(h), :]).astype(att.dtype)
+
+    masks = tile_masks(frame, n, tokens // TILE, False, place, counts, lists)
+    attend(masks, (ra_ref, rb_ref), query, finish)
 
 
 def add_normed(blocks):
@@ -150,24 +185,32 @@
         finish(proj * scale)
 
 
-def spatial_kernel(frame, n_groups, place, counts, lists, q_ref, a_ref, b_ref, ra_ref, rb_ref, h_ref, w_ref, g_ref, *rest):
-    outs, (att, mix) = rest[:n_groups], rest[n_groups:]
-    attend(frame, place, counts, lists, q_ref, (a_ref, b_ref, ra_ref, rb_ref), att)
-
-    def finish(normed):
-        mix[...] = (h_ref[0].astype(F32) + normed * g_ref[...]).astype(BF)
-
-    add_normed([(lambda: contract(att[0], w_ref[...], 0, 0), finish)])
-    share = mix.shape[0] // n_groups
+def spatial_kernel(n_groups, place, counts, lists, qn_ref, sum_ref, ra_ref, rb_ref, h_ref, w_ref, g_ref, *rest):
+    outs, (att, hid, mix, sem) = rest[:n_groups], rest[n_groups:]
+    copy = pltpu.make_async_copy(h_ref.at[pl.ds(0, hid.shape[0])], hid, sem)
+    copy.start()
+    remote_attend(0, place, counts, lists, qn_ref, sum_ref, ra_ref, rb_ref, att)
+    copy.wait()
+    n, tokens, _ = hid.shape
+
+    def block(f):
+        def finish(normed):
+            mix[f] = (hid[f].astype(F32) + normed * g_ref[...]).astype(BF)
+
+        return lambda: contract(att[f], w_ref[...], 0, 0), finish
+
+    add_normed([block(f) for f in range(n)])
+    share = tokens // n_groups
     for j, out in enumerate(outs):
         group = peer(place[0], j, n_groups)
-        out[...] = mix[pl.ds(pl.multiple_of(group * share, SUB), share), :]
-
-
-def late_kernel(frame, n_groups, halves, place, counts, lists, q_ref, a_ref, b_ref, ra_ref, rb_ref, *rest):
+        for f in range(n):
+            out[f] = mix[f, pl.ds(pl.multiple_of(group * share, SUB), share), :]
+
+
+def late_kernel(frame, n_groups, halves, place, counts, lists, qn_ref, sum_ref, ra_ref, rb_ref, *rest):
     outs, (att, rows) = rest[:n_groups * halves], rest[n_groups * halves:]
-    n, width, tokens = q_ref.shape
-    attend(frame, place, counts, lists, q_ref, (a_ref, b_ref, ra_ref, rb_ref), att)
+    n, width, tokens = qn_ref.shape
+    remote_attend(frame, place, counts, lists, qn_ref, sum_ref, ra_ref, rb_ref, att)
     for f in range(n):
         rows[:, f * width:(f + 1) * width] = att[f].T.astype(BF)
     size = tokens // n_groups // halves
@@ -220,28 +263,30 @@
     return c ^ (frame & 1) if paired(chunks, n_groups * SUB, frames) else c
 
 
-def project(w_ref, x, out):
+def project(w_ref, x, out, base=0):
     width = w_ref.shape[0] // 3
     cut = w_ref.shape[0] // 2
     heads = width // HEAD_DIM
-    parts = [contract(w_ref[i * cut:(i + 1) * cut, :], x[...], 1, 1) for i in range(2)]
+    parts = [contract(w_ref[i * cut:(i + 1) * cut, :], x, 1, 1) for i in range(2)]
     for h in range(3 * heads):
         i, at = divmod(h * HEAD_DIM, cut)
         y = parts[i][at:at + HEAD_DIM, :]
         if h < 2 * heads:
             y = y * head_scale(y)
-        out[head(h), :] = y.astype(BF)
-
-
-def project_kernel(frame, frames, *refs):
+        out[head(h), base:base + x.shape[0]] = y.astype(BF)
+
+
+def project_kernel(frames, *refs):
     pieces, w_ref, out, x = refs[:-3], refs[-3], refs[-2], refs[-1]
     n_groups = len(pieces)
-    chunks = pieces[0].shape[0] // SUB
-    for c in range(chunks):
-        for j, piece in enumerate(pieces):
-            at = (slot(c, frame, chunks, n_groups, frames) * n_groups + j) * SUB
-            x[at:at + SUB, :] = piece[c * SUB:(c + 1) * SUB, :]
-    project(w_ref, x, out)
+    n, share, _ = pieces[0].shape
+    chunks = share // SUB
+    for f in range(n):
+        for c in range(chunks):
+            for j, piece in enumerate(pieces):
+                at = (slot(c, f, chunks, n_groups, frames) * n_groups + j) * SUB
+                x[f, at:at + SUB, :] = piece[f, c * SUB:(c + 1) * SUB, :]
+        project(w_ref, x[f], out, f * x.shape[1])
 
 
 def late_project_kernel(frame, frames, *refs):
@@ -263,7 +308,7 @@
         x[...] = (b[...].astype(F32) + normed * g_ref[...]).astype(BF)
 
     add_normed([(lambda: contract(a[...], w_ref[...], 1, 0), finish)])
-    project(qkv_ref, x, out)
+    project(qkv_ref, x[...], out)
 
 
 def temporal_kernel(n_groups, *refs):
@@ -313,9 +358,9 @@
 
 def output_kernel(n_groups, js, early, half, halves, aliased, place, *refs):
     n = len(js)
-    atts, pieces = refs[:n], refs[n:n * (1 + early)]
-    late_ref, w_ref, g_ref = refs[n * (1 + early):n * (1 + early) + 3]
-    out, buf, sems = refs[n * (1 + early) + 3 + aliased:]
+    atts, pieces = refs[:n], refs[n:2 * n]
+    late_ref, w_ref, g_ref = refs[2 * n:2 * n + 3]
+    out, buf, sems = refs[2 * n + 3 + aliased:]
     _, late, rows, _ = late_ref.shape
     width = w_ref.shape[0]
     frames = early + late
@@ -330,7 +375,7 @@
             for k, i in enumerate(some):
                 j = js[i]
                 for f in range(frames):
-                    mine = pieces[i * early + f][...] if f < early else late_ref[j, f - early]
+                    mine = pieces[i][f] if f < early else late_ref[j, f - early]
                     at = (k * frames + f) * rows
                     part = normed[at:at + rows, :] * g_ref[...]
                     buf[i, f] = (mine.astype(F32) + part).astype(BF)
@@ -367,7 +412,7 @@
     share = tokens // groups
     halves = 2 if share % (4 * SUB) == 0 else 1
     rows = share // halves
-    queries = jnp.transpose(spatial_queries, (0, 2, 1))
+    queries = pltpu.with_memory_space_constraint(jnp.transpose(spatial_queries, (0, 2, 1)), pltpu.HBM)
     keys = pltpu.with_memory_space_constraint(jnp.transpose(spatial_keys, (0, 2, 1)), pltpu.HBM)
     values = pltpu.with_memory_space_constraint(jnp.transpose(spatial_values, (0, 2, 1)), pltpu.HBM)
     hidden_far = pltpu.with_memory_space_constraint(hidden, pltpu.HBM)
@@ -397,9 +442,6 @@
             input_output_aliases=alias or {},
             compiler_params=vmem(limit),
         )
-
-    def frame_block(f):
-        return pl.BlockSpec((1, width, tokens), lambda *_: (f, 0, 0))
 
     late = frames // 2
     early = frames - late
@@ -429,45 +471,55 @@
         halos.append((a, b, lax.ppermute(a, "strip", near), lax.ppermute(b, "strip", far)))
     far_hidden = send(own_hidden)
 
-    mixed = [[None] * early for _ in range(groups)]
-    projected = []
-    for f in range(early):
-        edge_block = pl.BlockSpec((1,) + edge.shape, lambda *_, f=f: (f, 0, 0))
-        parts = call(
-            functools.partial(spatial_kernel, f, groups),
-            [smem, smem, smem, frame_block(f)]
-            + [edge_block] * 4
-            + [
-                pl.BlockSpec((1, tokens, model), lambda *_, f=f: (f, 0, 0)),
-                whole((width, model)),
-                whole((1, model)),
-            ],
-            [whole((share, model))] * groups,
-            [jax.ShapeDtypeStruct((share, model), BF)] * groups,
-            [pltpu.VMEM((1, width, tokens), BF), pltpu.VMEM((tokens, model), BF)],
-        )(place, counts, lists, queries, *halos[0], hidden, spatial_out_weight, gain_one)
-        for j in range(groups):
-            mixed[j][f] = parts[j]
-        arrived = send(parts)
-        projected.append(
+    sum_shape = (late, width // HEAD_DIM * (HEAD_DIM + 8), tokens)
+    own_sums = []
+    for some in range(2):
+        block = pl.BlockSpec((late, width, tokens), lambda *_, some=some: (some, 0, 0))
+        own_sums.append(
             call(
-                functools.partial(project_kernel, f, frames),
-                [whole((share, model))] * groups + [whole((3 * width, model))],
-                whole((3 * width, tokens)),
-                jax.ShapeDtypeStruct((3 * width, tokens), BF),
-                [pltpu.VMEM((tokens, model), BF)],
-            )(*arrived, qkv_weight)
+                functools.partial(local_kernel, some * late),
+                [smem, smem, smem, block] + [whole((late,) + edge.shape)] * 2,
+                [whole((late, width, tokens)), whole(sum_shape)],
+                [
+                    jax.ShapeDtypeStruct((late, width, tokens), BF),
+                    jax.ShapeDtypeStruct(sum_shape, F32),
+                ],
+            )(place, counts, lists, queries, *halos[some][:2])
         )
+    sum_specs = [whole((late, width, tokens)), whole(sum_shape)]
+
+    mixed = call(
+        functools.partial(spatial_kernel, groups),
+        [smem, smem, smem]
+        + sum_specs
+        + [whole((late,) + edge.shape)] * 2
+        + [any_spec, whole((width, model)), whole((1, model))],
+        [whole((early, share, model))] * groups,
+        [jax.ShapeDtypeStruct((early, share, model), BF)] * groups,
+        [
+            pltpu.VMEM((early, width, tokens), BF),
+            pltpu.VMEM((early, tokens, model), BF),
+            pltpu.VMEM((early, tokens, model), BF),
+            pltpu.SemaphoreType.DMA,
+        ],
+    )(place, counts, lists, *own_sums[0], *halos[0][2:], hidden_far, spatial_out_weight, gain_one)
+    arrived = send(mixed)
+    projected = call(
+        functools.partial(project_kernel, frames),
+        [whole((early, share, model))] * groups + [whole((3 * width, model))],
+        whole((3 * width, early * tokens)),
+        jax.ShapeDtypeStruct((3 * width, early * tokens), BF),
+        [pltpu.VMEM((early, tokens, model), BF)],
+    )(*arrived, qkv_weight)
 
     late_shape = (rows, late * width)
     own_late = call(
         functools.partial(late_kernel, early, groups, halves),
-        [smem, smem, smem, pl.BlockSpec((late, width, tokens), lambda *_: (1, 0, 0))]
-        + [whole((late,) + edge.shape)] * 4,
+        [smem, smem, smem] + sum_specs + [whole((late,) + edge.shape)] * 2,
         [whole(late_shape)] * (groups * halves),
         [jax.ShapeDtypeStruct(late_shape, BF)] * (groups * halves),
         [pltpu.VMEM((late, width, tokens), F32), pltpu.VMEM((tokens, late * width), BF)],
-    )(place, counts, lists, queries, *halos[1])
+    )(place, counts, lists, *own_sums[1], *halos[1][2:])
     own_late = [own_late[half * groups:(half + 1) * groups] for half in range(halves)]
     far_late = []
     for half in range(halves):
@@ -493,12 +545,15 @@
         )(*far_late[half], *far_hidden, spatial_out_weight, gain_one, qkv_weight)
         back = call(
             functools.partial(temporal_kernel, groups),
-            [pl.BlockSpec((3 * width, lanes), lambda *_, half=half: (0, half))] * early
+            [
+                pl.BlockSpec((3 * width, lanes), lambda *_, at=f * halves + half: (0, at))
+                for f in range(early)
+            ]
             + [pl.BlockSpec((3 * width, lanes), lambda *_, f=f: (0, f)) for f in range(late)],
             [whole(back_shape)] * groups,
             [jax.ShapeDtypeStruct(back_shape, BF)] * groups,
             [pltpu.VMEM((rows // SUB, width, groups * frames * SUB), F32)],
-        )(*projected, *[late_projected] * late)
+        )(*[projected] * early, *[late_projected] * late)
         home = {
             j: lax.ppermute(back[j], "frame", [(b, a) for a, b in out_pairs(j)])
             for j in reversed(range(1, groups))
@@ -516,7 +571,7 @@
 
     out = None
     for half in range(halves):
-        piece = pl.BlockSpec((rows, model), lambda *_, half=half: (half, 0))
+        piece = pl.BlockSpec((early, rows, model), lambda *_, half=half: (0, half, 0))
         cuts = [groups]
         for lo, hi in zip([0] + cuts, cuts):
             js = range(lo, hi)
@@ -527,7 +582,7 @@
                 functools.partial(output_kernel, groups, tuple(js), early, half, halves, len(extra)),
                 [smem]
                 + [whole(back_shape)] * len(js)
-                + [piece] * (len(js) * early)
+                + [piece] * len(js)
                 + [pl.BlockSpec((groups, late, rows, model), lambda *_, half=half: (0, 0, half, 0))]
                 + [whole((width, model)), whole((1, model))]
                 + [any_spec] * len(extra),
@@ -537,11 +592,11 @@
                     pltpu.VMEM((len(js), frames, rows, model), BF),
                     pltpu.SemaphoreType.DMA((len(js),)),
                 ],
-                alias={4 + len(js) * (1 + early): 0} if extra else None,
+                alias={4 + 2 * len(js): 0} if extra else None,
             )(
                 place,
                 *[returned[half][j] for j in js],
-                *[mixed[j][f] for j in js for f in range(early)],
+                *[mixed[j] for j in js],
                 late_mixed,
                 temporal_out_weight,
                 gain_two,

time: 89.2 us -> 84.2 us (0.944)
  the two profiles are of different devices: /device:TPU:19 before, /device:TPU:0 now
where the time goes in v4:
time: 84.2 us; the launch traced here: 83.7 us
  Pallas kernels  32.8 us (39%)
  waiting for transfers between devices  28.4 us (34%)
  starting transfers between devices  22 us (26%)
    ppermute x12, waiting for transfers between devices, send(): lax.ppermute(parts[j], 'frame', out_pairs(j))  11.5 us
    ppermute x2, waiting for transfers between devices, shards(): lax.ppermute(a, 'strip', near)  10.2 us
    ppermute x12, starting transfers between devices, send(): lax.ppermute(parts[j], 'frame', out_pairs(j))  8.87 us
    ppermute x2, starting transfers between devices, shards(): lax.ppermute(a, 'strip', near)  7.55 us
    ppermute x6, waiting for transfers between devices, shards(): lax.ppermute(back[j], 'frame', [(b, a) for a, b in out_pairs(j)])  6.59 us
    pallas_call x2, Pallas kernels, shards(): call(functools.partial(output_kernel, groups, tuple(js), early, half, hal...  5.65 us
    pallas_call x2, Pallas kernels, shards(): call(functools.partial(local_kernel, some * late), [smem, smem, smem, blo...  4.93 us
    pallas_call x2, Pallas kernels, shards(): call(functools.partial(late_project_kernel, early, frames), late_specs +...  4.52 us
  transfers between devices with their start and end apart: 22, of which 9 were waited for; matrix products, arithmetic and copies ran while one was open for 0% of the time, Pallas kernels for 28%

profile of v4, /device:TPU:0, one launch (start us, length us, event | category | flops | bytes accessed | tf_op | source)
XLA Modules:
  0.0 83.7 jit_solution(15059734887194726863)
XLA Ops:
  0.0 0.1 pad_add_fusion.place
  0.1 2.5 %shard_map.109 = (bf16[2,1152,128]{2,1,0:T(8,128)(2,1)S(1)}, bf16[2,1152,128]{2,1,0:T(8,128)(2,1)S(1)}, bf16[2,64,1152]{2,1,0:T(8,128)(2,1)S(1)}, bf16[2,64,1152...) custom-call(s32[2]{0:T(128)S(1)} %pad_add_fusion.place, ...), custom_call_target="tpu_custom_call" | custom-call | tf_op jit(solution)/shard_map/pallas_call | solution.py:460
  2.6 0.0 copy-start.5
  2.6 0.0 copy-start.3
  2.6 0.0 copy-start.4
  2.6 3.1 %collective-permute-start = (bf16[2,1152,128]{2,1,0:T(8,128)(2,1)S(1)}, bf16[2,1152,128]{2,1,0:T(8,128)(2,1)S(1)}, u32[]{:S(2)}, u32[]{:S(2)}) collective-permute-start(bf16[2,1152,128]{2,1,0:T(8,128)(2,1)S(1)} %get-tuple-element.37.a_ref), channel_id=1, source_target_pairs={{0,1},{1,0},{2,3},{3,2},{4,5},{5,4},{6,7},{7,6},{8,9},{9,8},{10,11... | collective-permute-start | bytes 1769480 | tf_op jit(solution)/shard_map/ppermute | solution.py:471
  5.8 0.7 collective-permute-start.1
  6.5 1.5 %shard_map.113 = (bf16[2,1152,128]{2,1,0:T(8,128)(2,1)S(1)}, bf16[2,1152,128]{2,1,0:T(8,128)(2,1)S(1)}) custom-call(s32[2]{0:T(128)S(1)} %pad_add_fusion.place, bf16[4,576,256]{2,1,0:T(8,128)(2,1)} %bitcast.20, bf16[4,576,256]{2,1,0:T(8,128)(2,1)} %bitcast.22), custom_call_target="tpu_custom_call" | custom-call | tf_op jit(solution)/shard_map/pallas_call | solution.py:460
  8.0 0.0 copy-start.1
  8.0 4.4 %collective-permute-start.5 = (bf16[2,1152,128]{2,1,0:T(8,128)(2,1)S(1)}, bf16[2,1152,128]{2,1,0:T(8,128)(2,1)S(1)}, u32[]{:S(2)}, u32[]{:S(2)}) collective-permute-start(bf16[2,1152,128]{2,1,0:T(8,128)(2,1)S(1)} %get-tuple-element.45.a_ref), channel_id=1, source_target_pairs={{0,1},{1,0},{2,3},{3,2},{4,5},{5,4},{6,7},{7,6},{8,9},{9,8},{10,11... | collective-permute-start | bytes 1769480 | tf_op jit(solution)/shard_map/ppermute | solution.py:471
  12.4 0.7 collective-permute-start.6
  13.1 0.1 collective-permute-start.10
  13.2 6.8 %collective-permute-done.ra_ref = bf16[2,1152,128]{2,1,0:T(8,128)(2,1)S(1)} collective-permute-done((bf16[2,1152,128]{2,1,0:T(8,128)(2,1)S(1)}, bf16[2,1152,128]{2,1,0:T(8,128)(2,1)S(1)}, u32[]{:S(2)}, u32[]{:S(2)}) %collective-permute-start) | collective-permute-done | bytes 589856 | tf_op jit(solution)/shard_map/ppermute | solution.py:471
  19.9 2.0 %collective-permute-start.11 = (bf16[2,64,1152]{2,1,0:T(8,128)(2,1)S(1)}, bf16[2,64,1152]{2,1,0:T(8,128)(2,1)S(1)}, u32[]{:S(2)}, u32[]{:S(2)}) collective-permute-start(bf16[2,64,1152]{2,1,0:T(8,128)(2,1)S(1)} %get-tuple-element.55.refs_10_), channel_id=1, source_target_pairs={{0,8},{4,12},{8,0},{12,4},{1,9},{5,13},{9,1},{13,5},{2,10},{6,14},... | collective-permute-start | bytes 884744 | tf_op jit(solution)/shard_map/ppermute | solution.py:453
  21.9 0.0 collective-permute-done.1.rb_ref
  21.9 0.0 collective-permute-start.12
  21.9 2.4 %shard_map.110 = (bf16[2,576,256]{2,1,0:T(8,128)(2,1)S(1)}, f32[2,640,256]{2,1,0:T(8,128)S(1)}) custom-call(s32[2]{0:T(128)S(1)} %pad_add_fusion.place, s32[2,4]{1,0:T(2,128)S(1)} %bitcast.15, s32[3,2,4]{2,1,0:T(2,128)S(1)} %bitcast.11, bf16[4,576,256]{2,1,0:T(8,128)(2,1)} %bitcast.23, bf16[2,1152,128]{2,1,0:T(8,128)(2,1)S(1)} %get-tuple-element.37.a_ref, ...), custom_call_target="tpu_custom_call" | custom-call | tf_op jit(solution)/shard_map/pallas_call | solution.py:479
  24.4 3.6 %shard_map.111 = (bf16[2,64,1152]{2,1,0:T(8,128)(2,1)S(1)}, bf16[2,64,1152]{2,1,0:T(8,128)(2,1)S(1)}, bf16[2,64,1152]{2,1,0:T(8,128)(2,1)S(1)}, bf16[2,64,1152]{2,1,0:T(8,128)(2,1)S(1)}) custom-call(s32[2]{0:T(128)S(1)} %pad_add_fusion.place, s32[2,4]{1,0:T(2,128)S(1)} %bitcast.16, s32[3,2,4]{2,1,0:T(2,128)S(1)} %bitcast.12, ...), custom_call_target="tpu_custom_call" | custom-call | tf_op jit(solution)/shard_map/pallas_call | solution.py:491
  28.0 0.0 collective-permute-done.10.refs_5_
  28.0 0.2 collective-permute-start.2
  28.2 3.5 %collective-permute-done.5.ra_ref = bf16[2,1152,128]{2,1,0:T(8,128)(2,1)S(1)} collective-permute-done((bf16[2,1152,128]{2,1,0:T(8,128)(2,1)S(1)}, bf16[2,1152,128]{2,1,0:T(8,128)(2,1)S(1)}, u32[]{:S(2)}, u32[]{:S(2)}) %collective-permute-start.5) | collective-permute-done | bytes 589856 | tf_op jit(solution)/shard_map/ppermute | solution.py:471
  31.7 1.7 %collective-permute-start.3 = (bf16[2,64,1152]{2,1,0:T(8,128)(2,1)S(1)}, bf16[2,64,1152]{2,1,0:T(8,128)(2,1)S(1)}, u32[]{:S(2)}, u32[]{:S(2)}) collective-permute-start(bf16[2,64,1152]{2,1,0:T(8,128)(2,1)S(1)} %get-tuple-element.43.refs_6_), channel_id=1, source_target_pairs={{0,8},{4,12},{8,0},{12,4},{1,9},{5,13},{9,1},{13,5},{2,10},{6,14},... | collective-permute-start | bytes 884744 | tf_op jit(solution)/shard_map/ppermute | solution.py:453
  33.4 0.0 collective-permute-done.6.rb_ref
  33.4 0.0 collective-permute-start.4
  33.4 2.5 %shard_map.114 = (bf16[2,576,256]{2,1,0:T(8,128)(2,1)S(1)}, f32[2,640,256]{2,1,0:T(8,128)S(1)}) custom-call(s32[2]{0:T(128)S(1)} %pad_add_fusion.place, s32[2,4]{1,0:T(2,128)S(1)} %bitcast.17, s32[3,2,4]{2,1,0:T(2,128)S(1)} %bitcast.13, bf16[4,576,256]{2,1,0:T(8,128)(2,1)} %bitcast.24, bf16[2,1152,128]{2,1,0:T(8,128)(2,1)S(1)} %get-tuple-element.45.a_ref, ...), custom_call_target="tpu_custom_call" | custom-call | tf_op jit(solution)/shard_map/pallas_call | solution.py:479
  36.0 2.2 %shard_map.115 = (bf16[32,1152]{1,0:T(8,128)(2,1)S(1)}, bf16[32,1152]{1,0:T(8,128)(2,1)S(1)}, bf16[32,1152]{1,0:T(8,128)(2,1)S(1)}, bf16[32,1152]{1,0:T(8,128)(2...) custom-call(s32[2]{0:T(128)S(1)} %pad_add_fusion.place, ...), custom_call_target="tpu_custom_call" | custom-call | tf_op jit(solution)/shard_map/pallas_call | solution.py:516
  38.2 0.0 collective-permute-done.11.refs_6_
  38.2 0.5 collective-permute-start.16
  38.7 0.0 collective-permute-done.12.refs_7_
  38.7 1.7 %collective-permute-start.17 = (bf16[32,1152]{1,0:T(8,128)(2,1)S(1)}, bf16[32,1152]{1,0:T(8,128)(2,1)S(1)}, u32[]{:S(2)}, u32[]{:S(2)}) collective-permute-start(bf16[32,1152]{1,0:T(8,128)(2,1)S(1)} %get-tuple-element.63.refs_2_), channel_id=1, source_target_pairs={{0,8},{4,12},{8,0},{12,4},{1,9},{5,13},{9,1},{13,5},{2,10},{6,14},... | collective-permute-start | bytes 221192 | tf_op jit(solution)/shard_map/ppermute | solution.py:453
  40.4 0.0 collective-permute-done.16.refs_1_
  40.4 0.9 %collective-permute-start.18 = (bf16[32,1152]{1,0:T(8,128)(2,1)S(1)}, bf16[32,1152]{1,0:T(8,128)(2,1)S(1)}, u32[]{:S(2)}, u32[]{:S(2)}) collective-permute-start(bf16[32,1152]{1,0:T(8,128)(2,1)S(1)} %get-tuple-element.64.refs_3_), channel_id=1, source_target_pairs={{0,12},{4,8},{8,4},{12,0},{1,13},{5,9},{9,5},{13,1},{2,14},{6,10},... | collective-permute-start | bytes 221192 | tf_op jit(solution)/shard_map/ppermute | solution.py:453
  41.3 7.3 %collective-permute-done.17.refs_2_ = bf16[32,1152]{1,0:T(8,128)(2,1)S(1)} collective-permute-done((bf16[32,1152]{1,0:T(8,128)(2,1)S(1)}, bf16[32,1152]{1,0:T(8,128)(2,1)S(1)}, u32[]{:S(2)}, u32[]{:S(2)}) %collective-permute-start.17) | collective-permute-done | bytes 73760 | tf_op jit(solution)/shard_map/ppermute | solution.py:453
  48.6 0.0 collective-permute-done.18.refs_3_
  48.6 2.2 %shard_map.119.refs_2_.refs_3_ = bf16[1728,256]{1,0:T(8,128)(2,1)S(1)} custom-call(bf16[32,1152]{1,0:T(8,128)(2,1)S(1)} %get-tuple-element.61.refs_0_, bf16[32,1152]{1,0:T(8,128)(2,1)S(1)} %collective-permute-done.16.refs_1_, bf16[32,1152]{1,0:T(8,128)(2,1)S(1)} %collective-permute-done.17.refs_2_, bf16[32,1152]{1,0:T(8,128)(2,1)S(1)} %collective-permute-done.18.refs_3_, ...), custom_call_target="tpu_custom_call" | custom-call | tf_op jit(solution)/shard_map/pallas_call | solution.py:535
  50.8 0.0 collective-permute-done.2.refs_1_
  50.8 0.0 collective-permute-done.3.refs_2_
  50.8 0.0 collective-permute-done.4.refs_3_
  50.8 2.5 %shard_map.112.refs_0_.refs_1_ = bf16[1728,512]{1,0:T(8,128)(2,1)S(1)} custom-call(bf16[2,64,1152]{2,1,0:T(8,128)(2,1)S(1)} %get-tuple-element.41.refs_0_.refs_4_, bf16[2,64,1152]{2,1,0:T(8,128)(2,1)S(1)} %collective-permute-done.2.refs_1_, bf16[2,64,1152]{2,1,0:T(8,128)(2,1)S(1)} %collective-permute-done.3.refs_2_, ...), custom_call_target="tpu_custom_call" | custom-call | tf_op jit(solution)/shard_map/pallas_call | solution.py:507
  53.4 1.9 %shard_map.120 = (bf16[32,2304]{1,0:T(8,128)(2,1)S(1)}, bf16[32,2304]{1,0:T(8,128)(2,1)S(1)}, bf16[32,2304]{1,0:T(8,128)(2,1)S(1)}, bf16[32,2304]{1,0:T(8,128)(2,1)S(1)}) custom-call(bf16[1728,512]{1,0:T(8,128)(2,1)S(1)} %shard_map.112.refs_0_.refs_1_, bf16[1728,512]{1,0:T(8,128)(2,1)S(1)} %shard_map.112.refs_0_.refs_1_, ...), custom_call_target="tpu_custom_call" | custom-call | tf_op jit(solution)/shard_map/pallas_call | solution.py:546
  55.2 0.7 collective-permute-start.19
  55.9 0.1 collective-permute-start.7
  56.0 1.4 %collective-permute-start.8 = (bf16[32,1152]{1,0:T(8,128)(2,1)S(1)}, bf16[32,1152]{1,0:T(8,128)(2,1)S(1)}, u32[]{:S(2)}, u32[]{:S(2)}) collective-permute-start(bf16[32,1152]{1,0:T(8,128)(2,1)S(1)} %get-tuple-element.51.refs_6_), channel_id=1, source_target_pairs={{0,8},{4,12},{8,0},{12,4},{1,9},{5,13},{9,1},{13,5},{2,10},{6,14},... | collective-permute-start | bytes 221192 | tf_op jit(solution)/shard_map/ppermute | solution.py:453
  57.4 0.4 collective-permute-start.9
  57.8 0.0 collective-permute-done.7.refs_1_
  57.8 3.0 %collective-permute-done.8.refs_2_ = bf16[32,1152]{1,0:T(8,128)(2,1)S(1)} collective-permute-done((bf16[32,1152]{1,0:T(8,128)(2,1)S(1)}, bf16[32,1152]{1,0:T(8,128)(2,1)S(1)}, u32[]{:S(2)}, u32[]{:S(2)}) %collective-permute-start.8) | collective-permute-done | bytes 73760 | tf_op jit(solution)/shard_map/ppermute | solution.py:453
  60.8 1.2 %collective-permute-done.9.refs_3_ = bf16[32,1152]{1,0:T(8,128)(2,1)S(1)} collective-permute-done((bf16[32,1152]{1,0:T(8,128)(2,1)S(1)}, bf16[32,1152]{1,0:T(8,128)(2,1)S(1)}, u32[]{:S(2)}, u32[]{:S(2)}) %collective-permute-start.9) | collective-permute-done | bytes 73760 | tf_op jit(solution)/shard_map/ppermute | solution.py:453
  62.0 2.3 %shard_map.116.refs_2_.refs_3_ = bf16[1728,256]{1,0:T(8,128)(2,1)S(1)} custom-call(bf16[32,1152]{1,0:T(8,128)(2,1)S(1)} %get-tuple-element.49.refs_0_.refs_4_, bf16[32,1152]{1,0:T(8,128)(2,1)S(1)} %collective-permute-done.7.refs_1_, bf16[32,1152]{1,0:T(8,128)(2,1)S(1)} %collective-permute-done.8.refs_2_, ...), custom_call_target="tpu_custom_call" | custom-call | tf_op jit(solution)/shard_map/pallas_call | solution.py:535
  64.3 0.0 copy-start.6
  64.3 1.9 %shard_map.117 = (bf16[32,2304]{1,0:T(8,128)(2,1)S(1)}, bf16[32,2304]{1,0:T(8,128)(2,1)S(1)}, bf16[32,2304]{1,0:T(8,128)(2,1)S(1)}, bf16[32,2304]{1,0:T(8,128)(2,1)S(1)}) custom-call(bf16[1728,512]{1,0:T(8,128)(2,1)S(1)} %shard_map.112.refs_0_.refs_1_, bf16[1728,512]{1,0:T(8,128)(2,1)S(1)} %shard_map.112.refs_0_.refs_1_, ...), custom_call_target="tpu_custom_call" | custom-call | tf_op jit(solution)/shard_map/pallas_call | solution.py:546
  66.2 1.1 %collective-permute-start.20 = (bf16[32,2304]{1,0:T(8,128)(2,1)S(1)}, bf16[32,2304]{1,0:T(8,128)(2,1)S(1)}, u32[]{:S(2)}, u32[]{:S(2)}) collective-permute-start(bf16[32,2304]{1,0:T(8,128)(2,1)S(1)} %get-tuple-element.67), channel_id=1, source_target_pairs={{8,0},{12,4},{0,8},{4,12},{9,1},{13,5},{1,9},{5,13},{10,2},{14,6},... | collective-permute-start | bytes 442376 | tf_op jit(solution)/shard_map/ppermute | solution.py:558
  67.3 0.4 collective-permute-start.21
  67.7 0.7 collective-permute-start.13
  68.4 1.1 %collective-permute-start.14 = (bf16[32,2304]{1,0:T(8,128)(2,1)S(1)}, bf16[32,2304]{1,0:T(8,128)(2,1)S(1)}, u32[]{:S(2)}, u32[]{:S(2)}) collective-permute-start(bf16[32,2304]{1,0:T(8,128)(2,1)S(1)} %get-tuple-element.59), channel_id=1, source_target_pairs={{8,0},{12,4},{0,8},{4,12},{9,1},{13,5},{1,9},{5,13},{10,2},{14,6},... | collective-permute-start | bytes 442376 | tf_op jit(solution)/shard_map/ppermute | solution.py:558
  69.5 0.0 collective-permute-done.19.refs_1_
  69.5 0.3 collective-permute-start.15
  69.8 1.5 %shard_map.118.refs_8_ = bf16[4,2,64,1152]{3,2,1,0:T(8,128)(2,1)S(1)} custom-call(bf16[32,1152]{1,0:T(8,128)(2,1)S(1)} %get-tuple-element.61.refs_0_, bf16[32,1152]{1,0:T(8,128)(2,1)S(1)} %get-tuple-element.62.refs_1_, bf16[32,1152]{1,0:T(8,128)(2,1)S(1)} %get-tuple-element.63.refs_2_, bf16[32,1152]{1,0:T(8,128)(2,1)S(1)} %get-tuple-element.64.refs_3_, ...), custom_call_target="tpu_custom_call" | custom-call | tf_op jit(solution)/shard_map/pallas_call | solution.py:563
  71.3 1.7 %collective-permute-done.20.refs_2_ = bf16[32,2304]{1,0:T(8,128)(2,1)S(1)} collective-permute-done((bf16[32,2304]{1,0:T(8,128)(2,1)S(1)}, bf16[32,2304]{1,0:T(8,128)(2,1)S(1)}, u32[]{:S(2)}, u32[]{:S(2)}) %collective-permute-start.20) | collective-permute-done | bytes 147488 | tf_op jit(solution)/shard_map/ppermute | solution.py:558
  73.0 1.8 %collective-permute-done.21.refs_3_ = bf16[32,2304]{1,0:T(8,128)(2,1)S(1)} collective-permute-done((bf16[32,2304]{1,0:T(8,128)(2,1)S(1)}, bf16[32,2304]{1,0:T(8,128)(2,1)S(1)}, u32[]{:S(2)}, u32[]{:S(2)}) %collective-permute-start.21) | collective-permute-done | bytes 147488 | tf_op jit(solution)/shard_map/ppermute | solution.py:558
  74.7 2.8 %shard_map.121.refs_11_ = bf16[4,256,1152]{2,1,0:T(8,128)(2,1)} custom-call(s32[2]{0:T(128)S(1)} %pad_add_fusion.place, bf16[32,2304]{1,0:T(8,128)(2,1)S(1)} %get-tuple-element.65.refs_0_, bf16[32,2304]{1,0:T(8,128)(2,1)S(1)} %collective-permute-done.19.refs_1_, bf16[32,2304]{1,0:T(8,128)(2,1)S(1)} %collective-permute-done.20.refs_2_, ...), custom_call_target="tpu_custom_call" | custom-call | tf_op jit(solution)/shard_map/pallas_call | solution.py:581
  77.6 0.0 collective-permute-done.13.refs_1_
  77.6 1.7 %collective-permute-done.14.refs_2_ = bf16[32,2304]{1,0:T(8,128)(2,1)S(1)} collective-permute-done((bf16[32,2304]{1,0:T(8,128)(2,1)S(1)}, bf16[32,2304]{1,0:T(8,128)(2,1)S(1)}, u32[]{:S(2)}, u32[]{:S(2)}) %collective-permute-start.14) | collective-permute-done | bytes 147488 | tf_op jit(solution)/shard_map/ppermute | solution.py:558
  79.3 1.5 %collective-permute-done.15.refs_3_ = bf16[32,2304]{1,0:T(8,128)(2,1)S(1)} collective-permute-done((bf16[32,2304]{1,0:T(8,128)(2,1)S(1)}, bf16[32,2304]{1,0:T(8,128)(2,1)S(1)}, u32[]{:S(2)}, u32[]{:S(2)}) %collective-permute-start.15) | collective-permute-done | bytes 147488 | tf_op jit(solution)/shard_map/ppermute | solution.py:558
  80.8 2.8 %shard_map.122 = bf16[4,256,1152]{2,1,0:T(8,128)(2,1)} custom-call(s32[2]{0:T(128)S(1)} %pad_add_fusion.place, bf16[32,2304]{1,0:T(8,128)(2,1)S(1)} %get-tuple-element.57.refs_0_, bf16[32,2304]{1,0:T(8,128)(2,1)S(1)} %collective-permute-done.13.refs_1_, bf16[32,2304]{1,0:T(8,128)(2,1)S(1)} %collective-permute-done.14.refs_2_, ...), custom_call_target="tpu_custom_call", output_to_operand_aliasing={{}: (12, {})} | custom-call | tf_op jit(solution)/shard_map/pallas_call | solution.py:581
  (11 shorter events, 0.0 us)
Async XLA Ops:
  2.6 19.3 %copy-start.5 = (f32[1152]{0:T(1024)S(1)}, f32[1152]{0:T(1024)}, u32[]{:S(2)}) copy-start(f32[1152]{0:T(1024)} %param.16) | copy-start | bytes 13828
  2.6 19.3 %copy-start.3 = (s32[4,2,3]{0,1,2:T(2,128)S(1)}, s32[4,2,3]{0,1,2:T(2,128)}, u32[]{:S(2)}) copy-start(s32[4,2,3]{0,1,2:T(2,128)} %param.20) | copy-start | bytes 292
  2.6 19.3 %copy-start.4 = (s32[4,2]{0,1:T(2,128)S(1)}, s32[4,2]{0,1:T(2,128)}, u32[]{:S(2)}) copy-start(s32[4,2]{0,1:T(2,128)} %param.21) | copy-start | bytes 100
  2.6 17.3 %collective-permute-start = (bf16[2,1152,128]{2,1,0:T(8,128)(2,1)S(1)}, bf16[2,1152,128]{2,1,0:T(8,128)(2,1)S(1)}, u32[]{:S(2)}, u32[]{:S(2)}) collective-permute-start(bf16[2,1152,128]{2,1,0:T(8,128)(2,1)S(1)} %get-tuple-element.37.a_ref), channel_id=1, source_target_pairs={{0,1},{1,0},{2,3},{3,2},{4,5},{5,4},{6,7},{7,6},{8,9},{9,8},{10,11... | collective-permute-start | bytes 1769480 | tf_op jit(solution)/shard_map/ppermute | solution.py:471
  5.8 16.1 %collective-permute-start.1 = (bf16[2,1152,128]{2,1,0:T(8,128)(2,1)S(1)}, bf16[2,1152,128]{2,1,0:T(8,128)(2,1)S(1)}, u32[]{:S(2)}, u32[]{:S(2)}) collective-permute-start(bf16[2,1152,128]{2,1,0:T(8,128)(2,1)S(1)} %get-tuple-element.38.b_ref), channel_id=1, source_target_pairs={{1,2},{2,1},{5,6},{6,5},{9,10},{10,9},{13,14},{14,13},{17,18},{18,... | collective-permute-start | bytes 1769480 | tf_op jit(solution)/shard_map/ppermute | solution.py:471
  8.0 16.4 %copy-start.1 = (bf16[576,1152]{1,0:T(8,128)(2,1)S(1)}, bf16[576,1152]{1,0:T(8,128)(2,1)}, u32[]{:S(2)}) copy-start(bf16[576,1152]{1,0:T(8,128)(2,1)} %refs_8_.3) | copy-start | bytes 3981316
  8.0 23.8 %collective-permute-start.5 = (bf16[2,1152,128]{2,1,0:T(8,128)(2,1)S(1)}, bf16[2,1152,128]{2,1,0:T(8,128)(2,1)S(1)}, u32[]{:S(2)}, u32[]{:S(2)}) collective-permute-start(bf16[2,1152,128]{2,1,0:T(8,128)(2,1)S(1)} %get-tuple-element.45.a_ref), channel_id=1, source_target_pairs={{0,1},{1,0},{2,3},{3,2},{4,5},{5,4},{6,7},{7,6},{8,9},{9,8},{10,11... | collective-permute-start | bytes 1769480 | tf_op jit(solution)/shard_map/ppermute | solution.py:471
  12.4 21.0 %collective-permute-start.6 = (bf16[2,1152,128]{2,1,0:T(8,128)(2,1)S(1)}, bf16[2,1152,128]{2,1,0:T(8,128)(2,1)S(1)}, u32[]{:S(2)}, u32[]{:S(2)}) collective-permute-start(bf16[2,1152,128]{2,1,0:T(8,128)(2,1)S(1)} %get-tuple-element.46.b_ref), channel_id=1, source_target_pairs={{1,2},{2,1},{5,6},{6,5},{9,10},{10,9},{13,14},{14,13},{17,18},{18,... | collective-permute-start | bytes 1769480 | tf_op jit(solution)/shard_map/ppermute | solution.py:471
  13.1 14.9 %collective-permute-start.10 = (bf16[2,64,1152]{2,1,0:T(8,128)(2,1)S(1)}, bf16[2,64,1152]{2,1,0:T(8,128)(2,1)S(1)}, u32[]{:S(2)}, u32[]{:S(2)}) collective-permute-start(bf16[2,64,1152]{2,1,0:T(8,128)(2,1)S(1)} %get-tuple-element.54.refs_9_), channel_id=1, source_target_pairs={{0,4},{4,0},{8,12},{12,8},{1,5},{5,1},{9,13},{13,9},{2,6},{6,2},{1... | collective-permute-start | bytes 884744 | tf_op jit(solution)/shard_map/ppermute | solution.py:453
  19.9 18.3 %collective-permute-start.11 = (bf16[2,64,1152]{2,1,0:T(8,128)(2,1)S(1)}, bf16[2,64,1152]{2,1,0:T(8,128)(2,1)S(1)}, u32[]{:S(2)}, u32[]{:S(2)}) collective-permute-start(bf16[2,64,1152]{2,1,0:T(8,128)(2,1)S(1)} %get-tuple-element.55.refs_10_), channel_id=1, source_target_pairs={{0,8},{4,12},{8,0},{12,4},{1,9},{5,13},{9,1},{13,5},{2,10},{6,14},... | collective-permute-start | bytes 884744 | tf_op jit(solution)/shard_map/ppermute | solution.py:453
  21.9 16.8 %collective-permute-start.12 = (bf16[2,64,1152]{2,1,0:T(8,128)(2,1)S(1)}, bf16[2,64,1152]{2,1,0:T(8,128)(2,1)S(1)}, u32[]{:S(2)}, u32[]{:S(2)}) collective-permute-start(bf16[2,64,1152]{2,1,0:T(8,128)(2,1)S(1)} %get-tuple-element.56.refs_11_), channel_id=1, source_target_pairs={{0,12},{4,8},{8,4},{12,0},{1,13},{5,9},{9,5},{13,1},{2,14},{6,10},... | collective-permute-start | bytes 884744 | tf_op jit(solution)/shard_map/ppermute | solution.py:453
  28.0 22.8 %collective-permute-start.2 = (bf16[2,64,1152]{2,1,0:T(8,128)(2,1)S(1)}, bf16[2,64,1152]{2,1,0:T(8,128)(2,1)S(1)}, u32[]{:S(2)}, u32[]{:S(2)}) collective-permute-start(bf16[2,64,1152]{2,1,0:T(8,128)(2,1)S(1)} %get-tuple-element.42.refs_5_), channel_id=1, source_target_pairs={{0,4},{4,0},{8,12},{12,8},{1,5},{5,1},{9,13},{13,9},{2,6},{6,2},{1... | collective-permute-start | bytes 884744 | tf_op jit(solution)/shard_map/ppermute | solution.py:453
  31.7 19.1 %collective-permute-start.3 = (bf16[2,64,1152]{2,1,0:T(8,128)(2,1)S(1)}, bf16[2,64,1152]{2,1,0:T(8,128)(2,1)S(1)}, u32[]{:S(2)}, u32[]{:S(2)}) collective-permute-start(bf16[2,64,1152]{2,1,0:T(8,128)(2,1)S(1)} %get-tuple-element.43.refs_6_), channel_id=1, source_target_pairs={{0,8},{4,12},{8,0},{12,4},{1,9},{5,13},{9,1},{13,5},{2,10},{6,14},... | collective-permute-start | bytes 884744 | tf_op jit(solution)/shard_map/ppermute | solution.py:453
  33.4 17.4 %collective-permute-start.4 = (bf16[2,64,1152]{2,1,0:T(8,128)(2,1)S(1)}, bf16[2,64,1152]{2,1,0:T(8,128)(2,1)S(1)}, u32[]{:S(2)}, u32[]{:S(2)}) collective-permute-start(bf16[2,64,1152]{2,1,0:T(8,128)(2,1)S(1)} %get-tuple-element.44.refs_7_), channel_id=1, source_target_pairs={{0,12},{4,8},{8,4},{12,0},{1,13},{5,9},{9,5},{13,1},{2,14},{6,10},... | collective-permute-start | bytes 884744 | tf_op jit(solution)/shard_map/ppermute | solution.py:453
  33.4 15.2 %copy-start = (bf16[1152,1728]{0,1:T(8,128)(2,1)S(1)}, bf16[1152,1728]{0,1:T(8,128)(2,1)}, u32[]{:S(2)}) copy-start(bf16[1152,1728]{0,1:T(8,128)(2,1)} %param.17) | copy-start | bytes 11943940
  38.2 2.2 %collective-permute-start.16 = (bf16[32,1152]{1,0:T(8,128)(2,1)S(1)}, bf16[32,1152]{1,0:T(8,128)(2,1)S(1)}, u32[]{:S(2)}, u32[]{:S(2)}) collective-permute-start(bf16[32,1152]{1,0:T(8,128)(2,1)S(1)} %get-tuple-element.62.refs_1_), channel_id=1, source_target_pairs={{0,4},{4,0},{8,12},{12,8},{1,5},{5,1},{9,13},{13,9},{2,6},{6,2},{1... | collective-permute-start | bytes 221192 | tf_op jit(solution)/shard_map/ppermute | solution.py:453
  38.7 9.9 %collective-permute-start.17 = (bf16[32,1152]{1,0:T(8,128)(2,1)S(1)}, bf16[32,1152]{1,0:T(8,128)(2,1)S(1)}, u32[]{:S(2)}, u32[]{:S(2)}) collective-permute-start(bf16[32,1152]{1,0:T(8,128)(2,1)S(1)} %get-tuple-element.63.refs_2_), channel_id=1, source_target_pairs={{0,8},{4,12},{8,0},{12,4},{1,9},{5,13},{9,1},{13,5},{2,10},{6,14},... | collective-permute-start | bytes 221192 | tf_op jit(solution)/shard_map/ppermute | solution.py:453
  40.4 8.2 %collective-permute-start.18 = (bf16[32,1152]{1,0:T(8,128)(2,1)S(1)}, bf16[32,1152]{1,0:T(8,128)(2,1)S(1)}, u32[]{:S(2)}, u32[]{:S(2)}) collective-permute-start(bf16[32,1152]{1,0:T(8,128)(2,1)S(1)} %get-tuple-element.64.refs_3_), channel_id=1, source_target_pairs={{0,12},{4,8},{8,4},{12,0},{1,13},{5,9},{9,5},{13,1},{2,14},{6,10},... | collective-permute-start | bytes 221192 | tf_op jit(solution)/shard_map/ppermute | solution.py:453
  55.2 14.2 %collective-permute-start.19 = (bf16[32,2304]{1,0:T(8,128)(2,1)S(1)}, bf16[32,2304]{1,0:T(8,128)(2,1)S(1)}, u32[]{:S(2)}, u32[]{:S(2)}) collective-permute-start(bf16[32,2304]{1,0:T(8,128)(2,1)S(1)} %get-tuple-element.66), channel_id=1, source_target_pairs={{4,0},{0,4},{12,8},{8,12},{5,1},{1,5},{13,9},{9,13},{6,2},{2,6},{1... | collective-permute-start | bytes 442376 | tf_op jit(solution)/shard_map/ppermute | solution.py:558
  55.9 1.9 %collective-permute-start.7 = (bf16[32,1152]{1,0:T(8,128)(2,1)S(1)}, bf16[32,1152]{1,0:T(8,128)(2,1)S(1)}, u32[]{:S(2)}, u32[]{:S(2)}) collective-permute-start(bf16[32,1152]{1,0:T(8,128)(2,1)S(1)} %get-tuple-element.50.refs_5_), channel_id=1, source_target_pairs={{0,4},{4,0},{8,12},{12,8},{1,5},{5,1},{9,13},{13,9},{2,6},{6,2},{1... | collective-permute-start | bytes 221192 | tf_op jit(solution)/shard_map/ppermute | solution.py:453
  56.0 4.8 %collective-permute-start.8 = (bf16[32,1152]{1,0:T(8,128)(2,1)S(1)}, bf16[32,1152]{1,0:T(8,128)(2,1)S(1)}, u32[]{:S(2)}, u32[]{:S(2)}) collective-permute-start(bf16[32,1152]{1,0:T(8,128)(2,1)S(1)} %get-tuple-element.51.refs_6_), channel_id=1, source_target_pairs={{0,8},{4,12},{8,0},{12,4},{1,9},{5,13},{9,1},{13,5},{2,10},{6,14},... | collective-permute-start | bytes 221192 | tf_op jit(solution)/shard_map/ppermute | solution.py:453
  57.4 4.6 %collective-permute-start.9 = (bf16[32,1152]{1,0:T(8,128)(2,1)S(1)}, bf16[32,1152]{1,0:T(8,128)(2,1)S(1)}, u32[]{:S(2)}, u32[]{:S(2)}) collective-permute-start(bf16[32,1152]{1,0:T(8,128)(2,1)S(1)} %get-tuple-element.52.refs_7_), channel_id=1, source_target_pairs={{0,12},{4,8},{8,4},{12,0},{1,13},{5,9},{9,5},{13,1},{2,14},{6,10},... | collective-permute-start | bytes 221192 | tf_op jit(solution)/shard_map/ppermute | solution.py:453
  64.3 5.5 %copy-start.6 = (f32[1152]{0:T(1024)S(1)}, f32[1152]{0:T(1024)}, u32[]{:S(2)}) copy-start(f32[1152]{0:T(1024)} %param.19) | copy-start | bytes 13828
  66.2 6.8 %collective-permute-start.20 = (bf16[32,2304]{1,0:T(8,128)(2,1)S(1)}, bf16[32,2304]{1,0:T(8,128)(2,1)S(1)}, u32[]{:S(2)}, u32[]{:S(2)}) collective-permute-start(bf16[32,2304]{1,0:T(8,128)(2,1)S(1)} %get-tuple-element.67), channel_id=1, source_target_pairs={{8,0},{12,4},{0,8},{4,12},{9,1},{13,5},{1,9},{5,13},{10,2},{14,6},... | collective-permute-start | bytes 442376 | tf_op jit(solution)/shard_map/ppermute | solution.py:558
  67.3 7.4 %collective-permute-start.21 = (bf16[32,2304]{1,0:T(8,128)(2,1)S(1)}, bf16[32,2304]{1,0:T(8,128)(2,1)S(1)}, u32[]{:S(2)}, u32[]{:S(2)}) collective-permute-start(bf16[32,2304]{1,0:T(8,128)(2,1)S(1)} %get-tuple-element.68), channel_id=1, source_target_pairs={{12,0},{8,4},{4,8},{0,12},{13,1},{9,5},{5,9},{1,13},{14,2},{10,6},... | collective-permute-start | bytes 442376 | tf_op jit(solution)/shard_map/ppermute | solution.py:558
  67.7 9.8 %collective-permute-start.13 = (bf16[32,2304]{1,0:T(8,128)(2,1)S(1)}, bf16[32,2304]{1,0:T(8,128)(2,1)S(1)}, u32[]{:S(2)}, u32[]{:S(2)}) collective-permute-start(bf16[32,2304]{1,0:T(8,128)(2,1)S(1)} %get-tuple-element.58), channel_id=1, source_target_pairs={{4,0},{0,4},{12,8},{8,12},{5,1},{1,5},{13,9},{9,13},{6,2},{2,6},{1... | collective-permute-start | bytes 442376 | tf_op jit(solution)/shard_map/ppermute | solution.py:558
  68.4 10.9 %collective-permute-start.14 = (bf16[32,2304]{1,0:T(8,128)(2,1)S(1)}, bf16[32,2304]{1,0:T(8,128)(2,1)S(1)}, u32[]{:S(2)}, u32[]{:S(2)}) collective-permute-start(bf16[32,2304]{1,0:T(8,128)(2,1)S(1)} %get-tuple-element.59), channel_id=1, source_target_pairs={{8,0},{12,4},{0,8},{4,12},{9,1},{13,5},{1,9},{5,13},{10,2},{14,6},... | collective-permute-start | bytes 442376 | tf_op jit(solution)/shard_map/ppermute | solution.py:558
  69.5 11.3 %collective-permute-start.15 = (bf16[32,2304]{1,0:T(8,128)(2,1)S(1)}, bf16[32,2304]{1,0:T(8,128)(2,1)S(1)}, u32[]{:S(2)}, u32[]{:S(2)}) collective-permute-start(bf16[32,2304]{1,0:T(8,128)(2,1)S(1)} %get-tuple-element.60), channel_id=1, source_target_pairs={{12,0},{8,4},{4,8},{0,12},{13,1},{9,5},{5,9},{1,13},{14,2},{10,6},... | collective-permute-start | bytes 442376 | tf_op jit(solution)/shard_map/ppermute | solution.py:558
  69.8 5.0 %copy-start.2 = (bf16[576,1152]{1,0:T(8,128)(2,1)S(1)}, bf16[576,1152]{1,0:T(8,128)(2,1)}, u32[]{:S(2)}) copy-start(bf16[576,1152]{1,0:T(8,128)(2,1)} %refs_9_.3) | copy-start | bytes 3981316

commit v5 on v4

--- a/solution.py
+++ b/solution.py
@@ -185,11 +185,11 @@
         finish(proj * scale)
 
 
-def spatial_kernel(n_groups, place, counts, lists, qn_ref, sum_ref, ra_ref, rb_ref, h_ref, w_ref, g_ref, *rest):
+def spatial_kernel(frame, n_groups, place, counts, lists, qn_ref, sum_ref, ra_ref, rb_ref, h_ref, w_ref, g_ref, *rest):
     outs, (att, hid, mix, sem) = rest[:n_groups], rest[n_groups:]
-    copy = pltpu.make_async_copy(h_ref.at[pl.ds(0, hid.shape[0])], hid, sem)
+    copy = pltpu.make_async_copy(h_ref.at[pl.ds(frame, hid.shape[0])], hid, sem)
     copy.start()
-    remote_attend(0, place, counts, lists, qn_ref, sum_ref, ra_ref, rb_ref, att)
+    remote_attend(frame, place, counts, lists, qn_ref, sum_ref, ra_ref, rb_ref, att)
     copy.wait()
     n, tokens, _ = hid.shape
 
@@ -263,7 +263,7 @@
     return c ^ (frame & 1) if paired(chunks, n_groups * SUB, frames) else c
 
 
-def project(w_ref, x, out, base=0):
+def project(w_ref, x, out):
     width = w_ref.shape[0] // 3
     cut = w_ref.shape[0] // 2
     heads = width // HEAD_DIM
@@ -273,20 +273,18 @@
         y = parts[i][at:at + HEAD_DIM, :]
         if h < 2 * heads:
             y = y * head_scale(y)
-        out[head(h), base:base + x.shape[0]] = y.astype(BF)
-
-
-def project_kernel(frames, *refs):
+        out[head(h), :] = y.astype(BF)
+
+
+def project_kernel(frame, frames, *refs):
     pieces, w_ref, out, x = refs[:-3], refs[-3], refs[-2], refs[-1]
     n_groups = len(pieces)
-    n, share, _ = pieces[0].shape
-    chunks = share // SUB
-    for f in range(n):
-        for c in range(chunks):
-            for j, piece in enumerate(pieces):
-                at = (slot(c, f, chunks, n_groups, frames) * n_groups + j) * SUB
-                x[f, at:at + SUB, :] = piece[f, c * SUB:(c + 1) * SUB, :]
-        project(w_ref, x[f], out, f * x.shape[1])
+    chunks = pieces[0].shape[1] // SUB
+    for c in range(chunks):
+        for j, piece in enumerate(pieces):
+            at = (slot(c, frame, chunks, n_groups, frames) * n_groups + j) * SUB
+            x[at:at + SUB, :] = piece[0, c * SUB:(c + 1) * SUB, :]
+    project(w_ref, x[...], out)
 
 
 def late_project_kernel(frame, frames, *refs):
@@ -358,9 +356,9 @@
 
 def output_kernel(n_groups, js, early, half, halves, aliased, place, *refs):
     n = len(js)
-    atts, pieces = refs[:n], refs[n:2 * n]
-    late_ref, w_ref, g_ref = refs[2 * n:2 * n + 3]
-    out, buf, sems = refs[2 * n + 3 + aliased:]
+    atts, pieces = refs[:n], refs[n:n * (1 + early)]
+    late_ref, w_ref, g_ref = refs[n * (1 + early):n * (1 + early) + 3]
+    out, buf, sems = refs[n * (1 + early) + 3 + aliased:]
     _, late, rows, _ = late_ref.shape
     width = w_ref.shape[0]
     frames = early + late
@@ -375,7 +373,7 @@
             for k, i in enumerate(some):
                 j = js[i]
                 for f in range(frames):
-                    mine = pieces[i][f] if f < early else late_ref[j, f - early]
+                    mine = pieces[i * early + f][0] if f < early else late_ref[j, f - early]
                     at = (k * frames + f) * rows
                     part = normed[at:at + rows, :] * g_ref[...]
                     buf[i, f] = (mine.astype(F32) + part).astype(BF)
@@ -456,7 +454,7 @@
     halos = []
     for some in range(2):
         block = pl.BlockSpec((late, width, tokens), lambda *_, some=some: (some, 0, 0))
-        split = groups if some == 0 else 0
+        split = groups if some == 1 else 0
         a, b, *pieces = call(
             prep_kernel,
             [smem, block, block] + [any_spec] * bool(split),
@@ -488,29 +486,37 @@
         )
     sum_specs = [whole((late, width, tokens)), whole(sum_shape)]
 
-    mixed = call(
-        functools.partial(spatial_kernel, groups),
-        [smem, smem, smem]
-        + sum_specs
-        + [whole((late,) + edge.shape)] * 2
-        + [any_spec, whole((width, model)), whole((1, model))],
-        [whole((early, share, model))] * groups,
-        [jax.ShapeDtypeStruct((early, share, model), BF)] * groups,
-        [
-            pltpu.VMEM((early, width, tokens), BF),
-            pltpu.VMEM((early, tokens, model), BF),
-            pltpu.VMEM((early, tokens, model), BF),
-            pltpu.SemaphoreType.DMA,
-        ],
-    )(place, counts, lists, *own_sums[0], *halos[0][2:], hidden_far, spatial_out_weight, gain_one)
-    arrived = send(mixed)
-    projected = call(
-        functools.partial(project_kernel, frames),
-        [whole((early, share, model))] * groups + [whole((3 * width, model))],
-        whole((3 * width, early * tokens)),
-        jax.ShapeDtypeStruct((3 * width, early * tokens), BF),
-        [pltpu.VMEM((early, tokens, model), BF)],
-    )(*arrived, qkv_weight)
+    def one(shape, f):
+        return pl.BlockSpec((1,) + shape[1:], lambda *_: (f, 0, 0))
+
+    mixed, projected = [], []
+    for f in range(early):
+        mixed.append(
+            call(
+                functools.partial(spatial_kernel, f, groups),
+                [smem, smem, smem, one((late, width, tokens), f), one(sum_shape, f)]
+                + [one((late,) + edge.shape, f)] * 2
+                + [any_spec, whole((width, model)), whole((1, model))],
+                [whole((1, share, model))] * groups,
+                [jax.ShapeDtypeStruct((1, share, model), BF)] * groups,
+                [
+                    pltpu.VMEM((1, width, tokens), BF),
+                    pltpu.VMEM((1, tokens, model), BF),
+                    pltpu.VMEM((1, tokens, model), BF),
+                    pltpu.SemaphoreType.DMA,
+                ],
+            )(place, counts, lists, *own_sums[0], *halos[0][2:], hidden_far, spatial_out_weight, gain_one)
+        )
+        arrived = send(mixed[f])
+        projected.append(
+            call(
+                functools.partial(project_kernel, f, frames),
+                [whole((1, share, model))] * groups + [whole((3 * width, model))],
+                whole((3 * width, tokens)),
+                jax.ShapeDtypeStruct((3 * width, tokens), BF),
+                [pltpu.VMEM((tokens, model), BF)],
+            )(*arrived, qkv_weight)
+        )
 
     late_shape = (rows, late * width)
     own_late = call(
@@ -545,15 +551,12 @@
         )(*far_late[half], *far_hidden, spatial_out_weight, gain_one, qkv_weight)
         back = call(
             functools.partial(temporal_kernel, groups),
-            [
-                pl.BlockSpec((3 * width, lanes), lambda *_, at=f * halves + half: (0, at))
-                for f in range(early)
-            ]
+            [pl.BlockSpec((3 * width, lanes), lambda *_, half=half: (0, half))] * early
             + [pl.BlockSpec((3 * width, lanes), lambda *_, f=f: (0, f)) for f in range(late)],
             [whole(back_shape)] * groups,
             [jax.ShapeDtypeStruct(back_shape, BF)] * groups,
             [pltpu.VMEM((rows // SUB, width, groups * frames * SUB), F32)],
-        )(*[projected] * early, *[late_projected] * late)
+        )(*projected, *[late_projected] * late)
         home = {
             j: lax.ppermute(back[j], "frame", [(b, a) for a, b in out_pairs(j)])
             for j in reversed(range(1, groups))
@@ -571,8 +574,8 @@
 
     out = None
     for half in range(halves):
-        piece = pl.BlockSpec((early, rows, model), lambda *_, half=half: (0, half, 0))
-        cuts = [groups]
+        piece = pl.BlockSpec((1, rows, model), lambda *_, half=half: (0, half, 0))
+        cuts = [groups] if half + 1 < halves else [groups // 2, groups]
         for lo, hi in zip([0] + cuts, cuts):
             js = range(lo, hi)
             if not js:
@@ -582,7 +585,7 @@
                 functools.partial(output_kernel, groups, tuple(js), early, half, halves, len(extra)),
                 [smem]
                 + [whole(back_shape)] * len(js)
-                + [piece] * len(js)
+                + [piece] * (len(js) * early)
                 + [pl.BlockSpec((groups, late, rows, model), lambda *_, half=half: (0, 0, half, 0))]
                 + [whole((width, model)), whole((1, model))]
                 + [any_spec] * len(extra),
@@ -592,11 +595,11 @@
                     pltpu.VMEM((len(js), frames, rows, model), BF),
                     pltpu.SemaphoreType.DMA((len(js),)),
                 ],
-                alias={4 + 2 * len(js): 0} if extra else None,
+                alias={4 + len(js) * (1 + early): 0} if extra else None,
             )(
                 place,
                 *[returned[half][j] for j in js],
-                *[mixed[j] for j in js],
+                *[mixed[f][j] for j in js for f in range(early)],
                 late_mixed,
                 temporal_out_weight,
                 gain_two,

time: 84.2 us -> 86.3 us (1.025)
  Pallas kernels: 32.8 us -> 37.5 us
  waiting for transfers between devices: 28.4 us -> 24.4 us
  starting transfers between devices: 22 us -> 23.3 us
    ppermute x6, waiting for transfers between devices: 6.59 us -> 2.31 us  [shards(): lax.ppermute(back[j], 'frame', [(b, a) for a, b in out_pairs(j)])]
    pallas_call x2 -> x4, Pallas kernels: 6.18 us -> 9.46 us  [the longest x2 6.73 us: shards(): call(functools.partial(spatial_kernel, f, groups), [smem, smem, smem, one...]
    pallas_call x2 -> x3, Pallas kernels: 5.65 us -> 7.28 us  [shards(): call(functools.partial(output_kernel, groups, tuple(js), early, half, hal...]
    ppermute x12 -> x15, starting transfers between devices: 8.87 us -> 10.2 us  [send(): lax.ppermute(parts[j], 'frame', out_pairs(j))]
    ppermute x12 -> x15, waiting for transfers between devices: 11.5 us -> 12.5 us  [send(): lax.ppermute(parts[j], 'frame', out_pairs(j))]
  transfers between devices with their start and end apart: 22 -> 25, of which waited for: 9 -> 10; matrix products, arithmetic and copies ran while one was open for 0% -> 0% of each run, Pallas kernels for 28% -> 35%
where the time goes in v5:
time: 86.3 us; the launch traced here: 85.8 us
  Pallas kernels  37.5 us (43%)
  waiting for transfers between devices  24.4 us (28%)
  starting transfers between devices  23.3 us (27%)
    ppermute x15, waiting for transfers between devices, send(): lax.ppermute(parts[j], 'frame', out_pairs(j))  12.5 us
    ppermute x15, starting transfers between devices, send(): lax.ppermute(parts[j], 'frame', out_pairs(j))  10.2 us
    ppermute x2, waiting for transfers between devices, shards(): lax.ppermute(a, 'strip', near)  9.6 us
    ppermute x2, starting transfers between devices, shards(): lax.ppermute(a, 'strip', near)  7.55 us
    pallas_call x3, Pallas kernels, shards(): call(functools.partial(output_kernel, groups, tuple(js), early, half, hal...  7.28 us
    pallas_call x2, Pallas kernels, shards(): call(functools.partial(spatial_kernel, f, groups), [smem, smem, smem, one...  6.73 us
    pallas_call x2, Pallas kernels, shards(): call(functools.partial(local_kernel, some * late), [smem, smem, smem, blo...  4.78 us
    pallas_call x2, Pallas kernels, shards(): call(functools.partial(late_project_kernel, early, frames), late_specs +...  4.34 us
  transfers between devices with their start and end apart: 25, of which 10 were waited for; matrix products, arithmetic and copies ran while one was open for 0% of the time, Pallas kernels for 35%

profile of v5, /device:TPU:0, one launch (start us, length us, event | category | flops | bytes accessed | tf_op | source)
XLA Modules:
  0.0 85.8 jit_solution(10206526614616335213)
XLA Ops:
  0.0 0.1 pad_add_fusion.place
  0.1 1.5 %shard_map.109 = (bf16[2,1152,128]{2,1,0:T(8,128)(2,1)S(1)}, bf16[2,1152,128]{2,1,0:T(8,128)(2,1)S(1)}) custom-call(s32[2]{0:T(128)S(1)} %pad_add_fusion.place, bf16[4,576,256]{2,1,0:T(8,128)(2,1)} %bitcast.22, bf16[4,576,256]{2,1,0:T(8,128)(2,1)} %bitcast.24), custom_call_target="tpu_custom_call" | custom-call | tf_op jit(solution)/shard_map/pallas_call | solution.py:458
  1.6 3.1 %collective-permute-start = (bf16[2,1152,128]{2,1,0:T(8,128)(2,1)S(1)}, bf16[2,1152,128]{2,1,0:T(8,128)(2,1)S(1)}, u32[]{:S(2)}, u32[]{:S(2)}) collective-permute-start(bf16[2,1152,128]{2,1,0:T(8,128)(2,1)S(1)} %get-tuple-element.41.a_ref), channel_id=1, source_target_pairs={{0,1},{1,0},{2,3},{3,2},{4,5},{5,4},{6,7},{7,6},{8,9},{9,8},{10,11... | collective-permute-start | bytes 1769480 | tf_op jit(solution)/shard_map/ppermute | solution.py:469
  4.7 0.8 collective-permute-start.1
  5.5 2.5 %shard_map.115 = (bf16[2,1152,128]{2,1,0:T(8,128)(2,1)S(1)}, bf16[2,1152,128]{2,1,0:T(8,128)(2,1)S(1)}, bf16[2,64,1152]{2,1,0:T(8,128)(2,1)S(1)}, bf16[2,64,1152...) custom-call(s32[2]{0:T(128)S(1)} %pad_add_fusion.place, ...), custom_call_target="tpu_custom_call" | custom-call | tf_op jit(solution)/shard_map/pallas_call | solution.py:458
  8.1 0.0 copy-start.1
  8.1 4.4 %collective-permute-start.8 = (bf16[2,1152,128]{2,1,0:T(8,128)(2,1)S(1)}, bf16[2,1152,128]{2,1,0:T(8,128)(2,1)S(1)}, u32[]{:S(2)}, u32[]{:S(2)}) collective-permute-start(bf16[2,1152,128]{2,1,0:T(8,128)(2,1)S(1)} %get-tuple-element.53.a_ref), channel_id=1, source_target_pairs={{0,1},{1,0},{2,3},{3,2},{4,5},{5,4},{6,7},{7,6},{8,9},{9,8},{10,11... | collective-permute-start | bytes 1769480 | tf_op jit(solution)/shard_map/ppermute | solution.py:469
  12.5 0.7 collective-permute-start.9
  13.2 0.1 collective-permute-start.13
  13.3 5.6 %collective-permute-done.ra_ref = bf16[2,1152,128]{2,1,0:T(8,128)(2,1)S(1)} collective-permute-done((bf16[2,1152,128]{2,1,0:T(8,128)(2,1)S(1)}, bf16[2,1152,128]{2,1,0:T(8,128)(2,1)S(1)}, u32[]{:S(2)}, u32[]{:S(2)}) %collective-permute-start) | collective-permute-done | bytes 589856 | tf_op jit(solution)/shard_map/ppermute | solution.py:469
  18.9 2.0 %collective-permute-start.14 = (bf16[2,64,1152]{2,1,0:T(8,128)(2,1)S(1)}, bf16[2,64,1152]{2,1,0:T(8,128)(2,1)S(1)}, u32[]{:S(2)}, u32[]{:S(2)}) collective-permute-start(bf16[2,64,1152]{2,1,0:T(8,128)(2,1)S(1)} %get-tuple-element.63.refs_10_), channel_id=1, source_target_pairs={{0,8},{4,12},{8,0},{12,4},{1,9},{5,13},{9,1},{13,5},{2,10},{6,14},... | collective-permute-start | bytes 884744 | tf_op jit(solution)/shard_map/ppermute | solution.py:451
  20.8 0.0 collective-permute-done.1.rb_ref
  20.8 0.0 collective-permute-start.15
  20.9 2.4 %shard_map.110 = (bf16[2,576,256]{2,1,0:T(8,128)(2,1)S(1)}, f32[2,640,256]{2,1,0:T(8,128)S(1)}) custom-call(s32[2]{0:T(128)S(1)} %pad_add_fusion.place, s32[2,4]{1,0:T(2,128)S(1)} %bitcast.17, s32[3,2,4]{2,1,0:T(2,128)S(1)} %bitcast.12, bf16[4,576,256]{2,1,0:T(8,128)(2,1)} %bitcast.26, bf16[2,1152,128]{2,1,0:T(8,128)(2,1)S(1)} %get-tuple-element.41.a_ref, ...), custom_call_target="tpu_custom_call" | custom-call | tf_op jit(solution)/shard_map/pallas_call | solution.py:477
  23.3 3.4 %shard_map.111 = (bf16[1,64,1152]{2,1,0:T(8,128)(2,1)S(1)}, bf16[1,64,1152]{2,1,0:T(8,128)(2,1)S(1)}, bf16[1,64,1152]{2,1,0:T(8,128)(2,1)S(1)}, bf16[1,64,1152]{2,1,0:T(8,128)(2,1)S(1)}) custom-call(s32[2]{0:T(128)S(1)} %pad_add_fusion.place, s32[2,4]{1,0:T(2,128)S(1)} %bitcast.18, s32[3,2,4]{2,1,0:T(2,128)S(1)} %bitcast.13, ...), custom_call_target="tpu_custom_call" | custom-call | tf_op jit(solution)/shard_map/pallas_call | solution.py:495
  26.7 4.0 %collective-permute-done.8.ra_ref = bf16[2,1152,128]{2,1,0:T(8,128)(2,1)S(1)} collective-permute-done((bf16[2,1152,128]{2,1,0:T(8,128)(2,1)S(1)}, bf16[2,1152,128]{2,1,0:T(8,128)(2,1)S(1)}, u32[]{:S(2)}, u32[]{:S(2)}) %collective-permute-start.8) | collective-permute-done | bytes 589856 | tf_op jit(solution)/shard_map/ppermute | solution.py:469
  30.7 0.0 collective-permute-start.2
  30.7 2.4 %shard_map.116 = (bf16[2,576,256]{2,1,0:T(8,128)(2,1)S(1)}, f32[2,640,256]{2,1,0:T(8,128)S(1)}) custom-call(s32[2]{0:T(128)S(1)} %pad_add_fusion.place, s32[2,4]{1,0:T(2,128)S(1)} %bitcast.19, s32[3,2,4]{2,1,0:T(2,128)S(1)} %bitcast.14, bf16[4,576,256]{2,1,0:T(8,128)(2,1)} %bitcast.27, bf16[2,1152,128]{2,1,0:T(8,128)(2,1)S(1)} %get-tuple-element.53.a_ref, ...), custom_call_target="tpu_custom_call" | custom-call | tf_op jit(solution)/shard_map/pallas_call | solution.py:477
  33.1 2.2 %shard_map.117 = (bf16[32,1152]{1,0:T(8,128)(2,1)S(1)}, bf16[32,1152]{1,0:T(8,128)(2,1)S(1)}, bf16[32,1152]{1,0:T(8,128)(2,1)S(1)}, bf16[32,1152]{1,0:T(8,128)(2...) custom-call(s32[2]{0:T(128)S(1)} %pad_add_fusion.place, ...), custom_call_target="tpu_custom_call" | custom-call | tf_op jit(solution)/shard_map/pallas_call | solution.py:522
  35.3 0.6 collective-permute-start.19
  35.9 0.0 collective-permute-done.13.refs_5_
  35.9 1.7 %collective-permute-start.20 = (bf16[32,1152]{1,0:T(8,128)(2,1)S(1)}, bf16[32,1152]{1,0:T(8,128)(2,1)S(1)}, u32[]{:S(2)}, u32[]{:S(2)}) collective-permute-start(bf16[32,1152]{1,0:T(8,128)(2,1)S(1)} %get-tuple-element.69.refs_2_), channel_id=1, source_target_pairs={{0,8},{4,12},{8,0},{12,4},{1,9},{5,13},{9,1},{13,5},{2,10},{6,14},... | collective-permute-start | bytes 221192 | tf_op jit(solution)/shard_map/ppermute | solution.py:451
  37.6 0.0 collective-permute-done.14.refs_6_
  37.6 0.0 collective-permute-start.21
  37.6 3.4 %shard_map.113 = (bf16[1,64,1152]{2,1,0:T(8,128)(2,1)S(1)}, bf16[1,64,1152]{2,1,0:T(8,128)(2,1)S(1)}, bf16[1,64,1152]{2,1,0:T(8,128)(2,1)S(1)}, bf16[1,64,1152]{2,1,0:T(8,128)(2,1)S(1)}) custom-call(s32[2]{0:T(128)S(1)} %pad_add_fusion.place, s32[2,4]{1,0:T(2,128)S(1)} %bitcast.21, s32[3,2,4]{2,1,0:T(2,128)S(1)} %bitcast.16, ...), custom_call_target="tpu_custom_call" | custom-call | tf_op jit(solution)/shard_map/pallas_call | solution.py:495
  40.9 0.0 collective-permute-done.15.refs_7_
  40.9 1.5 %collective-permute-start.3 = (bf16[1,64,1152]{2,1,0:T(8,128)(2,1)S(1)}, bf16[1,64,1152]{2,1,0:T(8,128)(2,1)S(1)}, u32[]{:S(2)}, u32[]{:S(2)}) collective-permute-start(bf16[1,64,1152]{2,1,0:T(8,128)(2,1)S(1)} %get-tuple-element.47.refs_8_.refs_2_), channel_id=1, source_target_pairs={{0,8},{4,12},{8,0},{12,4},{1,9},{5,13},{9,1},{13,5},{2,10},{6,14},... | collective-permute-start | bytes 442376 | tf_op jit(solution)/shard_map/ppermute | solution.py:451
  42.4 0.0 collective-permute-done.19.refs_1_
  42.4 0.4 collective-permute-start.4
  42.8 0.0 collective-permute-done.20.refs_2_
  42.8 0.3 collective-permute-start.5
  43.2 0.0 collective-permute-done.21.refs_3_
  43.2 1.4 %collective-permute-start.6 = (bf16[1,64,1152]{2,1,0:T(8,128)(2,1)S(1)}, bf16[1,64,1152]{2,1,0:T(8,128)(2,1)S(1)}, u32[]{:S(2)}, u32[]{:S(2)}) collective-permute-start(bf16[1,64,1152]{2,1,0:T(8,128)(2,1)S(1)} %get-tuple-element.51.refs_9_.refs_3_), channel_id=1, source_target_pairs={{0,8},{4,12},{8,0},{12,4},{1,9},{5,13},{9,1},{13,5},{2,10},{6,14},... | collective-permute-start | bytes 442376 | tf_op jit(solution)/shard_map/ppermute | solution.py:451
  44.6 0.1 collective-permute-start.7
  44.7 2.2 %shard_map.121.refs_2_.refs_3_ = bf16[1728,256]{1,0:T(8,128)(2,1)S(1)} custom-call(bf16[32,1152]{1,0:T(8,128)(2,1)S(1)} %get-tuple-element.67.refs_0_, bf16[32,1152]{1,0:T(8,128)(2,1)S(1)} %collective-permute-done.19.refs_1_, bf16[32,1152]{1,0:T(8,128)(2,1)S(1)} %collective-permute-done.20.refs_2_, bf16[32,1152]{1,0:T(8,128)(2,1)S(1)} %collective-permute-done.21.refs_3_, ...), custom_call_target="tpu_custom_call" | custom-call | tf_op jit(solution)/shard_map/pallas_call | solution.py:541
  46.9 0.8 collective-permute-done.3.refs_2_
  47.7 2.1 %collective-permute-done.4.refs_3_ = bf16[1,64,1152]{2,1,0:T(8,128)(2,1)S(1)} collective-permute-done((bf16[1,64,1152]{2,1,0:T(8,128)(2,1)S(1)}, bf16[1,64,1152]{2,1,0:T(8,128)(2,1)S(1)}, u32[]{:S(2)}, u32[]{:S(2)}) %collective-permute-start.4) | collective-permute-done | bytes 147488 | tf_op jit(solution)/shard_map/ppermute | solution.py:451
  49.8 1.4 %shard_map.112.refs_0_ = bf16[1728,256]{1,0:T(8,128)(2,1)S(1)} custom-call(bf16[1,64,1152]{2,1,0:T(8,128)(2,1)S(1)} %get-tuple-element.45.refs_0_.refs_4_.refs_2_, bf16[1,64,1152]{2,1,0:T(8,128)(2,1)S(1)} %collective-permute-done.2.refs_1_, bf16[1,64,1152]{2,1,0:T(8,128)(2,1)S(1)} %collective-permute-done.3.refs_2_, ...), custom_call_target="tpu_custom_call" | custom-call | tf_op jit(solution)/shard_map/pallas_call | solution.py:512
  51.2 2.8 %collective-permute-done.6.refs_2_ = bf16[1,64,1152]{2,1,0:T(8,128)(2,1)S(1)} collective-permute-done((bf16[1,64,1152]{2,1,0:T(8,128)(2,1)S(1)}, bf16[1,64,1152]{2,1,0:T(8,128)(2,1)S(1)}, u32[]{:S(2)}, u32[]{:S(2)}) %collective-permute-start.6) | collective-permute-done | bytes 147488 | tf_op jit(solution)/shard_map/ppermute | solution.py:451
  54.1 2.1 %collective-permute-done.7.refs_3_ = bf16[1,64,1152]{2,1,0:T(8,128)(2,1)S(1)} collective-permute-done((bf16[1,64,1152]{2,1,0:T(8,128)(2,1)S(1)}, bf16[1,64,1152]{2,1,0:T(8,128)(2,1)S(1)}, u32[]{:S(2)}, u32[]{:S(2)}) %collective-permute-start.7) | collective-permute-done | bytes 147488 | tf_op jit(solution)/shard_map/ppermute | solution.py:451
  56.2 1.4 %shard_map.114.refs_1_ = bf16[1728,256]{1,0:T(8,128)(2,1)S(1)} custom-call(bf16[1,64,1152]{2,1,0:T(8,128)(2,1)S(1)} %get-tuple-element.49.refs_0_.refs_5_.refs_3_, bf16[1,64,1152]{2,1,0:T(8,128)(2,1)S(1)} %collective-permute-done.5.refs_1_, bf16[1,64,1152]{2,1,0:T(8,128)(2,1)S(1)} %collective-permute-done.6.refs_2_, ...), custom_call_target="tpu_custom_call" | custom-call | tf_op jit(solution)/shard_map/pallas_call | solution.py:512
  57.5 2.0 %shard_map.122 = (bf16[32,2304]{1,0:T(8,128)(2,1)S(1)}, bf16[32,2304]{1,0:T(8,128)(2,1)S(1)}, bf16[32,2304]{1,0:T(8,128)(2,1)S(1)}, bf16[32,2304]{1,0:T(8,128)(2,1)S(1)}) custom-call(bf16[1728,256]{1,0:T(8,128)(2,1)S(1)} %shard_map.112.refs_0_, bf16[1728,256]{1,0:T(8,128)(2,1)S(1)} %shard_map.114.refs_1_, bf16[1728,256]{1,0:T(8,128)(2,1)S(1)} %shard_map.121.refs_2_.refs_3_, ...), custom_call_target="tpu_custom_call" | custom-call | tf_op jit(solution)/shard_map/pallas_call | solution.py:552
  59.6 0.4 collective-permute-start.22
  60.0 0.2 collective-permute-start.10
  60.2 2.0 %collective-permute-start.11 = (bf16[32,1152]{1,0:T(8,128)(2,1)S(1)}, bf16[32,1152]{1,0:T(8,128)(2,1)S(1)}, u32[]{:S(2)}, u32[]{:S(2)}) collective-permute-start(bf16[32,1152]{1,0:T(8,128)(2,1)S(1)} %get-tuple-element.59.refs_6_), channel_id=1, source_target_pairs={{0,8},{4,12},{8,0},{12,4},{1,9},{5,13},{9,1},{13,5},{2,10},{6,14},... | collective-permute-start | bytes 221192 | tf_op jit(solution)/shard_map/ppermute | solution.py:451
  62.1 0.0 collective-permute-start.12
  62.1 2.6 %collective-permute-done.11.refs_2_ = bf16[32,1152]{1,0:T(8,128)(2,1)S(1)} collective-permute-done((bf16[32,1152]{1,0:T(8,128)(2,1)S(1)}, bf16[32,1152]{1,0:T(8,128)(2,1)S(1)}, u32[]{:S(2)}, u32[]{:S(2)}) %collective-permute-start.11) | collective-permute-done | bytes 73760 | tf_op jit(solution)/shard_map/ppermute | solution.py:451
  64.7 1.9 %collective-permute-done.12.refs_3_ = bf16[32,1152]{1,0:T(8,128)(2,1)S(1)} collective-permute-done((bf16[32,1152]{1,0:T(8,128)(2,1)S(1)}, bf16[32,1152]{1,0:T(8,128)(2,1)S(1)}, u32[]{:S(2)}, u32[]{:S(2)}) %collective-permute-start.12) | collective-permute-done | bytes 73760 | tf_op jit(solution)/shard_map/ppermute | solution.py:451
  66.7 2.2 %shard_map.118.refs_2_.refs_3_ = bf16[1728,256]{1,0:T(8,128)(2,1)S(1)} custom-call(bf16[32,1152]{1,0:T(8,128)(2,1)S(1)} %get-tuple-element.57.refs_0_.refs_4_, bf16[32,1152]{1,0:T(8,128)(2,1)S(1)} %collective-permute-done.10.refs_1_, bf16[32,1152]{1,0:T(8,128)(2,1)S(1)} %collective-permute-done.11.refs_2_, ...), custom_call_target="tpu_custom_call" | custom-call | tf_op jit(solution)/shard_map/pallas_call | solution.py:541
  68.8 0.6 collective-permute-start.23
  69.4 0.9 %collective-permute-start.24 = (bf16[32,2304]{1,0:T(8,128)(2,1)S(1)}, bf16[32,2304]{1,0:T(8,128)(2,1)S(1)}, u32[]{:S(2)}, u32[]{:S(2)}) collective-permute-start(bf16[32,2304]{1,0:T(8,128)(2,1)S(1)} %get-tuple-element.76), channel_id=1, source_target_pairs={{12,0},{8,4},{4,8},{0,12},{13,1},{9,5},{5,9},{1,13},{14,2},{10,6},... | collective-permute-start | bytes 442376 | tf_op jit(solution)/shard_map/ppermute | solution.py:561
  70.4 1.9 %shard_map.119 = (bf16[32,2304]{1,0:T(8,128)(2,1)S(1)}, bf16[32,2304]{1,0:T(8,128)(2,1)S(1)}, bf16[32,2304]{1,0:T(8,128)(2,1)S(1)}, bf16[32,2304]{1,0:T(8,128)(2,1)S(1)}) custom-call(bf16[1728,256]{1,0:T(8,128)(2,1)S(1)} %shard_map.112.refs_0_, bf16[1728,256]{1,0:T(8,128)(2,1)S(1)} %shard_map.114.refs_1_, bf16[1728,256]{1,0:T(8,128)(2,1)S(1)} %shard_map.118.refs_2_.refs_3_, ...), custom_call_target="tpu_custom_call" | custom-call | tf_op jit(solution)/shard_map/pallas_call | solution.py:552
  72.2 0.7 collective-permute-start.18
  73.0 0.5 collective-permute-start.16
  73.5 0.0 collective-permute-done.22.refs_1_
  73.5 0.9 %collective-permute-start.17 = (bf16[32,2304]{1,0:T(8,128)(2,1)S(1)}, bf16[32,2304]{1,0:T(8,128)(2,1)S(1)}, u32[]{:S(2)}, u32[]{:S(2)}) collective-permute-start(bf16[32,2304]{1,0:T(8,128)(2,1)S(1)} %get-tuple-element.66), channel_id=1, source_target_pairs={{12,0},{8,4},{4,8},{0,12},{13,1},{9,5},{5,9},{1,13},{14,2},{10,6},... | collective-permute-start | bytes 442376 | tf_op jit(solution)/shard_map/ppermute | solution.py:561
  74.4 1.5 %shard_map.120.refs_12_.refs_6_ = bf16[4,2,64,1152]{3,2,1,0:T(8,128)(2,1)S(1)} custom-call(bf16[32,1152]{1,0:T(8,128)(2,1)S(1)} %get-tuple-element.67.refs_0_, bf16[32,1152]{1,0:T(8,128)(2,1)S(1)} %get-tuple-element.68.refs_1_, bf16[32,1152]{1,0:T(8,128)(2,1)S(1)} %get-tuple-element.69.refs_2_, bf16[32,1152]{1,0:T(8,128)(2,1)S(1)} %get-tuple-element.70.refs_3_, ...), custom_call_target="tpu_custom_call" | custom-call | tf_op jit(solution)/shard_map/pallas_call | solution.py:566
  76.0 0.0 collective-permute-done.23.refs_2_
  76.0 1.1 %collective-permute-done.24.refs_3_ = bf16[32,2304]{1,0:T(8,128)(2,1)S(1)} collective-permute-done((bf16[32,2304]{1,0:T(8,128)(2,1)S(1)}, bf16[32,2304]{1,0:T(8,128)(2,1)S(1)}, u32[]{:S(2)}, u32[]{:S(2)}) %collective-permute-start.24) | collective-permute-done | bytes 147488 | tf_op jit(solution)/shard_map/ppermute | solution.py:561
  77.1 2.8 %shard_map.123.refs_9_ = bf16[4,256,1152]{2,1,0:T(8,128)(2,1)} custom-call(s32[2]{0:T(128)S(1)} %pad_add_fusion.place, bf16[32,2304]{1,0:T(8,128)(2,1)S(1)} %get-tuple-element.73.refs_0_, bf16[32,2304]{1,0:T(8,128)(2,1)S(1)} %collective-permute-done.22.refs_1_, bf16[32,2304]{1,0:T(8,128)(2,1)S(1)} %collective-permute-done.23.refs_2_, ...), custom_call_target="tpu_custom_call" | custom-call | tf_op jit(solution)/shard_map/pallas_call | solution.py:584
  79.9 0.0 collective-permute-done.18.refs_1_
  79.9 2.2 %shard_map.124.refs_9_ = bf16[4,256,1152]{2,1,0:T(8,128)(2,1)} custom-call(s32[2]{0:T(128)S(1)} %pad_add_fusion.place, bf16[32,2304]{1,0:T(8,128)(2,1)S(1)} %get-tuple-element.71.refs_0_, bf16[32,2304]{1,0:T(8,128)(2,1)S(1)} %collective-permute-done.18.refs_1_, ...), custom_call_target="tpu_custom_call", output_to_operand_aliasing={{}: (10, {})} | custom-call | tf_op jit(solution)/shard_map/pallas_call | solution.py:584
  82.2 1.2 %collective-permute-done.17.refs_1_ = bf16[32,2304]{1,0:T(8,128)(2,1)S(1)} collective-permute-done((bf16[32,2304]{1,0:T(8,128)(2,1)S(1)}, bf16[32,2304]{1,0:T(8,128)(2,1)S(1)}, u32[]{:S(2)}, u32[]{:S(2)}) %collective-permute-start.17) | collective-permute-done | bytes 147488 | tf_op jit(solution)/shard_map/ppermute | solution.py:561
  83.4 2.2 %shard_map.125 = bf16[4,256,1152]{2,1,0:T(8,128)(2,1)} custom-call(s32[2]{0:T(128)S(1)} %pad_add_fusion.place, bf16[32,2304]{1,0:T(8,128)(2,1)S(1)} %collective-permute-done.16.refs_0_, bf16[32,2304]{1,0:T(8,128)(2,1)S(1)} %collective-permute-done.17.refs_1_, ...), custom_call_target="tpu_custom_call", output_to_operand_aliasing={{}: (10, {})} | custom-call | tf_op jit(solution)/shard_map/pallas_call | solution.py:584
  (20 shorter events, 0.0 us)
Async XLA Ops:
  1.6 17.3 %collective-permute-start = (bf16[2,1152,128]{2,1,0:T(8,128)(2,1)S(1)}, bf16[2,1152,128]{2,1,0:T(8,128)(2,1)S(1)}, u32[]{:S(2)}, u32[]{:S(2)}) collective-permute-start(bf16[2,1152,128]{2,1,0:T(8,128)(2,1)S(1)} %get-tuple-element.41.a_ref), channel_id=1, source_target_pairs={{0,1},{1,0},{2,3},{3,2},{4,5},{5,4},{6,7},{7,6},{8,9},{9,8},{10,11... | collective-permute-start | bytes 1769480 | tf_op jit(solution)/shard_map/ppermute | solution.py:469
  4.7 16.1 %copy-start.5 = (f32[1152]{0:T(1024)S(1)}, f32[1152]{0:T(1024)}, u32[]{:S(2)}) copy-start(f32[1152]{0:T(1024)} %param.16) | copy-start | bytes 13828
  4.7 16.2 %copy-start.3 = (s32[4,2,3]{0,1,2:T(2,128)S(1)}, s32[4,2,3]{0,1,2:T(2,128)}, u32[]{:S(2)}) copy-start(s32[4,2,3]{0,1,2:T(2,128)} %param.20) | copy-start | bytes 292
  4.7 16.2 %copy-start.4 = (s32[4,2]{0,1:T(2,128)S(1)}, s32[4,2]{0,1:T(2,128)}, u32[]{:S(2)}) copy-start(s32[4,2]{0,1:T(2,128)} %param.21) | copy-start | bytes 100
  4.7 16.1 %collective-permute-start.1 = (bf16[2,1152,128]{2,1,0:T(8,128)(2,1)S(1)}, bf16[2,1152,128]{2,1,0:T(8,128)(2,1)S(1)}, u32[]{:S(2)}, u32[]{:S(2)}) collective-permute-start(bf16[2,1152,128]{2,1,0:T(8,128)(2,1)S(1)} %get-tuple-element.42.b_ref), channel_id=1, source_target_pairs={{1,2},{2,1},{5,6},{6,5},{9,10},{10,9},{13,14},{14,13},{17,18},{18,... | collective-permute-start | bytes 1769480 | tf_op jit(solution)/shard_map/ppermute | solution.py:469
  8.1 15.2 %copy-start.1 = (bf16[576,1152]{1,0:T(8,128)(2,1)S(1)}, bf16[576,1152]{1,0:T(8,128)(2,1)}, u32[]{:S(2)}) copy-start(bf16[576,1152]{1,0:T(8,128)(2,1)} %refs_8_.3) | copy-start | bytes 3981316
  8.1 22.6 %collective-permute-start.8 = (bf16[2,1152,128]{2,1,0:T(8,128)(2,1)S(1)}, bf16[2,1152,128]{2,1,0:T(8,128)(2,1)S(1)}, u32[]{:S(2)}, u32[]{:S(2)}) collective-permute-start(bf16[2,1152,128]{2,1,0:T(8,128)(2,1)S(1)} %get-tuple-element.53.a_ref), channel_id=1, source_target_pairs={{0,1},{1,0},{2,3},{3,2},{4,5},{5,4},{6,7},{7,6},{8,9},{9,8},{10,11... | collective-permute-start | bytes 1769480 | tf_op jit(solution)/shard_map/ppermute | solution.py:469
  12.5 20.6 %collective-permute-start.9 = (bf16[2,1152,128]{2,1,0:T(8,128)(2,1)S(1)}, bf16[2,1152,128]{2,1,0:T(8,128)(2,1)S(1)}, u32[]{:S(2)}, u32[]{:S(2)}) collective-permute-start(bf16[2,1152,128]{2,1,0:T(8,128)(2,1)S(1)} %get-tuple-element.54.b_ref), channel_id=1, source_target_pairs={{1,2},{2,1},{5,6},{6,5},{9,10},{10,9},{13,14},{14,13},{17,18},{18,... | collective-permute-start | bytes 1769480 | tf_op jit(solution)/shard_map/ppermute | solution.py:469
  13.2 22.7 %collective-permute-start.13 = (bf16[2,64,1152]{2,1,0:T(8,128)(2,1)S(1)}, bf16[2,64,1152]{2,1,0:T(8,128)(2,1)S(1)}, u32[]{:S(2)}, u32[]{:S(2)}) collective-permute-start(bf16[2,64,1152]{2,1,0:T(8,128)(2,1)S(1)} %get-tuple-element.62.refs_9_), channel_id=1, source_target_pairs={{0,4},{4,0},{8,12},{12,8},{1,5},{5,1},{9,13},{13,9},{2,6},{6,2},{1... | collective-permute-start | bytes 884744 | tf_op jit(solution)/shard_map/ppermute | solution.py:451
  18.9 18.7 %collective-permute-start.14 = (bf16[2,64,1152]{2,1,0:T(8,128)(2,1)S(1)}, bf16[2,64,1152]{2,1,0:T(8,128)(2,1)S(1)}, u32[]{:S(2)}, u32[]{:S(2)}) collective-permute-start(bf16[2,64,1152]{2,1,0:T(8,128)(2,1)S(1)} %get-tuple-element.63.refs_10_), channel_id=1, source_target_pairs={{0,8},{4,12},{8,0},{12,4},{1,9},{5,13},{9,1},{13,5},{2,10},{6,14},... | collective-permute-start | bytes 884744 | tf_op jit(solution)/shard_map/ppermute | solution.py:451
  20.8 20.1 %collective-permute-start.15 = (bf16[2,64,1152]{2,1,0:T(8,128)(2,1)S(1)}, bf16[2,64,1152]{2,1,0:T(8,128)(2,1)S(1)}, u32[]{:S(2)}, u32[]{:S(2)}) collective-permute-start(bf16[2,64,1152]{2,1,0:T(8,128)(2,1)S(1)} %get-tuple-element.64.refs_11_), channel_id=1, source_target_pairs={{0,12},{4,8},{8,4},{12,0},{1,13},{5,9},{9,5},{13,1},{2,14},{6,10},... | collective-permute-start | bytes 884744 | tf_op jit(solution)/shard_map/ppermute | solution.py:451
  30.7 13.9 %collective-permute-start.2 = (bf16[1,64,1152]{2,1,0:T(8,128)(2,1)S(1)}, bf16[1,64,1152]{2,1,0:T(8,128)(2,1)S(1)}, u32[]{:S(2)}, u32[]{:S(2)}) collective-permute-start(bf16[1,64,1152]{2,1,0:T(8,128)(2,1)S(1)} %get-tuple-element.46.refs_6_.refs_4_), channel_id=1, source_target_pairs={{0,4},{4,0},{8,12},{12,8},{1,5},{5,1},{9,13},{13,9},{2,6},{6,2},{1... | collective-permute-start | bytes 442376 | tf_op jit(solution)/shard_map/ppermute | solution.py:451
  35.3 7.1 %collective-permute-start.19 = (bf16[32,1152]{1,0:T(8,128)(2,1)S(1)}, bf16[32,1152]{1,0:T(8,128)(2,1)S(1)}, u32[]{:S(2)}, u32[]{:S(2)}) collective-permute-start(bf16[32,1152]{1,0:T(8,128)(2,1)S(1)} %get-tuple-element.68.refs_1_), channel_id=1, source_target_pairs={{0,4},{4,0},{8,12},{12,8},{1,5},{5,1},{9,13},{13,9},{2,6},{6,2},{1... | collective-permute-start | bytes 221192 | tf_op jit(solution)/shard_map/ppermute | solution.py:451
  35.9 7.0 %collective-permute-start.20 = (bf16[32,1152]{1,0:T(8,128)(2,1)S(1)}, bf16[32,1152]{1,0:T(8,128)(2,1)S(1)}, u32[]{:S(2)}, u32[]{:S(2)}) collective-permute-start(bf16[32,1152]{1,0:T(8,128)(2,1)S(1)} %get-tuple-element.69.refs_2_), channel_id=1, source_target_pairs={{0,8},{4,12},{8,0},{12,4},{1,9},{5,13},{9,1},{13,5},{2,10},{6,14},... | collective-permute-start | bytes 221192 | tf_op jit(solution)/shard_map/ppermute | solution.py:451
  37.6 5.6 %collective-permute-start.21 = (bf16[32,1152]{1,0:T(8,128)(2,1)S(1)}, bf16[32,1152]{1,0:T(8,128)(2,1)S(1)}, u32[]{:S(2)}, u32[]{:S(2)}) collective-permute-start(bf16[32,1152]{1,0:T(8,128)(2,1)S(1)} %get-tuple-element.70.refs_3_), channel_id=1, source_target_pairs={{0,12},{4,8},{8,4},{12,0},{1,13},{5,9},{9,5},{13,1},{2,14},{6,10},... | collective-permute-start | bytes 221192 | tf_op jit(solution)/shard_map/ppermute | solution.py:451
  37.6 7.2 %copy-start = (bf16[1152,1728]{0,1:T(8,128)(2,1)S(1)}, bf16[1152,1728]{0,1:T(8,128)(2,1)}, u32[]{:S(2)}) copy-start(bf16[1152,1728]{0,1:T(8,128)(2,1)} %param.17) | copy-start | bytes 11943940
  40.9 6.8 %collective-permute-start.3 = (bf16[1,64,1152]{2,1,0:T(8,128)(2,1)S(1)}, bf16[1,64,1152]{2,1,0:T(8,128)(2,1)S(1)}, u32[]{:S(2)}, u32[]{:S(2)}) collective-permute-start(bf16[1,64,1152]{2,1,0:T(8,128)(2,1)S(1)} %get-tuple-element.47.refs_8_.refs_2_), channel_id=1, source_target_pairs={{0,8},{4,12},{8,0},{12,4},{1,9},{5,13},{9,1},{13,5},{2,10},{6,14},... | collective-permute-start | bytes 442376 | tf_op jit(solution)/shard_map/ppermute | solution.py:451
  42.4 7.4 %collective-permute-start.4 = (bf16[1,64,1152]{2,1,0:T(8,128)(2,1)S(1)}, bf16[1,64,1152]{2,1,0:T(8,128)(2,1)S(1)}, u32[]{:S(2)}, u32[]{:S(2)}) collective-permute-start(bf16[1,64,1152]{2,1,0:T(8,128)(2,1)S(1)} %get-tuple-element.48.refs_10_.refs_4_), channel_id=1, source_target_pairs={{0,12},{4,8},{8,4},{12,0},{1,13},{5,9},{9,5},{13,1},{2,14},{6,10},... | collective-permute-start | bytes 442376 | tf_op jit(solution)/shard_map/ppermute | solution.py:451
  42.8 8.4 %collective-permute-start.5 = (bf16[1,64,1152]{2,1,0:T(8,128)(2,1)S(1)}, bf16[1,64,1152]{2,1,0:T(8,128)(2,1)S(1)}, u32[]{:S(2)}, u32[]{:S(2)}) collective-permute-start(bf16[1,64,1152]{2,1,0:T(8,128)(2,1)S(1)} %get-tuple-element.50.refs_7_.refs_5_), channel_id=1, source_target_pairs={{0,4},{4,0},{8,12},{12,8},{1,5},{5,1},{9,13},{13,9},{2,6},{6,2},{1... | collective-permute-start | bytes 442376 | tf_op jit(solution)/shard_map/ppermute | solution.py:451
  43.2 10.9 %collective-permute-start.6 = (bf16[1,64,1152]{2,1,0:T(8,128)(2,1)S(1)}, bf16[1,64,1152]{2,1,0:T(8,128)(2,1)S(1)}, u32[]{:S(2)}, u32[]{:S(2)}) collective-permute-start(bf16[1,64,1152]{2,1,0:T(8,128)(2,1)S(1)} %get-tuple-element.51.refs_9_.refs_3_), channel_id=1, source_target_pairs={{0,8},{4,12},{8,0},{12,4},{1,9},{5,13},{9,1},{13,5},{2,10},{6,14},... | collective-permute-start | bytes 442376 | tf_op jit(solution)/shard_map/ppermute | solution.py:451
  44.6 11.6 %collective-permute-start.7 = (bf16[1,64,1152]{2,1,0:T(8,128)(2,1)S(1)}, bf16[1,64,1152]{2,1,0:T(8,128)(2,1)S(1)}, u32[]{:S(2)}, u32[]{:S(2)}) collective-permute-start(bf16[1,64,1152]{2,1,0:T(8,128)(2,1)S(1)} %get-tuple-element.52.refs_11_.refs_5_), channel_id=1, source_target_pairs={{0,12},{4,8},{8,4},{12,0},{1,13},{5,9},{9,5},{13,1},{2,14},{6,10},... | collective-permute-start | bytes 442376 | tf_op jit(solution)/shard_map/ppermute | solution.py:451
  59.6 13.9 %collective-permute-start.22 = (bf16[32,2304]{1,0:T(8,128)(2,1)S(1)}, bf16[32,2304]{1,0:T(8,128)(2,1)S(1)}, u32[]{:S(2)}, u32[]{:S(2)}) collective-permute-start(bf16[32,2304]{1,0:T(8,128)(2,1)S(1)} %get-tuple-element.74), channel_id=1, source_target_pairs={{4,0},{0,4},{12,8},{8,12},{5,1},{1,5},{13,9},{9,13},{6,2},{2,6},{1... | collective-permute-start | bytes 442376 | tf_op jit(solution)/shard_map/ppermute | solution.py:561
  60.0 2.1 %collective-permute-start.10 = (bf16[32,1152]{1,0:T(8,128)(2,1)S(1)}, bf16[32,1152]{1,0:T(8,128)(2,1)S(1)}, u32[]{:S(2)}, u32[]{:S(2)}) collective-permute-start(bf16[32,1152]{1,0:T(8,128)(2,1)S(1)} %get-tuple-element.58.refs_5_), channel_id=1, source_target_pairs={{0,4},{4,0},{8,12},{12,8},{1,5},{5,1},{9,13},{13,9},{2,6},{6,2},{1... | collective-permute-start | bytes 221192 | tf_op jit(solution)/shard_map/ppermute | solution.py:451
  60.2 4.6 %collective-permute-start.11 = (bf16[32,1152]{1,0:T(8,128)(2,1)S(1)}, bf16[32,1152]{1,0:T(8,128)(2,1)S(1)}, u32[]{:S(2)}, u32[]{:S(2)}) collective-permute-start(bf16[32,1152]{1,0:T(8,128)(2,1)S(1)} %get-tuple-element.59.refs_6_), channel_id=1, source_target_pairs={{0,8},{4,12},{8,0},{12,4},{1,9},{5,13},{9,1},{13,5},{2,10},{6,14},... | collective-permute-start | bytes 221192 | tf_op jit(solution)/shard_map/ppermute | solution.py:451
  62.1 4.6 %collective-permute-start.12 = (bf16[32,1152]{1,0:T(8,128)(2,1)S(1)}, bf16[32,1152]{1,0:T(8,128)(2,1)S(1)}, u32[]{:S(2)}, u32[]{:S(2)}) collective-permute-start(bf16[32,1152]{1,0:T(8,128)(2,1)S(1)} %get-tuple-element.60.refs_7_), channel_id=1, source_target_pairs={{0,12},{4,8},{8,4},{12,0},{1,13},{5,9},{9,5},{13,1},{2,14},{6,10},... | collective-permute-start | bytes 221192 | tf_op jit(solution)/shard_map/ppermute | solution.py:451
  68.8 7.1 %collective-permute-start.23 = (bf16[32,2304]{1,0:T(8,128)(2,1)S(1)}, bf16[32,2304]{1,0:T(8,128)(2,1)S(1)}, u32[]{:S(2)}, u32[]{:S(2)}) collective-permute-start(bf16[32,2304]{1,0:T(8,128)(2,1)S(1)} %get-tuple-element.75), channel_id=1, source_target_pairs={{8,0},{12,4},{0,8},{4,12},{9,1},{13,5},{1,9},{5,13},{10,2},{14,6},... | collective-permute-start | bytes 442376 | tf_op jit(solution)/shard_map/ppermute | solution.py:561
  69.4 5.0 %copy-start.6 = (f32[1152]{0:T(1024)S(1)}, f32[1152]{0:T(1024)}, u32[]{:S(2)}) copy-start(f32[1152]{0:T(1024)} %param.19) | copy-start | bytes 13828
  69.4 7.6 %collective-permute-start.24 = (bf16[32,2304]{1,0:T(8,128)(2,1)S(1)}, bf16[32,2304]{1,0:T(8,128)(2,1)S(1)}, u32[]{:S(2)}, u32[]{:S(2)}) collective-permute-start(bf16[32,2304]{1,0:T(8,128)(2,1)S(1)} %get-tuple-element.76), channel_id=1, source_target_pairs={{12,0},{8,4},{4,8},{0,12},{13,1},{9,5},{5,9},{1,13},{14,2},{10,6},... | collective-permute-start | bytes 442376 | tf_op jit(solution)/shard_map/ppermute | solution.py:561
  72.2 7.7 %collective-permute-start.18 = (bf16[32,2304]{1,0:T(8,128)(2,1)S(1)}, bf16[32,2304]{1,0:T(8,128)(2,1)S(1)}, u32[]{:S(2)}, u32[]{:S(2)}) collective-permute-start(bf16[32,2304]{1,0:T(8,128)(2,1)S(1)} %get-tuple-element.72), channel_id=1, source_target_pairs={{4,0},{0,4},{12,8},{8,12},{5,1},{1,5},{13,9},{9,13},{6,2},{2,6},{1... | collective-permute-start | bytes 442376 | tf_op jit(solution)/shard_map/ppermute | solution.py:561
  73.0 9.2 %collective-permute-start.16 = (bf16[32,2304]{1,0:T(8,128)(2,1)S(1)}, bf16[32,2304]{1,0:T(8,128)(2,1)S(1)}, u32[]{:S(2)}, u32[]{:S(2)}) collective-permute-start(bf16[32,2304]{1,0:T(8,128)(2,1)S(1)} %get-tuple-element.65), channel_id=1, source_target_pairs={{8,0},{12,4},{0,8},{4,12},{9,1},{13,5},{1,9},{5,13},{10,2},{14,6},... | collective-permute-start | bytes 442376 | tf_op jit(solution)/shard_map/ppermute | solution.py:561
  73.5 9.9 %collective-permute-start.17 = (bf16[32,2304]{1,0:T(8,128)(2,1)S(1)}, bf16[32,2304]{1,0:T(8,128)(2,1)S(1)}, u32[]{:S(2)}, u32[]{:S(2)}) collective-permute-start(bf16[32,2304]{1,0:T(8,128)(2,1)S(1)} %get-tuple-element.66), channel_id=1, source_target_pairs={{12,0},{8,4},{4,8},{0,12},{13,1},{9,5},{5,9},{1,13},{14,2},{10,6},... | collective-permute-start | bytes 442376 | tf_op jit(solution)/shard_map/ppermute | solution.py:561
  74.4 2.7 %copy-start.2 = (bf16[576,1152]{1,0:T(8,128)(2,1)S(1)}, bf16[576,1152]{1,0:T(8,128)(2,1)}, u32[]{:S(2)}) copy-start(bf16[576,1152]{1,0:T(8,128)(2,1)} %refs_7_.3) | copy-start | bytes 3981316

commit v6 on v5

--- a/solution.py
+++ b/solution.py
@@ -186,16 +186,13 @@
 
 
 def spatial_kernel(frame, n_groups, place, counts, lists, qn_ref, sum_ref, ra_ref, rb_ref, h_ref, w_ref, g_ref, *rest):
-    outs, (att, hid, mix, sem) = rest[:n_groups], rest[n_groups:]
-    copy = pltpu.make_async_copy(h_ref.at[pl.ds(frame, hid.shape[0])], hid, sem)
-    copy.start()
+    outs, (att, mix) = rest[:n_groups], rest[n_groups:]
     remote_attend(frame, place, counts, lists, qn_ref, sum_ref, ra_ref, rb_ref, att)
-    copy.wait()
-    n, tokens, _ = hid.shape
+    n, tokens, _ = h_ref.shape
 
     def block(f):
         def finish(normed):
-            mix[f] = (hid[f].astype(F32) + normed * g_ref[...]).astype(BF)
+            mix[f] = (h_ref[f].astype(F32) + normed * g_ref[...]).astype(BF)
 
         return lambda: contract(att[f], w_ref[...], 0, 0), finish
 
@@ -496,16 +493,14 @@
                 functools.partial(spatial_kernel, f, groups),
                 [smem, smem, smem, one((late, width, tokens), f), one(sum_shape, f)]
                 + [one((late,) + edge.shape, f)] * 2
-                + [any_spec, whole((width, model)), whole((1, model))],
+                + [one(hidden.shape, f), whole((width, model)), whole((1, model))],
                 [whole((1, share, model))] * groups,
                 [jax.ShapeDtypeStruct((1, share, model), BF)] * groups,
                 [
                     pltpu.VMEM((1, width, tokens), BF),
                     pltpu.VMEM((1, tokens, model), BF),
-                    pltpu.VMEM((1, tokens, model), BF),
-                    pltpu.SemaphoreType.DMA,
                 ],
-            )(place, counts, lists, *own_sums[0], *halos[0][2:], hidden_far, spatial_out_weight, gain_one)
+            )(place, counts, lists, *own_sums[0], *halos[0][2:], hidden, spatial_out_weight, gain_one)
         )
         arrived = send(mixed[f])
         projected.append(

time: 86.3 us -> 85.2 us (0.987)
  Pallas kernels: 37.5 us -> 35.6 us
    pallas_call x2, Pallas kernels: 6.73 us -> 4.69 us  [shards(): call(functools.partial(spatial_kernel, f, groups), [smem, smem, smem, one...]
  transfers between devices with their start and end apart: 25 -> 25, of which waited for: 10 -> 10; matrix products, arithmetic and copies ran while one was open for 0% -> 0% of each run, Pallas kernels for 35% -> 34%
where the time goes in v6:
time: 85.2 us; the launch traced here: 84.7 us
  Pallas kernels  35.6 us (42%)
  waiting for transfers between devices  25.2 us (30%)
  starting transfers between devices  23.3 us (27%)
    ppermute x15, waiting for transfers between devices, send(): lax.ppermute(parts[j], 'frame', out_pairs(j))  12.5 us
    ppermute x2, waiting for transfers between devices, shards(): lax.ppermute(a, 'strip', near)  10.4 us
    ppermute x15, starting transfers between devices, send(): lax.ppermute(parts[j], 'frame', out_pairs(j))  10.1 us
    ppermute x2, starting transfers between devices, shards(): lax.ppermute(a, 'strip', near)  7.55 us
    pallas_call x3, Pallas kernels, shards(): call(functools.partial(output_kernel, groups, tuple(js), early, half, hal...  7.26 us
    pallas_call x2, Pallas kernels, shards(): call(functools.partial(local_kernel, some * late), [smem, smem, smem, blo...  4.78 us
    pallas_call x2, Pallas kernels, shards(): call(functools.partial(spatial_kernel, f, groups), [smem, smem, smem, one...  4.69 us
    pallas_call x2, Pallas kernels, shards(): call(functools.partial(late_project_kernel, early, frames), late_specs +...  4.33 us
  transfers between devices with their start and end apart: 25, of which 10 were waited for; matrix products, arithmetic and copies ran while one was open for 0% of the time, Pallas kernels for 34%

profile of v6, /device:TPU:0, one launch (start us, length us, event | category | flops | bytes accessed | tf_op | source)
XLA Modules:
  0.0 84.7 jit_solution(15878139353890149753)
XLA Ops:
  0.0 0.1 pad_add_fusion.place
  0.1 1.5 %shard_map.109 = (bf16[2,1152,128]{2,1,0:T(8,128)(2,1)S(1)}, bf16[2,1152,128]{2,1,0:T(8,128)(2,1)S(1)}) custom-call(s32[2]{0:T(128)S(1)} %pad_add_fusion.place, bf16[4,576,256]{2,1,0:T(8,128)(2,1)} %bitcast.22, bf16[4,576,256]{2,1,0:T(8,128)(2,1)} %bitcast.24), custom_call_target="tpu_custom_call" | custom-call | tf_op jit(solution)/shard_map/pallas_call | solution.py:455
  1.6 3.1 %collective-permute-start = (bf16[2,1152,128]{2,1,0:T(8,128)(2,1)S(1)}, bf16[2,1152,128]{2,1,0:T(8,128)(2,1)S(1)}, u32[]{:S(2)}, u32[]{:S(2)}) collective-permute-start(bf16[2,1152,128]{2,1,0:T(8,128)(2,1)S(1)} %get-tuple-element.41.a_ref), channel_id=1, source_target_pairs={{0,1},{1,0},{2,3},{3,2},{4,5},{5,4},{6,7},{7,6},{8,9},{9,8},{10,11... | collective-permute-start | bytes 1769480 | tf_op jit(solution)/shard_map/ppermute | solution.py:466
  4.7 0.8 collective-permute-start.1
  5.5 0.0 copy-start.2
  5.5 2.7 %shard_map.115 = (bf16[2,1152,128]{2,1,0:T(8,128)(2,1)S(1)}, bf16[2,1152,128]{2,1,0:T(8,128)(2,1)S(1)}, bf16[2,64,1152]{2,1,0:T(8,128)(2,1)S(1)}, bf16[2,64,1152...) custom-call(s32[2]{0:T(128)S(1)} %pad_add_fusion.place, ...), custom_call_target="tpu_custom_call" | custom-call | tf_op jit(solution)/shard_map/pallas_call | solution.py:455
  8.2 0.0 copy-start.1
  8.2 4.4 %collective-permute-start.8 = (bf16[2,1152,128]{2,1,0:T(8,128)(2,1)S(1)}, bf16[2,1152,128]{2,1,0:T(8,128)(2,1)S(1)}, u32[]{:S(2)}, u32[]{:S(2)}) collective-permute-start(bf16[2,1152,128]{2,1,0:T(8,128)(2,1)S(1)} %get-tuple-element.53.a_ref), channel_id=1, source_target_pairs={{0,1},{1,0},{2,3},{3,2},{4,5},{5,4},{6,7},{7,6},{8,9},{9,8},{10,11... | collective-permute-start | bytes 1769480 | tf_op jit(solution)/shard_map/ppermute | solution.py:466
  12.7 0.7 collective-permute-start.9
  13.4 0.1 collective-permute-start.13
  13.4 5.4 %collective-permute-done.ra_ref = bf16[2,1152,128]{2,1,0:T(8,128)(2,1)S(1)} collective-permute-done((bf16[2,1152,128]{2,1,0:T(8,128)(2,1)S(1)}, bf16[2,1152,128]{2,1,0:T(8,128)(2,1)S(1)}, u32[]{:S(2)}, u32[]{:S(2)}) %collective-permute-start) | collective-permute-done | bytes 589856 | tf_op jit(solution)/shard_map/ppermute | solution.py:466
  18.9 2.0 %collective-permute-start.14 = (bf16[2,64,1152]{2,1,0:T(8,128)(2,1)S(1)}, bf16[2,64,1152]{2,1,0:T(8,128)(2,1)S(1)}, u32[]{:S(2)}, u32[]{:S(2)}) collective-permute-start(bf16[2,64,1152]{2,1,0:T(8,128)(2,1)S(1)} %get-tuple-element.63.refs_10_), channel_id=1, source_target_pairs={{0,8},{4,12},{8,0},{12,4},{1,9},{5,13},{9,1},{13,5},{2,10},{6,14},... | collective-permute-start | bytes 884744 | tf_op jit(solution)/shard_map/ppermute | solution.py:448
  20.8 0.0 collective-permute-done.1.rb_ref
  20.8 0.0 collective-permute-start.15
  20.9 2.4 %shard_map.110 = (bf16[2,576,256]{2,1,0:T(8,128)(2,1)S(1)}, f32[2,640,256]{2,1,0:T(8,128)S(1)}) custom-call(s32[2]{0:T(128)S(1)} %pad_add_fusion.place, s32[2,4]{1,0:T(2,128)S(1)} %bitcast.17, s32[3,2,4]{2,1,0:T(2,128)S(1)} %bitcast.12, bf16[4,576,256]{2,1,0:T(8,128)(2,1)} %bitcast.26, bf16[2,1152,128]{2,1,0:T(8,128)(2,1)S(1)} %get-tuple-element.41.a_ref, ...), custom_call_target="tpu_custom_call" | custom-call | tf_op jit(solution)/shard_map/pallas_call | solution.py:474
  23.3 2.3 %shard_map.111 = (bf16[1,64,1152]{2,1,0:T(8,128)(2,1)S(1)}, bf16[1,64,1152]{2,1,0:T(8,128)(2,1)S(1)}, bf16[1,64,1152]{2,1,0:T(8,128)(2,1)S(1)}, bf16[1,64,1152]{2,1,0:T(8,128)(2,1)S(1)}) custom-call(s32[2]{0:T(128)S(1)} %pad_add_fusion.place, s32[2,4]{1,0:T(2,128)S(1)} %bitcast.18, s32[3,2,4]{2,1,0:T(2,128)S(1)} %bitcast.13, ...), custom_call_target="tpu_custom_call" | custom-call | tf_op jit(solution)/shard_map/pallas_call | solution.py:492
  25.7 5.0 %collective-permute-done.8.ra_ref = bf16[2,1152,128]{2,1,0:T(8,128)(2,1)S(1)} collective-permute-done((bf16[2,1152,128]{2,1,0:T(8,128)(2,1)S(1)}, bf16[2,1152,128]{2,1,0:T(8,128)(2,1)S(1)}, u32[]{:S(2)}, u32[]{:S(2)}) %collective-permute-start.8) | collective-permute-done | bytes 589856 | tf_op jit(solution)/shard_map/ppermute | solution.py:466
  30.7 0.0 collective-permute-start.2
  30.7 2.4 %shard_map.116 = (bf16[2,576,256]{2,1,0:T(8,128)(2,1)S(1)}, f32[2,640,256]{2,1,0:T(8,128)S(1)}) custom-call(s32[2]{0:T(128)S(1)} %pad_add_fusion.place, s32[2,4]{1,0:T(2,128)S(1)} %bitcast.19, s32[3,2,4]{2,1,0:T(2,128)S(1)} %bitcast.14, bf16[4,576,256]{2,1,0:T(8,128)(2,1)} %bitcast.27, bf16[2,1152,128]{2,1,0:T(8,128)(2,1)S(1)} %get-tuple-element.53.a_ref, ...), custom_call_target="tpu_custom_call" | custom-call | tf_op jit(solution)/shard_map/pallas_call | solution.py:474
  33.1 2.2 %shard_map.117 = (bf16[32,1152]{1,0:T(8,128)(2,1)S(1)}, bf16[32,1152]{1,0:T(8,128)(2,1)S(1)}, bf16[32,1152]{1,0:T(8,128)(2,1)S(1)}, bf16[32,1152]{1,0:T(8,128)(2...) custom-call(s32[2]{0:T(128)S(1)} %pad_add_fusion.place, ...), custom_call_target="tpu_custom_call" | custom-call | tf_op jit(solution)/shard_map/pallas_call | solution.py:517
  35.3 0.6 collective-permute-start.19
  35.9 1.7 %collective-permute-start.20 = (bf16[32,1152]{1,0:T(8,128)(2,1)S(1)}, bf16[32,1152]{1,0:T(8,128)(2,1)S(1)}, u32[]{:S(2)}, u32[]{:S(2)}) collective-permute-start(bf16[32,1152]{1,0:T(8,128)(2,1)S(1)} %get-tuple-element.69.refs_2_), channel_id=1, source_target_pairs={{0,8},{4,12},{8,0},{12,4},{1,9},{5,13},{9,1},{13,5},{2,10},{6,14},... | collective-permute-start | bytes 221192 | tf_op jit(solution)/shard_map/ppermute | solution.py:448
  37.5 0.0 collective-permute-done.14.refs_6_
  37.5 0.0 collective-permute-start.21
  37.5 2.3 %shard_map.113 = (bf16[1,64,1152]{2,1,0:T(8,128)(2,1)S(1)}, bf16[1,64,1152]{2,1,0:T(8,128)(2,1)S(1)}, bf16[1,64,1152]{2,1,0:T(8,128)(2,1)S(1)}, bf16[1,64,1152]{2,1,0:T(8,128)(2,1)S(1)}) custom-call(s32[2]{0:T(128)S(1)} %pad_add_fusion.place, s32[2,4]{1,0:T(2,128)S(1)} %bitcast.21, s32[3,2,4]{2,1,0:T(2,128)S(1)} %bitcast.16, ...), custom_call_target="tpu_custom_call" | custom-call | tf_op jit(solution)/shard_map/pallas_call | solution.py:492
  39.9 1.5 %collective-permute-start.3 = (bf16[1,64,1152]{2,1,0:T(8,128)(2,1)S(1)}, bf16[1,64,1152]{2,1,0:T(8,128)(2,1)S(1)}, u32[]{:S(2)}, u32[]{:S(2)}) collective-permute-start(bf16[1,64,1152]{2,1,0:T(8,128)(2,1)S(1)} %get-tuple-element.47.refs_8_.refs_2_), channel_id=1, source_target_pairs={{0,8},{4,12},{8,0},{12,4},{1,9},{5,13},{9,1},{13,5},{2,10},{6,14},... | collective-permute-start | bytes 442376 | tf_op jit(solution)/shard_map/ppermute | solution.py:448
  41.4 0.4 collective-permute-start.4
  41.8 0.0 collective-permute-done.20.refs_2_
  41.8 0.3 collective-permute-start.5
  42.1 0.0 collective-permute-done.21.refs_3_
  42.1 1.4 %collective-permute-start.6 = (bf16[1,64,1152]{2,1,0:T(8,128)(2,1)S(1)}, bf16[1,64,1152]{2,1,0:T(8,128)(2,1)S(1)}, u32[]{:S(2)}, u32[]{:S(2)}) collective-permute-start(bf16[1,64,1152]{2,1,0:T(8,128)(2,1)S(1)} %get-tuple-element.51.refs_9_.refs_3_), channel_id=1, source_target_pairs={{0,8},{4,12},{8,0},{12,4},{1,9},{5,13},{9,1},{13,5},{2,10},{6,14},... | collective-permute-start | bytes 442376 | tf_op jit(solution)/shard_map/ppermute | solution.py:448
  43.6 0.0 collective-permute-done.2.refs_1_
  43.6 0.1 collective-permute-start.7
  43.7 2.2 %shard_map.121.refs_2_.refs_3_ = bf16[1728,256]{1,0:T(8,128)(2,1)S(1)} custom-call(bf16[32,1152]{1,0:T(8,128)(2,1)S(1)} %get-tuple-element.67.refs_0_, bf16[32,1152]{1,0:T(8,128)(2,1)S(1)} %collective-permute-done.19.refs_1_, bf16[32,1152]{1,0:T(8,128)(2,1)S(1)} %collective-permute-done.20.refs_2_, bf16[32,1152]{1,0:T(8,128)(2,1)S(1)} %collective-permute-done.21.refs_3_, ...), custom_call_target="tpu_custom_call" | custom-call | tf_op jit(solution)/shard_map/pallas_call | solution.py:536
  45.9 0.8 collective-permute-done.3.refs_2_
  46.7 2.1 %collective-permute-done.4.refs_3_ = bf16[1,64,1152]{2,1,0:T(8,128)(2,1)S(1)} collective-permute-done((bf16[1,64,1152]{2,1,0:T(8,128)(2,1)S(1)}, bf16[1,64,1152]{2,1,0:T(8,128)(2,1)S(1)}, u32[]{:S(2)}, u32[]{:S(2)}) %collective-permute-start.4) | collective-permute-done | bytes 147488 | tf_op jit(solution)/shard_map/ppermute | solution.py:448
  48.8 1.4 %shard_map.112.refs_0_ = bf16[1728,256]{1,0:T(8,128)(2,1)S(1)} custom-call(bf16[1,64,1152]{2,1,0:T(8,128)(2,1)S(1)} %get-tuple-element.45.refs_0_.refs_4_.refs_2_, bf16[1,64,1152]{2,1,0:T(8,128)(2,1)S(1)} %collective-permute-done.2.refs_1_, bf16[1,64,1152]{2,1,0:T(8,128)(2,1)S(1)} %collective-permute-done.3.refs_2_, ...), custom_call_target="tpu_custom_call" | custom-call | tf_op jit(solution)/shard_map/pallas_call | solution.py:507
  50.2 2.8 %collective-permute-done.6.refs_2_ = bf16[1,64,1152]{2,1,0:T(8,128)(2,1)S(1)} collective-permute-done((bf16[1,64,1152]{2,1,0:T(8,128)(2,1)S(1)}, bf16[1,64,1152]{2,1,0:T(8,128)(2,1)S(1)}, u32[]{:S(2)}, u32[]{:S(2)}) %collective-permute-start.6) | collective-permute-done | bytes 147488 | tf_op jit(solution)/shard_map/ppermute | solution.py:448
  53.0 2.1 %collective-permute-done.7.refs_3_ = bf16[1,64,1152]{2,1,0:T(8,128)(2,1)S(1)} collective-permute-done((bf16[1,64,1152]{2,1,0:T(8,128)(2,1)S(1)}, bf16[1,64,1152]{2,1,0:T(8,128)(2,1)S(1)}, u32[]{:S(2)}, u32[]{:S(2)}) %collective-permute-start.7) | collective-permute-done | bytes 147488 | tf_op jit(solution)/shard_map/ppermute | solution.py:448
  55.1 1.4 %shard_map.114.refs_1_ = bf16[1728,256]{1,0:T(8,128)(2,1)S(1)} custom-call(bf16[1,64,1152]{2,1,0:T(8,128)(2,1)S(1)} %get-tuple-element.49.refs_0_.refs_5_.refs_3_, bf16[1,64,1152]{2,1,0:T(8,128)(2,1)S(1)} %collective-permute-done.5.refs_1_, bf16[1,64,1152]{2,1,0:T(8,128)(2,1)S(1)} %collective-permute-done.6.refs_2_, ...), custom_call_target="tpu_custom_call" | custom-call | tf_op jit(solution)/shard_map/pallas_call | solution.py:507
  56.5 2.0 %shard_map.122 = (bf16[32,2304]{1,0:T(8,128)(2,1)S(1)}, bf16[32,2304]{1,0:T(8,128)(2,1)S(1)}, bf16[32,2304]{1,0:T(8,128)(2,1)S(1)}, bf16[32,2304]{1,0:T(8,128)(2,1)S(1)}) custom-call(bf16[1728,256]{1,0:T(8,128)(2,1)S(1)} %shard_map.112.refs_0_, bf16[1728,256]{1,0:T(8,128)(2,1)S(1)} %shard_map.114.refs_1_, bf16[1728,256]{1,0:T(8,128)(2,1)S(1)} %shard_map.121.refs_2_.refs_3_, ...), custom_call_target="tpu_custom_call" | custom-call | tf_op jit(solution)/shard_map/pallas_call | solution.py:547
  58.5 0.4 collective-permute-start.22
  58.9 0.2 collective-permute-start.10
  59.1 1.9 %collective-permute-start.11 = (bf16[32,1152]{1,0:T(8,128)(2,1)S(1)}, bf16[32,1152]{1,0:T(8,128)(2,1)S(1)}, u32[]{:S(2)}, u32[]{:S(2)}) collective-permute-start(bf16[32,1152]{1,0:T(8,128)(2,1)S(1)} %get-tuple-element.59.refs_6_), channel_id=1, source_target_pairs={{0,8},{4,12},{8,0},{12,4},{1,9},{5,13},{9,1},{13,5},{2,10},{6,14},... | collective-permute-start | bytes 221192 | tf_op jit(solution)/shard_map/ppermute | solution.py:448
  61.0 0.0 collective-permute-start.12
  61.0 0.0 collective-permute-done.10.refs_1_
  61.0 2.6 %collective-permute-done.11.refs_2_ = bf16[32,1152]{1,0:T(8,128)(2,1)S(1)} collective-permute-done((bf16[32,1152]{1,0:T(8,128)(2,1)S(1)}, bf16[32,1152]{1,0:T(8,128)(2,1)S(1)}, u32[]{:S(2)}, u32[]{:S(2)}) %collective-permute-start.11) | collective-permute-done | bytes 73760 | tf_op jit(solution)/shard_map/ppermute | solution.py:448
  63.6 2.0 %collective-permute-done.12.refs_3_ = bf16[32,1152]{1,0:T(8,128)(2,1)S(1)} collective-permute-done((bf16[32,1152]{1,0:T(8,128)(2,1)S(1)}, bf16[32,1152]{1,0:T(8,128)(2,1)S(1)}, u32[]{:S(2)}, u32[]{:S(2)}) %collective-permute-start.12) | collective-permute-done | bytes 73760 | tf_op jit(solution)/shard_map/ppermute | solution.py:448
  65.6 2.2 %shard_map.118.refs_2_.refs_3_ = bf16[1728,256]{1,0:T(8,128)(2,1)S(1)} custom-call(bf16[32,1152]{1,0:T(8,128)(2,1)S(1)} %get-tuple-element.57.refs_0_.refs_4_, bf16[32,1152]{1,0:T(8,128)(2,1)S(1)} %collective-permute-done.10.refs_1_, bf16[32,1152]{1,0:T(8,128)(2,1)S(1)} %collective-permute-done.11.refs_2_, ...), custom_call_target="tpu_custom_call" | custom-call | tf_op jit(solution)/shard_map/pallas_call | solution.py:536
  67.8 0.6 collective-permute-start.23
  68.4 0.9 %collective-permute-start.24 = (bf16[32,2304]{1,0:T(8,128)(2,1)S(1)}, bf16[32,2304]{1,0:T(8,128)(2,1)S(1)}, u32[]{:S(2)}, u32[]{:S(2)}) collective-permute-start(bf16[32,2304]{1,0:T(8,128)(2,1)S(1)} %get-tuple-element.76), channel_id=1, source_target_pairs={{12,0},{8,4},{4,8},{0,12},{13,1},{9,5},{5,9},{1,13},{14,2},{10,6},... | collective-permute-start | bytes 442376 | tf_op jit(solution)/shard_map/ppermute | solution.py:556
  69.3 1.9 %shard_map.119 = (bf16[32,2304]{1,0:T(8,128)(2,1)S(1)}, bf16[32,2304]{1,0:T(8,128)(2,1)S(1)}, bf16[32,2304]{1,0:T(8,128)(2,1)S(1)}, bf16[32,2304]{1,0:T(8,128)(2,1)S(1)}) custom-call(bf16[1728,256]{1,0:T(8,128)(2,1)S(1)} %shard_map.112.refs_0_, bf16[1728,256]{1,0:T(8,128)(2,1)S(1)} %shard_map.114.refs_1_, bf16[1728,256]{1,0:T(8,128)(2,1)S(1)} %shard_map.118.refs_2_.refs_3_, ...), custom_call_target="tpu_custom_call" | custom-call | tf_op jit(solution)/shard_map/pallas_call | solution.py:547
  71.2 0.7 collective-permute-start.18
  71.9 0.5 collective-permute-start.16
  72.4 0.0 collective-permute-done.22.refs_1_
  72.4 0.9 %collective-permute-start.17 = (bf16[32,2304]{1,0:T(8,128)(2,1)S(1)}, bf16[32,2304]{1,0:T(8,128)(2,1)S(1)}, u32[]{:S(2)}, u32[]{:S(2)}) collective-permute-start(bf16[32,2304]{1,0:T(8,128)(2,1)S(1)} %get-tuple-element.66), channel_id=1, source_target_pairs={{12,0},{8,4},{4,8},{0,12},{13,1},{9,5},{5,9},{1,13},{14,2},{10,6},... | collective-permute-start | bytes 442376 | tf_op jit(solution)/shard_map/ppermute | solution.py:556
  73.4 1.5 %shard_map.120.refs_12_.refs_6_ = bf16[4,2,64,1152]{3,2,1,0:T(8,128)(2,1)S(1)} custom-call(bf16[32,1152]{1,0:T(8,128)(2,1)S(1)} %get-tuple-element.67.refs_0_, bf16[32,1152]{1,0:T(8,128)(2,1)S(1)} %get-tuple-element.68.refs_1_, bf16[32,1152]{1,0:T(8,128)(2,1)S(1)} %get-tuple-element.69.refs_2_, bf16[32,1152]{1,0:T(8,128)(2,1)S(1)} %get-tuple-element.70.refs_3_, ...), custom_call_target="tpu_custom_call" | custom-call | tf_op jit(solution)/shard_map/pallas_call | solution.py:561
  74.9 0.0 collective-permute-done.23.refs_2_
  74.9 1.1 %collective-permute-done.24.refs_3_ = bf16[32,2304]{1,0:T(8,128)(2,1)S(1)} collective-permute-done((bf16[32,2304]{1,0:T(8,128)(2,1)S(1)}, bf16[32,2304]{1,0:T(8,128)(2,1)S(1)}, u32[]{:S(2)}, u32[]{:S(2)}) %collective-permute-start.24) | collective-permute-done | bytes 147488 | tf_op jit(solution)/shard_map/ppermute | solution.py:556
  76.0 2.8 %shard_map.123.refs_9_ = bf16[4,256,1152]{2,1,0:T(8,128)(2,1)} custom-call(s32[2]{0:T(128)S(1)} %pad_add_fusion.place, bf16[32,2304]{1,0:T(8,128)(2,1)S(1)} %get-tuple-element.73.refs_0_, bf16[32,2304]{1,0:T(8,128)(2,1)S(1)} %collective-permute-done.22.refs_1_, bf16[32,2304]{1,0:T(8,128)(2,1)S(1)} %collective-permute-done.23.refs_2_, ...), custom_call_target="tpu_custom_call" | custom-call | tf_op jit(solution)/shard_map/pallas_call | solution.py:579
  78.9 0.0 collective-permute-done.18.refs_1_
  78.9 2.2 %shard_map.124.refs_9_ = bf16[4,256,1152]{2,1,0:T(8,128)(2,1)} custom-call(s32[2]{0:T(128)S(1)} %pad_add_fusion.place, bf16[32,2304]{1,0:T(8,128)(2,1)S(1)} %get-tuple-element.71.refs_0_, bf16[32,2304]{1,0:T(8,128)(2,1)S(1)} %collective-permute-done.18.refs_1_, ...), custom_call_target="tpu_custom_call", output_to_operand_aliasing={{}: (10, {})} | custom-call | tf_op jit(solution)/shard_map/pallas_call | solution.py:579
  81.1 1.2 %collective-permute-done.17.refs_1_ = bf16[32,2304]{1,0:T(8,128)(2,1)S(1)} collective-permute-done((bf16[32,2304]{1,0:T(8,128)(2,1)S(1)}, bf16[32,2304]{1,0:T(8,128)(2,1)S(1)}, u32[]{:S(2)}, u32[]{:S(2)}) %collective-permute-start.17) | collective-permute-done | bytes 147488 | tf_op jit(solution)/shard_map/ppermute | solution.py:556
  82.3 2.2 %shard_map.125 = bf16[4,256,1152]{2,1,0:T(8,128)(2,1)} custom-call(s32[2]{0:T(128)S(1)} %pad_add_fusion.place, bf16[32,2304]{1,0:T(8,128)(2,1)S(1)} %collective-permute-done.16.refs_0_, bf16[32,2304]{1,0:T(8,128)(2,1)S(1)} %collective-permute-done.17.refs_1_, ...), custom_call_target="tpu_custom_call", output_to_operand_aliasing={{}: (10, {})} | custom-call | tf_op jit(solution)/shard_map/pallas_call | solution.py:579
  (22 shorter events, 0.1 us)
Async XLA Ops:
  1.6 17.3 %collective-permute-start = (bf16[2,1152,128]{2,1,0:T(8,128)(2,1)S(1)}, bf16[2,1152,128]{2,1,0:T(8,128)(2,1)S(1)}, u32[]{:S(2)}, u32[]{:S(2)}) collective-permute-start(bf16[2,1152,128]{2,1,0:T(8,128)(2,1)S(1)} %get-tuple-element.41.a_ref), channel_id=1, source_target_pairs={{0,1},{1,0},{2,3},{3,2},{4,5},{5,4},{6,7},{7,6},{8,9},{9,8},{10,11... | collective-permute-start | bytes 1769480 | tf_op jit(solution)/shard_map/ppermute | solution.py:466
  4.7 16.1 %copy-start.6 = (f32[1152]{0:T(1024)S(1)}, f32[1152]{0:T(1024)}, u32[]{:S(2)}) copy-start(f32[1152]{0:T(1024)} %param.16) | copy-start | bytes 13828
  4.7 16.2 %copy-start.4 = (s32[4,2,3]{0,1,2:T(2,128)S(1)}, s32[4,2,3]{0,1,2:T(2,128)}, u32[]{:S(2)}) copy-start(s32[4,2,3]{0,1,2:T(2,128)} %param.20) | copy-start | bytes 292
  4.7 16.2 %copy-start.5 = (s32[4,2]{0,1:T(2,128)S(1)}, s32[4,2]{0,1:T(2,128)}, u32[]{:S(2)}) copy-start(s32[4,2]{0,1:T(2,128)} %param.21) | copy-start | bytes 100
  4.7 16.1 %collective-permute-start.1 = (bf16[2,1152,128]{2,1,0:T(8,128)(2,1)S(1)}, bf16[2,1152,128]{2,1,0:T(8,128)(2,1)S(1)}, u32[]{:S(2)}, u32[]{:S(2)}) collective-permute-start(bf16[2,1152,128]{2,1,0:T(8,128)(2,1)S(1)} %get-tuple-element.42.b_ref), channel_id=1, source_target_pairs={{1,2},{2,1},{5,6},{6,5},{9,10},{10,9},{13,14},{14,13},{17,18},{18,... | collective-permute-start | bytes 1769480 | tf_op jit(solution)/shard_map/ppermute | solution.py:466
  5.5 17.8 %copy-start.2 = (bf16[4,256,1152]{2,1,0:T(8,128)(2,1)S(1)}, bf16[4,256,1152]{2,1,0:T(8,128)(2,1)}, u32[]{:S(2)}) copy-start(bf16[4,256,1152]{2,1,0:T(8,128)(2,1)} %refs_0_.1) | copy-start | bytes 7077892
  8.2 15.1 %copy-start.1 = (bf16[576,1152]{1,0:T(8,128)(2,1)S(1)}, bf16[576,1152]{1,0:T(8,128)(2,1)}, u32[]{:S(2)}) copy-start(bf16[576,1152]{1,0:T(8,128)(2,1)} %refs_8_.3) | copy-start | bytes 3981316
  8.2 22.4 %collective-permute-start.8 = (bf16[2,1152,128]{2,1,0:T(8,128)(2,1)S(1)}, bf16[2,1152,128]{2,1,0:T(8,128)(2,1)S(1)}, u32[]{:S(2)}, u32[]{:S(2)}) collective-permute-start(bf16[2,1152,128]{2,1,0:T(8,128)(2,1)S(1)} %get-tuple-element.53.a_ref), channel_id=1, source_target_pairs={{0,1},{1,0},{2,3},{3,2},{4,5},{5,4},{6,7},{7,6},{8,9},{9,8},{10,11... | collective-permute-start | bytes 1769480 | tf_op jit(solution)/shard_map/ppermute | solution.py:466
  12.7 20.4 %collective-permute-start.9 = (bf16[2,1152,128]{2,1,0:T(8,128)(2,1)S(1)}, bf16[2,1152,128]{2,1,0:T(8,128)(2,1)S(1)}, u32[]{:S(2)}, u32[]{:S(2)}) collective-permute-start(bf16[2,1152,128]{2,1,0:T(8,128)(2,1)S(1)} %get-tuple-element.54.b_ref), channel_id=1, source_target_pairs={{1,2},{2,1},{5,6},{6,5},{9,10},{10,9},{13,14},{14,13},{17,18},{18,... | collective-permute-start | bytes 1769480 | tf_op jit(solution)/shard_map/ppermute | solution.py:466
  13.4 22.5 %collective-permute-start.13 = (bf16[2,64,1152]{2,1,0:T(8,128)(2,1)S(1)}, bf16[2,64,1152]{2,1,0:T(8,128)(2,1)S(1)}, u32[]{:S(2)}, u32[]{:S(2)}) collective-permute-start(bf16[2,64,1152]{2,1,0:T(8,128)(2,1)S(1)} %get-tuple-element.62.refs_9_), channel_id=1, source_target_pairs={{0,4},{4,0},{8,12},{12,8},{1,5},{5,1},{9,13},{13,9},{2,6},{6,2},{1... | collective-permute-start | bytes 884744 | tf_op jit(solution)/shard_map/ppermute | solution.py:448
  18.9 18.7 %collective-permute-start.14 = (bf16[2,64,1152]{2,1,0:T(8,128)(2,1)S(1)}, bf16[2,64,1152]{2,1,0:T(8,128)(2,1)S(1)}, u32[]{:S(2)}, u32[]{:S(2)}) collective-permute-start(bf16[2,64,1152]{2,1,0:T(8,128)(2,1)S(1)} %get-tuple-element.63.refs_10_), channel_id=1, source_target_pairs={{0,8},{4,12},{8,0},{12,4},{1,9},{5,13},{9,1},{13,5},{2,10},{6,14},... | collective-permute-start | bytes 884744 | tf_op jit(solution)/shard_map/ppermute | solution.py:448
  20.8 19.1 %collective-permute-start.15 = (bf16[2,64,1152]{2,1,0:T(8,128)(2,1)S(1)}, bf16[2,64,1152]{2,1,0:T(8,128)(2,1)S(1)}, u32[]{:S(2)}, u32[]{:S(2)}) collective-permute-start(bf16[2,64,1152]{2,1,0:T(8,128)(2,1)S(1)} %get-tuple-element.64.refs_11_), channel_id=1, source_target_pairs={{0,12},{4,8},{8,4},{12,0},{1,13},{5,9},{9,5},{13,1},{2,14},{6,10},... | collective-permute-start | bytes 884744 | tf_op jit(solution)/shard_map/ppermute | solution.py:448
  30.7 12.9 %collective-permute-start.2 = (bf16[1,64,1152]{2,1,0:T(8,128)(2,1)S(1)}, bf16[1,64,1152]{2,1,0:T(8,128)(2,1)S(1)}, u32[]{:S(2)}, u32[]{:S(2)}) collective-permute-start(bf16[1,64,1152]{2,1,0:T(8,128)(2,1)S(1)} %get-tuple-element.46.refs_6_.refs_4_), channel_id=1, source_target_pairs={{0,4},{4,0},{8,12},{12,8},{1,5},{5,1},{9,13},{13,9},{2,6},{6,2},{1... | collective-permute-start | bytes 442376 | tf_op jit(solution)/shard_map/ppermute | solution.py:448
  35.3 6.1 %collective-permute-start.19 = (bf16[32,1152]{1,0:T(8,128)(2,1)S(1)}, bf16[32,1152]{1,0:T(8,128)(2,1)S(1)}, u32[]{:S(2)}, u32[]{:S(2)}) collective-permute-start(bf16[32,1152]{1,0:T(8,128)(2,1)S(1)} %get-tuple-element.68.refs_1_), channel_id=1, source_target_pairs={{0,4},{4,0},{8,12},{12,8},{1,5},{5,1},{9,13},{13,9},{2,6},{6,2},{1... | collective-permute-start | bytes 221192 | tf_op jit(solution)/shard_map/ppermute | solution.py:448
  35.9 5.9 %collective-permute-start.20 = (bf16[32,1152]{1,0:T(8,128)(2,1)S(1)}, bf16[32,1152]{1,0:T(8,128)(2,1)S(1)}, u32[]{:S(2)}, u32[]{:S(2)}) collective-permute-start(bf16[32,1152]{1,0:T(8,128)(2,1)S(1)} %get-tuple-element.69.refs_2_), channel_id=1, source_target_pairs={{0,8},{4,12},{8,0},{12,4},{1,9},{5,13},{9,1},{13,5},{2,10},{6,14},... | collective-permute-start | bytes 221192 | tf_op jit(solution)/shard_map/ppermute | solution.py:448
  37.5 4.6 %collective-permute-start.21 = (bf16[32,1152]{1,0:T(8,128)(2,1)S(1)}, bf16[32,1152]{1,0:T(8,128)(2,1)S(1)}, u32[]{:S(2)}, u32[]{:S(2)}) collective-permute-start(bf16[32,1152]{1,0:T(8,128)(2,1)S(1)} %get-tuple-element.70.refs_3_), channel_id=1, source_target_pairs={{0,12},{4,8},{8,4},{12,0},{1,13},{5,9},{9,5},{13,1},{2,14},{6,10},... | collective-permute-start | bytes 221192 | tf_op jit(solution)/shard_map/ppermute | solution.py:448
  37.5 6.1 %copy-start = (bf16[1152,1728]{0,1:T(8,128)(2,1)S(1)}, bf16[1152,1728]{0,1:T(8,128)(2,1)}, u32[]{:S(2)}) copy-start(bf16[1152,1728]{0,1:T(8,128)(2,1)} %param.17) | copy-start | bytes 11943940
  39.9 6.8 %collective-permute-start.3 = (bf16[1,64,1152]{2,1,0:T(8,128)(2,1)S(1)}, bf16[1,64,1152]{2,1,0:T(8,128)(2,1)S(1)}, u32[]{:S(2)}, u32[]{:S(2)}) collective-permute-start(bf16[1,64,1152]{2,1,0:T(8,128)(2,1)S(1)} %get-tuple-element.47.refs_8_.refs_2_), channel_id=1, source_target_pairs={{0,8},{4,12},{8,0},{12,4},{1,9},{5,13},{9,1},{13,5},{2,10},{6,14},... | collective-permute-start | bytes 442376 | tf_op jit(solution)/shard_map/ppermute | solution.py:448
  41.4 7.4 %collective-permute-start.4 = (bf16[1,64,1152]{2,1,0:T(8,128)(2,1)S(1)}, bf16[1,64,1152]{2,1,0:T(8,128)(2,1)S(1)}, u32[]{:S(2)}, u32[]{:S(2)}) collective-permute-start(bf16[1,64,1152]{2,1,0:T(8,128)(2,1)S(1)} %get-tuple-element.48.refs_10_.refs_4_), channel_id=1, source_target_pairs={{0,12},{4,8},{8,4},{12,0},{1,13},{5,9},{9,5},{13,1},{2,14},{6,10},... | collective-permute-start | bytes 442376 | tf_op jit(solution)/shard_map/ppermute | solution.py:448
  41.8 8.4 %collective-permute-start.5 = (bf16[1,64,1152]{2,1,0:T(8,128)(2,1)S(1)}, bf16[1,64,1152]{2,1,0:T(8,128)(2,1)S(1)}, u32[]{:S(2)}, u32[]{:S(2)}) collective-permute-start(bf16[1,64,1152]{2,1,0:T(8,128)(2,1)S(1)} %get-tuple-element.50.refs_7_.refs_5_), channel_id=1, source_target_pairs={{0,4},{4,0},{8,12},{12,8},{1,5},{5,1},{9,13},{13,9},{2,6},{6,2},{1... | collective-permute-start | bytes 442376 | tf_op jit(solution)/shard_map/ppermute | solution.py:448
  42.1 10.9 %collective-permute-start.6 = (bf16[1,64,1152]{2,1,0:T(8,128)(2,1)S(1)}, bf16[1,64,1152]{2,1,0:T(8,128)(2,1)S(1)}, u32[]{:S(2)}, u32[]{:S(2)}) collective-permute-start(bf16[1,64,1152]{2,1,0:T(8,128)(2,1)S(1)} %get-tuple-element.51.refs_9_.refs_3_), channel_id=1, source_target_pairs={{0,8},{4,12},{8,0},{12,4},{1,9},{5,13},{9,1},{13,5},{2,10},{6,14},... | collective-permute-start | bytes 442376 | tf_op jit(solution)/shard_map/ppermute | solution.py:448
  43.6 11.6 %collective-permute-start.7 = (bf16[1,64,1152]{2,1,0:T(8,128)(2,1)S(1)}, bf16[1,64,1152]{2,1,0:T(8,128)(2,1)S(1)}, u32[]{:S(2)}, u32[]{:S(2)}) collective-permute-start(bf16[1,64,1152]{2,1,0:T(8,128)(2,1)S(1)} %get-tuple-element.52.refs_11_.refs_5_), channel_id=1, source_target_pairs={{0,12},{4,8},{8,4},{12,0},{1,13},{5,9},{9,5},{13,1},{2,14},{6,10},... | collective-permute-start | bytes 442376 | tf_op jit(solution)/shard_map/ppermute | solution.py:448
  58.5 13.9 %collective-permute-start.22 = (bf16[32,2304]{1,0:T(8,128)(2,1)S(1)}, bf16[32,2304]{1,0:T(8,128)(2,1)S(1)}, u32[]{:S(2)}, u32[]{:S(2)}) collective-permute-start(bf16[32,2304]{1,0:T(8,128)(2,1)S(1)} %get-tuple-element.74), channel_id=1, source_target_pairs={{4,0},{0,4},{12,8},{8,12},{5,1},{1,5},{13,9},{9,13},{6,2},{2,6},{1... | collective-permute-start | bytes 442376 | tf_op jit(solution)/shard_map/ppermute | solution.py:556
  58.9 2.1 %collective-permute-start.10 = (bf16[32,1152]{1,0:T(8,128)(2,1)S(1)}, bf16[32,1152]{1,0:T(8,128)(2,1)S(1)}, u32[]{:S(2)}, u32[]{:S(2)}) collective-permute-start(bf16[32,1152]{1,0:T(8,128)(2,1)S(1)} %get-tuple-element.58.refs_5_), channel_id=1, source_target_pairs={{0,4},{4,0},{8,12},{12,8},{1,5},{5,1},{9,13},{13,9},{2,6},{6,2},{1... | collective-permute-start | bytes 221192 | tf_op jit(solution)/shard_map/ppermute | solution.py:448
  59.1 4.5 %collective-permute-start.11 = (bf16[32,1152]{1,0:T(8,128)(2,1)S(1)}, bf16[32,1152]{1,0:T(8,128)(2,1)S(1)}, u32[]{:S(2)}, u32[]{:S(2)}) collective-permute-start(bf16[32,1152]{1,0:T(8,128)(2,1)S(1)} %get-tuple-element.59.refs_6_), channel_id=1, source_target_pairs={{0,8},{4,12},{8,0},{12,4},{1,9},{5,13},{9,1},{13,5},{2,10},{6,14},... | collective-permute-start | bytes 221192 | tf_op jit(solution)/shard_map/ppermute | solution.py:448
  61.0 4.6 %collective-permute-start.12 = (bf16[32,1152]{1,0:T(8,128)(2,1)S(1)}, bf16[32,1152]{1,0:T(8,128)(2,1)S(1)}, u32[]{:S(2)}, u32[]{:S(2)}) collective-permute-start(bf16[32,1152]{1,0:T(8,128)(2,1)S(1)} %get-tuple-element.60.refs_7_), channel_id=1, source_target_pairs={{0,12},{4,8},{8,4},{12,0},{1,13},{5,9},{9,5},{13,1},{2,14},{6,10},... | collective-permute-start | bytes 221192 | tf_op jit(solution)/shard_map/ppermute | solution.py:448
  67.8 7.1 %collective-permute-start.23 = (bf16[32,2304]{1,0:T(8,128)(2,1)S(1)}, bf16[32,2304]{1,0:T(8,128)(2,1)S(1)}, u32[]{:S(2)}, u32[]{:S(2)}) collective-permute-start(bf16[32,2304]{1,0:T(8,128)(2,1)S(1)} %get-tuple-element.75), channel_id=1, source_target_pairs={{8,0},{12,4},{0,8},{4,12},{9,1},{13,5},{1,9},{5,13},{10,2},{14,6},... | collective-permute-start | bytes 442376 | tf_op jit(solution)/shard_map/ppermute | solution.py:556
  68.4 5.0 %copy-start.7 = (f32[1152]{0:T(1024)S(1)}, f32[1152]{0:T(1024)}, u32[]{:S(2)}) copy-start(f32[1152]{0:T(1024)} %param.19) | copy-start | bytes 13828
  68.4 7.6 %collective-permute-start.24 = (bf16[32,2304]{1,0:T(8,128)(2,1)S(1)}, bf16[32,2304]{1,0:T(8,128)(2,1)S(1)}, u32[]{:S(2)}, u32[]{:S(2)}) collective-permute-start(bf16[32,2304]{1,0:T(8,128)(2,1)S(1)} %get-tuple-element.76), channel_id=1, source_target_pairs={{12,0},{8,4},{4,8},{0,12},{13,1},{9,5},{5,9},{1,13},{14,2},{10,6},... | collective-permute-start | bytes 442376 | tf_op jit(solution)/shard_map/ppermute | solution.py:556
  71.2 7.7 %collective-permute-start.18 = (bf16[32,2304]{1,0:T(8,128)(2,1)S(1)}, bf16[32,2304]{1,0:T(8,128)(2,1)S(1)}, u32[]{:S(2)}, u32[]{:S(2)}) collective-permute-start(bf16[32,2304]{1,0:T(8,128)(2,1)S(1)} %get-tuple-element.72), channel_id=1, source_target_pairs={{4,0},{0,4},{12,8},{8,12},{5,1},{1,5},{13,9},{9,13},{6,2},{2,6},{1... | collective-permute-start | bytes 442376 | tf_op jit(solution)/shard_map/ppermute | solution.py:556
  71.9 9.2 %collective-permute-start.16 = (bf16[32,2304]{1,0:T(8,128)(2,1)S(1)}, bf16[32,2304]{1,0:T(8,128)(2,1)S(1)}, u32[]{:S(2)}, u32[]{:S(2)}) collective-permute-start(bf16[32,2304]{1,0:T(8,128)(2,1)S(1)} %get-tuple-element.65), channel_id=1, source_target_pairs={{8,0},{12,4},{0,8},{4,12},{9,1},{13,5},{1,9},{5,13},{10,2},{14,6},... | collective-permute-start | bytes 442376 | tf_op jit(solution)/shard_map/ppermute | solution.py:556
  72.4 9.9 %collective-permute-start.17 = (bf16[32,2304]{1,0:T(8,128)(2,1)S(1)}, bf16[32,2304]{1,0:T(8,128)(2,1)S(1)}, u32[]{:S(2)}, u32[]{:S(2)}) collective-permute-start(bf16[32,2304]{1,0:T(8,128)(2,1)S(1)} %get-tuple-element.66), channel_id=1, source_target_pairs={{12,0},{8,4},{4,8},{0,12},{13,1},{9,5},{5,9},{1,13},{14,2},{10,6},... | collective-permute-start | bytes 442376 | tf_op jit(solution)/shard_map/ppermute | solution.py:556
  73.3 2.7 %copy-start.3 = (bf16[576,1152]{1,0:T(8,128)(2,1)S(1)}, bf16[576,1152]{1,0:T(8,128)(2,1)}, u32[]{:S(2)}) copy-start(bf16[576,1152]{1,0:T(8,128)(2,1)} %refs_7_.3) | copy-start | bytes 3981316

commit v7 on v6

--- a/solution.py
+++ b/solution.py
@@ -162,14 +162,16 @@
     attend(masks, (a_ref, b_ref), query, finish)
 
 
-def remote_attend(frame, place, counts, lists, qn_ref, sum_ref, ra_ref, rb_ref, att):
-    n, _, tokens = qn_ref.shape
+def remote_attend(frame, place, counts, lists, qn_ref, sum_ref, ra_ref, rb_ref, att, done=None):
+    n, width, tokens = qn_ref.shape
 
     def query(f, h):
         return qn_ref[f, head(h), :]
 
     def finish(f, h, o):
         att[f, head(h), :] = averaged(o + sum_ref[f, sums(h), :]).astype(att.dtype)
+        if done and (h + 1) * HEAD_DIM == width:
+            done(f)
 
     masks = tile_masks(frame, n, tokens // TILE, False, place, counts, lists)
     attend(masks, (ra_ref, rb_ref), query, finish)
@@ -206,10 +208,12 @@
 
 def late_kernel(frame, n_groups, halves, place, counts, lists, qn_ref, sum_ref, ra_ref, rb_ref, *rest):
     outs, (att, rows) = rest[:n_groups * halves], rest[n_groups * halves:]
-    n, width, tokens = qn_ref.shape
-    remote_attend(frame, place, counts, lists, qn_ref, sum_ref, ra_ref, rb_ref, att)
-    for f in range(n):
+    _, width, tokens = qn_ref.shape
+
+    def turn(f):
         rows[:, f * width:(f + 1) * width] = att[f].T.astype(BF)
+
+    remote_attend(frame, place, counts, lists, qn_ref, sum_ref, ra_ref, rb_ref, att, turn)
     size = tokens // n_groups // halves
     for half in range(halves):
         for j in range(n_groups):
@@ -340,15 +344,18 @@
 
     def gather(c, h, p):
         att[c, head(h), :] = averaged(contract(with_ones(take(c, head(h, 2 * width))), p, 1, 0))
+        if (h + 1) * HEAD_DIM == width:
+            turn(c)
+
+    def turn(c):
+        turned = att[c].T.astype(BF)
+        for j, out in enumerate(outs):
+            for f in range(frames):
+                at = (f ^ (c & 1) if pair else f) * lanes + j * SUB
+                out[c * SUB:(c + 1) * SUB, f * width:(f + 1) * width] = turned[at:at + SUB, :]
 
     steps = [(c, h) for c in range(chunks) for h in range(width // HEAD_DIM)]
     pipeline(steps, scores, weigh, gather)
-    turned = [att[c].T.astype(BF) for c in range(chunks)]
-    for j, out in enumerate(outs):
-        for c in range(chunks):
-            for f in range(frames):
-                at = (f ^ (c & 1) if pair else f) * lanes + j * SUB
-                out[c * SUB:(c + 1) * SUB, f * width:(f + 1) * width] = turned[c][at:at + SUB, :]
 
 
 def output_kernel(n_groups, js, early, half, halves, aliased, place, *refs):

time: 85.2 us -> 85.1 us (level)
  no operation moved by 1% of the time
where the time goes in v7:
time: 85.1 us; the launch traced here: 84.7 us
  Pallas kernels  35.5 us (42%)
  waiting for transfers between devices  25.3 us (30%)
  starting transfers between devices  23.3 us (27%)
    ppermute x15, waiting for transfers between devices, send(): lax.ppermute(parts[j], 'frame', out_pairs(j))  12.5 us
    ppermute x2, waiting for transfers between devices, shards(): lax.ppermute(a, 'strip', near)  10.4 us
    ppermute x15, starting transfers between devices, send(): lax.ppermute(parts[j], 'frame', out_pairs(j))  10.1 us
    ppermute x2, starting transfers between devices, shards(): lax.ppermute(a, 'strip', near)  7.55 us
    pallas_call x3, Pallas kernels, shards(): call(functools.partial(output_kernel, groups, tuple(js), early, half, hal...  7.26 us
    pallas_call x2, Pallas kernels, shards(): call(functools.partial(local_kernel, some * late), [smem, smem, smem, blo...  4.78 us
    pallas_call x2, Pallas kernels, shards(): call(functools.partial(spatial_kernel, f, groups), [smem, smem, smem, one...  4.69 us
    pallas_call x2, Pallas kernels, shards(): call(functools.partial(late_project_kernel, early, frames), late_specs +...  4.33 us
  transfers between devices with their start and end apart: 25, of which 10 were waited for; matrix products, arithmetic and copies ran while one was open for 0% of the time, Pallas kernels for 34%

profile of v7, /device:TPU:0, one launch (start us, length us, event | category | flops | bytes accessed | tf_op | source)
XLA Modules:
  0.0 84.7 jit_solution(486876571363338949)
XLA Ops:
  0.0 0.1 pad_add_fusion.place
  0.1 1.5 %shard_map.109 = (bf16[2,1152,128]{2,1,0:T(8,128)(2,1)S(1)}, bf16[2,1152,128]{2,1,0:T(8,128)(2,1)S(1)}) custom-call(s32[2]{0:T(128)S(1)} %pad_add_fusion.place, bf16[4,576,256]{2,1,0:T(8,128)(2,1)} %bitcast.22, bf16[4,576,256]{2,1,0:T(8,128)(2,1)} %bitcast.24), custom_call_target="tpu_custom_call" | custom-call | tf_op jit(solution)/shard_map/pallas_call | solution.py:462
  1.6 3.1 %collective-permute-start = (bf16[2,1152,128]{2,1,0:T(8,128)(2,1)S(1)}, bf16[2,1152,128]{2,1,0:T(8,128)(2,1)S(1)}, u32[]{:S(2)}, u32[]{:S(2)}) collective-permute-start(bf16[2,1152,128]{2,1,0:T(8,128)(2,1)S(1)} %get-tuple-element.41.a_ref), channel_id=1, source_target_pairs={{0,1},{1,0},{2,3},{3,2},{4,5},{5,4},{6,7},{7,6},{8,9},{9,8},{10,11... | collective-permute-start | bytes 1769480 | tf_op jit(solution)/shard_map/ppermute | solution.py:473
  4.7 0.8 collective-permute-start.1
  5.5 0.0 copy-start.2
  5.5 2.7 %shard_map.115 = (bf16[2,1152,128]{2,1,0:T(8,128)(2,1)S(1)}, bf16[2,1152,128]{2,1,0:T(8,128)(2,1)S(1)}, bf16[2,64,1152]{2,1,0:T(8,128)(2,1)S(1)}, bf16[2,64,1152...) custom-call(s32[2]{0:T(128)S(1)} %pad_add_fusion.place, ...), custom_call_target="tpu_custom_call" | custom-call | tf_op jit(solution)/shard_map/pallas_call | solution.py:462
  8.2 0.0 copy-start.1
  8.2 4.4 %collective-permute-start.8 = (bf16[2,1152,128]{2,1,0:T(8,128)(2,1)S(1)}, bf16[2,1152,128]{2,1,0:T(8,128)(2,1)S(1)}, u32[]{:S(2)}, u32[]{:S(2)}) collective-permute-start(bf16[2,1152,128]{2,1,0:T(8,128)(2,1)S(1)} %get-tuple-element.53.a_ref), channel_id=1, source_target_pairs={{0,1},{1,0},{2,3},{3,2},{4,5},{5,4},{6,7},{7,6},{8,9},{9,8},{10,11... | collective-permute-start | bytes 1769480 | tf_op jit(solution)/shard_map/ppermute | solution.py:473
  12.7 0.7 collective-permute-start.9
  13.4 0.1 collective-permute-start.13
  13.4 5.4 %collective-permute-done.ra_ref = bf16[2,1152,128]{2,1,0:T(8,128)(2,1)S(1)} collective-permute-done((bf16[2,1152,128]{2,1,0:T(8,128)(2,1)S(1)}, bf16[2,1152,128]{2,1,0:T(8,128)(2,1)S(1)}, u32[]{:S(2)}, u32[]{:S(2)}) %collective-permute-start) | collective-permute-done | bytes 589856 | tf_op jit(solution)/shard_map/ppermute | solution.py:473
  18.9 2.0 %collective-permute-start.14 = (bf16[2,64,1152]{2,1,0:T(8,128)(2,1)S(1)}, bf16[2,64,1152]{2,1,0:T(8,128)(2,1)S(1)}, u32[]{:S(2)}, u32[]{:S(2)}) collective-permute-start(bf16[2,64,1152]{2,1,0:T(8,128)(2,1)S(1)} %get-tuple-element.63.refs_10_), channel_id=1, source_target_pairs={{0,8},{4,12},{8,0},{12,4},{1,9},{5,13},{9,1},{13,5},{2,10},{6,14},... | collective-permute-start | bytes 884744 | tf_op jit(solution)/shard_map/ppermute | solution.py:455
  20.8 0.0 collective-permute-done.1.rb_ref
  20.8 0.0 collective-permute-start.15
  20.9 2.4 %shard_map.110 = (bf16[2,576,256]{2,1,0:T(8,128)(2,1)S(1)}, f32[2,640,256]{2,1,0:T(8,128)S(1)}) custom-call(s32[2]{0:T(128)S(1)} %pad_add_fusion.place, s32[2,4]{1,0:T(2,128)S(1)} %bitcast.17, s32[3,2,4]{2,1,0:T(2,128)S(1)} %bitcast.12, bf16[4,576,256]{2,1,0:T(8,128)(2,1)} %bitcast.26, bf16[2,1152,128]{2,1,0:T(8,128)(2,1)S(1)} %get-tuple-element.41.a_ref, ...), custom_call_target="tpu_custom_call" | custom-call | tf_op jit(solution)/shard_map/pallas_call | solution.py:481
  23.3 2.3 %shard_map.111 = (bf16[1,64,1152]{2,1,0:T(8,128)(2,1)S(1)}, bf16[1,64,1152]{2,1,0:T(8,128)(2,1)S(1)}, bf16[1,64,1152]{2,1,0:T(8,128)(2,1)S(1)}, bf16[1,64,1152]{2,1,0:T(8,128)(2,1)S(1)}) custom-call(s32[2]{0:T(128)S(1)} %pad_add_fusion.place, s32[2,4]{1,0:T(2,128)S(1)} %bitcast.18, s32[3,2,4]{2,1,0:T(2,128)S(1)} %bitcast.13, ...), custom_call_target="tpu_custom_call" | custom-call | tf_op jit(solution)/shard_map/pallas_call | solution.py:499
  25.7 5.0 %collective-permute-done.8.ra_ref = bf16[2,1152,128]{2,1,0:T(8,128)(2,1)S(1)} collective-permute-done((bf16[2,1152,128]{2,1,0:T(8,128)(2,1)S(1)}, bf16[2,1152,128]{2,1,0:T(8,128)(2,1)S(1)}, u32[]{:S(2)}, u32[]{:S(2)}) %collective-permute-start.8) | collective-permute-done | bytes 589856 | tf_op jit(solution)/shard_map/ppermute | solution.py:473
  30.7 0.0 collective-permute-start.2
  30.7 2.4 %shard_map.116 = (bf16[2,576,256]{2,1,0:T(8,128)(2,1)S(1)}, f32[2,640,256]{2,1,0:T(8,128)S(1)}) custom-call(s32[2]{0:T(128)S(1)} %pad_add_fusion.place, s32[2,4]{1,0:T(2,128)S(1)} %bitcast.19, s32[3,2,4]{2,1,0:T(2,128)S(1)} %bitcast.14, bf16[4,576,256]{2,1,0:T(8,128)(2,1)} %bitcast.27, bf16[2,1152,128]{2,1,0:T(8,128)(2,1)S(1)} %get-tuple-element.53.a_ref, ...), custom_call_target="tpu_custom_call" | custom-call | tf_op jit(solution)/shard_map/pallas_call | solution.py:481
  33.1 0.0 collective-permute-done.9.rb_ref
  33.1 2.2 %shard_map.117 = (bf16[32,1152]{1,0:T(8,128)(2,1)S(1)}, bf16[32,1152]{1,0:T(8,128)(2,1)S(1)}, bf16[32,1152]{1,0:T(8,128)(2,1)S(1)}, bf16[32,1152]{1,0:T(8,128)(2...) custom-call(s32[2]{0:T(128)S(1)} %pad_add_fusion.place, ...), custom_call_target="tpu_custom_call" | custom-call | tf_op jit(solution)/shard_map/pallas_call | solution.py:524
  35.3 0.6 collective-permute-start.19
  35.9 0.0 collective-permute-done.13.refs_5_
  35.9 1.7 %collective-permute-start.20 = (bf16[32,1152]{1,0:T(8,128)(2,1)S(1)}, bf16[32,1152]{1,0:T(8,128)(2,1)S(1)}, u32[]{:S(2)}, u32[]{:S(2)}) collective-permute-start(bf16[32,1152]{1,0:T(8,128)(2,1)S(1)} %get-tuple-element.69.refs_2_), channel_id=1, source_target_pairs={{0,8},{4,12},{8,0},{12,4},{1,9},{5,13},{9,1},{13,5},{2,10},{6,14},... | collective-permute-start | bytes 221192 | tf_op jit(solution)/shard_map/ppermute | solution.py:455
  37.5 0.0 collective-permute-done.14.refs_6_
  37.6 0.0 collective-permute-start.21
  37.6 2.3 %shard_map.113 = (bf16[1,64,1152]{2,1,0:T(8,128)(2,1)S(1)}, bf16[1,64,1152]{2,1,0:T(8,128)(2,1)S(1)}, bf16[1,64,1152]{2,1,0:T(8,128)(2,1)S(1)}, bf16[1,64,1152]{2,1,0:T(8,128)(2,1)S(1)}) custom-call(s32[2]{0:T(128)S(1)} %pad_add_fusion.place, s32[2,4]{1,0:T(2,128)S(1)} %bitcast.21, s32[3,2,4]{2,1,0:T(2,128)S(1)} %bitcast.16, ...), custom_call_target="tpu_custom_call" | custom-call | tf_op jit(solution)/shard_map/pallas_call | solution.py:499
  39.9 0.0 collective-permute-done.15.refs_7_
  39.9 1.5 %collective-permute-start.3 = (bf16[1,64,1152]{2,1,0:T(8,128)(2,1)S(1)}, bf16[1,64,1152]{2,1,0:T(8,128)(2,1)S(1)}, u32[]{:S(2)}, u32[]{:S(2)}) collective-permute-start(bf16[1,64,1152]{2,1,0:T(8,128)(2,1)S(1)} %get-tuple-element.47.refs_8_.refs_2_), channel_id=1, source_target_pairs={{0,8},{4,12},{8,0},{12,4},{1,9},{5,13},{9,1},{13,5},{2,10},{6,14},... | collective-permute-start | bytes 442376 | tf_op jit(solution)/shard_map/ppermute | solution.py:455
  41.4 0.4 collective-permute-start.4
  41.8 0.3 collective-permute-start.5
  42.1 1.4 %collective-permute-start.6 = (bf16[1,64,1152]{2,1,0:T(8,128)(2,1)S(1)}, bf16[1,64,1152]{2,1,0:T(8,128)(2,1)S(1)}, u32[]{:S(2)}, u32[]{:S(2)}) collective-permute-start(bf16[1,64,1152]{2,1,0:T(8,128)(2,1)S(1)} %get-tuple-element.51.refs_9_.refs_3_), channel_id=1, source_target_pairs={{0,8},{4,12},{8,0},{12,4},{1,9},{5,13},{9,1},{13,5},{2,10},{6,14},... | collective-permute-start | bytes 442376 | tf_op jit(solution)/shard_map/ppermute | solution.py:455
  43.6 0.1 collective-permute-start.7
  43.7 2.2 %shard_map.121.refs_2_.refs_3_ = bf16[1728,256]{1,0:T(8,128)(2,1)S(1)} custom-call(bf16[32,1152]{1,0:T(8,128)(2,1)S(1)} %get-tuple-element.67.refs_0_, bf16[32,1152]{1,0:T(8,128)(2,1)S(1)} %collective-permute-done.19.refs_1_, bf16[32,1152]{1,0:T(8,128)(2,1)S(1)} %collective-permute-done.20.refs_2_, bf16[32,1152]{1,0:T(8,128)(2,1)S(1)} %collective-permute-done.21.refs_3_, ...), custom_call_target="tpu_custom_call" | custom-call | tf_op jit(solution)/shard_map/pallas_call | solution.py:543
  45.9 0.8 %collective-permute-done.3.refs_2_ = bf16[1,64,1152]{2,1,0:T(8,128)(2,1)S(1)} collective-permute-done((bf16[1,64,1152]{2,1,0:T(8,128)(2,1)S(1)}, bf16[1,64,1152]{2,1,0:T(8,128)(2,1)S(1)}, u32[]{:S(2)}, u32[]{:S(2)}) %collective-permute-start.3) | collective-permute-done | bytes 147488 | tf_op jit(solution)/shard_map/ppermute | solution.py:455
  46.7 2.1 %collective-permute-done.4.refs_3_ = bf16[1,64,1152]{2,1,0:T(8,128)(2,1)S(1)} collective-permute-done((bf16[1,64,1152]{2,1,0:T(8,128)(2,1)S(1)}, bf16[1,64,1152]{2,1,0:T(8,128)(2,1)S(1)}, u32[]{:S(2)}, u32[]{:S(2)}) %collective-permute-start.4) | collective-permute-done | bytes 147488 | tf_op jit(solution)/shard_map/ppermute | solution.py:455
  48.8 1.4 %shard_map.112.refs_0_ = bf16[1728,256]{1,0:T(8,128)(2,1)S(1)} custom-call(bf16[1,64,1152]{2,1,0:T(8,128)(2,1)S(1)} %get-tuple-element.45.refs_0_.refs_4_.refs_2_, bf16[1,64,1152]{2,1,0:T(8,128)(2,1)S(1)} %collective-permute-done.2.refs_1_, bf16[1,64,1152]{2,1,0:T(8,128)(2,1)S(1)} %collective-permute-done.3.refs_2_, ...), custom_call_target="tpu_custom_call" | custom-call | tf_op jit(solution)/shard_map/pallas_call | solution.py:514
  50.2 0.0 collective-permute-done.5.refs_1_
  50.2 2.8 %collective-permute-done.6.refs_2_ = bf16[1,64,1152]{2,1,0:T(8,128)(2,1)S(1)} collective-permute-done((bf16[1,64,1152]{2,1,0:T(8,128)(2,1)S(1)}, bf16[1,64,1152]{2,1,0:T(8,128)(2,1)S(1)}, u32[]{:S(2)}, u32[]{:S(2)}) %collective-permute-start.6) | collective-permute-done | bytes 147488 | tf_op jit(solution)/shard_map/ppermute | solution.py:455
  53.0 2.1 %collective-permute-done.7.refs_3_ = bf16[1,64,1152]{2,1,0:T(8,128)(2,1)S(1)} collective-permute-done((bf16[1,64,1152]{2,1,0:T(8,128)(2,1)S(1)}, bf16[1,64,1152]{2,1,0:T(8,128)(2,1)S(1)}, u32[]{:S(2)}, u32[]{:S(2)}) %collective-permute-start.7) | collective-permute-done | bytes 147488 | tf_op jit(solution)/shard_map/ppermute | solution.py:455
  55.2 1.4 %shard_map.114.refs_1_ = bf16[1728,256]{1,0:T(8,128)(2,1)S(1)} custom-call(bf16[1,64,1152]{2,1,0:T(8,128)(2,1)S(1)} %get-tuple-element.49.refs_0_.refs_5_.refs_3_, bf16[1,64,1152]{2,1,0:T(8,128)(2,1)S(1)} %collective-permute-done.5.refs_1_, bf16[1,64,1152]{2,1,0:T(8,128)(2,1)S(1)} %collective-permute-done.6.refs_2_, ...), custom_call_target="tpu_custom_call" | custom-call | tf_op jit(solution)/shard_map/pallas_call | solution.py:514
  56.5 2.0 %shard_map.122 = (bf16[32,2304]{1,0:T(8,128)(2,1)S(1)}, bf16[32,2304]{1,0:T(8,128)(2,1)S(1)}, bf16[32,2304]{1,0:T(8,128)(2,1)S(1)}, bf16[32,2304]{1,0:T(8,128)(2,1)S(1)}) custom-call(bf16[1728,256]{1,0:T(8,128)(2,1)S(1)} %shard_map.112.refs_0_, bf16[1728,256]{1,0:T(8,128)(2,1)S(1)} %shard_map.114.refs_1_, bf16[1728,256]{1,0:T(8,128)(2,1)S(1)} %shard_map.121.refs_2_.refs_3_, ...), custom_call_target="tpu_custom_call" | custom-call | tf_op jit(solution)/shard_map/pallas_call | solution.py:554
  58.5 0.4 collective-permute-start.22
  58.9 0.2 collective-permute-start.10
  59.1 1.9 %collective-permute-start.11 = (bf16[32,1152]{1,0:T(8,128)(2,1)S(1)}, bf16[32,1152]{1,0:T(8,128)(2,1)S(1)}, u32[]{:S(2)}, u32[]{:S(2)}) collective-permute-start(bf16[32,1152]{1,0:T(8,128)(2,1)S(1)} %get-tuple-element.59.refs_6_), channel_id=1, source_target_pairs={{0,8},{4,12},{8,0},{12,4},{1,9},{5,13},{9,1},{13,5},{2,10},{6,14},... | collective-permute-start | bytes 221192 | tf_op jit(solution)/shard_map/ppermute | solution.py:455
  61.0 0.0 collective-permute-start.12
  61.0 0.0 collective-permute-done.10.refs_1_
  61.0 2.6 %collective-permute-done.11.refs_2_ = bf16[32,1152]{1,0:T(8,128)(2,1)S(1)} collective-permute-done((bf16[32,1152]{1,0:T(8,128)(2,1)S(1)}, bf16[32,1152]{1,0:T(8,128)(2,1)S(1)}, u32[]{:S(2)}, u32[]{:S(2)}) %collective-permute-start.11) | collective-permute-done | bytes 73760 | tf_op jit(solution)/shard_map/ppermute | solution.py:455
  63.6 1.9 %collective-permute-done.12.refs_3_ = bf16[32,1152]{1,0:T(8,128)(2,1)S(1)} collective-permute-done((bf16[32,1152]{1,0:T(8,128)(2,1)S(1)}, bf16[32,1152]{1,0:T(8,128)(2,1)S(1)}, u32[]{:S(2)}, u32[]{:S(2)}) %collective-permute-start.12) | collective-permute-done | bytes 73760 | tf_op jit(solution)/shard_map/ppermute | solution.py:455
  65.5 2.2 %shard_map.118.refs_2_.refs_3_ = bf16[1728,256]{1,0:T(8,128)(2,1)S(1)} custom-call(bf16[32,1152]{1,0:T(8,128)(2,1)S(1)} %get-tuple-element.57.refs_0_.refs_4_, bf16[32,1152]{1,0:T(8,128)(2,1)S(1)} %collective-permute-done.10.refs_1_, bf16[32,1152]{1,0:T(8,128)(2,1)S(1)} %collective-permute-done.11.refs_2_, ...), custom_call_target="tpu_custom_call" | custom-call | tf_op jit(solution)/shard_map/pallas_call | solution.py:543
  67.7 0.6 collective-permute-start.23
  68.3 0.9 %collective-permute-start.24 = (bf16[32,2304]{1,0:T(8,128)(2,1)S(1)}, bf16[32,2304]{1,0:T(8,128)(2,1)S(1)}, u32[]{:S(2)}, u32[]{:S(2)}) collective-permute-start(bf16[32,2304]{1,0:T(8,128)(2,1)S(1)} %get-tuple-element.76), channel_id=1, source_target_pairs={{12,0},{8,4},{4,8},{0,12},{13,1},{9,5},{5,9},{1,13},{14,2},{10,6},... | collective-permute-start | bytes 442376 | tf_op jit(solution)/shard_map/ppermute | solution.py:563
  69.3 1.8 %shard_map.119 = (bf16[32,2304]{1,0:T(8,128)(2,1)S(1)}, bf16[32,2304]{1,0:T(8,128)(2,1)S(1)}, bf16[32,2304]{1,0:T(8,128)(2,1)S(1)}, bf16[32,2304]{1,0:T(8,128)(2,1)S(1)}) custom-call(bf16[1728,256]{1,0:T(8,128)(2,1)S(1)} %shard_map.112.refs_0_, bf16[1728,256]{1,0:T(8,128)(2,1)S(1)} %shard_map.114.refs_1_, bf16[1728,256]{1,0:T(8,128)(2,1)S(1)} %shard_map.118.refs_2_.refs_3_, ...), custom_call_target="tpu_custom_call" | custom-call | tf_op jit(solution)/shard_map/pallas_call | solution.py:554
  71.1 0.7 collective-permute-start.18
  71.8 0.5 collective-permute-start.16
  72.4 0.0 collective-permute-done.22.refs_1_
  72.4 0.9 %collective-permute-start.17 = (bf16[32,2304]{1,0:T(8,128)(2,1)S(1)}, bf16[32,2304]{1,0:T(8,128)(2,1)S(1)}, u32[]{:S(2)}, u32[]{:S(2)}) collective-permute-start(bf16[32,2304]{1,0:T(8,128)(2,1)S(1)} %get-tuple-element.66), channel_id=1, source_target_pairs={{12,0},{8,4},{4,8},{0,12},{13,1},{9,5},{5,9},{1,13},{14,2},{10,6},... | collective-permute-start | bytes 442376 | tf_op jit(solution)/shard_map/ppermute | solution.py:563
  73.3 1.5 %shard_map.120.refs_12_.refs_6_ = bf16[4,2,64,1152]{3,2,1,0:T(8,128)(2,1)S(1)} custom-call(bf16[32,1152]{1,0:T(8,128)(2,1)S(1)} %get-tuple-element.67.refs_0_, bf16[32,1152]{1,0:T(8,128)(2,1)S(1)} %get-tuple-element.68.refs_1_, bf16[32,1152]{1,0:T(8,128)(2,1)S(1)} %get-tuple-element.69.refs_2_, bf16[32,1152]{1,0:T(8,128)(2,1)S(1)} %get-tuple-element.70.refs_3_, ...), custom_call_target="tpu_custom_call" | custom-call | tf_op jit(solution)/shard_map/pallas_call | solution.py:568
  74.8 0.0 collective-permute-done.23.refs_2_
  74.9 1.1 %collective-permute-done.24.refs_3_ = bf16[32,2304]{1,0:T(8,128)(2,1)S(1)} collective-permute-done((bf16[32,2304]{1,0:T(8,128)(2,1)S(1)}, bf16[32,2304]{1,0:T(8,128)(2,1)S(1)}, u32[]{:S(2)}, u32[]{:S(2)}) %collective-permute-start.24) | collective-permute-done | bytes 147488 | tf_op jit(solution)/shard_map/ppermute | solution.py:563
  76.0 2.8 %shard_map.123.refs_9_ = bf16[4,256,1152]{2,1,0:T(8,128)(2,1)} custom-call(s32[2]{0:T(128)S(1)} %pad_add_fusion.place, bf16[32,2304]{1,0:T(8,128)(2,1)S(1)} %get-tuple-element.73.refs_0_, bf16[32,2304]{1,0:T(8,128)(2,1)S(1)} %collective-permute-done.22.refs_1_, bf16[32,2304]{1,0:T(8,128)(2,1)S(1)} %collective-permute-done.23.refs_2_, ...), custom_call_target="tpu_custom_call" | custom-call | tf_op jit(solution)/shard_map/pallas_call | solution.py:586
  78.8 2.2 %shard_map.124.refs_9_ = bf16[4,256,1152]{2,1,0:T(8,128)(2,1)} custom-call(s32[2]{0:T(128)S(1)} %pad_add_fusion.place, bf16[32,2304]{1,0:T(8,128)(2,1)S(1)} %get-tuple-element.71.refs_0_, bf16[32,2304]{1,0:T(8,128)(2,1)S(1)} %collective-permute-done.18.refs_1_, ...), custom_call_target="tpu_custom_call", output_to_operand_aliasing={{}: (10, {})} | custom-call | tf_op jit(solution)/shard_map/pallas_call | solution.py:586
  81.0 1.2 %collective-permute-done.17.refs_1_ = bf16[32,2304]{1,0:T(8,128)(2,1)S(1)} collective-permute-done((bf16[32,2304]{1,0:T(8,128)(2,1)S(1)}, bf16[32,2304]{1,0:T(8,128)(2,1)S(1)}, u32[]{:S(2)}, u32[]{:S(2)}) %collective-permute-start.17) | collective-permute-done | bytes 147488 | tf_op jit(solution)/shard_map/ppermute | solution.py:563
  82.3 2.2 %shard_map.125 = bf16[4,256,1152]{2,1,0:T(8,128)(2,1)} custom-call(s32[2]{0:T(128)S(1)} %pad_add_fusion.place, bf16[32,2304]{1,0:T(8,128)(2,1)S(1)} %collective-permute-done.16.refs_0_, bf16[32,2304]{1,0:T(8,128)(2,1)S(1)} %collective-permute-done.17.refs_1_, ...), custom_call_target="tpu_custom_call", output_to_operand_aliasing={{}: (10, {})} | custom-call | tf_op jit(solution)/shard_map/pallas_call | solution.py:586
  (22 shorter events, 0.1 us)
Async XLA Ops:
  1.6 17.3 %collective-permute-start = (bf16[2,1152,128]{2,1,0:T(8,128)(2,1)S(1)}, bf16[2,1152,128]{2,1,0:T(8,128)(2,1)S(1)}, u32[]{:S(2)}, u32[]{:S(2)}) collective-permute-start(bf16[2,1152,128]{2,1,0:T(8,128)(2,1)S(1)} %get-tuple-element.41.a_ref), channel_id=1, source_target_pairs={{0,1},{1,0},{2,3},{3,2},{4,5},{5,4},{6,7},{7,6},{8,9},{9,8},{10,11... | collective-permute-start | bytes 1769480 | tf_op jit(solution)/shard_map/ppermute | solution.py:473
  4.7 16.1 %copy-start.6 = (f32[1152]{0:T(1024)S(1)}, f32[1152]{0:T(1024)}, u32[]{:S(2)}) copy-start(f32[1152]{0:T(1024)} %param.16) | copy-start | bytes 13828
  4.7 16.2 %copy-start.4 = (s32[4,2,3]{0,1,2:T(2,128)S(1)}, s32[4,2,3]{0,1,2:T(2,128)}, u32[]{:S(2)}) copy-start(s32[4,2,3]{0,1,2:T(2,128)} %param.20) | copy-start | bytes 292
  4.7 16.2 %copy-start.5 = (s32[4,2]{0,1:T(2,128)S(1)}, s32[4,2]{0,1:T(2,128)}, u32[]{:S(2)}) copy-start(s32[4,2]{0,1:T(2,128)} %param.21) | copy-start | bytes 100
  4.7 16.1 %collective-permute-start.1 = (bf16[2,1152,128]{2,1,0:T(8,128)(2,1)S(1)}, bf16[2,1152,128]{2,1,0:T(8,128)(2,1)S(1)}, u32[]{:S(2)}, u32[]{:S(2)}) collective-permute-start(bf16[2,1152,128]{2,1,0:T(8,128)(2,1)S(1)} %get-tuple-element.42.b_ref), channel_id=1, source_target_pairs={{1,2},{2,1},{5,6},{6,5},{9,10},{10,9},{13,14},{14,13},{17,18},{18,... | collective-permute-start | bytes 1769480 | tf_op jit(solution)/shard_map/ppermute | solution.py:473
  5.5 17.8 %copy-start.2 = (bf16[4,256,1152]{2,1,0:T(8,128)(2,1)S(1)}, bf16[4,256,1152]{2,1,0:T(8,128)(2,1)}, u32[]{:S(2)}) copy-start(bf16[4,256,1152]{2,1,0:T(8,128)(2,1)} %refs_0_.1) | copy-start | bytes 7077892
  8.2 15.1 %copy-start.1 = (bf16[576,1152]{1,0:T(8,128)(2,1)S(1)}, bf16[576,1152]{1,0:T(8,128)(2,1)}, u32[]{:S(2)}) copy-start(bf16[576,1152]{1,0:T(8,128)(2,1)} %refs_8_.3) | copy-start | bytes 3981316
  8.2 22.4 %collective-permute-start.8 = (bf16[2,1152,128]{2,1,0:T(8,128)(2,1)S(1)}, bf16[2,1152,128]{2,1,0:T(8,128)(2,1)S(1)}, u32[]{:S(2)}, u32[]{:S(2)}) collective-permute-start(bf16[2,1152,128]{2,1,0:T(8,128)(2,1)S(1)} %get-tuple-element.53.a_ref), channel_id=1, source_target_pairs={{0,1},{1,0},{2,3},{3,2},{4,5},{5,4},{6,7},{7,6},{8,9},{9,8},{10,11... | collective-permute-start | bytes 1769480 | tf_op jit(solution)/shard_map/ppermute | solution.py:473
  12.7 20.4 %collective-permute-start.9 = (bf16[2,1152,128]{2,1,0:T(8,128)(2,1)S(1)}, bf16[2,1152,128]{2,1,0:T(8,128)(2,1)S(1)}, u32[]{:S(2)}, u32[]{:S(2)}) collective-permute-start(bf16[2,1152,128]{2,1,0:T(8,128)(2,1)S(1)} %get-tuple-element.54.b_ref), channel_id=1, source_target_pairs={{1,2},{2,1},{5,6},{6,5},{9,10},{10,9},{13,14},{14,13},{17,18},{18,... | collective-permute-start | bytes 1769480 | tf_op jit(solution)/shard_map/ppermute | solution.py:473
  13.4 22.5 %collective-permute-start.13 = (bf16[2,64,1152]{2,1,0:T(8,128)(2,1)S(1)}, bf16[2,64,1152]{2,1,0:T(8,128)(2,1)S(1)}, u32[]{:S(2)}, u32[]{:S(2)}) collective-permute-start(bf16[2,64,1152]{2,1,0:T(8,128)(2,1)S(1)} %get-tuple-element.62.refs_9_), channel_id=1, source_target_pairs={{0,4},{4,0},{8,12},{12,8},{1,5},{5,1},{9,13},{13,9},{2,6},{6,2},{1... | collective-permute-start | bytes 884744 | tf_op jit(solution)/shard_map/ppermute | solution.py:455
  18.9 18.7 %collective-permute-start.14 = (bf16[2,64,1152]{2,1,0:T(8,128)(2,1)S(1)}, bf16[2,64,1152]{2,1,0:T(8,128)(2,1)S(1)}, u32[]{:S(2)}, u32[]{:S(2)}) collective-permute-start(bf16[2,64,1152]{2,1,0:T(8,128)(2,1)S(1)} %get-tuple-element.63.refs_10_), channel_id=1, source_target_pairs={{0,8},{4,12},{8,0},{12,4},{1,9},{5,13},{9,1},{13,5},{2,10},{6,14},... | collective-permute-start | bytes 884744 | tf_op jit(solution)/shard_map/ppermute | solution.py:455
  20.8 19.1 %collective-permute-start.15 = (bf16[2,64,1152]{2,1,0:T(8,128)(2,1)S(1)}, bf16[2,64,1152]{2,1,0:T(8,128)(2,1)S(1)}, u32[]{:S(2)}, u32[]{:S(2)}) collective-permute-start(bf16[2,64,1152]{2,1,0:T(8,128)(2,1)S(1)} %get-tuple-element.64.refs_11_), channel_id=1, source_target_pairs={{0,12},{4,8},{8,4},{12,0},{1,13},{5,9},{9,5},{13,1},{2,14},{6,10},... | collective-permute-start | bytes 884744 | tf_op jit(solution)/shard_map/ppermute | solution.py:455
  30.7 12.9 %collective-permute-start.2 = (bf16[1,64,1152]{2,1,0:T(8,128)(2,1)S(1)}, bf16[1,64,1152]{2,1,0:T(8,128)(2,1)S(1)}, u32[]{:S(2)}, u32[]{:S(2)}) collective-permute-start(bf16[1,64,1152]{2,1,0:T(8,128)(2,1)S(1)} %get-tuple-element.46.refs_6_.refs_4_), channel_id=1, source_target_pairs={{0,4},{4,0},{8,12},{12,8},{1,5},{5,1},{9,13},{13,9},{2,6},{6,2},{1... | collective-permute-start | bytes 442376 | tf_op jit(solution)/shard_map/ppermute | solution.py:455
  35.3 6.1 %collective-permute-start.19 = (bf16[32,1152]{1,0:T(8,128)(2,1)S(1)}, bf16[32,1152]{1,0:T(8,128)(2,1)S(1)}, u32[]{:S(2)}, u32[]{:S(2)}) collective-permute-start(bf16[32,1152]{1,0:T(8,128)(2,1)S(1)} %get-tuple-element.68.refs_1_), channel_id=1, source_target_pairs={{0,4},{4,0},{8,12},{12,8},{1,5},{5,1},{9,13},{13,9},{2,6},{6,2},{1... | collective-permute-start | bytes 221192 | tf_op jit(solution)/shard_map/ppermute | solution.py:455
  35.9 5.9 %collective-permute-start.20 = (bf16[32,1152]{1,0:T(8,128)(2,1)S(1)}, bf16[32,1152]{1,0:T(8,128)(2,1)S(1)}, u32[]{:S(2)}, u32[]{:S(2)}) collective-permute-start(bf16[32,1152]{1,0:T(8,128)(2,1)S(1)} %get-tuple-element.69.refs_2_), channel_id=1, source_target_pairs={{0,8},{4,12},{8,0},{12,4},{1,9},{5,13},{9,1},{13,5},{2,10},{6,14},... | collective-permute-start | bytes 221192 | tf_op jit(solution)/shard_map/ppermute | solution.py:455
  37.6 4.6 %collective-permute-start.21 = (bf16[32,1152]{1,0:T(8,128)(2,1)S(1)}, bf16[32,1152]{1,0:T(8,128)(2,1)S(1)}, u32[]{:S(2)}, u32[]{:S(2)}) collective-permute-start(bf16[32,1152]{1,0:T(8,128)(2,1)S(1)} %get-tuple-element.70.refs_3_), channel_id=1, source_target_pairs={{0,12},{4,8},{8,4},{12,0},{1,13},{5,9},{9,5},{13,1},{2,14},{6,10},... | collective-permute-start | bytes 221192 | tf_op jit(solution)/shard_map/ppermute | solution.py:455
  37.6 6.1 %copy-start = (bf16[1152,1728]{0,1:T(8,128)(2,1)S(1)}, bf16[1152,1728]{0,1:T(8,128)(2,1)}, u32[]{:S(2)}) copy-start(bf16[1152,1728]{0,1:T(8,128)(2,1)} %param.17) | copy-start | bytes 11943940
  39.9 6.8 %collective-permute-start.3 = (bf16[1,64,1152]{2,1,0:T(8,128)(2,1)S(1)}, bf16[1,64,1152]{2,1,0:T(8,128)(2,1)S(1)}, u32[]{:S(2)}, u32[]{:S(2)}) collective-permute-start(bf16[1,64,1152]{2,1,0:T(8,128)(2,1)S(1)} %get-tuple-element.47.refs_8_.refs_2_), channel_id=1, source_target_pairs={{0,8},{4,12},{8,0},{12,4},{1,9},{5,13},{9,1},{13,5},{2,10},{6,14},... | collective-permute-start | bytes 442376 | tf_op jit(solution)/shard_map/ppermute | solution.py:455
  41.4 7.4 %collective-permute-start.4 = (bf16[1,64,1152]{2,1,0:T(8,128)(2,1)S(1)}, bf16[1,64,1152]{2,1,0:T(8,128)(2,1)S(1)}, u32[]{:S(2)}, u32[]{:S(2)}) collective-permute-start(bf16[1,64,1152]{2,1,0:T(8,128)(2,1)S(1)} %get-tuple-element.48.refs_10_.refs_4_), channel_id=1, source_target_pairs={{0,12},{4,8},{8,4},{12,0},{1,13},{5,9},{9,5},{13,1},{2,14},{6,10},... | collective-permute-start | bytes 442376 | tf_op jit(solution)/shard_map/ppermute | solution.py:455
  41.8 8.4 %collective-permute-start.5 = (bf16[1,64,1152]{2,1,0:T(8,128)(2,1)S(1)}, bf16[1,64,1152]{2,1,0:T(8,128)(2,1)S(1)}, u32[]{:S(2)}, u32[]{:S(2)}) collective-permute-start(bf16[1,64,1152]{2,1,0:T(8,128)(2,1)S(1)} %get-tuple-element.50.refs_7_.refs_5_), channel_id=1, source_target_pairs={{0,4},{4,0},{8,12},{12,8},{1,5},{5,1},{9,13},{13,9},{2,6},{6,2},{1... | collective-permute-start | bytes 442376 | tf_op jit(solution)/shard_map/ppermute | solution.py:455
  42.1 10.9 %collective-permute-start.6 = (bf16[1,64,1152]{2,1,0:T(8,128)(2,1)S(1)}, bf16[1,64,1152]{2,1,0:T(8,128)(2,1)S(1)}, u32[]{:S(2)}, u32[]{:S(2)}) collective-permute-start(bf16[1,64,1152]{2,1,0:T(8,128)(2,1)S(1)} %get-tuple-element.51.refs_9_.refs_3_), channel_id=1, source_target_pairs={{0,8},{4,12},{8,0},{12,4},{1,9},{5,13},{9,1},{13,5},{2,10},{6,14},... | collective-permute-start | bytes 442376 | tf_op jit(solution)/shard_map/ppermute | solution.py:455
  43.6 11.6 %collective-permute-start.7 = (bf16[1,64,1152]{2,1,0:T(8,128)(2,1)S(1)}, bf16[1,64,1152]{2,1,0:T(8,128)(2,1)S(1)}, u32[]{:S(2)}, u32[]{:S(2)}) collective-permute-start(bf16[1,64,1152]{2,1,0:T(8,128)(2,1)S(1)} %get-tuple-element.52.refs_11_.refs_5_), channel_id=1, source_target_pairs={{0,12},{4,8},{8,4},{12,0},{1,13},{5,9},{9,5},{13,1},{2,14},{6,10},... | collective-permute-start | bytes 442376 | tf_op jit(solution)/shard_map/ppermute | solution.py:455
  58.5 13.9 %collective-permute-start.22 = (bf16[32,2304]{1,0:T(8,128)(2,1)S(1)}, bf16[32,2304]{1,0:T(8,128)(2,1)S(1)}, u32[]{:S(2)}, u32[]{:S(2)}) collective-permute-start(bf16[32,2304]{1,0:T(8,128)(2,1)S(1)} %get-tuple-element.74), channel_id=1, source_target_pairs={{4,0},{0,4},{12,8},{8,12},{5,1},{1,5},{13,9},{9,13},{6,2},{2,6},{1... | collective-permute-start | bytes 442376 | tf_op jit(solution)/shard_map/ppermute | solution.py:563
  58.9 2.1 %collective-permute-start.10 = (bf16[32,1152]{1,0:T(8,128)(2,1)S(1)}, bf16[32,1152]{1,0:T(8,128)(2,1)S(1)}, u32[]{:S(2)}, u32[]{:S(2)}) collective-permute-start(bf16[32,1152]{1,0:T(8,128)(2,1)S(1)} %get-tuple-element.58.refs_5_), channel_id=1, source_target_pairs={{0,4},{4,0},{8,12},{12,8},{1,5},{5,1},{9,13},{13,9},{2,6},{6,2},{1... | collective-permute-start | bytes 221192 | tf_op jit(solution)/shard_map/ppermute | solution.py:455
  59.1 4.5 %collective-permute-start.11 = (bf16[32,1152]{1,0:T(8,128)(2,1)S(1)}, bf16[32,1152]{1,0:T(8,128)(2,1)S(1)}, u32[]{:S(2)}, u32[]{:S(2)}) collective-permute-start(bf16[32,1152]{1,0:T(8,128)(2,1)S(1)} %get-tuple-element.59.refs_6_), channel_id=1, source_target_pairs={{0,8},{4,12},{8,0},{12,4},{1,9},{5,13},{9,1},{13,5},{2,10},{6,14},... | collective-permute-start | bytes 221192 | tf_op jit(solution)/shard_map/ppermute | solution.py:455
  61.0 4.5 %collective-permute-start.12 = (bf16[32,1152]{1,0:T(8,128)(2,1)S(1)}, bf16[32,1152]{1,0:T(8,128)(2,1)S(1)}, u32[]{:S(2)}, u32[]{:S(2)}) collective-permute-start(bf16[32,1152]{1,0:T(8,128)(2,1)S(1)} %get-tuple-element.60.refs_7_), channel_id=1, source_target_pairs={{0,12},{4,8},{8,4},{12,0},{1,13},{5,9},{9,5},{13,1},{2,14},{6,10},... | collective-permute-start | bytes 221192 | tf_op jit(solution)/shard_map/ppermute | solution.py:455
  67.7 7.1 %collective-permute-start.23 = (bf16[32,2304]{1,0:T(8,128)(2,1)S(1)}, bf16[32,2304]{1,0:T(8,128)(2,1)S(1)}, u32[]{:S(2)}, u32[]{:S(2)}) collective-permute-start(bf16[32,2304]{1,0:T(8,128)(2,1)S(1)} %get-tuple-element.75), channel_id=1, source_target_pairs={{8,0},{12,4},{0,8},{4,12},{9,1},{13,5},{1,9},{5,13},{10,2},{14,6},... | collective-permute-start | bytes 442376 | tf_op jit(solution)/shard_map/ppermute | solution.py:563
  68.3 5.0 %copy-start.7 = (f32[1152]{0:T(1024)S(1)}, f32[1152]{0:T(1024)}, u32[]{:S(2)}) copy-start(f32[1152]{0:T(1024)} %param.19) | copy-start | bytes 13828
  68.3 7.6 %collective-permute-start.24 = (bf16[32,2304]{1,0:T(8,128)(2,1)S(1)}, bf16[32,2304]{1,0:T(8,128)(2,1)S(1)}, u32[]{:S(2)}, u32[]{:S(2)}) collective-permute-start(bf16[32,2304]{1,0:T(8,128)(2,1)S(1)} %get-tuple-element.76), channel_id=1, source_target_pairs={{12,0},{8,4},{4,8},{0,12},{13,1},{9,5},{5,9},{1,13},{14,2},{10,6},... | collective-permute-start | bytes 442376 | tf_op jit(solution)/shard_map/ppermute | solution.py:563
  71.1 7.7 %collective-permute-start.18 = (bf16[32,2304]{1,0:T(8,128)(2,1)S(1)}, bf16[32,2304]{1,0:T(8,128)(2,1)S(1)}, u32[]{:S(2)}, u32[]{:S(2)}) collective-permute-start(bf16[32,2304]{1,0:T(8,128)(2,1)S(1)} %get-tuple-element.72), channel_id=1, source_target_pairs={{4,0},{0,4},{12,8},{8,12},{5,1},{1,5},{13,9},{9,13},{6,2},{2,6},{1... | collective-permute-start | bytes 442376 | tf_op jit(solution)/shard_map/ppermute | solution.py:563
  71.8 9.2 %collective-permute-start.16 = (bf16[32,2304]{1,0:T(8,128)(2,1)S(1)}, bf16[32,2304]{1,0:T(8,128)(2,1)S(1)}, u32[]{:S(2)}, u32[]{:S(2)}) collective-permute-start(bf16[32,2304]{1,0:T(8,128)(2,1)S(1)} %get-tuple-element.65), channel_id=1, source_target_pairs={{8,0},{12,4},{0,8},{4,12},{9,1},{13,5},{1,9},{5,13},{10,2},{14,6},... | collective-permute-start | bytes 442376 | tf_op jit(solution)/shard_map/ppermute | solution.py:563
  72.4 9.9 %collective-permute-start.17 = (bf16[32,2304]{1,0:T(8,128)(2,1)S(1)}, bf16[32,2304]{1,0:T(8,128)(2,1)S(1)}, u32[]{:S(2)}, u32[]{:S(2)}) collective-permute-start(bf16[32,2304]{1,0:T(8,128)(2,1)S(1)} %get-tuple-element.66), channel_id=1, source_target_pairs={{12,0},{8,4},{4,8},{0,12},{13,1},{9,5},{5,9},{1,13},{14,2},{10,6},... | collective-permute-start | bytes 442376 | tf_op jit(solution)/shard_map/ppermute | solution.py:563
  73.3 2.7 %copy-start.3 = (bf16[576,1152]{1,0:T(8,128)(2,1)S(1)}, bf16[576,1152]{1,0:T(8,128)(2,1)}, u32[]{:S(2)}) copy-start(bf16[576,1152]{1,0:T(8,128)(2,1)} %refs_7_.3) | copy-start | bytes 3981316

commit v8 on v7

--- a/solution.py
+++ b/solution.py
@@ -211,7 +211,7 @@
     _, width, tokens = qn_ref.shape
 
     def turn(f):
-        rows[:, f * width:(f + 1) * width] = att[f].T.astype(BF)
+        rows[:, f * width:(f + 1) * width] = att[f].T
 
     remote_attend(frame, place, counts, lists, qn_ref, sum_ref, ra_ref, rb_ref, att, turn)
     size = tokens // n_groups // halves
@@ -274,7 +274,8 @@
         y = parts[i][at:at + HEAD_DIM, :]
         if h < 2 * heads:
             y = y * head_scale(y)
-        out[head(h), :] = y.astype(BF)
+        pad = jnp.full((8, y.shape[1]), 0.0 if h < 2 * heads else 1.0, F32)
+        out[sums(h), :] = jnp.concatenate([y, pad], axis=0).astype(BF)
 
 
 def project_kernel(frame, frames, *refs):
@@ -293,7 +294,8 @@
     atts, hids = refs[:n_groups], refs[n_groups:2 * n_groups]
     w_ref, g_ref, qkv_ref, out, a, b, x = refs[2 * n_groups:]
     width = w_ref.shape[0]
-    n, rows, _ = hids[0].shape
+    n = hids[0].shape[0]
+    rows = atts[0].shape[0]
     chunks = rows // SUB
     for f in range(n):
         for c in range(chunks):
@@ -310,24 +312,29 @@
     project(qkv_ref, x[...], out)
 
 
-def temporal_kernel(n_groups, *refs):
-    frames = len(refs) - n_groups - 1
-    ins, outs, att = refs[:frames], refs[frames:frames + n_groups], refs[-1]
+def temporal_kernel(n_groups, late, half, span, *refs):
+    early_refs, late_ref = refs[:-n_groups - 2], refs[-n_groups - 2]
+    outs, att = refs[-n_groups - 1:-1], refs[-1]
+    early = len(early_refs)
+    frames = early + late
+    ins = [(ref, half * span) for ref in early_refs] + [(late_ref, f * span) for f in range(late)]
     lanes = n_groups * SUB
-    chunks = ins[0].shape[1] // lanes
-    width = ins[0].shape[0] // 3
+    chunks = span // lanes
+    heads = late_ref.shape[0] // 3 // (HEAD_DIM + 8)
+    width = heads * HEAD_DIM
     rows = frames * lanes
     pair = paired(chunks, lanes, frames)
     row_pos = lax.broadcasted_iota(jnp.int32, (rows, rows), 0) % SUB
     col_pos = lax.broadcasted_iota(jnp.int32, (rows, rows), 1) % SUB
     same = jnp.where(row_pos == col_pos, 1.0, 0.0).astype(BF)
-    low = lax.broadcasted_iota(jnp.int32, (HEAD_DIM, TILE), 1) < lanes
+    low = lax.broadcasted_iota(jnp.int32, (HEAD_DIM + 8, TILE), 1) < lanes
 
     def take(c, where):
         if not pair:
-            return jnp.concatenate([r[where, c * lanes:(c + 1) * lanes] for r in ins], axis=1)
-        tile = slice(c // 2 * TILE, (c // 2 + 1) * TILE)
-        got = [r[where, tile] for r in ins]
+            return jnp.concatenate(
+                [r[where, at + c * lanes:at + (c + 1) * lanes] for r, at in ins], axis=1
+            )
+        got = [r[where, at + c // 2 * TILE:at + (c // 2 + 1) * TILE] for r, at in ins]
         return jnp.concatenate(
             [
                 jnp.where(low, got[m + (c & 1)], got[m + 1 - (c & 1)])
@@ -337,24 +344,24 @@
         )
 
     def scores(c, h):
-        return contract(take(c, head(h, width)), take(c, head(h)), 0, 0)
+        return contract(take(c, sums(heads + h)), take(c, sums(h)), 0, 0)
 
     def weigh(s):
         return jnp.exp2(s * EXP2_SCALE).astype(BF) * same
 
     def gather(c, h, p):
-        att[c, head(h), :] = averaged(contract(with_ones(take(c, head(h, 2 * width))), p, 1, 0))
-        if (h + 1) * HEAD_DIM == width:
+        att[c, head(h), :] = averaged(contract(take(c, sums(2 * heads + h)), p, 1, 0)).astype(BF)
+        if h + 1 == heads:
             turn(c)
 
     def turn(c):
-        turned = att[c].T.astype(BF)
+        turned = att[c].T
         for j, out in enumerate(outs):
             for f in range(frames):
                 at = (f ^ (c & 1) if pair else f) * lanes + j * SUB
                 out[c * SUB:(c + 1) * SUB, f * width:(f + 1) * width] = turned[at:at + SUB, :]
 
-    steps = [(c, h) for c in range(chunks) for h in range(width // HEAD_DIM)]
+    steps = [(c, h) for c in range(chunks) for h in range(heads)]
     pipeline(steps, scores, weigh, gather)
 
 
@@ -363,7 +370,9 @@
     atts, pieces = refs[:n], refs[n:n * (1 + early)]
     late_ref, w_ref, g_ref = refs[n * (1 + early):n * (1 + early) + 3]
     out, buf, sems = refs[n * (1 + early) + 3 + aliased:]
-    _, late, rows, _ = late_ref.shape
+    late = late_ref.shape[1]
+    rows = atts[0].shape[0]
+    cut = slice(half * rows, (half + 1) * rows)
     width = w_ref.shape[0]
     frames = early + late
     copies = []
@@ -377,7 +386,7 @@
             for k, i in enumerate(some):
                 j = js[i]
                 for f in range(frames):
-                    mine = pieces[i * early + f][0] if f < early else late_ref[j, f - early]
+                    mine = pieces[i * early + f][0, cut, :] if f < early else late_ref[j, f - early, cut, :]
                     at = (k * frames + f) * rows
                     part = normed[at:at + rows, :] * g_ref[...]
                     buf[i, f] = (mine.astype(F32) + part).astype(BF)
@@ -473,7 +482,9 @@
         halos.append((a, b, lax.ppermute(a, "strip", near), lax.ppermute(b, "strip", far)))
     far_hidden = send(own_hidden)
 
-    sum_shape = (late, width // HEAD_DIM * (HEAD_DIM + 8), tokens)
+    padded = width // HEAD_DIM * (HEAD_DIM + 8)
+    qkv_rows = 3 * padded
+    sum_shape = (late, padded, tokens)
     own_sums = []
     for some in range(2):
         block = pl.BlockSpec((late, width, tokens), lambda *_, some=some: (some, 0, 0))
@@ -514,8 +525,8 @@
             call(
                 functools.partial(project_kernel, f, frames),
                 [whole((1, share, model))] * groups + [whole((3 * width, model))],
-                whole((3 * width, tokens)),
-                jax.ShapeDtypeStruct((3 * width, tokens), BF),
+                whole((qkv_rows, tokens)),
+                jax.ShapeDtypeStruct((qkv_rows, tokens), BF),
                 [pltpu.VMEM((tokens, model), BF)],
             )(*arrived, qkv_weight)
         )
@@ -526,7 +537,7 @@
         [smem, smem, smem] + sum_specs + [whole((late,) + edge.shape)] * 2,
         [whole(late_shape)] * (groups * halves),
         [jax.ShapeDtypeStruct(late_shape, BF)] * (groups * halves),
-        [pltpu.VMEM((late, width, tokens), F32), pltpu.VMEM((tokens, late * width), BF)],
+        [pltpu.VMEM((late, width, tokens), BF), pltpu.VMEM((tokens, late * width), BF)],
     )(place, counts, lists, *own_sums[1], *halos[1][2:])
     own_late = [own_late[half * groups:(half + 1) * groups] for half in range(halves)]
     far_late = []
@@ -543,8 +554,8 @@
         late_projected = call(
             functools.partial(late_project_kernel, early, frames),
             late_specs + [whole((3 * width, model))],
-            whole((3 * width, late * lanes)),
-            jax.ShapeDtypeStruct((3 * width, late * lanes), BF),
+            whole((qkv_rows, late * lanes)),
+            jax.ShapeDtypeStruct((qkv_rows, late * lanes), BF),
             [
                 pltpu.VMEM((late * lanes, width), BF),
                 pltpu.VMEM((late * lanes, model), BF),
@@ -552,13 +563,12 @@
             ],
         )(*far_late[half], *far_hidden, spatial_out_weight, gain_one, qkv_weight)
         back = call(
-            functools.partial(temporal_kernel, groups),
-            [pl.BlockSpec((3 * width, lanes), lambda *_, half=half: (0, half))] * early
-            + [pl.BlockSpec((3 * width, lanes), lambda *_, f=f: (0, f)) for f in range(late)],
+            functools.partial(temporal_kernel, groups, late, half, lanes),
+            [whole((qkv_rows, tokens))] * early + [whole((qkv_rows, late * lanes))],
             [whole(back_shape)] * groups,
             [jax.ShapeDtypeStruct(back_shape, BF)] * groups,
-            [pltpu.VMEM((rows // SUB, width, groups * frames * SUB), F32)],
-        )(*projected, *[late_projected] * late)
+            [pltpu.VMEM((rows // SUB, width, groups * frames * SUB), BF)],
+        )(*projected, late_projected)
         home = {
             j: lax.ppermute(back[j], "frame", [(b, a) for a, b in out_pairs(j)])
             for j in reversed(range(1, groups))
@@ -576,7 +586,6 @@
 
     out = None
     for half in range(halves):
-        piece = pl.BlockSpec((1, rows, model), lambda *_, half=half: (0, half, 0))
         cuts = [groups] if half + 1 < halves else [groups // 2, groups]
         for lo, hi in zip([0] + cuts, cuts):
             js = range(lo, hi)
@@ -587,8 +596,8 @@
                 functools.partial(output_kernel, groups, tuple(js), early, half, halves, len(extra)),
                 [smem]
                 + [whole(back_shape)] * len(js)
-                + [piece] * (len(js) * early)
-                + [pl.BlockSpec((groups, late, rows, model), lambda *_, half=half: (0, 0, half, 0))]
+                + [whole((1, share, model))] * (len(js) * early)
+                + [whole((groups, late, share, model))]
                 + [whole((width, model)), whole((1, model))]
                 + [any_spec] * len(extra),
                 any_spec,

time: 85.1 us -> 84.8 us (level)
  no operation moved by 1% of the time
where the time goes in v8:
time: 84.8 us; the launch traced here: 84.3 us
  Pallas kernels  35.3 us (42%)
  waiting for transfers between devices  25.1 us (30%)
  starting transfers between devices  23.3 us (27%)
    ppermute x15, waiting for transfers between devices, send(): lax.ppermute(parts[j], 'frame', out_pairs(j))  12.3 us
    ppermute x2, waiting for transfers between devices, shards(): lax.ppermute(a, 'strip', near)  10.4 us
    ppermute x15, starting transfers between devices, send(): lax.ppermute(parts[j], 'frame', out_pairs(j))  10.1 us
    ppermute x2, starting transfers between devices, shards(): lax.ppermute(a, 'strip', near)  7.55 us
    pallas_call x3, Pallas kernels, shards(): call(functools.partial(output_kernel, groups, tuple(js), early, half, hal...  7.29 us
    pallas_call x2, Pallas kernels, shards(): call(functools.partial(local_kernel, some * late), [smem, smem, smem, blo...  4.78 us
    pallas_call x2, Pallas kernels, shards(): call(functools.partial(spatial_kernel, f, groups), [smem, smem, smem, one...  4.68 us
    pallas_call x2, Pallas kernels, shards(): call(functools.partial(late_project_kernel, early, frames), late_specs +...  4.34 us
  transfers between devices with their start and end apart: 25, of which 10 were waited for; matrix products, arithmetic and copies ran while one was open for 0% of the time, Pallas kernels for 34%

profile of v8, /device:TPU:0, one launch (start us, length us, event | category | flops | bytes accessed | tf_op | source)
XLA Modules:
  0.0 84.3 jit_solution(14148592580492648183)
XLA Ops:
  0.0 0.1 pad_add_fusion.place
  0.1 1.5 %shard_map.109 = (bf16[2,1152,128]{2,1,0:T(8,128)(2,1)S(1)}, bf16[2,1152,128]{2,1,0:T(8,128)(2,1)S(1)}) custom-call(s32[2]{0:T(128)S(1)} %pad_add_fusion.place, bf16[4,576,256]{2,1,0:T(8,128)(2,1)} %bitcast.22, bf16[4,576,256]{2,1,0:T(8,128)(2,1)} %bitcast.24), custom_call_target="tpu_custom_call" | custom-call | tf_op jit(solution)/shard_map/pallas_call | solution.py:471
  1.6 3.1 %collective-permute-start = (bf16[2,1152,128]{2,1,0:T(8,128)(2,1)S(1)}, bf16[2,1152,128]{2,1,0:T(8,128)(2,1)S(1)}, u32[]{:S(2)}, u32[]{:S(2)}) collective-permute-start(bf16[2,1152,128]{2,1,0:T(8,128)(2,1)S(1)} %get-tuple-element.41.a_ref), channel_id=1, source_target_pairs={{0,1},{1,0},{2,3},{3,2},{4,5},{5,4},{6,7},{7,6},{8,9},{9,8},{10,11... | collective-permute-start | bytes 1769480 | tf_op jit(solution)/shard_map/ppermute | solution.py:482
  4.7 0.8 collective-permute-start.1
  5.5 0.0 copy-start.2
  5.5 2.7 %shard_map.115 = (bf16[2,1152,128]{2,1,0:T(8,128)(2,1)S(1)}, bf16[2,1152,128]{2,1,0:T(8,128)(2,1)S(1)}, bf16[2,64,1152]{2,1,0:T(8,128)(2,1)S(1)}, bf16[2,64,1152...) custom-call(s32[2]{0:T(128)S(1)} %pad_add_fusion.place, ...), custom_call_target="tpu_custom_call" | custom-call | tf_op jit(solution)/shard_map/pallas_call | solution.py:471
  8.2 0.0 copy-start.1
  8.2 4.4 %collective-permute-start.8 = (bf16[2,1152,128]{2,1,0:T(8,128)(2,1)S(1)}, bf16[2,1152,128]{2,1,0:T(8,128)(2,1)S(1)}, u32[]{:S(2)}, u32[]{:S(2)}) collective-permute-start(bf16[2,1152,128]{2,1,0:T(8,128)(2,1)S(1)} %get-tuple-element.53.a_ref), channel_id=1, source_target_pairs={{0,1},{1,0},{2,3},{3,2},{4,5},{5,4},{6,7},{7,6},{8,9},{9,8},{10,11... | collective-permute-start | bytes 1769480 | tf_op jit(solution)/shard_map/ppermute | solution.py:482
  12.7 0.7 collective-permute-start.9
  13.4 0.1 collective-permute-start.13
  13.4 5.4 %collective-permute-done.ra_ref = bf16[2,1152,128]{2,1,0:T(8,128)(2,1)S(1)} collective-permute-done((bf16[2,1152,128]{2,1,0:T(8,128)(2,1)S(1)}, bf16[2,1152,128]{2,1,0:T(8,128)(2,1)S(1)}, u32[]{:S(2)}, u32[]{:S(2)}) %collective-permute-start) | collective-permute-done | bytes 589856 | tf_op jit(solution)/shard_map/ppermute | solution.py:482
  18.9 2.0 %collective-permute-start.14 = (bf16[2,64,1152]{2,1,0:T(8,128)(2,1)S(1)}, bf16[2,64,1152]{2,1,0:T(8,128)(2,1)S(1)}, u32[]{:S(2)}, u32[]{:S(2)}) collective-permute-start(bf16[2,64,1152]{2,1,0:T(8,128)(2,1)S(1)} %get-tuple-element.63.refs_10_), channel_id=1, source_target_pairs={{0,8},{4,12},{8,0},{12,4},{1,9},{5,13},{9,1},{13,5},{2,10},{6,14},... | collective-permute-start | bytes 884744 | tf_op jit(solution)/shard_map/ppermute | solution.py:464
  20.8 0.0 collective-permute-done.1.rb_ref
  20.8 0.0 collective-permute-start.15
  20.9 2.4 %shard_map.110 = (bf16[2,576,256]{2,1,0:T(8,128)(2,1)S(1)}, f32[2,640,256]{2,1,0:T(8,128)S(1)}) custom-call(s32[2]{0:T(128)S(1)} %pad_add_fusion.place, s32[2,4]{1,0:T(2,128)S(1)} %bitcast.17, s32[3,2,4]{2,1,0:T(2,128)S(1)} %bitcast.12, bf16[4,576,256]{2,1,0:T(8,128)(2,1)} %bitcast.26, bf16[2,1152,128]{2,1,0:T(8,128)(2,1)S(1)} %get-tuple-element.41.a_ref, ...), custom_call_target="tpu_custom_call" | custom-call | tf_op jit(solution)/shard_map/pallas_call | solution.py:492
  23.3 2.3 %shard_map.111 = (bf16[1,64,1152]{2,1,0:T(8,128)(2,1)S(1)}, bf16[1,64,1152]{2,1,0:T(8,128)(2,1)S(1)}, bf16[1,64,1152]{2,1,0:T(8,128)(2,1)S(1)}, bf16[1,64,1152]{2,1,0:T(8,128)(2,1)S(1)}) custom-call(s32[2]{0:T(128)S(1)} %pad_add_fusion.place, s32[2,4]{1,0:T(2,128)S(1)} %bitcast.18, s32[3,2,4]{2,1,0:T(2,128)S(1)} %bitcast.13, ...), custom_call_target="tpu_custom_call" | custom-call | tf_op jit(solution)/shard_map/pallas_call | solution.py:510
  25.7 5.0 %collective-permute-done.8.ra_ref = bf16[2,1152,128]{2,1,0:T(8,128)(2,1)S(1)} collective-permute-done((bf16[2,1152,128]{2,1,0:T(8,128)(2,1)S(1)}, bf16[2,1152,128]{2,1,0:T(8,128)(2,1)S(1)}, u32[]{:S(2)}, u32[]{:S(2)}) %collective-permute-start.8) | collective-permute-done | bytes 589856 | tf_op jit(solution)/shard_map/ppermute | solution.py:482
  30.7 0.0 collective-permute-start.2
  30.7 2.4 %shard_map.116 = (bf16[2,576,256]{2,1,0:T(8,128)(2,1)S(1)}, f32[2,640,256]{2,1,0:T(8,128)S(1)}) custom-call(s32[2]{0:T(128)S(1)} %pad_add_fusion.place, s32[2,4]{1,0:T(2,128)S(1)} %bitcast.19, s32[3,2,4]{2,1,0:T(2,128)S(1)} %bitcast.14, bf16[4,576,256]{2,1,0:T(8,128)(2,1)} %bitcast.27, bf16[2,1152,128]{2,1,0:T(8,128)(2,1)S(1)} %get-tuple-element.53.a_ref, ...), custom_call_target="tpu_custom_call" | custom-call | tf_op jit(solution)/shard_map/pallas_call | solution.py:492
  33.1 0.0 collective-permute-done.9.rb_ref
  33.1 2.2 %shard_map.117 = (bf16[32,1152]{1,0:T(8,128)(2,1)S(1)}, bf16[32,1152]{1,0:T(8,128)(2,1)S(1)}, bf16[32,1152]{1,0:T(8,128)(2,1)S(1)}, bf16[32,1152]{1,0:T(8,128)(2...) custom-call(s32[2]{0:T(128)S(1)} %pad_add_fusion.place, ...), custom_call_target="tpu_custom_call" | custom-call | tf_op jit(solution)/shard_map/pallas_call | solution.py:535
  35.3 0.6 collective-permute-start.19
  35.8 0.0 collective-permute-done.13.refs_5_
  35.8 1.7 %collective-permute-start.20 = (bf16[32,1152]{1,0:T(8,128)(2,1)S(1)}, bf16[32,1152]{1,0:T(8,128)(2,1)S(1)}, u32[]{:S(2)}, u32[]{:S(2)}) collective-permute-start(bf16[32,1152]{1,0:T(8,128)(2,1)S(1)} %get-tuple-element.69.refs_2_), channel_id=1, source_target_pairs={{0,8},{4,12},{8,0},{12,4},{1,9},{5,13},{9,1},{13,5},{2,10},{6,14},... | collective-permute-start | bytes 221192 | tf_op jit(solution)/shard_map/ppermute | solution.py:464
  37.5 0.0 collective-permute-done.14.refs_6_
  37.5 0.0 collective-permute-start.21
  37.5 2.3 %shard_map.113 = (bf16[1,64,1152]{2,1,0:T(8,128)(2,1)S(1)}, bf16[1,64,1152]{2,1,0:T(8,128)(2,1)S(1)}, bf16[1,64,1152]{2,1,0:T(8,128)(2,1)S(1)}, bf16[1,64,1152]{2,1,0:T(8,128)(2,1)S(1)}) custom-call(s32[2]{0:T(128)S(1)} %pad_add_fusion.place, s32[2,4]{1,0:T(2,128)S(1)} %bitcast.21, s32[3,2,4]{2,1,0:T(2,128)S(1)} %bitcast.16, ...), custom_call_target="tpu_custom_call" | custom-call | tf_op jit(solution)/shard_map/pallas_call | solution.py:510
  39.9 0.0 collective-permute-done.15.refs_7_
  39.9 1.5 %collective-permute-start.3 = (bf16[1,64,1152]{2,1,0:T(8,128)(2,1)S(1)}, bf16[1,64,1152]{2,1,0:T(8,128)(2,1)S(1)}, u32[]{:S(2)}, u32[]{:S(2)}) collective-permute-start(bf16[1,64,1152]{2,1,0:T(8,128)(2,1)S(1)} %get-tuple-element.47.refs_8_.refs_2_), channel_id=1, source_target_pairs={{0,8},{4,12},{8,0},{12,4},{1,9},{5,13},{9,1},{13,5},{2,10},{6,14},... | collective-permute-start | bytes 442376 | tf_op jit(solution)/shard_map/ppermute | solution.py:464
  41.4 0.0 collective-permute-done.19.refs_1_
  41.4 0.4 collective-permute-start.4
  41.8 0.3 collective-permute-start.5
  42.1 0.0 collective-permute-done.21.refs_3_
  42.1 1.4 %collective-permute-start.6 = (bf16[1,64,1152]{2,1,0:T(8,128)(2,1)S(1)}, bf16[1,64,1152]{2,1,0:T(8,128)(2,1)S(1)}, u32[]{:S(2)}, u32[]{:S(2)}) collective-permute-start(bf16[1,64,1152]{2,1,0:T(8,128)(2,1)S(1)} %get-tuple-element.51.refs_9_.refs_3_), channel_id=1, source_target_pairs={{0,8},{4,12},{8,0},{12,4},{1,9},{5,13},{9,1},{13,5},{2,10},{6,14},... | collective-permute-start | bytes 442376 | tf_op jit(solution)/shard_map/ppermute | solution.py:464
  43.5 0.0 collective-permute-done.2.refs_1_
  43.5 0.1 collective-permute-start.7
  43.7 2.2 %shard_map.121.refs_2_ = bf16[1920,256]{1,0:T(8,128)(2,1)S(1)} custom-call(bf16[32,1152]{1,0:T(8,128)(2,1)S(1)} %get-tuple-element.67.refs_0_, bf16[32,1152]{1,0:T(8,128)(2,1)S(1)} %collective-permute-done.19.refs_1_, bf16[32,1152]{1,0:T(8,128)(2,1)S(1)} %collective-permute-done.20.refs_2_, bf16[32,1152]{1,0:T(8,128)(2,1)S(1)} %collective-permute-done.21.refs_3_, ...), custom_call_target="tpu_custom_call" | custom-call | tf_op jit(solution)/shard_map/pallas_call | solution.py:554
  45.8 0.8 collective-permute-done.3.refs_2_
  46.7 2.1 %collective-permute-done.4.refs_3_ = bf16[1,64,1152]{2,1,0:T(8,128)(2,1)S(1)} collective-permute-done((bf16[1,64,1152]{2,1,0:T(8,128)(2,1)S(1)}, bf16[1,64,1152]{2,1,0:T(8,128)(2,1)S(1)}, u32[]{:S(2)}, u32[]{:S(2)}) %collective-permute-start.4) | collective-permute-done | bytes 147488 | tf_op jit(solution)/shard_map/ppermute | solution.py:464
  48.8 1.4 %shard_map.112.refs_0_ = bf16[1920,256]{1,0:T(8,128)(2,1)S(1)} custom-call(bf16[1,64,1152]{2,1,0:T(8,128)(2,1)S(1)} %get-tuple-element.45.refs_0_.refs_4_.refs_2_, bf16[1,64,1152]{2,1,0:T(8,128)(2,1)S(1)} %collective-permute-done.2.refs_1_, bf16[1,64,1152]{2,1,0:T(8,128)(2,1)S(1)} %collective-permute-done.3.refs_2_, ...), custom_call_target="tpu_custom_call" | custom-call | tf_op jit(solution)/shard_map/pallas_call | solution.py:525
  50.2 0.0 collective-permute-done.5.refs_1_
  50.2 2.8 %collective-permute-done.6.refs_2_ = bf16[1,64,1152]{2,1,0:T(8,128)(2,1)S(1)} collective-permute-done((bf16[1,64,1152]{2,1,0:T(8,128)(2,1)S(1)}, bf16[1,64,1152]{2,1,0:T(8,128)(2,1)S(1)}, u32[]{:S(2)}, u32[]{:S(2)}) %collective-permute-start.6) | collective-permute-done | bytes 147488 | tf_op jit(solution)/shard_map/ppermute | solution.py:464
  53.0 2.1 %collective-permute-done.7.refs_3_ = bf16[1,64,1152]{2,1,0:T(8,128)(2,1)S(1)} collective-permute-done((bf16[1,64,1152]{2,1,0:T(8,128)(2,1)S(1)}, bf16[1,64,1152]{2,1,0:T(8,128)(2,1)S(1)}, u32[]{:S(2)}, u32[]{:S(2)}) %collective-permute-start.7) | collective-permute-done | bytes 147488 | tf_op jit(solution)/shard_map/ppermute | solution.py:464
  55.1 1.4 %shard_map.114.refs_1_ = bf16[1920,256]{1,0:T(8,128)(2,1)S(1)} custom-call(bf16[1,64,1152]{2,1,0:T(8,128)(2,1)S(1)} %get-tuple-element.49.refs_0_.refs_5_.refs_3_, bf16[1,64,1152]{2,1,0:T(8,128)(2,1)S(1)} %collective-permute-done.5.refs_1_, bf16[1,64,1152]{2,1,0:T(8,128)(2,1)S(1)} %collective-permute-done.6.refs_2_, ...), custom_call_target="tpu_custom_call" | custom-call | tf_op jit(solution)/shard_map/pallas_call | solution.py:525
  56.5 1.8 %shard_map.122 = (bf16[32,2304]{1,0:T(8,128)(2,1)S(1)}, bf16[32,2304]{1,0:T(8,128)(2,1)S(1)}, bf16[32,2304]{1,0:T(8,128)(2,1)S(1)}, bf16[32,2304]{1,0:T(8,128)(2,1)S(1)}) custom-call(bf16[1920,256]{1,0:T(8,128)(2,1)S(1)} %shard_map.112.refs_0_, bf16[1920,256]{1,0:T(8,128)(2,1)S(1)} %shard_map.114.refs_1_, bf16[1920,256]{1,0:T(8,128)(2,1)S(1)} %shard_map.121.refs_2_), custom_call_target="tpu_custom_call" | custom-call | tf_op jit(solution)/shard_map/pallas_call | solution.py:565
  58.3 0.4 collective-permute-start.22
  58.7 0.3 collective-permute-start.10
  59.0 1.8 %collective-permute-start.11 = (bf16[32,1152]{1,0:T(8,128)(2,1)S(1)}, bf16[32,1152]{1,0:T(8,128)(2,1)S(1)}, u32[]{:S(2)}, u32[]{:S(2)}) collective-permute-start(bf16[32,1152]{1,0:T(8,128)(2,1)S(1)} %get-tuple-element.59.refs_6_), channel_id=1, source_target_pairs={{0,8},{4,12},{8,0},{12,4},{1,9},{5,13},{9,1},{13,5},{2,10},{6,14},... | collective-permute-start | bytes 221192 | tf_op jit(solution)/shard_map/ppermute | solution.py:464
  60.8 2.7 %collective-permute-done.11.refs_2_ = bf16[32,1152]{1,0:T(8,128)(2,1)S(1)} collective-permute-done((bf16[32,1152]{1,0:T(8,128)(2,1)S(1)}, bf16[32,1152]{1,0:T(8,128)(2,1)S(1)}, u32[]{:S(2)}, u32[]{:S(2)}) %collective-permute-start.11) | collective-permute-done | bytes 73760 | tf_op jit(solution)/shard_map/ppermute | solution.py:464
  63.5 1.7 %collective-permute-done.12.refs_3_ = bf16[32,1152]{1,0:T(8,128)(2,1)S(1)} collective-permute-done((bf16[32,1152]{1,0:T(8,128)(2,1)S(1)}, bf16[32,1152]{1,0:T(8,128)(2,1)S(1)}, u32[]{:S(2)}, u32[]{:S(2)}) %collective-permute-start.12) | collective-permute-done | bytes 73760 | tf_op jit(solution)/shard_map/ppermute | solution.py:464
  65.2 2.2 %shard_map.118.refs_2_ = bf16[1920,256]{1,0:T(8,128)(2,1)S(1)} custom-call(bf16[32,1152]{1,0:T(8,128)(2,1)S(1)} %get-tuple-element.57.refs_0_.refs_4_, bf16[32,1152]{1,0:T(8,128)(2,1)S(1)} %collective-permute-done.10.refs_1_, bf16[32,1152]{1,0:T(8,128)(2,1)S(1)} %collective-permute-done.11.refs_2_, bf16[32,1152]{1,0:T(8,128)(2,1)S(1)} %collective-permute-done.12.refs_3_, ...), custom_call_target="tpu_custom_call" | custom-call | tf_op jit(solution)/shard_map/pallas_call | solution.py:554
  67.4 0.9 %collective-permute-start.23 = (bf16[32,2304]{1,0:T(8,128)(2,1)S(1)}, bf16[32,2304]{1,0:T(8,128)(2,1)S(1)}, u32[]{:S(2)}, u32[]{:S(2)}) collective-permute-start(bf16[32,2304]{1,0:T(8,128)(2,1)S(1)} %get-tuple-element.75), channel_id=1, source_target_pairs={{8,0},{12,4},{0,8},{4,12},{9,1},{13,5},{1,9},{5,13},{10,2},{14,6},... | collective-permute-start | bytes 442376 | tf_op jit(solution)/shard_map/ppermute | solution.py:573
  68.3 0.6 collective-permute-start.24
  68.9 1.8 %shard_map.119 = (bf16[32,2304]{1,0:T(8,128)(2,1)S(1)}, bf16[32,2304]{1,0:T(8,128)(2,1)S(1)}, bf16[32,2304]{1,0:T(8,128)(2,1)S(1)}, bf16[32,2304]{1,0:T(8,128)(2,1)S(1)}) custom-call(bf16[1920,256]{1,0:T(8,128)(2,1)S(1)} %shard_map.112.refs_0_, bf16[1920,256]{1,0:T(8,128)(2,1)S(1)} %shard_map.114.refs_1_, bf16[1920,256]{1,0:T(8,128)(2,1)S(1)} %shard_map.118.refs_2_), custom_call_target="tpu_custom_call" | custom-call | tf_op jit(solution)/shard_map/pallas_call | solution.py:565
  70.7 0.7 collective-permute-start.18
  71.5 0.9 %collective-permute-start.16 = (bf16[32,2304]{1,0:T(8,128)(2,1)S(1)}, bf16[32,2304]{1,0:T(8,128)(2,1)S(1)}, u32[]{:S(2)}, u32[]{:S(2)}) collective-permute-start(bf16[32,2304]{1,0:T(8,128)(2,1)S(1)} %get-tuple-element.65), channel_id=1, source_target_pairs={{8,0},{12,4},{0,8},{4,12},{9,1},{13,5},{1,9},{5,13},{10,2},{14,6},... | collective-permute-start | bytes 442376 | tf_op jit(solution)/shard_map/ppermute | solution.py:573
  72.3 0.0 collective-permute-done.22.refs_1_
  72.3 0.6 collective-permute-start.17
  72.9 1.5 %shard_map.120.refs_12_.refs_6_ = bf16[4,2,64,1152]{3,2,1,0:T(8,128)(2,1)S(1)} custom-call(bf16[32,1152]{1,0:T(8,128)(2,1)S(1)} %get-tuple-element.67.refs_0_, bf16[32,1152]{1,0:T(8,128)(2,1)S(1)} %get-tuple-element.68.refs_1_, bf16[32,1152]{1,0:T(8,128)(2,1)S(1)} %get-tuple-element.69.refs_2_, bf16[32,1152]{1,0:T(8,128)(2,1)S(1)} %get-tuple-element.70.refs_3_, ...), custom_call_target="tpu_custom_call" | custom-call | tf_op jit(solution)/shard_map/pallas_call | solution.py:578
  74.5 1.3 %collective-permute-done.24.refs_3_ = bf16[32,2304]{1,0:T(8,128)(2,1)S(1)} collective-permute-done((bf16[32,2304]{1,0:T(8,128)(2,1)S(1)}, bf16[32,2304]{1,0:T(8,128)(2,1)S(1)}, u32[]{:S(2)}, u32[]{:S(2)}) %collective-permute-start.24) | collective-permute-done | bytes 147488 | tf_op jit(solution)/shard_map/ppermute | solution.py:573
  75.7 2.9 %shard_map.123.refs_9_ = bf16[4,256,1152]{2,1,0:T(8,128)(2,1)} custom-call(s32[2]{0:T(128)S(1)} %pad_add_fusion.place, bf16[32,2304]{1,0:T(8,128)(2,1)S(1)} %get-tuple-element.73.refs_0_, bf16[32,2304]{1,0:T(8,128)(2,1)S(1)} %collective-permute-done.22.refs_1_, bf16[32,2304]{1,0:T(8,128)(2,1)S(1)} %collective-permute-done.23.refs_2_, ...), custom_call_target="tpu_custom_call" | custom-call | tf_op jit(solution)/shard_map/pallas_call | solution.py:595
  78.6 2.2 %shard_map.124.refs_9_ = bf16[4,256,1152]{2,1,0:T(8,128)(2,1)} custom-call(s32[2]{0:T(128)S(1)} %pad_add_fusion.place, bf16[32,2304]{1,0:T(8,128)(2,1)S(1)} %get-tuple-element.71.refs_0_, bf16[32,2304]{1,0:T(8,128)(2,1)S(1)} %collective-permute-done.18.refs_1_, ...), custom_call_target="tpu_custom_call", output_to_operand_aliasing={{}: (10, {})} | custom-call | tf_op jit(solution)/shard_map/pallas_call | solution.py:595
  80.8 1.1 %collective-permute-done.17.refs_1_ = bf16[32,2304]{1,0:T(8,128)(2,1)S(1)} collective-permute-done((bf16[32,2304]{1,0:T(8,128)(2,1)S(1)}, bf16[32,2304]{1,0:T(8,128)(2,1)S(1)}, u32[]{:S(2)}, u32[]{:S(2)}) %collective-permute-start.17) | collective-permute-done | bytes 147488 | tf_op jit(solution)/shard_map/ppermute | solution.py:573
  81.9 2.2 %shard_map.125 = bf16[4,256,1152]{2,1,0:T(8,128)(2,1)} custom-call(s32[2]{0:T(128)S(1)} %pad_add_fusion.place, bf16[32,2304]{1,0:T(8,128)(2,1)S(1)} %collective-permute-done.16.refs_0_, bf16[32,2304]{1,0:T(8,128)(2,1)S(1)} %collective-permute-done.17.refs_1_, ...), custom_call_target="tpu_custom_call", output_to_operand_aliasing={{}: (10, {})} | custom-call | tf_op jit(solution)/shard_map/pallas_call | solution.py:595
  (22 shorter events, 0.1 us)
Async XLA Ops:
  1.6 17.3 %collective-permute-start = (bf16[2,1152,128]{2,1,0:T(8,128)(2,1)S(1)}, bf16[2,1152,128]{2,1,0:T(8,128)(2,1)S(1)}, u32[]{:S(2)}, u32[]{:S(2)}) collective-permute-start(bf16[2,1152,128]{2,1,0:T(8,128)(2,1)S(1)} %get-tuple-element.41.a_ref), channel_id=1, source_target_pairs={{0,1},{1,0},{2,3},{3,2},{4,5},{5,4},{6,7},{7,6},{8,9},{9,8},{10,11... | collective-permute-start | bytes 1769480 | tf_op jit(solution)/shard_map/ppermute | solution.py:482
  4.7 16.1 %copy-start.6 = (f32[1152]{0:T(1024)S(1)}, f32[1152]{0:T(1024)}, u32[]{:S(2)}) copy-start(f32[1152]{0:T(1024)} %param.16) | copy-start | bytes 13828
  4.7 16.2 %copy-start.4 = (s32[4,2,3]{0,1,2:T(2,128)S(1)}, s32[4,2,3]{0,1,2:T(2,128)}, u32[]{:S(2)}) copy-start(s32[4,2,3]{0,1,2:T(2,128)} %param.20) | copy-start | bytes 292
  4.7 16.2 %copy-start.5 = (s32[4,2]{0,1:T(2,128)S(1)}, s32[4,2]{0,1:T(2,128)}, u32[]{:S(2)}) copy-start(s32[4,2]{0,1:T(2,128)} %param.21) | copy-start | bytes 100
  4.7 16.1 %collective-permute-start.1 = (bf16[2,1152,128]{2,1,0:T(8,128)(2,1)S(1)}, bf16[2,1152,128]{2,1,0:T(8,128)(2,1)S(1)}, u32[]{:S(2)}, u32[]{:S(2)}) collective-permute-start(bf16[2,1152,128]{2,1,0:T(8,128)(2,1)S(1)} %get-tuple-element.42.b_ref), channel_id=1, source_target_pairs={{1,2},{2,1},{5,6},{6,5},{9,10},{10,9},{13,14},{14,13},{17,18},{18,... | collective-permute-start | bytes 1769480 | tf_op jit(solution)/shard_map/ppermute | solution.py:482
  5.5 17.8 %copy-start.2 = (bf16[4,256,1152]{2,1,0:T(8,128)(2,1)S(1)}, bf16[4,256,1152]{2,1,0:T(8,128)(2,1)}, u32[]{:S(2)}) copy-start(bf16[4,256,1152]{2,1,0:T(8,128)(2,1)} %refs_0_.1) | copy-start | bytes 7077892
  8.2 15.1 %copy-start.1 = (bf16[576,1152]{1,0:T(8,128)(2,1)S(1)}, bf16[576,1152]{1,0:T(8,128)(2,1)}, u32[]{:S(2)}) copy-start(bf16[576,1152]{1,0:T(8,128)(2,1)} %refs_8_.3) | copy-start | bytes 3981316
  8.2 22.4 %collective-permute-start.8 = (bf16[2,1152,128]{2,1,0:T(8,128)(2,1)S(1)}, bf16[2,1152,128]{2,1,0:T(8,128)(2,1)S(1)}, u32[]{:S(2)}, u32[]{:S(2)}) collective-permute-start(bf16[2,1152,128]{2,1,0:T(8,128)(2,1)S(1)} %get-tuple-element.53.a_ref), channel_id=1, source_target_pairs={{0,1},{1,0},{2,3},{3,2},{4,5},{5,4},{6,7},{7,6},{8,9},{9,8},{10,11... | collective-permute-start | bytes 1769480 | tf_op jit(solution)/shard_map/ppermute | solution.py:482
  12.7 20.4 %collective-permute-start.9 = (bf16[2,1152,128]{2,1,0:T(8,128)(2,1)S(1)}, bf16[2,1152,128]{2,1,0:T(8,128)(2,1)S(1)}, u32[]{:S(2)}, u32[]{:S(2)}) collective-permute-start(bf16[2,1152,128]{2,1,0:T(8,128)(2,1)S(1)} %get-tuple-element.54.b_ref), channel_id=1, source_target_pairs={{1,2},{2,1},{5,6},{6,5},{9,10},{10,9},{13,14},{14,13},{17,18},{18,... | collective-permute-start | bytes 1769480 | tf_op jit(solution)/shard_map/ppermute | solution.py:482
  13.4 22.5 %collective-permute-start.13 = (bf16[2,64,1152]{2,1,0:T(8,128)(2,1)S(1)}, bf16[2,64,1152]{2,1,0:T(8,128)(2,1)S(1)}, u32[]{:S(2)}, u32[]{:S(2)}) collective-permute-start(bf16[2,64,1152]{2,1,0:T(8,128)(2,1)S(1)} %get-tuple-element.62.refs_9_), channel_id=1, source_target_pairs={{0,4},{4,0},{8,12},{12,8},{1,5},{5,1},{9,13},{13,9},{2,6},{6,2},{1... | collective-permute-start | bytes 884744 | tf_op jit(solution)/shard_map/ppermute | solution.py:464
  18.9 18.6 %collective-permute-start.14 = (bf16[2,64,1152]{2,1,0:T(8,128)(2,1)S(1)}, bf16[2,64,1152]{2,1,0:T(8,128)(2,1)S(1)}, u32[]{:S(2)}, u32[]{:S(2)}) collective-permute-start(bf16[2,64,1152]{2,1,0:T(8,128)(2,1)S(1)} %get-tuple-element.63.refs_10_), channel_id=1, source_target_pairs={{0,8},{4,12},{8,0},{12,4},{1,9},{5,13},{9,1},{13,5},{2,10},{6,14},... | collective-permute-start | bytes 884744 | tf_op jit(solution)/shard_map/ppermute | solution.py:464
  20.8 19.0 %collective-permute-start.15 = (bf16[2,64,1152]{2,1,0:T(8,128)(2,1)S(1)}, bf16[2,64,1152]{2,1,0:T(8,128)(2,1)S(1)}, u32[]{:S(2)}, u32[]{:S(2)}) collective-permute-start(bf16[2,64,1152]{2,1,0:T(8,128)(2,1)S(1)} %get-tuple-element.64.refs_11_), channel_id=1, source_target_pairs={{0,12},{4,8},{8,4},{12,0},{1,13},{5,9},{9,5},{13,1},{2,14},{6,10},... | collective-permute-start | bytes 884744 | tf_op jit(solution)/shard_map/ppermute | solution.py:464
  30.7 12.9 %collective-permute-start.2 = (bf16[1,64,1152]{2,1,0:T(8,128)(2,1)S(1)}, bf16[1,64,1152]{2,1,0:T(8,128)(2,1)S(1)}, u32[]{:S(2)}, u32[]{:S(2)}) collective-permute-start(bf16[1,64,1152]{2,1,0:T(8,128)(2,1)S(1)} %get-tuple-element.46.refs_6_.refs_4_), channel_id=1, source_target_pairs={{0,4},{4,0},{8,12},{12,8},{1,5},{5,1},{9,13},{13,9},{2,6},{6,2},{1... | collective-permute-start | bytes 442376 | tf_op jit(solution)/shard_map/ppermute | solution.py:464
  35.3 6.1 %collective-permute-start.19 = (bf16[32,1152]{1,0:T(8,128)(2,1)S(1)}, bf16[32,1152]{1,0:T(8,128)(2,1)S(1)}, u32[]{:S(2)}, u32[]{:S(2)}) collective-permute-start(bf16[32,1152]{1,0:T(8,128)(2,1)S(1)} %get-tuple-element.68.refs_1_), channel_id=1, source_target_pairs={{0,4},{4,0},{8,12},{12,8},{1,5},{5,1},{9,13},{13,9},{2,6},{6,2},{1... | collective-permute-start | bytes 221192 | tf_op jit(solution)/shard_map/ppermute | solution.py:464
  35.8 5.9 %collective-permute-start.20 = (bf16[32,1152]{1,0:T(8,128)(2,1)S(1)}, bf16[32,1152]{1,0:T(8,128)(2,1)S(1)}, u32[]{:S(2)}, u32[]{:S(2)}) collective-permute-start(bf16[32,1152]{1,0:T(8,128)(2,1)S(1)} %get-tuple-element.69.refs_2_), channel_id=1, source_target_pairs={{0,8},{4,12},{8,0},{12,4},{1,9},{5,13},{9,1},{13,5},{2,10},{6,14},... | collective-permute-start | bytes 221192 | tf_op jit(solution)/shard_map/ppermute | solution.py:464
  37.5 4.6 %collective-permute-start.21 = (bf16[32,1152]{1,0:T(8,128)(2,1)S(1)}, bf16[32,1152]{1,0:T(8,128)(2,1)S(1)}, u32[]{:S(2)}, u32[]{:S(2)}) collective-permute-start(bf16[32,1152]{1,0:T(8,128)(2,1)S(1)} %get-tuple-element.70.refs_3_), channel_id=1, source_target_pairs={{0,12},{4,8},{8,4},{12,0},{1,13},{5,9},{9,5},{13,1},{2,14},{6,10},... | collective-permute-start | bytes 221192 | tf_op jit(solution)/shard_map/ppermute | solution.py:464
  37.5 6.1 %copy-start = (bf16[1152,1728]{0,1:T(8,128)(2,1)S(1)}, bf16[1152,1728]{0,1:T(8,128)(2,1)}, u32[]{:S(2)}) copy-start(bf16[1152,1728]{0,1:T(8,128)(2,1)} %param.17) | copy-start | bytes 11943940
  39.9 6.8 %collective-permute-start.3 = (bf16[1,64,1152]{2,1,0:T(8,128)(2,1)S(1)}, bf16[1,64,1152]{2,1,0:T(8,128)(2,1)S(1)}, u32[]{:S(2)}, u32[]{:S(2)}) collective-permute-start(bf16[1,64,1152]{2,1,0:T(8,128)(2,1)S(1)} %get-tuple-element.47.refs_8_.refs_2_), channel_id=1, source_target_pairs={{0,8},{4,12},{8,0},{12,4},{1,9},{5,13},{9,1},{13,5},{2,10},{6,14},... | collective-permute-start | bytes 442376 | tf_op jit(solution)/shard_map/ppermute | solution.py:464
  41.4 7.4 %collective-permute-start.4 = (bf16[1,64,1152]{2,1,0:T(8,128)(2,1)S(1)}, bf16[1,64,1152]{2,1,0:T(8,128)(2,1)S(1)}, u32[]{:S(2)}, u32[]{:S(2)}) collective-permute-start(bf16[1,64,1152]{2,1,0:T(8,128)(2,1)S(1)} %get-tuple-element.48.refs_10_.refs_4_), channel_id=1, source_target_pairs={{0,12},{4,8},{8,4},{12,0},{1,13},{5,9},{9,5},{13,1},{2,14},{6,10},... | collective-permute-start | bytes 442376 | tf_op jit(solution)/shard_map/ppermute | solution.py:464
  41.8 8.4 %collective-permute-start.5 = (bf16[1,64,1152]{2,1,0:T(8,128)(2,1)S(1)}, bf16[1,64,1152]{2,1,0:T(8,128)(2,1)S(1)}, u32[]{:S(2)}, u32[]{:S(2)}) collective-permute-start(bf16[1,64,1152]{2,1,0:T(8,128)(2,1)S(1)} %get-tuple-element.50.refs_7_.refs_5_), channel_id=1, source_target_pairs={{0,4},{4,0},{8,12},{12,8},{1,5},{5,1},{9,13},{13,9},{2,6},{6,2},{1... | collective-permute-start | bytes 442376 | tf_op jit(solution)/shard_map/ppermute | solution.py:464
  42.1 10.9 %collective-permute-start.6 = (bf16[1,64,1152]{2,1,0:T(8,128)(2,1)S(1)}, bf16[1,64,1152]{2,1,0:T(8,128)(2,1)S(1)}, u32[]{:S(2)}, u32[]{:S(2)}) collective-permute-start(bf16[1,64,1152]{2,1,0:T(8,128)(2,1)S(1)} %get-tuple-element.51.refs_9_.refs_3_), channel_id=1, source_target_pairs={{0,8},{4,12},{8,0},{12,4},{1,9},{5,13},{9,1},{13,5},{2,10},{6,14},... | collective-permute-start | bytes 442376 | tf_op jit(solution)/shard_map/ppermute | solution.py:464
  43.5 11.6 %collective-permute-start.7 = (bf16[1,64,1152]{2,1,0:T(8,128)(2,1)S(1)}, bf16[1,64,1152]{2,1,0:T(8,128)(2,1)S(1)}, u32[]{:S(2)}, u32[]{:S(2)}) collective-permute-start(bf16[1,64,1152]{2,1,0:T(8,128)(2,1)S(1)} %get-tuple-element.52.refs_11_.refs_5_), channel_id=1, source_target_pairs={{0,12},{4,8},{8,4},{12,0},{1,13},{5,9},{9,5},{13,1},{2,14},{6,10},... | collective-permute-start | bytes 442376 | tf_op jit(solution)/shard_map/ppermute | solution.py:464
  58.3 14.0 %collective-permute-start.22 = (bf16[32,2304]{1,0:T(8,128)(2,1)S(1)}, bf16[32,2304]{1,0:T(8,128)(2,1)S(1)}, u32[]{:S(2)}, u32[]{:S(2)}) collective-permute-start(bf16[32,2304]{1,0:T(8,128)(2,1)S(1)} %get-tuple-element.74), channel_id=1, source_target_pairs={{4,0},{0,4},{12,8},{8,12},{5,1},{1,5},{13,9},{9,13},{6,2},{2,6},{1... | collective-permute-start | bytes 442376 | tf_op jit(solution)/shard_map/ppermute | solution.py:573
  58.7 2.1 %collective-permute-start.10 = (bf16[32,1152]{1,0:T(8,128)(2,1)S(1)}, bf16[32,1152]{1,0:T(8,128)(2,1)S(1)}, u32[]{:S(2)}, u32[]{:S(2)}) collective-permute-start(bf16[32,1152]{1,0:T(8,128)(2,1)S(1)} %get-tuple-element.58.refs_5_), channel_id=1, source_target_pairs={{0,4},{4,0},{8,12},{12,8},{1,5},{5,1},{9,13},{13,9},{2,6},{6,2},{1... | collective-permute-start | bytes 221192 | tf_op jit(solution)/shard_map/ppermute | solution.py:464
  59.0 4.5 %collective-permute-start.11 = (bf16[32,1152]{1,0:T(8,128)(2,1)S(1)}, bf16[32,1152]{1,0:T(8,128)(2,1)S(1)}, u32[]{:S(2)}, u32[]{:S(2)}) collective-permute-start(bf16[32,1152]{1,0:T(8,128)(2,1)S(1)} %get-tuple-element.59.refs_6_), channel_id=1, source_target_pairs={{0,8},{4,12},{8,0},{12,4},{1,9},{5,13},{9,1},{13,5},{2,10},{6,14},... | collective-permute-start | bytes 221192 | tf_op jit(solution)/shard_map/ppermute | solution.py:464
  60.8 4.4 %collective-permute-start.12 = (bf16[32,1152]{1,0:T(8,128)(2,1)S(1)}, bf16[32,1152]{1,0:T(8,128)(2,1)S(1)}, u32[]{:S(2)}, u32[]{:S(2)}) collective-permute-start(bf16[32,1152]{1,0:T(8,128)(2,1)S(1)} %get-tuple-element.60.refs_7_), channel_id=1, source_target_pairs={{0,12},{4,8},{8,4},{12,0},{1,13},{5,9},{9,5},{13,1},{2,14},{6,10},... | collective-permute-start | bytes 221192 | tf_op jit(solution)/shard_map/ppermute | solution.py:464
  67.4 7.1 %collective-permute-start.23 = (bf16[32,2304]{1,0:T(8,128)(2,1)S(1)}, bf16[32,2304]{1,0:T(8,128)(2,1)S(1)}, u32[]{:S(2)}, u32[]{:S(2)}) collective-permute-start(bf16[32,2304]{1,0:T(8,128)(2,1)S(1)} %get-tuple-element.75), channel_id=1, source_target_pairs={{8,0},{12,4},{0,8},{4,12},{9,1},{13,5},{1,9},{5,13},{10,2},{14,6},... | collective-permute-start | bytes 442376 | tf_op jit(solution)/shard_map/ppermute | solution.py:573
  68.3 4.6 %copy-start.7 = (f32[1152]{0:T(1024)S(1)}, f32[1152]{0:T(1024)}, u32[]{:S(2)}) copy-start(f32[1152]{0:T(1024)} %param.19) | copy-start | bytes 13828
  68.3 7.4 %collective-permute-start.24 = (bf16[32,2304]{1,0:T(8,128)(2,1)S(1)}, bf16[32,2304]{1,0:T(8,128)(2,1)S(1)}, u32[]{:S(2)}, u32[]{:S(2)}) collective-permute-start(bf16[32,2304]{1,0:T(8,128)(2,1)S(1)} %get-tuple-element.76), channel_id=1, source_target_pairs={{12,0},{8,4},{4,8},{0,12},{13,1},{9,5},{5,9},{1,13},{14,2},{10,6},... | collective-permute-start | bytes 442376 | tf_op jit(solution)/shard_map/ppermute | solution.py:573
  70.7 7.9 %collective-permute-start.18 = (bf16[32,2304]{1,0:T(8,128)(2,1)S(1)}, bf16[32,2304]{1,0:T(8,128)(2,1)S(1)}, u32[]{:S(2)}, u32[]{:S(2)}) collective-permute-start(bf16[32,2304]{1,0:T(8,128)(2,1)S(1)} %get-tuple-element.72), channel_id=1, source_target_pairs={{4,0},{0,4},{12,8},{8,12},{5,1},{1,5},{13,9},{9,13},{6,2},{2,6},{1... | collective-permute-start | bytes 442376 | tf_op jit(solution)/shard_map/ppermute | solution.py:573
  71.5 9.4 %collective-permute-start.16 = (bf16[32,2304]{1,0:T(8,128)(2,1)S(1)}, bf16[32,2304]{1,0:T(8,128)(2,1)S(1)}, u32[]{:S(2)}, u32[]{:S(2)}) collective-permute-start(bf16[32,2304]{1,0:T(8,128)(2,1)S(1)} %get-tuple-element.65), channel_id=1, source_target_pairs={{8,0},{12,4},{0,8},{4,12},{9,1},{13,5},{1,9},{5,13},{10,2},{14,6},... | collective-permute-start | bytes 442376 | tf_op jit(solution)/shard_map/ppermute | solution.py:573
  72.3 9.6 %collective-permute-start.17 = (bf16[32,2304]{1,0:T(8,128)(2,1)S(1)}, bf16[32,2304]{1,0:T(8,128)(2,1)S(1)}, u32[]{:S(2)}, u32[]{:S(2)}) collective-permute-start(bf16[32,2304]{1,0:T(8,128)(2,1)S(1)} %get-tuple-element.66), channel_id=1, source_target_pairs={{12,0},{8,4},{4,8},{0,12},{13,1},{9,5},{5,9},{1,13},{14,2},{10,6},... | collective-permute-start | bytes 442376 | tf_op jit(solution)/shard_map/ppermute | solution.py:573
  72.9 2.8 %copy-start.3 = (bf16[576,1152]{1,0:T(8,128)(2,1)S(1)}, bf16[576,1152]{1,0:T(8,128)(2,1)}, u32[]{:S(2)}) copy-start(bf16[576,1152]{1,0:T(8,128)(2,1)} %refs_7_.3) | copy-start | bytes 3981316

commit v9 on v8

--- a/solution.py
+++ b/solution.py
@@ -365,17 +365,32 @@
     pipeline(steps, scores, weigh, gather)
 
 
-def output_kernel(n_groups, js, early, half, halves, aliased, place, *refs):
+def output_kernel(n_groups, js, early, half, halves, before, last, aliased, place, *refs):
     n = len(js)
     atts, pieces = refs[:n], refs[n:n * (1 + early)]
     late_ref, w_ref, g_ref = refs[n * (1 + early):n * (1 + early) + 3]
-    out, buf, sems = refs[n * (1 + early) + 3 + aliased:]
+    rest = list(refs[n * (1 + early) + 3:])
+    handed = rest.pop(0) if before else None
+    rest = rest[aliased:]
+    out = rest.pop(0) if before or last else None
+    buf = rest.pop(0)
     late = late_ref.shape[1]
     rows = atts[0].shape[0]
     cut = slice(half * rows, (half + 1) * rows)
     width = w_ref.shape[0]
     frames = early + late
     copies = []
+
+    def write(src, j, some_half):
+        group = peer(place[0], j, n_groups)
+        at = pl.multiple_of((group * halves + some_half) * rows, SUB)
+        copy = pltpu.make_async_copy(src, out.at[:, pl.ds(at, rows), :], rest[0].at[len(copies)])
+        copy.start()
+        copies.append(copy)
+
+    if before:
+        for i, j in enumerate(before[0]):
+            write(handed.at[i], j, before[1])
 
     def block(some):
         def start():
@@ -390,15 +405,12 @@
                     at = (k * frames + f) * rows
                     part = normed[at:at + rows, :] * g_ref[...]
                     buf[i, f] = (mine.astype(F32) + part).astype(BF)
-                group = peer(place[0], j, n_groups)
-                at = pl.multiple_of((group * halves + half) * rows, SUB)
-                copy = pltpu.make_async_copy(buf.at[i], out.at[:, pl.ds(at, rows), :], sems.at[i])
-                copy.start()
-                copies.append(copy)
+                if last:
+                    write(buf.at[i], j, half)
 
         return start, finish
 
-    add_normed([block(some) for some in blocks_of(len(js), frames * rows)])
+    add_normed([block(some) for some in blocks_of(n, frames * rows)])
     for copy in copies:
         copy.wait()
 
@@ -584,38 +596,49 @@
         jax.ShapeDtypeStruct((groups, late, share, model), BF),
     )(*[x for some in own_late for x in some], *own_hidden, spatial_out_weight, gain_one)
 
-    out = None
-    for half in range(halves):
-        cuts = [groups] if half + 1 < halves else [groups // 2, groups]
-        for lo, hi in zip([0] + cuts, cuts):
-            js = range(lo, hi)
-            if not js:
-                continue
-            extra = [] if out is None else [out]
-            out = call(
-                functools.partial(output_kernel, groups, tuple(js), early, half, halves, len(extra)),
-                [smem]
-                + [whole(back_shape)] * len(js)
-                + [whole((1, share, model))] * (len(js) * early)
-                + [whole((groups, late, share, model))]
-                + [whole((width, model)), whole((1, model))]
-                + [any_spec] * len(extra),
-                any_spec,
-                jax.ShapeDtypeStruct((frames, tokens, model), BF),
-                [
-                    pltpu.VMEM((len(js), frames, rows, model), BF),
-                    pltpu.SemaphoreType.DMA((len(js),)),
-                ],
-                alias={4 + len(js) * (1 + early): 0} if extra else None,
-            )(
-                place,
-                *[returned[half][j] for j in js],
-                *[mixed[f][j] for j in js for f in range(early)],
-                late_mixed,
-                temporal_out_weight,
-                gain_two,
-                *extra,
-            )
+    order = [0, 1] + list(reversed(range(2, groups))) if groups > 1 else [0]
+    tail = max(1, groups // 4)
+    calls = [(tuple(order), half) for half in range(halves - 1)]
+    calls += [(tuple(js), halves - 1) for js in (order[:-tail], order[-tail:]) if js]
+    result = jax.ShapeDtypeStruct((frames, tokens, model), BF)
+    out = handed = before = None
+    for n, (js, half) in enumerate(calls):
+        last = n + 1 == len(calls)
+        rows_shape = (len(js), frames, rows, model)
+        extra = [] if out is None else [out]
+        writes = (len(before[0]) if before else 0) + (len(js) if last else 0)
+        in_specs = (
+            [smem]
+            + [whole(back_shape)] * len(js)
+            + [whole((1, share, model))] * (len(js) * early)
+            + [whole((groups, late, share, model)), whole((width, model)), whole((1, model))]
+            + ([whole(handed.shape)] if before else [])
+            + [any_spec] * len(extra)
+        )
+        outs = ([any_spec], [result]) if before or last else ([], [])
+        kept = ([], []) if last else ([whole(rows_shape)], [jax.ShapeDtypeStruct(rows_shape, BF)])
+        scratch = [pltpu.VMEM(rows_shape, BF)] * last + [pltpu.SemaphoreType.DMA((writes,))] * bool(writes)
+        got = call(
+            functools.partial(output_kernel, groups, js, early, half, halves, before, last, len(extra)),
+            in_specs,
+            outs[0] + kept[0],
+            outs[1] + kept[1],
+            scratch,
+            alias={len(in_specs) - 1: 0} if extra else None,
+        )(
+            place,
+            *[returned[half][j] for j in js],
+            *[mixed[f][j] for j in js for f in range(early)],
+            late_mixed,
+            temporal_out_weight,
+            gain_two,
+            *([handed] if before else []),
+            *extra,
+        )
+        got = list(got)
+        out = got.pop(0) if before or last else None
+        handed = None if last else got[0]
+        before = (js, half)
     return out
 
 

time: 84.8 us -> 85.5 us (level)
  waiting for transfers between devices: 25.1 us -> 26.3 us
    ppermute x6, waiting for transfers between devices: 2.37 us -> 3.56 us  [shards(): lax.ppermute(back[j], 'frame', [(b, a) for a, b in out_pairs(j)])]
  transfers between devices with their start and end apart: 25 -> 25, of which waited for: 10 -> 11; matrix products, arithmetic and copies ran while one was open for 0% -> 0% of each run, Pallas kernels for 34% -> 33%
where the time goes in v9:
time: 85.5 us; the launch traced here: 85.2 us
  Pallas kernels  34.7 us (41%)
  waiting for transfers between devices  26.3 us (31%)
  starting transfers between devices  23.6 us (28%)
    ppermute x15, waiting for transfers between devices, send(): lax.ppermute(parts[j], 'frame', out_pairs(j))  12.3 us
    ppermute x2, waiting for transfers between devices, shards(): lax.ppermute(a, 'strip', near)  10.4 us
    ppermute x15, starting transfers between devices, send(): lax.ppermute(parts[j], 'frame', out_pairs(j))  10.1 us
    ppermute x2, starting transfers between devices, shards(): lax.ppermute(a, 'strip', near)  7.55 us
    pallas_call x3, Pallas kernels, shards(): call(functools.partial(output_kernel, groups, js, early, half, halves, be...  6.66 us
    pallas_call x2, Pallas kernels, shards(): call(functools.partial(local_kernel, some * late), [smem, smem, smem, blo...  4.78 us
    pallas_call x2, Pallas kernels, shards(): call(functools.partial(spatial_kernel, f, groups), [smem, smem, smem, one...  4.68 us
    ppermute x6, starting transfers between devices, shards(): lax.ppermute(back[j], 'frame', [(b, a) for a, b in out_pairs(j)])  4.43 us
  transfers between devices with their start and end apart: 25, of which 11 were waited for; matrix products, arithmetic and copies ran while one was open for 0% of the time, Pallas kernels for 33%

profile of v9, /device:TPU:0, one launch (start us, length us, event | category | flops | bytes accessed | tf_op | source)
XLA Modules:
  0.0 85.2 jit_solution(17795478403051141414)
XLA Ops:
  0.0 0.1 pad_add_fusion.place
  0.1 1.5 %shard_map.109 = (bf16[2,1152,128]{2,1,0:T(8,128)(2,1)S(1)}, bf16[2,1152,128]{2,1,0:T(8,128)(2,1)S(1)}) custom-call(s32[2]{0:T(128)S(1)} %pad_add_fusion.place, bf16[4,576,256]{2,1,0:T(8,128)(2,1)} %bitcast.22, bf16[4,576,256]{2,1,0:T(8,128)(2,1)} %bitcast.24), custom_call_target="tpu_custom_call" | custom-call | tf_op jit(solution)/shard_map/pallas_call | solution.py:483
  1.6 3.1 %collective-permute-start = (bf16[2,1152,128]{2,1,0:T(8,128)(2,1)S(1)}, bf16[2,1152,128]{2,1,0:T(8,128)(2,1)S(1)}, u32[]{:S(2)}, u32[]{:S(2)}) collective-permute-start(bf16[2,1152,128]{2,1,0:T(8,128)(2,1)S(1)} %get-tuple-element.43.a_ref), channel_id=1, source_target_pairs={{0,1},{1,0},{2,3},{3,2},{4,5},{5,4},{6,7},{7,6},{8,9},{9,8},{10,11... | collective-permute-start | bytes 1769480 | tf_op jit(solution)/shard_map/ppermute | solution.py:494
  4.7 0.8 collective-permute-start.1
  5.5 0.0 copy-start.2
  5.5 2.7 %shard_map.115 = (bf16[2,1152,128]{2,1,0:T(8,128)(2,1)S(1)}, bf16[2,1152,128]{2,1,0:T(8,128)(2,1)S(1)}, bf16[2,64,1152]{2,1,0:T(8,128)(2,1)S(1)}, bf16[2,64,1152...) custom-call(s32[2]{0:T(128)S(1)} %pad_add_fusion.place, ...), custom_call_target="tpu_custom_call" | custom-call | tf_op jit(solution)/shard_map/pallas_call | solution.py:483
  8.2 0.0 copy-start.1
  8.2 4.4 %collective-permute-start.8 = (bf16[2,1152,128]{2,1,0:T(8,128)(2,1)S(1)}, bf16[2,1152,128]{2,1,0:T(8,128)(2,1)S(1)}, u32[]{:S(2)}, u32[]{:S(2)}) collective-permute-start(bf16[2,1152,128]{2,1,0:T(8,128)(2,1)S(1)} %get-tuple-element.55.a_ref), channel_id=1, source_target_pairs={{0,1},{1,0},{2,3},{3,2},{4,5},{5,4},{6,7},{7,6},{8,9},{9,8},{10,11... | collective-permute-start | bytes 1769480 | tf_op jit(solution)/shard_map/ppermute | solution.py:494
  12.7 0.7 collective-permute-start.9
  13.4 0.1 collective-permute-start.13
  13.4 5.4 %collective-permute-done.ra_ref = bf16[2,1152,128]{2,1,0:T(8,128)(2,1)S(1)} collective-permute-done((bf16[2,1152,128]{2,1,0:T(8,128)(2,1)S(1)}, bf16[2,1152,128]{2,1,0:T(8,128)(2,1)S(1)}, u32[]{:S(2)}, u32[]{:S(2)}) %collective-permute-start) | collective-permute-done | bytes 589856 | tf_op jit(solution)/shard_map/ppermute | solution.py:494
  18.9 2.0 %collective-permute-start.14 = (bf16[2,64,1152]{2,1,0:T(8,128)(2,1)S(1)}, bf16[2,64,1152]{2,1,0:T(8,128)(2,1)S(1)}, u32[]{:S(2)}, u32[]{:S(2)}) collective-permute-start(bf16[2,64,1152]{2,1,0:T(8,128)(2,1)S(1)} %get-tuple-element.65.refs_10_), channel_id=1, source_target_pairs={{0,8},{4,12},{8,0},{12,4},{1,9},{5,13},{9,1},{13,5},{2,10},{6,14},... | collective-permute-start | bytes 884744 | tf_op jit(solution)/shard_map/ppermute | solution.py:476
  20.8 0.0 collective-permute-done.1.rb_ref
  20.8 0.0 collective-permute-start.15
  20.9 2.4 %shard_map.110 = (bf16[2,576,256]{2,1,0:T(8,128)(2,1)S(1)}, f32[2,640,256]{2,1,0:T(8,128)S(1)}) custom-call(s32[2]{0:T(128)S(1)} %pad_add_fusion.place, s32[2,4]{1,0:T(2,128)S(1)} %bitcast.17, s32[3,2,4]{2,1,0:T(2,128)S(1)} %bitcast.12, bf16[4,576,256]{2,1,0:T(8,128)(2,1)} %bitcast.26, bf16[2,1152,128]{2,1,0:T(8,128)(2,1)S(1)} %get-tuple-element.43.a_ref, ...), custom_call_target="tpu_custom_call" | custom-call | tf_op jit(solution)/shard_map/pallas_call | solution.py:504
  23.3 2.3 %shard_map.111 = (bf16[1,64,1152]{2,1,0:T(8,128)(2,1)S(1)}, bf16[1,64,1152]{2,1,0:T(8,128)(2,1)S(1)}, bf16[1,64,1152]{2,1,0:T(8,128)(2,1)S(1)}, bf16[1,64,1152]{2,1,0:T(8,128)(2,1)S(1)}) custom-call(s32[2]{0:T(128)S(1)} %pad_add_fusion.place, s32[2,4]{1,0:T(2,128)S(1)} %bitcast.18, s32[3,2,4]{2,1,0:T(2,128)S(1)} %bitcast.13, ...), custom_call_target="tpu_custom_call" | custom-call | tf_op jit(solution)/shard_map/pallas_call | solution.py:522
  25.7 5.0 %collective-permute-done.8.ra_ref = bf16[2,1152,128]{2,1,0:T(8,128)(2,1)S(1)} collective-permute-done((bf16[2,1152,128]{2,1,0:T(8,128)(2,1)S(1)}, bf16[2,1152,128]{2,1,0:T(8,128)(2,1)S(1)}, u32[]{:S(2)}, u32[]{:S(2)}) %collective-permute-start.8) | collective-permute-done | bytes 589856 | tf_op jit(solution)/shard_map/ppermute | solution.py:494
  30.7 0.0 collective-permute-start.2
  30.7 2.4 %shard_map.116 = (bf16[2,576,256]{2,1,0:T(8,128)(2,1)S(1)}, f32[2,640,256]{2,1,0:T(8,128)S(1)}) custom-call(s32[2]{0:T(128)S(1)} %pad_add_fusion.place, s32[2,4]{1,0:T(2,128)S(1)} %bitcast.19, s32[3,2,4]{2,1,0:T(2,128)S(1)} %bitcast.14, bf16[4,576,256]{2,1,0:T(8,128)(2,1)} %bitcast.27, bf16[2,1152,128]{2,1,0:T(8,128)(2,1)S(1)} %get-tuple-element.55.a_ref, ...), custom_call_target="tpu_custom_call" | custom-call | tf_op jit(solution)/shard_map/pallas_call | solution.py:504
  33.1 0.0 collective-permute-done.9.rb_ref
  33.1 2.2 %shard_map.117 = (bf16[32,1152]{1,0:T(8,128)(2,1)S(1)}, bf16[32,1152]{1,0:T(8,128)(2,1)S(1)}, bf16[32,1152]{1,0:T(8,128)(2,1)S(1)}, bf16[32,1152]{1,0:T(8,128)(2...) custom-call(s32[2]{0:T(128)S(1)} %pad_add_fusion.place, ...), custom_call_target="tpu_custom_call" | custom-call | tf_op jit(solution)/shard_map/pallas_call | solution.py:547
  35.3 0.6 collective-permute-start.19
  35.8 0.0 collective-permute-done.13.refs_5_
  35.8 1.7 %collective-permute-start.20 = (bf16[32,1152]{1,0:T(8,128)(2,1)S(1)}, bf16[32,1152]{1,0:T(8,128)(2,1)S(1)}, u32[]{:S(2)}, u32[]{:S(2)}) collective-permute-start(bf16[32,1152]{1,0:T(8,128)(2,1)S(1)} %get-tuple-element.70.refs_2_), channel_id=1, source_target_pairs={{0,8},{4,12},{8,0},{12,4},{1,9},{5,13},{9,1},{13,5},{2,10},{6,14},... | collective-permute-start | bytes 221192 | tf_op jit(solution)/shard_map/ppermute | solution.py:476
  37.5 0.0 collective-permute-done.14.refs_6_
  37.5 0.0 collective-permute-start.21
  37.5 2.3 %shard_map.113 = (bf16[1,64,1152]{2,1,0:T(8,128)(2,1)S(1)}, bf16[1,64,1152]{2,1,0:T(8,128)(2,1)S(1)}, bf16[1,64,1152]{2,1,0:T(8,128)(2,1)S(1)}, bf16[1,64,1152]{2,1,0:T(8,128)(2,1)S(1)}) custom-call(s32[2]{0:T(128)S(1)} %pad_add_fusion.place, s32[2,4]{1,0:T(2,128)S(1)} %bitcast.21, s32[3,2,4]{2,1,0:T(2,128)S(1)} %bitcast.16, ...), custom_call_target="tpu_custom_call" | custom-call | tf_op jit(solution)/shard_map/pallas_call | solution.py:522
  39.9 1.5 %collective-permute-start.3 = (bf16[1,64,1152]{2,1,0:T(8,128)(2,1)S(1)}, bf16[1,64,1152]{2,1,0:T(8,128)(2,1)S(1)}, u32[]{:S(2)}, u32[]{:S(2)}) collective-permute-start(bf16[1,64,1152]{2,1,0:T(8,128)(2,1)S(1)} %get-tuple-element.49.refs_10_.refs_1_), channel_id=1, source_target_pairs={{0,8},{4,12},{8,0},{12,4},{1,9},{5,13},{9,1},{13,5},{2,10},{6,14},... | collective-permute-start | bytes 442376 | tf_op jit(solution)/shard_map/ppermute | solution.py:476
  41.4 0.4 collective-permute-start.4
  41.8 0.3 collective-permute-start.5
  42.1 0.0 collective-permute-done.21.refs_3_
  42.1 1.4 %collective-permute-start.6 = (bf16[1,64,1152]{2,1,0:T(8,128)(2,1)S(1)}, bf16[1,64,1152]{2,1,0:T(8,128)(2,1)S(1)}, u32[]{:S(2)}, u32[]{:S(2)}) collective-permute-start(bf16[1,64,1152]{2,1,0:T(8,128)(2,1)S(1)} %get-tuple-element.53.refs_11_.refs_2_), channel_id=1, source_target_pairs={{0,8},{4,12},{8,0},{12,4},{1,9},{5,13},{9,1},{13,5},{2,10},{6,14},... | collective-permute-start | bytes 442376 | tf_op jit(solution)/shard_map/ppermute | solution.py:476
  43.5 0.0 collective-permute-done.2.refs_1_
  43.5 0.1 collective-permute-start.7
  43.6 2.2 %shard_map.121.refs_2_ = bf16[1920,256]{1,0:T(8,128)(2,1)S(1)} custom-call(bf16[32,1152]{1,0:T(8,128)(2,1)S(1)} %get-tuple-element.68.refs_0_, bf16[32,1152]{1,0:T(8,128)(2,1)S(1)} %collective-permute-done.19.refs_1_, bf16[32,1152]{1,0:T(8,128)(2,1)S(1)} %collective-permute-done.20.refs_2_, bf16[32,1152]{1,0:T(8,128)(2,1)S(1)} %collective-permute-done.21.refs_3_, ...), custom_call_target="tpu_custom_call" | custom-call | tf_op jit(solution)/shard_map/pallas_call | solution.py:566
  45.8 0.9 collective-permute-done.3.refs_2_
  46.7 2.1 %collective-permute-done.4.refs_3_ = bf16[1,64,1152]{2,1,0:T(8,128)(2,1)S(1)} collective-permute-done((bf16[1,64,1152]{2,1,0:T(8,128)(2,1)S(1)}, bf16[1,64,1152]{2,1,0:T(8,128)(2,1)S(1)}, u32[]{:S(2)}, u32[]{:S(2)}) %collective-permute-start.4) | collective-permute-done | bytes 147488 | tf_op jit(solution)/shard_map/ppermute | solution.py:476
  48.8 1.4 %shard_map.112.refs_0_ = bf16[1920,256]{1,0:T(8,128)(2,1)S(1)} custom-call(bf16[1,64,1152]{2,1,0:T(8,128)(2,1)S(1)} %get-tuple-element.47.refs_0_.refs_4_.refs_3_, bf16[1,64,1152]{2,1,0:T(8,128)(2,1)S(1)} %collective-permute-done.2.refs_1_, bf16[1,64,1152]{2,1,0:T(8,128)(2,1)S(1)} %collective-permute-done.3.refs_2_, ...), custom_call_target="tpu_custom_call" | custom-call | tf_op jit(solution)/shard_map/pallas_call | solution.py:537
  50.2 0.0 collective-permute-done.5.refs_1_
  50.2 2.8 %collective-permute-done.6.refs_2_ = bf16[1,64,1152]{2,1,0:T(8,128)(2,1)S(1)} collective-permute-done((bf16[1,64,1152]{2,1,0:T(8,128)(2,1)S(1)}, bf16[1,64,1152]{2,1,0:T(8,128)(2,1)S(1)}, u32[]{:S(2)}, u32[]{:S(2)}) %collective-permute-start.6) | collective-permute-done | bytes 147488 | tf_op jit(solution)/shard_map/ppermute | solution.py:476
  53.0 2.1 %collective-permute-done.7.refs_3_ = bf16[1,64,1152]{2,1,0:T(8,128)(2,1)S(1)} collective-permute-done((bf16[1,64,1152]{2,1,0:T(8,128)(2,1)S(1)}, bf16[1,64,1152]{2,1,0:T(8,128)(2,1)S(1)}, u32[]{:S(2)}, u32[]{:S(2)}) %collective-permute-start.7) | collective-permute-done | bytes 147488 | tf_op jit(solution)/shard_map/ppermute | solution.py:476
  55.1 1.4 %shard_map.114.refs_1_ = bf16[1920,256]{1,0:T(8,128)(2,1)S(1)} custom-call(bf16[1,64,1152]{2,1,0:T(8,128)(2,1)S(1)} %get-tuple-element.51.refs_0_.refs_5_.refs_4_, bf16[1,64,1152]{2,1,0:T(8,128)(2,1)S(1)} %collective-permute-done.5.refs_1_, bf16[1,64,1152]{2,1,0:T(8,128)(2,1)S(1)} %collective-permute-done.6.refs_2_, ...), custom_call_target="tpu_custom_call" | custom-call | tf_op jit(solution)/shard_map/pallas_call | solution.py:537
  56.5 1.8 %shard_map.122 = (bf16[32,2304]{1,0:T(8,128)(2,1)S(1)}, bf16[32,2304]{1,0:T(8,128)(2,1)S(1)}, bf16[32,2304]{1,0:T(8,128)(2,1)S(1)}, bf16[32,2304]{1,0:T(8,128)(2,1)S(1)}) custom-call(bf16[1920,256]{1,0:T(8,128)(2,1)S(1)} %shard_map.112.refs_0_, bf16[1920,256]{1,0:T(8,128)(2,1)S(1)} %shard_map.114.refs_1_, bf16[1920,256]{1,0:T(8,128)(2,1)S(1)} %shard_map.121.refs_2_), custom_call_target="tpu_custom_call" | custom-call | tf_op jit(solution)/shard_map/pallas_call | solution.py:577
  58.3 0.4 collective-permute-start.22
  58.7 0.3 collective-permute-start.10
  58.9 1.8 %collective-permute-start.11 = (bf16[32,1152]{1,0:T(8,128)(2,1)S(1)}, bf16[32,1152]{1,0:T(8,128)(2,1)S(1)}, u32[]{:S(2)}, u32[]{:S(2)}) collective-permute-start(bf16[32,1152]{1,0:T(8,128)(2,1)S(1)} %get-tuple-element.61.refs_6_), channel_id=1, source_target_pairs={{0,8},{4,12},{8,0},{12,4},{1,9},{5,13},{9,1},{13,5},{2,10},{6,14},... | collective-permute-start | bytes 221192 | tf_op jit(solution)/shard_map/ppermute | solution.py:476
  60.8 2.7 %collective-permute-done.11.refs_2_ = bf16[32,1152]{1,0:T(8,128)(2,1)S(1)} collective-permute-done((bf16[32,1152]{1,0:T(8,128)(2,1)S(1)}, bf16[32,1152]{1,0:T(8,128)(2,1)S(1)}, u32[]{:S(2)}, u32[]{:S(2)}) %collective-permute-start.11) | collective-permute-done | bytes 73760 | tf_op jit(solution)/shard_map/ppermute | solution.py:476
  63.5 1.7 %collective-permute-done.12.refs_3_ = bf16[32,1152]{1,0:T(8,128)(2,1)S(1)} collective-permute-done((bf16[32,1152]{1,0:T(8,128)(2,1)S(1)}, bf16[32,1152]{1,0:T(8,128)(2,1)S(1)}, u32[]{:S(2)}, u32[]{:S(2)}) %collective-permute-start.12) | collective-permute-done | bytes 73760 | tf_op jit(solution)/shard_map/ppermute | solution.py:476
  65.2 2.2 %shard_map.118.refs_2_ = bf16[1920,256]{1,0:T(8,128)(2,1)S(1)} custom-call(bf16[32,1152]{1,0:T(8,128)(2,1)S(1)} %get-tuple-element.59.refs_0_.refs_4_, bf16[32,1152]{1,0:T(8,128)(2,1)S(1)} %collective-permute-done.10.refs_1_, bf16[32,1152]{1,0:T(8,128)(2,1)S(1)} %collective-permute-done.11.refs_2_, bf16[32,1152]{1,0:T(8,128)(2,1)S(1)} %collective-permute-done.12.refs_3_, ...), custom_call_target="tpu_custom_call" | custom-call | tf_op jit(solution)/shard_map/pallas_call | solution.py:566
  67.4 1.1 %collective-permute-start.23 = (bf16[32,2304]{1,0:T(8,128)(2,1)S(1)}, bf16[32,2304]{1,0:T(8,128)(2,1)S(1)}, u32[]{:S(2)}, u32[]{:S(2)}) collective-permute-start(bf16[32,2304]{1,0:T(8,128)(2,1)S(1)} %get-tuple-element.77), channel_id=1, source_target_pairs={{12,0},{8,4},{4,8},{0,12},{13,1},{9,5},{5,9},{1,13},{14,2},{10,6},... | collective-permute-start | bytes 442376 | tf_op jit(solution)/shard_map/ppermute | solution.py:585
  68.5 0.7 collective-permute-start.24
  69.2 1.8 %shard_map.119 = (bf16[32,2304]{1,0:T(8,128)(2,1)S(1)}, bf16[32,2304]{1,0:T(8,128)(2,1)S(1)}, bf16[32,2304]{1,0:T(8,128)(2,1)S(1)}, bf16[32,2304]{1,0:T(8,128)(2,1)S(1)}) custom-call(bf16[1920,256]{1,0:T(8,128)(2,1)S(1)} %shard_map.112.refs_0_, bf16[1920,256]{1,0:T(8,128)(2,1)S(1)} %shard_map.114.refs_1_, bf16[1920,256]{1,0:T(8,128)(2,1)S(1)} %shard_map.118.refs_2_), custom_call_target="tpu_custom_call" | custom-call | tf_op jit(solution)/shard_map/pallas_call | solution.py:577
  71.0 0.2 collective-permute-start.17
  71.2 1.3 %collective-permute-start.18 = (bf16[32,2304]{1,0:T(8,128)(2,1)S(1)}, bf16[32,2304]{1,0:T(8,128)(2,1)S(1)}, u32[]{:S(2)}, u32[]{:S(2)}) collective-permute-start(bf16[32,2304]{1,0:T(8,128)(2,1)S(1)} %get-tuple-element.74), channel_id=1, source_target_pairs={{12,0},{8,4},{4,8},{0,12},{13,1},{9,5},{5,9},{1,13},{14,2},{10,6},... | collective-permute-start | bytes 442376 | tf_op jit(solution)/shard_map/ppermute | solution.py:585
  72.5 0.0 collective-permute-done.22.refs_1_
  72.5 0.7 collective-permute-start.16
  73.2 1.5 %shard_map.120.refs_12_.refs_9_.refs_3_ = bf16[4,2,64,1152]{3,2,1,0:T(8,128)(2,1)S(1)} custom-call(bf16[32,1152]{1,0:T(8,128)(2,1)S(1)} %get-tuple-element.68.refs_0_, bf16[32,1152]{1,0:T(8,128)(2,1)S(1)} %get-tuple-element.69.refs_1_, bf16[32,1152]{1,0:T(8,128)(2,1)S(1)} %get-tuple-element.70.refs_2_, bf16[32,1152]{1,0:T(8,128)(2,1)S(1)} %get-tuple-element.71.refs_3_, ...), custom_call_target="tpu_custom_call" | custom-call | tf_op jit(solution)/shard_map/pallas_call | solution.py:590
  74.8 2.3 %collective-permute-done.24.refs_3_ = bf16[32,2304]{1,0:T(8,128)(2,1)S(1)} collective-permute-done((bf16[32,2304]{1,0:T(8,128)(2,1)S(1)}, bf16[32,2304]{1,0:T(8,128)(2,1)S(1)}, u32[]{:S(2)}, u32[]{:S(2)}) %collective-permute-start.24) | collective-permute-done | bytes 147488 | tf_op jit(solution)/shard_map/ppermute | solution.py:585
  77.0 2.1 %shard_map.123.refs_12_ = bf16[4,4,32,1152]{3,2,1,0:T(8,128)(2,1)S(1)} custom-call(s32[2]{0:T(128)S(1)} %pad_add_fusion.place, bf16[32,2304]{1,0:T(8,128)(2,1)S(1)} %get-tuple-element.75.refs_0_, bf16[32,2304]{1,0:T(8,128)(2,1)S(1)} %collective-permute-done.22.refs_1_, bf16[32,2304]{1,0:T(8,128)(2,1)S(1)} %collective-permute-done.23.refs_2_, ...), custom_call_target="tpu_custom_call" | custom-call | tf_op jit(solution)/shard_map/pallas_call | solution.py:621
  79.1 0.0 collective-permute-done.17.refs_1_
  79.1 0.5 collective-permute-done.18.refs_2_
  79.6 2.6 %shard_map.124 = (bf16[4,256,1152]{2,1,0:T(8,128)(2,1)}, bf16[3,4,32,1152]{3,2,1,0:T(8,128)(2,1)S(1)}) custom-call(s32[2]{0:T(128)S(1)} %pad_add_fusion.place, bf16[32,2304]{1,0:T(8,128)(2,1)S(1)} %get-tuple-element.72.refs_0_, bf16[32,2304]{1,0:T(8,128)(2,1)S(1)} %collective-permute-done.17.refs_1_, bf16[32,2304]{1,0:T(8,128)(2,1)S(1)} %collective-permute-done.18.refs_2_, ...), custom_call_target="tpu_custom_call" | custom-call | tf_op jit(solution)/shard_map/pallas_call | solution.py:621
  82.2 0.8 collective-permute-done.16.refs_0_
  83.1 1.9 %shard_map.125 = bf16[4,256,1152]{2,1,0:T(8,128)(2,1)} custom-call(s32[2]{0:T(128)S(1)} %pad_add_fusion.place, bf16[32,2304]{1,0:T(8,128)(2,1)S(1)} %collective-permute-done.16.refs_0_, bf16[1,64,1152]{2,1,0:T(8,128)(2,1)S(1)} %get-tuple-element.49.refs_10_.refs_1_, ...), custom_call_target="tpu_custom_call", output_to_operand_aliasing={{}: (8, {})} | custom-call | tf_op jit(solution)/shard_map/pallas_call | solution.py:621
  (22 shorter events, 0.1 us)
Async XLA Ops:
  1.6 17.3 %collective-permute-start = (bf16[2,1152,128]{2,1,0:T(8,128)(2,1)S(1)}, bf16[2,1152,128]{2,1,0:T(8,128)(2,1)S(1)}, u32[]{:S(2)}, u32[]{:S(2)}) collective-permute-start(bf16[2,1152,128]{2,1,0:T(8,128)(2,1)S(1)} %get-tuple-element.43.a_ref), channel_id=1, source_target_pairs={{0,1},{1,0},{2,3},{3,2},{4,5},{5,4},{6,7},{7,6},{8,9},{9,8},{10,11... | collective-permute-start | bytes 1769480 | tf_op jit(solution)/shard_map/ppermute | solution.py:494
  4.7 16.1 %copy-start.6 = (f32[1152]{0:T(1024)S(1)}, f32[1152]{0:T(1024)}, u32[]{:S(2)}) copy-start(f32[1152]{0:T(1024)} %param.16) | copy-start | bytes 13828
  4.7 16.2 %copy-start.4 = (s32[4,2,3]{0,1,2:T(2,128)S(1)}, s32[4,2,3]{0,1,2:T(2,128)}, u32[]{:S(2)}) copy-start(s32[4,2,3]{0,1,2:T(2,128)} %param.20) | copy-start | bytes 292
  4.7 16.2 %copy-start.5 = (s32[4,2]{0,1:T(2,128)S(1)}, s32[4,2]{0,1:T(2,128)}, u32[]{:S(2)}) copy-start(s32[4,2]{0,1:T(2,128)} %param.21) | copy-start | bytes 100
  4.7 16.1 %collective-permute-start.1 = (bf16[2,1152,128]{2,1,0:T(8,128)(2,1)S(1)}, bf16[2,1152,128]{2,1,0:T(8,128)(2,1)S(1)}, u32[]{:S(2)}, u32[]{:S(2)}) collective-permute-start(bf16[2,1152,128]{2,1,0:T(8,128)(2,1)S(1)} %get-tuple-element.44.b_ref), channel_id=1, source_target_pairs={{1,2},{2,1},{5,6},{6,5},{9,10},{10,9},{13,14},{14,13},{17,18},{18,... | collective-permute-start | bytes 1769480 | tf_op jit(solution)/shard_map/ppermute | solution.py:494
  5.5 17.8 %copy-start.2 = (bf16[4,256,1152]{2,1,0:T(8,128)(2,1)S(1)}, bf16[4,256,1152]{2,1,0:T(8,128)(2,1)}, u32[]{:S(2)}) copy-start(bf16[4,256,1152]{2,1,0:T(8,128)(2,1)} %refs_0_.1) | copy-start | bytes 7077892
  8.2 15.1 %copy-start.1 = (bf16[576,1152]{1,0:T(8,128)(2,1)S(1)}, bf16[576,1152]{1,0:T(8,128)(2,1)}, u32[]{:S(2)}) copy-start(bf16[576,1152]{1,0:T(8,128)(2,1)} %refs_8_.3) | copy-start | bytes 3981316
  8.2 22.4 %collective-permute-start.8 = (bf16[2,1152,128]{2,1,0:T(8,128)(2,1)S(1)}, bf16[2,1152,128]{2,1,0:T(8,128)(2,1)S(1)}, u32[]{:S(2)}, u32[]{:S(2)}) collective-permute-start(bf16[2,1152,128]{2,1,0:T(8,128)(2,1)S(1)} %get-tuple-element.55.a_ref), channel_id=1, source_target_pairs={{0,1},{1,0},{2,3},{3,2},{4,5},{5,4},{6,7},{7,6},{8,9},{9,8},{10,11... | collective-permute-start | bytes 1769480 | tf_op jit(solution)/shard_map/ppermute | solution.py:494
  12.7 20.4 %collective-permute-start.9 = (bf16[2,1152,128]{2,1,0:T(8,128)(2,1)S(1)}, bf16[2,1152,128]{2,1,0:T(8,128)(2,1)S(1)}, u32[]{:S(2)}, u32[]{:S(2)}) collective-permute-start(bf16[2,1152,128]{2,1,0:T(8,128)(2,1)S(1)} %get-tuple-element.56.b_ref), channel_id=1, source_target_pairs={{1,2},{2,1},{5,6},{6,5},{9,10},{10,9},{13,14},{14,13},{17,18},{18,... | collective-permute-start | bytes 1769480 | tf_op jit(solution)/shard_map/ppermute | solution.py:494
  13.4 22.5 %collective-permute-start.13 = (bf16[2,64,1152]{2,1,0:T(8,128)(2,1)S(1)}, bf16[2,64,1152]{2,1,0:T(8,128)(2,1)S(1)}, u32[]{:S(2)}, u32[]{:S(2)}) collective-permute-start(bf16[2,64,1152]{2,1,0:T(8,128)(2,1)S(1)} %get-tuple-element.64.refs_9_), channel_id=1, source_target_pairs={{0,4},{4,0},{8,12},{12,8},{1,5},{5,1},{9,13},{13,9},{2,6},{6,2},{1... | collective-permute-start | bytes 884744 | tf_op jit(solution)/shard_map/ppermute | solution.py:476
  18.9 18.6 %collective-permute-start.14 = (bf16[2,64,1152]{2,1,0:T(8,128)(2,1)S(1)}, bf16[2,64,1152]{2,1,0:T(8,128)(2,1)S(1)}, u32[]{:S(2)}, u32[]{:S(2)}) collective-permute-start(bf16[2,64,1152]{2,1,0:T(8,128)(2,1)S(1)} %get-tuple-element.65.refs_10_), channel_id=1, source_target_pairs={{0,8},{4,12},{8,0},{12,4},{1,9},{5,13},{9,1},{13,5},{2,10},{6,14},... | collective-permute-start | bytes 884744 | tf_op jit(solution)/shard_map/ppermute | solution.py:476
  20.8 19.0 %collective-permute-start.15 = (bf16[2,64,1152]{2,1,0:T(8,128)(2,1)S(1)}, bf16[2,64,1152]{2,1,0:T(8,128)(2,1)S(1)}, u32[]{:S(2)}, u32[]{:S(2)}) collective-permute-start(bf16[2,64,1152]{2,1,0:T(8,128)(2,1)S(1)} %get-tuple-element.66.refs_11_), channel_id=1, source_target_pairs={{0,12},{4,8},{8,4},{12,0},{1,13},{5,9},{9,5},{13,1},{2,14},{6,10},... | collective-permute-start | bytes 884744 | tf_op jit(solution)/shard_map/ppermute | solution.py:476
  30.7 12.9 %collective-permute-start.2 = (bf16[1,64,1152]{2,1,0:T(8,128)(2,1)S(1)}, bf16[1,64,1152]{2,1,0:T(8,128)(2,1)S(1)}, u32[]{:S(2)}, u32[]{:S(2)}) collective-permute-start(bf16[1,64,1152]{2,1,0:T(8,128)(2,1)S(1)} %get-tuple-element.48.refs_6_.refs_5_), channel_id=1, source_target_pairs={{0,4},{4,0},{8,12},{12,8},{1,5},{5,1},{9,13},{13,9},{2,6},{6,2},{1... | collective-permute-start | bytes 442376 | tf_op jit(solution)/shard_map/ppermute | solution.py:476
  35.3 6.1 %collective-permute-start.19 = (bf16[32,1152]{1,0:T(8,128)(2,1)S(1)}, bf16[32,1152]{1,0:T(8,128)(2,1)S(1)}, u32[]{:S(2)}, u32[]{:S(2)}) collective-permute-start(bf16[32,1152]{1,0:T(8,128)(2,1)S(1)} %get-tuple-element.69.refs_1_), channel_id=1, source_target_pairs={{0,4},{4,0},{8,12},{12,8},{1,5},{5,1},{9,13},{13,9},{2,6},{6,2},{1... | collective-permute-start | bytes 221192 | tf_op jit(solution)/shard_map/ppermute | solution.py:476
  35.8 5.9 %collective-permute-start.20 = (bf16[32,1152]{1,0:T(8,128)(2,1)S(1)}, bf16[32,1152]{1,0:T(8,128)(2,1)S(1)}, u32[]{:S(2)}, u32[]{:S(2)}) collective-permute-start(bf16[32,1152]{1,0:T(8,128)(2,1)S(1)} %get-tuple-element.70.refs_2_), channel_id=1, source_target_pairs={{0,8},{4,12},{8,0},{12,4},{1,9},{5,13},{9,1},{13,5},{2,10},{6,14},... | collective-permute-start | bytes 221192 | tf_op jit(solution)/shard_map/ppermute | solution.py:476
  37.5 4.6 %collective-permute-start.21 = (bf16[32,1152]{1,0:T(8,128)(2,1)S(1)}, bf16[32,1152]{1,0:T(8,128)(2,1)S(1)}, u32[]{:S(2)}, u32[]{:S(2)}) collective-permute-start(bf16[32,1152]{1,0:T(8,128)(2,1)S(1)} %get-tuple-element.71.refs_3_), channel_id=1, source_target_pairs={{0,12},{4,8},{8,4},{12,0},{1,13},{5,9},{9,5},{13,1},{2,14},{6,10},... | collective-permute-start | bytes 221192 | tf_op jit(solution)/shard_map/ppermute | solution.py:476
  37.5 6.1 %copy-start = (bf16[1152,1728]{0,1:T(8,128)(2,1)S(1)}, bf16[1152,1728]{0,1:T(8,128)(2,1)}, u32[]{:S(2)}) copy-start(bf16[1152,1728]{0,1:T(8,128)(2,1)} %param.17) | copy-start | bytes 11943940
  39.9 6.8 %collective-permute-start.3 = (bf16[1,64,1152]{2,1,0:T(8,128)(2,1)S(1)}, bf16[1,64,1152]{2,1,0:T(8,128)(2,1)S(1)}, u32[]{:S(2)}, u32[]{:S(2)}) collective-permute-start(bf16[1,64,1152]{2,1,0:T(8,128)(2,1)S(1)} %get-tuple-element.49.refs_10_.refs_1_), channel_id=1, source_target_pairs={{0,8},{4,12},{8,0},{12,4},{1,9},{5,13},{9,1},{13,5},{2,10},{6,14},... | collective-permute-start | bytes 442376 | tf_op jit(solution)/shard_map/ppermute | solution.py:476
  41.4 7.4 %collective-permute-start.4 = (bf16[1,64,1152]{2,1,0:T(8,128)(2,1)S(1)}, bf16[1,64,1152]{2,1,0:T(8,128)(2,1)S(1)}, u32[]{:S(2)}, u32[]{:S(2)}) collective-permute-start(bf16[1,64,1152]{2,1,0:T(8,128)(2,1)S(1)} %get-tuple-element.50.refs_8_.refs_7_), channel_id=1, source_target_pairs={{0,12},{4,8},{8,4},{12,0},{1,13},{5,9},{9,5},{13,1},{2,14},{6,10},... | collective-permute-start | bytes 442376 | tf_op jit(solution)/shard_map/ppermute | solution.py:476
  41.8 8.4 %collective-permute-start.5 = (bf16[1,64,1152]{2,1,0:T(8,128)(2,1)S(1)}, bf16[1,64,1152]{2,1,0:T(8,128)(2,1)S(1)}, u32[]{:S(2)}, u32[]{:S(2)}) collective-permute-start(bf16[1,64,1152]{2,1,0:T(8,128)(2,1)S(1)} %get-tuple-element.52.refs_7_.refs_6_), channel_id=1, source_target_pairs={{0,4},{4,0},{8,12},{12,8},{1,5},{5,1},{9,13},{13,9},{2,6},{6,2},{1... | collective-permute-start | bytes 442376 | tf_op jit(solution)/shard_map/ppermute | solution.py:476
  42.1 10.9 %collective-permute-start.6 = (bf16[1,64,1152]{2,1,0:T(8,128)(2,1)S(1)}, bf16[1,64,1152]{2,1,0:T(8,128)(2,1)S(1)}, u32[]{:S(2)}, u32[]{:S(2)}) collective-permute-start(bf16[1,64,1152]{2,1,0:T(8,128)(2,1)S(1)} %get-tuple-element.53.refs_11_.refs_2_), channel_id=1, source_target_pairs={{0,8},{4,12},{8,0},{12,4},{1,9},{5,13},{9,1},{13,5},{2,10},{6,14},... | collective-permute-start | bytes 442376 | tf_op jit(solution)/shard_map/ppermute | solution.py:476
  43.5 11.6 %collective-permute-start.7 = (bf16[1,64,1152]{2,1,0:T(8,128)(2,1)S(1)}, bf16[1,64,1152]{2,1,0:T(8,128)(2,1)S(1)}, u32[]{:S(2)}, u32[]{:S(2)}) collective-permute-start(bf16[1,64,1152]{2,1,0:T(8,128)(2,1)S(1)} %get-tuple-element.54.refs_9_.refs_8_), channel_id=1, source_target_pairs={{0,12},{4,8},{8,4},{12,0},{1,13},{5,9},{9,5},{13,1},{2,14},{6,10},... | collective-permute-start | bytes 442376 | tf_op jit(solution)/shard_map/ppermute | solution.py:476
  58.3 14.2 %collective-permute-start.22 = (bf16[32,2304]{1,0:T(8,128)(2,1)S(1)}, bf16[32,2304]{1,0:T(8,128)(2,1)S(1)}, u32[]{:S(2)}, u32[]{:S(2)}) collective-permute-start(bf16[32,2304]{1,0:T(8,128)(2,1)S(1)} %get-tuple-element.76), channel_id=1, source_target_pairs={{4,0},{0,4},{12,8},{8,12},{5,1},{1,5},{13,9},{9,13},{6,2},{2,6},{1... | collective-permute-start | bytes 442376 | tf_op jit(solution)/shard_map/ppermute | solution.py:585
  58.7 2.1 %collective-permute-start.10 = (bf16[32,1152]{1,0:T(8,128)(2,1)S(1)}, bf16[32,1152]{1,0:T(8,128)(2,1)S(1)}, u32[]{:S(2)}, u32[]{:S(2)}) collective-permute-start(bf16[32,1152]{1,0:T(8,128)(2,1)S(1)} %get-tuple-element.60.refs_5_), channel_id=1, source_target_pairs={{0,4},{4,0},{8,12},{12,8},{1,5},{5,1},{9,13},{13,9},{2,6},{6,2},{1... | collective-permute-start | bytes 221192 | tf_op jit(solution)/shard_map/ppermute | solution.py:476
  58.9 4.5 %collective-permute-start.11 = (bf16[32,1152]{1,0:T(8,128)(2,1)S(1)}, bf16[32,1152]{1,0:T(8,128)(2,1)S(1)}, u32[]{:S(2)}, u32[]{:S(2)}) collective-permute-start(bf16[32,1152]{1,0:T(8,128)(2,1)S(1)} %get-tuple-element.61.refs_6_), channel_id=1, source_target_pairs={{0,8},{4,12},{8,0},{12,4},{1,9},{5,13},{9,1},{13,5},{2,10},{6,14},... | collective-permute-start | bytes 221192 | tf_op jit(solution)/shard_map/ppermute | solution.py:476
  60.8 4.4 %collective-permute-start.12 = (bf16[32,1152]{1,0:T(8,128)(2,1)S(1)}, bf16[32,1152]{1,0:T(8,128)(2,1)S(1)}, u32[]{:S(2)}, u32[]{:S(2)}) collective-permute-start(bf16[32,1152]{1,0:T(8,128)(2,1)S(1)} %get-tuple-element.62.refs_7_), channel_id=1, source_target_pairs={{0,12},{4,8},{8,4},{12,0},{1,13},{5,9},{9,5},{13,1},{2,14},{6,10},... | collective-permute-start | bytes 221192 | tf_op jit(solution)/shard_map/ppermute | solution.py:476
  67.4 7.4 %collective-permute-start.23 = (bf16[32,2304]{1,0:T(8,128)(2,1)S(1)}, bf16[32,2304]{1,0:T(8,128)(2,1)S(1)}, u32[]{:S(2)}, u32[]{:S(2)}) collective-permute-start(bf16[32,2304]{1,0:T(8,128)(2,1)S(1)} %get-tuple-element.77), channel_id=1, source_target_pairs={{12,0},{8,4},{4,8},{0,12},{13,1},{9,5},{5,9},{1,13},{14,2},{10,6},... | collective-permute-start | bytes 442376 | tf_op jit(solution)/shard_map/ppermute | solution.py:585
  68.4 4.7 %copy-start.7 = (f32[1152]{0:T(1024)S(1)}, f32[1152]{0:T(1024)}, u32[]{:S(2)}) copy-start(f32[1152]{0:T(1024)} %param.19) | copy-start | bytes 13828
  68.5 8.6 %collective-permute-start.24 = (bf16[32,2304]{1,0:T(8,128)(2,1)S(1)}, bf16[32,2304]{1,0:T(8,128)(2,1)S(1)}, u32[]{:S(2)}, u32[]{:S(2)}) collective-permute-start(bf16[32,2304]{1,0:T(8,128)(2,1)S(1)} %get-tuple-element.78), channel_id=1, source_target_pairs={{8,0},{12,4},{0,8},{4,12},{9,1},{13,5},{1,9},{5,13},{10,2},{14,6},... | collective-permute-start | bytes 442376 | tf_op jit(solution)/shard_map/ppermute | solution.py:585
  71.0 8.2 %collective-permute-start.17 = (bf16[32,2304]{1,0:T(8,128)(2,1)S(1)}, bf16[32,2304]{1,0:T(8,128)(2,1)S(1)}, u32[]{:S(2)}, u32[]{:S(2)}) collective-permute-start(bf16[32,2304]{1,0:T(8,128)(2,1)S(1)} %get-tuple-element.73), channel_id=1, source_target_pairs={{4,0},{0,4},{12,8},{8,12},{5,1},{1,5},{13,9},{9,13},{6,2},{2,6},{1... | collective-permute-start | bytes 442376 | tf_op jit(solution)/shard_map/ppermute | solution.py:585
  71.2 8.4 %collective-permute-start.18 = (bf16[32,2304]{1,0:T(8,128)(2,1)S(1)}, bf16[32,2304]{1,0:T(8,128)(2,1)S(1)}, u32[]{:S(2)}, u32[]{:S(2)}) collective-permute-start(bf16[32,2304]{1,0:T(8,128)(2,1)S(1)} %get-tuple-element.74), channel_id=1, source_target_pairs={{12,0},{8,4},{4,8},{0,12},{13,1},{9,5},{5,9},{1,13},{14,2},{10,6},... | collective-permute-start | bytes 442376 | tf_op jit(solution)/shard_map/ppermute | solution.py:585
  72.5 10.6 %collective-permute-start.16 = (bf16[32,2304]{1,0:T(8,128)(2,1)S(1)}, bf16[32,2304]{1,0:T(8,128)(2,1)S(1)}, u32[]{:S(2)}, u32[]{:S(2)}) collective-permute-start(bf16[32,2304]{1,0:T(8,128)(2,1)S(1)} %get-tuple-element.67), channel_id=1, source_target_pairs={{8,0},{12,4},{0,8},{4,12},{9,1},{13,5},{1,9},{5,13},{10,2},{14,6},... | collective-permute-start | bytes 442376 | tf_op jit(solution)/shard_map/ppermute | solution.py:585
  73.2 3.8 %copy-start.3 = (bf16[576,1152]{1,0:T(8,128)(2,1)S(1)}, bf16[576,1152]{1,0:T(8,128)(2,1)}, u32[]{:S(2)}) copy-start(bf16[576,1152]{1,0:T(8,128)(2,1)} %refs_4_.1) | copy-start | bytes 3981316

commit v10 on v9

--- a/solution.py
+++ b/solution.py
@@ -473,7 +473,9 @@
         return [(i, peer(i, j, groups)) for i in range(groups)]
 
     def send(parts):
-        sent = {j: lax.ppermute(parts[j], "frame", out_pairs(j)) for j in reversed(range(1, groups))}
+        sent = {}
+        for j in range(1, groups):
+            sent[j] = lax.ppermute(parts[j], "frame", out_pairs(j))
         return [parts[0]] + [sent[j] for j in range(1, groups)]
 
     halos = []
@@ -581,10 +583,9 @@
             [jax.ShapeDtypeStruct(back_shape, BF)] * groups,
             [pltpu.VMEM((rows // SUB, width, groups * frames * SUB), BF)],
         )(*projected, late_projected)
-        home = {
-            j: lax.ppermute(back[j], "frame", [(b, a) for a, b in out_pairs(j)])
-            for j in reversed(range(1, groups))
-        }
+        home = {}
+        for j in range(1, groups):
+            home[j] = lax.ppermute(back[j], "frame", [(b, a) for a, b in out_pairs(j)])
         returned.append([back[0]] + [home[j] for j in range(1, groups)])
 
     late_mixed = call(
@@ -596,10 +597,10 @@
         jax.ShapeDtypeStruct((groups, late, share, model), BF),
     )(*[x for some in own_late for x in some], *own_hidden, spatial_out_weight, gain_one)
 
-    order = [0, 1] + list(reversed(range(2, groups))) if groups > 1 else [0]
     tail = max(1, groups // 4)
-    calls = [(tuple(order), half) for half in range(halves - 1)]
-    calls += [(tuple(js), halves - 1) for js in (order[:-tail], order[-tail:]) if js]
+    order = tuple(range(groups))
+    calls = [(order, half) for half in range(halves - 1)]
+    calls += [(js, halves - 1) for js in (order[:2], order[2:-tail], order[max(2, groups - tail):]) if js]
     result = jax.ShapeDtypeStruct((frames, tokens, model), BF)
     out = handed = before = None
     for n, (js, half) in enumerate(calls):

time: 85.5 us -> 81.7 us (0.956)
  waiting for transfers between devices: 26.3 us -> 21 us
  Pallas kernels: 34.7 us -> 36.2 us
    ppermute x21, waiting for transfers between devices: 15.9 us -> 10.6 us  [the longest x15 10.6 us: send(): sent[j] = lax.ppermute(parts[j], 'frame', out_pairs(j))]
    pallas_call x3 -> x4, Pallas kernels: 6.66 us -> 8.23 us  [shards(): call(functools.partial(output_kernel, groups, js, early, half, halves, be...]
  transfers between devices with their start and end apart: 25 -> 25, of which waited for: 11 -> 8; matrix products, arithmetic and copies ran while one was open for 0% -> 0% of each run, Pallas kernels for 33% -> 36%
where the time goes in v10:
time: 81.7 us; the launch traced here: 81.4 us
  Pallas kernels  36.2 us (44%)
  starting transfers between devices  23.5 us (29%)
  waiting for transfers between devices  21 us (26%)
    ppermute x15, waiting for transfers between devices, send(): sent[j] = lax.ppermute(parts[j], 'frame', out_pairs(j))  10.6 us
    ppermute x2, waiting for transfers between devices, shards(): lax.ppermute(a, 'strip', near)  10.4 us
    ppermute x15, starting transfers between devices, send(): sent[j] = lax.ppermute(parts[j], 'frame', out_pairs(j))  10.1 us
    pallas_call x4, Pallas kernels, shards(): call(functools.partial(output_kernel, groups, js, early, half, halves, be...  8.23 us
    ppermute x2, starting transfers between devices, shards(): lax.ppermute(a, 'strip', near)  7.55 us
    pallas_call x2, Pallas kernels, shards(): call(functools.partial(local_kernel, some * late), [smem, smem, smem, blo...  4.78 us
    pallas_call x2, Pallas kernels, shards(): call(functools.partial(spatial_kernel, f, groups), [smem, smem, smem, one...  4.68 us
    ppermute x6, starting transfers between devices, shards(): home[j] = lax.ppermute(back[j], 'frame', [(b, a) for a, b in out_pairs(j)])  4.36 us
  transfers between devices with their start and end apart: 25, of which 8 were waited for; matrix products, arithmetic and copies ran while one was open for 0% of the time, Pallas kernels for 36%

profile of v10, /device:TPU:0, one launch (start us, length us, event | category | flops | bytes accessed | tf_op | source)
XLA Modules:
  0.0 81.4 jit_solution(10076637373317522218)
XLA Ops:
  0.0 0.1 pad_add_fusion.place
  0.1 1.5 %shard_map.109 = (bf16[2,1152,128]{2,1,0:T(8,128)(2,1)S(1)}, bf16[2,1152,128]{2,1,0:T(8,128)(2,1)S(1)}) custom-call(s32[2]{0:T(128)S(1)} %pad_add_fusion.place, bf16[4,576,256]{2,1,0:T(8,128)(2,1)} %bitcast.22, bf16[4,576,256]{2,1,0:T(8,128)(2,1)} %bitcast.24), custom_call_target="tpu_custom_call" | custom-call | tf_op jit(solution)/shard_map/pallas_call | solution.py:485
  1.6 3.1 %collective-permute-start = (bf16[2,1152,128]{2,1,0:T(8,128)(2,1)S(1)}, bf16[2,1152,128]{2,1,0:T(8,128)(2,1)S(1)}, u32[]{:S(2)}, u32[]{:S(2)}) collective-permute-start(bf16[2,1152,128]{2,1,0:T(8,128)(2,1)S(1)} %get-tuple-element.45.a_ref), channel_id=1, source_target_pairs={{0,1},{1,0},{2,3},{3,2},{4,5},{5,4},{6,7},{7,6},{8,9},{9,8},{10,11... | collective-permute-start | bytes 1769480 | tf_op jit(solution)/shard_map/ppermute | solution.py:496
  4.7 0.8 %collective-permute-start.1 = (bf16[2,1152,128]{2,1,0:T(8,128)(2,1)S(1)}, bf16[2,1152,128]{2,1,0:T(8,128)(2,1)S(1)}, u32[]{:S(2)}, u32[]{:S(2)}) collective-permute-start(bf16[2,1152,128]{2,1,0:T(8,128)(2,1)S(1)} %get-tuple-element.46.b_ref), channel_id=1, source_target_pairs={{1,2},{2,1},{5,6},{6,5},{9,10},{10,9},{13,14},{14,13},{17,18},{18,... | collective-permute-start | bytes 1769480 | tf_op jit(solution)/shard_map/ppermute | solution.py:496
  5.5 0.0 copy-start.3
  5.5 2.7 %shard_map.115 = (bf16[2,1152,128]{2,1,0:T(8,128)(2,1)S(1)}, bf16[2,1152,128]{2,1,0:T(8,128)(2,1)S(1)}, bf16[2,64,1152]{2,1,0:T(8,128)(2,1)S(1)}, bf16[2,64,1152...) custom-call(s32[2]{0:T(128)S(1)} %pad_add_fusion.place, ...), custom_call_target="tpu_custom_call" | custom-call | tf_op jit(solution)/shard_map/pallas_call | solution.py:485
  8.2 0.0 copy-start.1
  8.2 4.4 %collective-permute-start.8 = (bf16[2,1152,128]{2,1,0:T(8,128)(2,1)S(1)}, bf16[2,1152,128]{2,1,0:T(8,128)(2,1)S(1)}, u32[]{:S(2)}, u32[]{:S(2)}) collective-permute-start(bf16[2,1152,128]{2,1,0:T(8,128)(2,1)S(1)} %get-tuple-element.57.a_ref), channel_id=1, source_target_pairs={{0,1},{1,0},{2,3},{3,2},{4,5},{5,4},{6,7},{7,6},{8,9},{9,8},{10,11... | collective-permute-start | bytes 1769480 | tf_op jit(solution)/shard_map/ppermute | solution.py:496
  12.7 0.7 collective-permute-start.9
  13.4 0.1 collective-permute-start.13
  13.4 5.4 %collective-permute-done.ra_ref = bf16[2,1152,128]{2,1,0:T(8,128)(2,1)S(1)} collective-permute-done((bf16[2,1152,128]{2,1,0:T(8,128)(2,1)S(1)}, bf16[2,1152,128]{2,1,0:T(8,128)(2,1)S(1)}, u32[]{:S(2)}, u32[]{:S(2)}) %collective-permute-start) | collective-permute-done | bytes 589856 | tf_op jit(solution)/shard_map/ppermute | solution.py:496
  18.9 2.0 %collective-permute-start.14 = (bf16[2,64,1152]{2,1,0:T(8,128)(2,1)S(1)}, bf16[2,64,1152]{2,1,0:T(8,128)(2,1)S(1)}, u32[]{:S(2)}, u32[]{:S(2)}) collective-permute-start(bf16[2,64,1152]{2,1,0:T(8,128)(2,1)S(1)} %get-tuple-element.67.refs_10_), channel_id=1, source_target_pairs={{0,8},{4,12},{8,0},{12,4},{1,9},{5,13},{9,1},{13,5},{2,10},{6,14},... | collective-permute-start | bytes 884744 | tf_op jit(solution)/shard_map/ppermute | solution.py:478
  20.8 0.0 collective-permute-done.1.rb_ref
  20.8 0.0 collective-permute-start.15
  20.9 2.4 %shard_map.110 = (bf16[2,576,256]{2,1,0:T(8,128)(2,1)S(1)}, f32[2,640,256]{2,1,0:T(8,128)S(1)}) custom-call(s32[2]{0:T(128)S(1)} %pad_add_fusion.place, s32[2,4]{1,0:T(2,128)S(1)} %bitcast.17, s32[3,2,4]{2,1,0:T(2,128)S(1)} %bitcast.12, bf16[4,576,256]{2,1,0:T(8,128)(2,1)} %bitcast.26, bf16[2,1152,128]{2,1,0:T(8,128)(2,1)S(1)} %get-tuple-element.45.a_ref, ...), custom_call_target="tpu_custom_call" | custom-call | tf_op jit(solution)/shard_map/pallas_call | solution.py:506
  23.3 2.3 %shard_map.111 = (bf16[1,64,1152]{2,1,0:T(8,128)(2,1)S(1)}, bf16[1,64,1152]{2,1,0:T(8,128)(2,1)S(1)}, bf16[1,64,1152]{2,1,0:T(8,128)(2,1)S(1)}, bf16[1,64,1152]{2,1,0:T(8,128)(2,1)S(1)}) custom-call(s32[2]{0:T(128)S(1)} %pad_add_fusion.place, s32[2,4]{1,0:T(2,128)S(1)} %bitcast.18, s32[3,2,4]{2,1,0:T(2,128)S(1)} %bitcast.13, ...), custom_call_target="tpu_custom_call" | custom-call | tf_op jit(solution)/shard_map/pallas_call | solution.py:524
  25.7 5.0 %collective-permute-done.8.ra_ref = bf16[2,1152,128]{2,1,0:T(8,128)(2,1)S(1)} collective-permute-done((bf16[2,1152,128]{2,1,0:T(8,128)(2,1)S(1)}, bf16[2,1152,128]{2,1,0:T(8,128)(2,1)S(1)}, u32[]{:S(2)}, u32[]{:S(2)}) %collective-permute-start.8) | collective-permute-done | bytes 589856 | tf_op jit(solution)/shard_map/ppermute | solution.py:496
  30.7 2.4 %shard_map.116 = (bf16[2,576,256]{2,1,0:T(8,128)(2,1)S(1)}, f32[2,640,256]{2,1,0:T(8,128)S(1)}) custom-call(s32[2]{0:T(128)S(1)} %pad_add_fusion.place, s32[2,4]{1,0:T(2,128)S(1)} %bitcast.19, s32[3,2,4]{2,1,0:T(2,128)S(1)} %bitcast.14, bf16[4,576,256]{2,1,0:T(8,128)(2,1)} %bitcast.27, bf16[2,1152,128]{2,1,0:T(8,128)(2,1)S(1)} %get-tuple-element.57.a_ref, ...), custom_call_target="tpu_custom_call" | custom-call | tf_op jit(solution)/shard_map/pallas_call | solution.py:506
  33.1 2.2 %shard_map.117 = (bf16[32,1152]{1,0:T(8,128)(2,1)S(1)}, bf16[32,1152]{1,0:T(8,128)(2,1)S(1)}, bf16[32,1152]{1,0:T(8,128)(2,1)S(1)}, bf16[32,1152]{1,0:T(8,128)(2...) custom-call(s32[2]{0:T(128)S(1)} %pad_add_fusion.place, ...), custom_call_target="tpu_custom_call" | custom-call | tf_op jit(solution)/shard_map/pallas_call | solution.py:549
  35.3 0.6 collective-permute-start.19
  35.8 0.0 collective-permute-done.13.refs_5_
  35.8 1.7 %collective-permute-start.20 = (bf16[32,1152]{1,0:T(8,128)(2,1)S(1)}, bf16[32,1152]{1,0:T(8,128)(2,1)S(1)}, u32[]{:S(2)}, u32[]{:S(2)}) collective-permute-start(bf16[32,1152]{1,0:T(8,128)(2,1)S(1)} %get-tuple-element.72.refs_2_), channel_id=1, source_target_pairs={{0,8},{4,12},{8,0},{12,4},{1,9},{5,13},{9,1},{13,5},{2,10},{6,14},... | collective-permute-start | bytes 221192 | tf_op jit(solution)/shard_map/ppermute | solution.py:478
  37.5 2.3 %shard_map.113 = (bf16[1,64,1152]{2,1,0:T(8,128)(2,1)S(1)}, bf16[1,64,1152]{2,1,0:T(8,128)(2,1)S(1)}, bf16[1,64,1152]{2,1,0:T(8,128)(2,1)S(1)}, bf16[1,64,1152]{2,1,0:T(8,128)(2,1)S(1)}) custom-call(s32[2]{0:T(128)S(1)} %pad_add_fusion.place, s32[2,4]{1,0:T(2,128)S(1)} %bitcast.21, s32[3,2,4]{2,1,0:T(2,128)S(1)} %bitcast.16, ...), custom_call_target="tpu_custom_call" | custom-call | tf_op jit(solution)/shard_map/pallas_call | solution.py:524
  39.9 1.5 %collective-permute-start.3 = (bf16[1,64,1152]{2,1,0:T(8,128)(2,1)S(1)}, bf16[1,64,1152]{2,1,0:T(8,128)(2,1)S(1)}, u32[]{:S(2)}, u32[]{:S(2)}) collective-permute-start(bf16[1,64,1152]{2,1,0:T(8,128)(2,1)S(1)} %get-tuple-element.51.refs_8_.refs_1_), channel_id=1, source_target_pairs={{0,8},{4,12},{8,0},{12,4},{1,9},{5,13},{9,1},{13,5},{2,10},{6,14},... | collective-permute-start | bytes 442376 | tf_op jit(solution)/shard_map/ppermute | solution.py:478
  41.4 0.4 collective-permute-start.4
  41.8 0.3 collective-permute-start.5
  42.1 0.0 collective-permute-done.21.refs_3_
  42.1 1.4 %collective-permute-start.6 = (bf16[1,64,1152]{2,1,0:T(8,128)(2,1)S(1)}, bf16[1,64,1152]{2,1,0:T(8,128)(2,1)S(1)}, u32[]{:S(2)}, u32[]{:S(2)}) collective-permute-start(bf16[1,64,1152]{2,1,0:T(8,128)(2,1)S(1)} %get-tuple-element.55.refs_9_.refs_2_), channel_id=1, source_target_pairs={{0,8},{4,12},{8,0},{12,4},{1,9},{5,13},{9,1},{13,5},{2,10},{6,14},... | collective-permute-start | bytes 442376 | tf_op jit(solution)/shard_map/ppermute | solution.py:478
  43.5 0.0 collective-permute-done.2.refs_1_
  43.5 0.1 collective-permute-start.7
  43.6 2.2 %shard_map.121.refs_2_ = bf16[1920,256]{1,0:T(8,128)(2,1)S(1)} custom-call(bf16[32,1152]{1,0:T(8,128)(2,1)S(1)} %get-tuple-element.70.refs_0_, bf16[32,1152]{1,0:T(8,128)(2,1)S(1)} %collective-permute-done.19.refs_1_, bf16[32,1152]{1,0:T(8,128)(2,1)S(1)} %collective-permute-done.20.refs_2_, bf16[32,1152]{1,0:T(8,128)(2,1)S(1)} %collective-permute-done.21.refs_3_, ...), custom_call_target="tpu_custom_call" | custom-call | tf_op jit(solution)/shard_map/pallas_call | solution.py:568
  45.8 0.8 %collective-permute-done.3.refs_2_ = bf16[1,64,1152]{2,1,0:T(8,128)(2,1)S(1)} collective-permute-done((bf16[1,64,1152]{2,1,0:T(8,128)(2,1)S(1)}, bf16[1,64,1152]{2,1,0:T(8,128)(2,1)S(1)}, u32[]{:S(2)}, u32[]{:S(2)}) %collective-permute-start.3) | collective-permute-done | bytes 147488 | tf_op jit(solution)/shard_map/ppermute | solution.py:478
  46.7 2.1 %collective-permute-done.4.refs_3_ = bf16[1,64,1152]{2,1,0:T(8,128)(2,1)S(1)} collective-permute-done((bf16[1,64,1152]{2,1,0:T(8,128)(2,1)S(1)}, bf16[1,64,1152]{2,1,0:T(8,128)(2,1)S(1)}, u32[]{:S(2)}, u32[]{:S(2)}) %collective-permute-start.4) | collective-permute-done | bytes 147488 | tf_op jit(solution)/shard_map/ppermute | solution.py:478
  48.8 1.4 %shard_map.112.refs_0_ = bf16[1920,256]{1,0:T(8,128)(2,1)S(1)} custom-call(bf16[1,64,1152]{2,1,0:T(8,128)(2,1)S(1)} %get-tuple-element.49.refs_0_.refs_4_.refs_2_, bf16[1,64,1152]{2,1,0:T(8,128)(2,1)S(1)} %collective-permute-done.2.refs_1_, bf16[1,64,1152]{2,1,0:T(8,128)(2,1)S(1)} %collective-permute-done.3.refs_2_, ...), custom_call_target="tpu_custom_call" | custom-call | tf_op jit(solution)/shard_map/pallas_call | solution.py:539
  50.2 0.0 collective-permute-done.5.refs_1_
  50.2 2.8 %collective-permute-done.6.refs_2_ = bf16[1,64,1152]{2,1,0:T(8,128)(2,1)S(1)} collective-permute-done((bf16[1,64,1152]{2,1,0:T(8,128)(2,1)S(1)}, bf16[1,64,1152]{2,1,0:T(8,128)(2,1)S(1)}, u32[]{:S(2)}, u32[]{:S(2)}) %collective-permute-start.6) | collective-permute-done | bytes 147488 | tf_op jit(solution)/shard_map/ppermute | solution.py:478
  53.0 2.1 %collective-permute-done.7.refs_3_ = bf16[1,64,1152]{2,1,0:T(8,128)(2,1)S(1)} collective-permute-done((bf16[1,64,1152]{2,1,0:T(8,128)(2,1)S(1)}, bf16[1,64,1152]{2,1,0:T(8,128)(2,1)S(1)}, u32[]{:S(2)}, u32[]{:S(2)}) %collective-permute-start.7) | collective-permute-done | bytes 147488 | tf_op jit(solution)/shard_map/ppermute | solution.py:478
  55.1 1.4 %shard_map.114.refs_1_ = bf16[1920,256]{1,0:T(8,128)(2,1)S(1)} custom-call(bf16[1,64,1152]{2,1,0:T(8,128)(2,1)S(1)} %get-tuple-element.53.refs_0_.refs_5_.refs_3_, bf16[1,64,1152]{2,1,0:T(8,128)(2,1)S(1)} %collective-permute-done.5.refs_1_, bf16[1,64,1152]{2,1,0:T(8,128)(2,1)S(1)} %collective-permute-done.6.refs_2_, ...), custom_call_target="tpu_custom_call" | custom-call | tf_op jit(solution)/shard_map/pallas_call | solution.py:539
  56.5 1.8 %shard_map.122 = (bf16[32,2304]{1,0:T(8,128)(2,1)S(1)}, bf16[32,2304]{1,0:T(8,128)(2,1)S(1)}, bf16[32,2304]{1,0:T(8,128)(2,1)S(1)}, bf16[32,2304]{1,0:T(8,128)(2,1)S(1)}) custom-call(bf16[1920,256]{1,0:T(8,128)(2,1)S(1)} %shard_map.112.refs_0_, bf16[1920,256]{1,0:T(8,128)(2,1)S(1)} %shard_map.114.refs_1_, bf16[1920,256]{1,0:T(8,128)(2,1)S(1)} %shard_map.121.refs_2_), custom_call_target="tpu_custom_call" | custom-call | tf_op jit(solution)/shard_map/pallas_call | solution.py:579
  58.3 0.4 collective-permute-start.22
  58.7 0.3 collective-permute-start.10
  58.9 1.8 %collective-permute-start.11 = (bf16[32,1152]{1,0:T(8,128)(2,1)S(1)}, bf16[32,1152]{1,0:T(8,128)(2,1)S(1)}, u32[]{:S(2)}, u32[]{:S(2)}) collective-permute-start(bf16[32,1152]{1,0:T(8,128)(2,1)S(1)} %get-tuple-element.63.refs_6_), channel_id=1, source_target_pairs={{0,8},{4,12},{8,0},{12,4},{1,9},{5,13},{9,1},{13,5},{2,10},{6,14},... | collective-permute-start | bytes 221192 | tf_op jit(solution)/shard_map/ppermute | solution.py:478
  60.8 1.6 %collective-permute-start.23 = (bf16[32,2304]{1,0:T(8,128)(2,1)S(1)}, bf16[32,2304]{1,0:T(8,128)(2,1)S(1)}, u32[]{:S(2)}, u32[]{:S(2)}) collective-permute-start(bf16[32,2304]{1,0:T(8,128)(2,1)S(1)} %get-tuple-element.79), channel_id=1, source_target_pairs={{8,0},{12,4},{0,8},{4,12},{9,1},{13,5},{1,9},{5,13},{10,2},{14,6},... | collective-permute-start | bytes 442376 | tf_op jit(solution)/shard_map/ppermute | solution.py:588
  62.4 0.0 collective-permute-done.10.refs_1_
  62.4 0.1 collective-permute-start.24
  62.5 0.9 %collective-permute-done.11.refs_2_ = bf16[32,1152]{1,0:T(8,128)(2,1)S(1)} collective-permute-done((bf16[32,1152]{1,0:T(8,128)(2,1)S(1)}, bf16[32,1152]{1,0:T(8,128)(2,1)S(1)}, u32[]{:S(2)}, u32[]{:S(2)}) %collective-permute-start.11) | collective-permute-done | bytes 73760 | tf_op jit(solution)/shard_map/ppermute | solution.py:478
  63.5 1.7 %collective-permute-done.12.refs_3_ = bf16[32,1152]{1,0:T(8,128)(2,1)S(1)} collective-permute-done((bf16[32,1152]{1,0:T(8,128)(2,1)S(1)}, bf16[32,1152]{1,0:T(8,128)(2,1)S(1)}, u32[]{:S(2)}, u32[]{:S(2)}) %collective-permute-start.12) | collective-permute-done | bytes 73760 | tf_op jit(solution)/shard_map/ppermute | solution.py:478
  65.2 2.2 %shard_map.118.refs_2_ = bf16[1920,256]{1,0:T(8,128)(2,1)S(1)} custom-call(bf16[32,1152]{1,0:T(8,128)(2,1)S(1)} %get-tuple-element.61.refs_0_.refs_4_, bf16[32,1152]{1,0:T(8,128)(2,1)S(1)} %collective-permute-done.10.refs_1_, bf16[32,1152]{1,0:T(8,128)(2,1)S(1)} %collective-permute-done.11.refs_2_, bf16[32,1152]{1,0:T(8,128)(2,1)S(1)} %collective-permute-done.12.refs_3_, ...), custom_call_target="tpu_custom_call" | custom-call | tf_op jit(solution)/shard_map/pallas_call | solution.py:568
  67.4 0.0 copy-start.7
  67.4 1.8 %shard_map.119 = (bf16[32,2304]{1,0:T(8,128)(2,1)S(1)}, bf16[32,2304]{1,0:T(8,128)(2,1)S(1)}, bf16[32,2304]{1,0:T(8,128)(2,1)S(1)}, bf16[32,2304]{1,0:T(8,128)(2,1)S(1)}) custom-call(bf16[1920,256]{1,0:T(8,128)(2,1)S(1)} %shard_map.112.refs_0_, bf16[1920,256]{1,0:T(8,128)(2,1)S(1)} %shard_map.114.refs_1_, bf16[1920,256]{1,0:T(8,128)(2,1)S(1)} %shard_map.118.refs_2_), custom_call_target="tpu_custom_call" | custom-call | tf_op jit(solution)/shard_map/pallas_call | solution.py:579
  69.2 0.2 collective-permute-start.18
  69.4 2.0 %collective-permute-start.17 = (bf16[32,2304]{1,0:T(8,128)(2,1)S(1)}, bf16[32,2304]{1,0:T(8,128)(2,1)S(1)}, u32[]{:S(2)}, u32[]{:S(2)}) collective-permute-start(bf16[32,2304]{1,0:T(8,128)(2,1)S(1)} %get-tuple-element.74), channel_id=1, source_target_pairs={{8,0},{12,4},{0,8},{4,12},{9,1},{13,5},{1,9},{5,13},{10,2},{14,6},... | collective-permute-start | bytes 442376 | tf_op jit(solution)/shard_map/ppermute | solution.py:588
  71.4 0.0 collective-permute-done.22.refs_1_
  71.4 0.0 collective-permute-start.16
  71.4 0.0 copy-start.2
  71.4 1.5 %shard_map.120.refs_12_.refs_6_.refs_3_ = bf16[4,2,64,1152]{3,2,1,0:T(8,128)(2,1)S(1)} custom-call(bf16[32,1152]{1,0:T(8,128)(2,1)S(1)} %get-tuple-element.70.refs_0_, bf16[32,1152]{1,0:T(8,128)(2,1)S(1)} %get-tuple-element.71.refs_1_, bf16[32,1152]{1,0:T(8,128)(2,1)S(1)} %get-tuple-element.72.refs_2_, bf16[32,1152]{1,0:T(8,128)(2,1)S(1)} %get-tuple-element.73.refs_3_, ...), custom_call_target="tpu_custom_call" | custom-call | tf_op jit(solution)/shard_map/pallas_call | solution.py:591
  73.0 0.0 collective-permute-done.23.refs_2_
  73.0 2.1 %shard_map.123.refs_9_ = bf16[4,4,32,1152]{3,2,1,0:T(8,128)(2,1)S(1)} custom-call(s32[2]{0:T(128)S(1)} %pad_add_fusion.place, bf16[32,2304]{1,0:T(8,128)(2,1)S(1)} %get-tuple-element.77.refs_0_, bf16[32,2304]{1,0:T(8,128)(2,1)S(1)} %collective-permute-done.22.refs_1_, bf16[32,2304]{1,0:T(8,128)(2,1)S(1)} %collective-permute-done.23.refs_2_, ...), custom_call_target="tpu_custom_call" | custom-call | tf_op jit(solution)/shard_map/pallas_call | solution.py:622
  75.1 0.0 collective-permute-done.18.refs_1_
  75.1 2.4 %shard_map.124 = (bf16[4,256,1152]{2,1,0:T(8,128)(2,1)}, bf16[2,4,32,1152]{3,2,1,0:T(8,128)(2,1)S(1)}) custom-call(s32[2]{0:T(128)S(1)} %pad_add_fusion.place, bf16[32,2304]{1,0:T(8,128)(2,1)S(1)} %get-tuple-element.75.refs_0_, bf16[32,2304]{1,0:T(8,128)(2,1)S(1)} %collective-permute-done.18.refs_1_, ...), custom_call_target="tpu_custom_call" | custom-call | tf_op jit(solution)/shard_map/pallas_call | solution.py:622
  77.5 0.0 collective-permute-done.17.refs_0_
  77.5 1.8 %shard_map.125 = (bf16[4,256,1152]{2,1,0:T(8,128)(2,1)}, bf16[1,4,32,1152]{3,2,1,0:T(8,128)(2,1)S(1)}) custom-call(s32[2]{0:T(128)S(1)} %pad_add_fusion.place, bf16[32,2304]{1,0:T(8,128)(2,1)S(1)} %collective-permute-done.17.refs_0_, bf16[1,64,1152]{2,1,0:T(8,128)(2,1)S(1)} %get-tuple-element.51.refs_8_.refs_1_, ...), custom_call_target="tpu_custom_call", output_to_operand_aliasing={{0}: (8, {})} | custom-call | tf_op jit(solution)/shard_map/pallas_call | solution.py:622
  79.4 0.0 collective-permute-done.16.refs_0_
  79.4 1.9 %shard_map.126 = bf16[4,256,1152]{2,1,0:T(8,128)(2,1)} custom-call(s32[2]{0:T(128)S(1)} %pad_add_fusion.place, bf16[32,2304]{1,0:T(8,128)(2,1)S(1)} %collective-permute-done.16.refs_0_, bf16[1,64,1152]{2,1,0:T(8,128)(2,1)S(1)} %get-tuple-element.52.refs_10_.refs_1_, ...), custom_call_target="tpu_custom_call", output_to_operand_aliasing={{}: (8, {})} | custom-call | tf_op jit(solution)/shard_map/pallas_call | solution.py:622
  (23 shorter events, 0.1 us)
Async XLA Ops:
  1.6 17.3 %collective-permute-start = (bf16[2,1152,128]{2,1,0:T(8,128)(2,1)S(1)}, bf16[2,1152,128]{2,1,0:T(8,128)(2,1)S(1)}, u32[]{:S(2)}, u32[]{:S(2)}) collective-permute-start(bf16[2,1152,128]{2,1,0:T(8,128)(2,1)S(1)} %get-tuple-element.45.a_ref), channel_id=1, source_target_pairs={{0,1},{1,0},{2,3},{3,2},{4,5},{5,4},{6,7},{7,6},{8,9},{9,8},{10,11... | collective-permute-start | bytes 1769480 | tf_op jit(solution)/shard_map/ppermute | solution.py:496
  4.7 16.1 %copy-start.6 = (f32[1152]{0:T(1024)S(1)}, f32[1152]{0:T(1024)}, u32[]{:S(2)}) copy-start(f32[1152]{0:T(1024)} %param.16) | copy-start | bytes 13828
  4.7 16.2 %copy-start.4 = (s32[4,2,3]{0,1,2:T(2,128)S(1)}, s32[4,2,3]{0,1,2:T(2,128)}, u32[]{:S(2)}) copy-start(s32[4,2,3]{0,1,2:T(2,128)} %param.20) | copy-start | bytes 292
  4.7 16.2 %copy-start.5 = (s32[4,2]{0,1:T(2,128)S(1)}, s32[4,2]{0,1:T(2,128)}, u32[]{:S(2)}) copy-start(s32[4,2]{0,1:T(2,128)} %param.21) | copy-start | bytes 100
  4.7 16.1 %collective-permute-start.1 = (bf16[2,1152,128]{2,1,0:T(8,128)(2,1)S(1)}, bf16[2,1152,128]{2,1,0:T(8,128)(2,1)S(1)}, u32[]{:S(2)}, u32[]{:S(2)}) collective-permute-start(bf16[2,1152,128]{2,1,0:T(8,128)(2,1)S(1)} %get-tuple-element.46.b_ref), channel_id=1, source_target_pairs={{1,2},{2,1},{5,6},{6,5},{9,10},{10,9},{13,14},{14,13},{17,18},{18,... | collective-permute-start | bytes 1769480 | tf_op jit(solution)/shard_map/ppermute | solution.py:496
  5.5 17.8 %copy-start.3 = (bf16[4,256,1152]{2,1,0:T(8,128)(2,1)S(1)}, bf16[4,256,1152]{2,1,0:T(8,128)(2,1)}, u32[]{:S(2)}) copy-start(bf16[4,256,1152]{2,1,0:T(8,128)(2,1)} %refs_0_.1) | copy-start | bytes 7077892
  8.2 15.1 %copy-start.1 = (bf16[576,1152]{1,0:T(8,128)(2,1)S(1)}, bf16[576,1152]{1,0:T(8,128)(2,1)}, u32[]{:S(2)}) copy-start(bf16[576,1152]{1,0:T(8,128)(2,1)} %refs_8_.3) | copy-start | bytes 3981316
  8.2 22.4 %collective-permute-start.8 = (bf16[2,1152,128]{2,1,0:T(8,128)(2,1)S(1)}, bf16[2,1152,128]{2,1,0:T(8,128)(2,1)S(1)}, u32[]{:S(2)}, u32[]{:S(2)}) collective-permute-start(bf16[2,1152,128]{2,1,0:T(8,128)(2,1)S(1)} %get-tuple-element.57.a_ref), channel_id=1, source_target_pairs={{0,1},{1,0},{2,3},{3,2},{4,5},{5,4},{6,7},{7,6},{8,9},{9,8},{10,11... | collective-permute-start | bytes 1769480 | tf_op jit(solution)/shard_map/ppermute | solution.py:496
  12.7 20.4 %collective-permute-start.9 = (bf16[2,1152,128]{2,1,0:T(8,128)(2,1)S(1)}, bf16[2,1152,128]{2,1,0:T(8,128)(2,1)S(1)}, u32[]{:S(2)}, u32[]{:S(2)}) collective-permute-start(bf16[2,1152,128]{2,1,0:T(8,128)(2,1)S(1)} %get-tuple-element.58.b_ref), channel_id=1, source_target_pairs={{1,2},{2,1},{5,6},{6,5},{9,10},{10,9},{13,14},{14,13},{17,18},{18,... | collective-permute-start | bytes 1769480 | tf_op jit(solution)/shard_map/ppermute | solution.py:496
  13.4 22.5 %collective-permute-start.13 = (bf16[2,64,1152]{2,1,0:T(8,128)(2,1)S(1)}, bf16[2,64,1152]{2,1,0:T(8,128)(2,1)S(1)}, u32[]{:S(2)}, u32[]{:S(2)}) collective-permute-start(bf16[2,64,1152]{2,1,0:T(8,128)(2,1)S(1)} %get-tuple-element.66.refs_9_), channel_id=1, source_target_pairs={{0,4},{4,0},{8,12},{12,8},{1,5},{5,1},{9,13},{13,9},{2,6},{6,2},{1... | collective-permute-start | bytes 884744 | tf_op jit(solution)/shard_map/ppermute | solution.py:478
  18.9 18.6 %collective-permute-start.14 = (bf16[2,64,1152]{2,1,0:T(8,128)(2,1)S(1)}, bf16[2,64,1152]{2,1,0:T(8,128)(2,1)S(1)}, u32[]{:S(2)}, u32[]{:S(2)}) collective-permute-start(bf16[2,64,1152]{2,1,0:T(8,128)(2,1)S(1)} %get-tuple-element.67.refs_10_), channel_id=1, source_target_pairs={{0,8},{4,12},{8,0},{12,4},{1,9},{5,13},{9,1},{13,5},{2,10},{6,14},... | collective-permute-start | bytes 884744 | tf_op jit(solution)/shard_map/ppermute | solution.py:478
  20.8 19.0 %collective-permute-start.15 = (bf16[2,64,1152]{2,1,0:T(8,128)(2,1)S(1)}, bf16[2,64,1152]{2,1,0:T(8,128)(2,1)S(1)}, u32[]{:S(2)}, u32[]{:S(2)}) collective-permute-start(bf16[2,64,1152]{2,1,0:T(8,128)(2,1)S(1)} %get-tuple-element.68.refs_11_), channel_id=1, source_target_pairs={{0,12},{4,8},{8,4},{12,0},{1,13},{5,9},{9,5},{13,1},{2,14},{6,10},... | collective-permute-start | bytes 884744 | tf_op jit(solution)/shard_map/ppermute | solution.py:478
  30.7 12.9 %collective-permute-start.2 = (bf16[1,64,1152]{2,1,0:T(8,128)(2,1)S(1)}, bf16[1,64,1152]{2,1,0:T(8,128)(2,1)S(1)}, u32[]{:S(2)}, u32[]{:S(2)}) collective-permute-start(bf16[1,64,1152]{2,1,0:T(8,128)(2,1)S(1)} %get-tuple-element.50.refs_6_.refs_4_), channel_id=1, source_target_pairs={{0,4},{4,0},{8,12},{12,8},{1,5},{5,1},{9,13},{13,9},{2,6},{6,2},{1... | collective-permute-start | bytes 442376 | tf_op jit(solution)/shard_map/ppermute | solution.py:478
  35.3 6.1 %collective-permute-start.19 = (bf16[32,1152]{1,0:T(8,128)(2,1)S(1)}, bf16[32,1152]{1,0:T(8,128)(2,1)S(1)}, u32[]{:S(2)}, u32[]{:S(2)}) collective-permute-start(bf16[32,1152]{1,0:T(8,128)(2,1)S(1)} %get-tuple-element.71.refs_1_), channel_id=1, source_target_pairs={{0,4},{4,0},{8,12},{12,8},{1,5},{5,1},{9,13},{13,9},{2,6},{6,2},{1... | collective-permute-start | bytes 221192 | tf_op jit(solution)/shard_map/ppermute | solution.py:478
  35.8 5.9 %collective-permute-start.20 = (bf16[32,1152]{1,0:T(8,128)(2,1)S(1)}, bf16[32,1152]{1,0:T(8,128)(2,1)S(1)}, u32[]{:S(2)}, u32[]{:S(2)}) collective-permute-start(bf16[32,1152]{1,0:T(8,128)(2,1)S(1)} %get-tuple-element.72.refs_2_), channel_id=1, source_target_pairs={{0,8},{4,12},{8,0},{12,4},{1,9},{5,13},{9,1},{13,5},{2,10},{6,14},... | collective-permute-start | bytes 221192 | tf_op jit(solution)/shard_map/ppermute | solution.py:478
  37.5 4.6 %collective-permute-start.21 = (bf16[32,1152]{1,0:T(8,128)(2,1)S(1)}, bf16[32,1152]{1,0:T(8,128)(2,1)S(1)}, u32[]{:S(2)}, u32[]{:S(2)}) collective-permute-start(bf16[32,1152]{1,0:T(8,128)(2,1)S(1)} %get-tuple-element.73.refs_3_), channel_id=1, source_target_pairs={{0,12},{4,8},{8,4},{12,0},{1,13},{5,9},{9,5},{13,1},{2,14},{6,10},... | collective-permute-start | bytes 221192 | tf_op jit(solution)/shard_map/ppermute | solution.py:478
  37.5 6.1 %copy-start = (bf16[1152,1728]{0,1:T(8,128)(2,1)S(1)}, bf16[1152,1728]{0,1:T(8,128)(2,1)}, u32[]{:S(2)}) copy-start(bf16[1152,1728]{0,1:T(8,128)(2,1)} %param.17) | copy-start | bytes 11943940
  39.9 6.8 %collective-permute-start.3 = (bf16[1,64,1152]{2,1,0:T(8,128)(2,1)S(1)}, bf16[1,64,1152]{2,1,0:T(8,128)(2,1)S(1)}, u32[]{:S(2)}, u32[]{:S(2)}) collective-permute-start(bf16[1,64,1152]{2,1,0:T(8,128)(2,1)S(1)} %get-tuple-element.51.refs_8_.refs_1_), channel_id=1, source_target_pairs={{0,8},{4,12},{8,0},{12,4},{1,9},{5,13},{9,1},{13,5},{2,10},{6,14},... | collective-permute-start | bytes 442376 | tf_op jit(solution)/shard_map/ppermute | solution.py:478
  41.4 7.4 %collective-permute-start.4 = (bf16[1,64,1152]{2,1,0:T(8,128)(2,1)S(1)}, bf16[1,64,1152]{2,1,0:T(8,128)(2,1)S(1)}, u32[]{:S(2)}, u32[]{:S(2)}) collective-permute-start(bf16[1,64,1152]{2,1,0:T(8,128)(2,1)S(1)} %get-tuple-element.52.refs_10_.refs_1_), channel_id=1, source_target_pairs={{0,12},{4,8},{8,4},{12,0},{1,13},{5,9},{9,5},{13,1},{2,14},{6,10},... | collective-permute-start | bytes 442376 | tf_op jit(solution)/shard_map/ppermute | solution.py:478
  41.8 8.4 %collective-permute-start.5 = (bf16[1,64,1152]{2,1,0:T(8,128)(2,1)S(1)}, bf16[1,64,1152]{2,1,0:T(8,128)(2,1)S(1)}, u32[]{:S(2)}, u32[]{:S(2)}) collective-permute-start(bf16[1,64,1152]{2,1,0:T(8,128)(2,1)S(1)} %get-tuple-element.54.refs_7_.refs_5_), channel_id=1, source_target_pairs={{0,4},{4,0},{8,12},{12,8},{1,5},{5,1},{9,13},{13,9},{2,6},{6,2},{1... | collective-permute-start | bytes 442376 | tf_op jit(solution)/shard_map/ppermute | solution.py:478
  42.1 10.9 %collective-permute-start.6 = (bf16[1,64,1152]{2,1,0:T(8,128)(2,1)S(1)}, bf16[1,64,1152]{2,1,0:T(8,128)(2,1)S(1)}, u32[]{:S(2)}, u32[]{:S(2)}) collective-permute-start(bf16[1,64,1152]{2,1,0:T(8,128)(2,1)S(1)} %get-tuple-element.55.refs_9_.refs_2_), channel_id=1, source_target_pairs={{0,8},{4,12},{8,0},{12,4},{1,9},{5,13},{9,1},{13,5},{2,10},{6,14},... | collective-permute-start | bytes 442376 | tf_op jit(solution)/shard_map/ppermute | solution.py:478
  43.5 11.6 %collective-permute-start.7 = (bf16[1,64,1152]{2,1,0:T(8,128)(2,1)S(1)}, bf16[1,64,1152]{2,1,0:T(8,128)(2,1)S(1)}, u32[]{:S(2)}, u32[]{:S(2)}) collective-permute-start(bf16[1,64,1152]{2,1,0:T(8,128)(2,1)S(1)} %get-tuple-element.56.refs_11_.refs_2_), channel_id=1, source_target_pairs={{0,12},{4,8},{8,4},{12,0},{1,13},{5,9},{9,5},{13,1},{2,14},{6,10},... | collective-permute-start | bytes 442376 | tf_op jit(solution)/shard_map/ppermute | solution.py:478
  58.3 13.1 %collective-permute-start.22 = (bf16[32,2304]{1,0:T(8,128)(2,1)S(1)}, bf16[32,2304]{1,0:T(8,128)(2,1)S(1)}, u32[]{:S(2)}, u32[]{:S(2)}) collective-permute-start(bf16[32,2304]{1,0:T(8,128)(2,1)S(1)} %get-tuple-element.78), channel_id=1, source_target_pairs={{4,0},{0,4},{12,8},{8,12},{5,1},{1,5},{13,9},{9,13},{6,2},{2,6},{1... | collective-permute-start | bytes 442376 | tf_op jit(solution)/shard_map/ppermute | solution.py:588
  58.7 3.7 %collective-permute-start.10 = (bf16[32,1152]{1,0:T(8,128)(2,1)S(1)}, bf16[32,1152]{1,0:T(8,128)(2,1)S(1)}, u32[]{:S(2)}, u32[]{:S(2)}) collective-permute-start(bf16[32,1152]{1,0:T(8,128)(2,1)S(1)} %get-tuple-element.62.refs_5_), channel_id=1, source_target_pairs={{0,4},{4,0},{8,12},{12,8},{1,5},{5,1},{9,13},{13,9},{2,6},{6,2},{1... | collective-permute-start | bytes 221192 | tf_op jit(solution)/shard_map/ppermute | solution.py:478
  58.9 4.5 %collective-permute-start.11 = (bf16[32,1152]{1,0:T(8,128)(2,1)S(1)}, bf16[32,1152]{1,0:T(8,128)(2,1)S(1)}, u32[]{:S(2)}, u32[]{:S(2)}) collective-permute-start(bf16[32,1152]{1,0:T(8,128)(2,1)S(1)} %get-tuple-element.63.refs_6_), channel_id=1, source_target_pairs={{0,8},{4,12},{8,0},{12,4},{1,9},{5,13},{9,1},{13,5},{2,10},{6,14},... | collective-permute-start | bytes 221192 | tf_op jit(solution)/shard_map/ppermute | solution.py:478
  60.8 4.4 %collective-permute-start.12 = (bf16[32,1152]{1,0:T(8,128)(2,1)S(1)}, bf16[32,1152]{1,0:T(8,128)(2,1)S(1)}, u32[]{:S(2)}, u32[]{:S(2)}) collective-permute-start(bf16[32,1152]{1,0:T(8,128)(2,1)S(1)} %get-tuple-element.64.refs_7_), channel_id=1, source_target_pairs={{0,12},{4,8},{8,4},{12,0},{1,13},{5,9},{9,5},{13,1},{2,14},{6,10},... | collective-permute-start | bytes 221192 | tf_op jit(solution)/shard_map/ppermute | solution.py:478
  60.8 12.2 %collective-permute-start.23 = (bf16[32,2304]{1,0:T(8,128)(2,1)S(1)}, bf16[32,2304]{1,0:T(8,128)(2,1)S(1)}, u32[]{:S(2)}, u32[]{:S(2)}) collective-permute-start(bf16[32,2304]{1,0:T(8,128)(2,1)S(1)} %get-tuple-element.79), channel_id=1, source_target_pairs={{8,0},{12,4},{0,8},{4,12},{9,1},{13,5},{1,9},{5,13},{10,2},{14,6},... | collective-permute-start | bytes 442376 | tf_op jit(solution)/shard_map/ppermute | solution.py:588
  62.4 10.6 %collective-permute-start.24 = (bf16[32,2304]{1,0:T(8,128)(2,1)S(1)}, bf16[32,2304]{1,0:T(8,128)(2,1)S(1)}, u32[]{:S(2)}, u32[]{:S(2)}) collective-permute-start(bf16[32,2304]{1,0:T(8,128)(2,1)S(1)} %get-tuple-element.80), channel_id=1, source_target_pairs={{12,0},{8,4},{4,8},{0,12},{13,1},{9,5},{5,9},{1,13},{14,2},{10,6},... | collective-permute-start | bytes 442376 | tf_op jit(solution)/shard_map/ppermute | solution.py:588
  67.4 4.0 %copy-start.7 = (f32[1152]{0:T(1024)S(1)}, f32[1152]{0:T(1024)}, u32[]{:S(2)}) copy-start(f32[1152]{0:T(1024)} %param.19) | copy-start | bytes 13828
  69.2 5.9 %collective-permute-start.18 = (bf16[32,2304]{1,0:T(8,128)(2,1)S(1)}, bf16[32,2304]{1,0:T(8,128)(2,1)S(1)}, u32[]{:S(2)}, u32[]{:S(2)}) collective-permute-start(bf16[32,2304]{1,0:T(8,128)(2,1)S(1)} %get-tuple-element.76), channel_id=1, source_target_pairs={{4,0},{0,4},{12,8},{8,12},{5,1},{1,5},{13,9},{9,13},{6,2},{2,6},{1... | collective-permute-start | bytes 442376 | tf_op jit(solution)/shard_map/ppermute | solution.py:588
  69.4 8.2 %collective-permute-start.17 = (bf16[32,2304]{1,0:T(8,128)(2,1)S(1)}, bf16[32,2304]{1,0:T(8,128)(2,1)S(1)}, u32[]{:S(2)}, u32[]{:S(2)}) collective-permute-start(bf16[32,2304]{1,0:T(8,128)(2,1)S(1)} %get-tuple-element.74), channel_id=1, source_target_pairs={{8,0},{12,4},{0,8},{4,12},{9,1},{13,5},{1,9},{5,13},{10,2},{14,6},... | collective-permute-start | bytes 442376 | tf_op jit(solution)/shard_map/ppermute | solution.py:588
  71.4 8.0 %collective-permute-start.16 = (bf16[32,2304]{1,0:T(8,128)(2,1)S(1)}, bf16[32,2304]{1,0:T(8,128)(2,1)S(1)}, u32[]{:S(2)}, u32[]{:S(2)}) collective-permute-start(bf16[32,2304]{1,0:T(8,128)(2,1)S(1)} %get-tuple-element.69), channel_id=1, source_target_pairs={{12,0},{8,4},{4,8},{0,12},{13,1},{9,5},{5,9},{1,13},{14,2},{10,6},... | collective-permute-start | bytes 442376 | tf_op jit(solution)/shard_map/ppermute | solution.py:588
  71.4 1.6 %copy-start.2 = (bf16[576,1152]{1,0:T(8,128)(2,1)S(1)}, bf16[576,1152]{1,0:T(8,128)(2,1)}, u32[]{:S(2)}) copy-start(bf16[576,1152]{1,0:T(8,128)(2,1)} %refs_4_.3) | copy-start | bytes 3981316

commit v11 on v10

--- a/solution.py
+++ b/solution.py
@@ -65,15 +65,15 @@
     gather(*steps[-1], behind)
 
 
-def prep_kernel(place, k_ref, v_ref, *refs):
+def prep_kernel(k_ref, v_ref, *refs):
     n, width, _ = k_ref.shape
-    even = place[1] % 2 == 0
+    even = lax.axis_index("strip") % 2 == 0
     copies = []
     if len(refs) > 2:
         src, (a_ref, b_ref), pieces, sems = refs[0], refs[1:3], refs[3:-1], refs[-1]
         late, share, _ = pieces[0].shape
         for j in reversed(range(len(pieces))):
-            start = pl.multiple_of(peer(place[0], j, len(pieces)) * share, SUB)
+            start = pl.multiple_of(peer(lax.axis_index("frame"), j, len(pieces)) * share, SUB)
             part = src.at[pl.ds(src.shape[0] - late, late), pl.ds(start, share), :]
             copies.append(pltpu.make_async_copy(part, pieces[j], sems.at[j]))
             copies[-1].start()
@@ -96,8 +96,8 @@
         copy.wait()
 
 
-def tile_masks(frame, n, tiles, local, place, counts, lists):
-    strip = place[1]
+def tile_masks(frame, n, tiles, local, counts, lists):
+    strip = lax.axis_index("strip")
     odd = strip % 2
     first = strip * tiles
     if local:
@@ -146,7 +146,7 @@
     return slice(h * (HEAD_DIM + 8), (h + 1) * (HEAD_DIM + 8))
 
 
-def local_kernel(frame, place, counts, lists, q_ref, a_ref, b_ref, qn_ref, sum_ref):
+def local_kernel(frame, counts, lists, q_ref, a_ref, b_ref, qn_ref, sum_ref, mask_ref):
     n, _, tokens = q_ref.shape
 
     def query(f, h):
@@ -158,12 +158,15 @@
     def finish(f, h, o):
         sum_ref[f, sums(h), :] = o
 
-    masks = tile_masks(frame, n, tokens // TILE, True, place, counts, lists)
+    for f, rows in enumerate(tile_masks(frame, n, tokens // TILE, False, counts, lists)):
+        for i, row in enumerate(rows):
+            mask_ref[f, i] = row
+    masks = tile_masks(frame, n, tokens // TILE, True, counts, lists)
     attend(masks, (a_ref, b_ref), query, finish)
 
 
-def remote_attend(frame, place, counts, lists, qn_ref, sum_ref, ra_ref, rb_ref, att, done=None):
-    n, width, tokens = qn_ref.shape
+def remote_attend(qn_ref, sum_ref, mask_ref, ra_ref, rb_ref, att, done=None):
+    n, width, _ = qn_ref.shape
 
     def query(f, h):
         return qn_ref[f, head(h), :]
@@ -173,7 +176,7 @@
         if done and (h + 1) * HEAD_DIM == width:
             done(f)
 
-    masks = tile_masks(frame, n, tokens // TILE, False, place, counts, lists)
+    masks = [[mask_ref[f, i] for i in range(2)] for f in range(n)]
     attend(masks, (ra_ref, rb_ref), query, finish)
 
 
@@ -187,9 +190,9 @@
         finish(proj * scale)
 
 
-def spatial_kernel(frame, n_groups, place, counts, lists, qn_ref, sum_ref, ra_ref, rb_ref, h_ref, w_ref, g_ref, *rest):
+def spatial_kernel(n_groups, qn_ref, sum_ref, mask_ref, ra_ref, rb_ref, h_ref, w_ref, g_ref, *rest):
     outs, (att, mix) = rest[:n_groups], rest[n_groups:]
-    remote_attend(frame, place, counts, lists, qn_ref, sum_ref, ra_ref, rb_ref, att)
+    remote_attend(qn_ref, sum_ref, mask_ref, ra_ref, rb_ref, att)
     n, tokens, _ = h_ref.shape
 
     def block(f):
@@ -201,23 +204,23 @@
     add_normed([block(f) for f in range(n)])
     share = tokens // n_groups
     for j, out in enumerate(outs):
-        group = peer(place[0], j, n_groups)
+        group = peer(lax.axis_index("frame"), j, n_groups)
         for f in range(n):
             out[f] = mix[f, pl.ds(pl.multiple_of(group * share, SUB), share), :]
 
 
-def late_kernel(frame, n_groups, halves, place, counts, lists, qn_ref, sum_ref, ra_ref, rb_ref, *rest):
+def late_kernel(n_groups, halves, qn_ref, sum_ref, mask_ref, ra_ref, rb_ref, *rest):
     outs, (att, rows) = rest[:n_groups * halves], rest[n_groups * halves:]
     _, width, tokens = qn_ref.shape
 
     def turn(f):
         rows[:, f * width:(f + 1) * width] = att[f].T
 
-    remote_attend(frame, place, counts, lists, qn_ref, sum_ref, ra_ref, rb_ref, att, turn)
+    remote_attend(qn_ref, sum_ref, mask_ref, ra_ref, rb_ref, att, turn)
     size = tokens // n_groups // halves
     for half in range(halves):
         for j in range(n_groups):
-            start = (peer(place[0], j, n_groups) * halves + half) * size
+            start = (peer(lax.axis_index("frame"), j, n_groups) * halves + half) * size
             outs[half * n_groups + j][...] = rows[pl.ds(pl.multiple_of(start, SUB), size), :]
 
 
@@ -365,7 +368,7 @@
     pipeline(steps, scores, weigh, gather)
 
 
-def output_kernel(n_groups, js, early, half, halves, before, last, aliased, place, *refs):
+def output_kernel(n_groups, js, early, half, halves, before, last, aliased, *refs):
     n = len(js)
     atts, pieces = refs[:n], refs[n:n * (1 + early)]
     late_ref, w_ref, g_ref = refs[n * (1 + early):n * (1 + early) + 3]
@@ -382,7 +385,7 @@
     copies = []
 
     def write(src, j, some_half):
-        group = peer(place[0], j, n_groups)
+        group = peer(lax.axis_index("frame"), j, n_groups)
         at = pl.multiple_of((group * halves + some_half) * rows, SUB)
         copy = pltpu.make_async_copy(src, out.at[:, pl.ds(at, rows), :], rest[0].at[len(copies)])
         copy.start()
@@ -444,7 +447,6 @@
     qkv_weight = temporal_qkv_weight.T
     gain_one = spatial_gain.reshape(1, model)
     gain_two = temporal_gain.reshape(1, model)
-    place = jnp.stack([lax.axis_index("frame"), lax.axis_index("strip")]).astype(jnp.int32)
     near = [(i, i ^ 1) for i in range(strips) if i ^ 1 < strips]
     far = [e for i in range(1, strips - 1, 2) for e in ((i, i + 1), (i + 1, i))]
     edge = jax.ShapeDtypeStruct((2 * width, TILE), BF)
@@ -484,13 +486,13 @@
         split = groups if some == 1 else 0
         a, b, *pieces = call(
             prep_kernel,
-            [smem, block, block] + [any_spec] * bool(split),
+            [block, block] + [any_spec] * bool(split),
             [whole((late,) + edge.shape)] * 2 + [any_spec] * split,
             [jax.ShapeDtypeStruct((late,) + edge.shape, BF)] * 2
             + [jax.ShapeDtypeStruct((late, share, model), BF)] * split,
             [pltpu.SemaphoreType.DMA((groups,))] * bool(split),
             limit=16,
-        )(place, keys, values, *[hidden_far] * bool(split))
+        )(keys, values, *[hidden_far] * bool(split))
         if split:
             own_hidden = pieces
         halos.append((a, b, lax.ppermute(a, "strip", near), lax.ppermute(b, "strip", far)))
@@ -499,31 +501,33 @@
     padded = width // HEAD_DIM * (HEAD_DIM + 8)
     qkv_rows = 3 * padded
     sum_shape = (late, padded, tokens)
+    mask_shape = (late, 2, SUB, tokens)
     own_sums = []
     for some in range(2):
         block = pl.BlockSpec((late, width, tokens), lambda *_, some=some: (some, 0, 0))
         own_sums.append(
             call(
                 functools.partial(local_kernel, some * late),
-                [smem, smem, smem, block] + [whole((late,) + edge.shape)] * 2,
-                [whole((late, width, tokens)), whole(sum_shape)],
+                [smem, smem, block] + [whole((late,) + edge.shape)] * 2,
+                [whole((late, width, tokens)), whole(sum_shape), whole(mask_shape)],
                 [
                     jax.ShapeDtypeStruct((late, width, tokens), BF),
                     jax.ShapeDtypeStruct(sum_shape, F32),
+                    jax.ShapeDtypeStruct(mask_shape, BF),
                 ],
-            )(place, counts, lists, queries, *halos[some][:2])
+            )(counts, lists, queries, *halos[some][:2])
         )
-    sum_specs = [whole((late, width, tokens)), whole(sum_shape)]
+    sum_specs = [whole((late, width, tokens)), whole(sum_shape), whole(mask_shape)]
 
     def one(shape, f):
-        return pl.BlockSpec((1,) + shape[1:], lambda *_: (f, 0, 0))
+        return pl.BlockSpec((1,) + shape[1:], lambda *_: (f,) + (0,) * (len(shape) - 1))
 
     mixed, projected = [], []
     for f in range(early):
         mixed.append(
             call(
-                functools.partial(spatial_kernel, f, groups),
-                [smem, smem, smem, one((late, width, tokens), f), one(sum_shape, f)]
+                functools.partial(spatial_kernel, groups),
+                [one((late, width, tokens), f), one(sum_shape, f), one(mask_shape, f)]
                 + [one((late,) + edge.shape, f)] * 2
                 + [one(hidden.shape, f), whole((width, model)), whole((1, model))],
                 [whole((1, share, model))] * groups,
@@ -532,7 +536,7 @@
                     pltpu.VMEM((1, width, tokens), BF),
                     pltpu.VMEM((1, tokens, model), BF),
                 ],
-            )(place, counts, lists, *own_sums[0], *halos[0][2:], hidden, spatial_out_weight, gain_one)
+            )(*own_sums[0], *halos[0][2:], hidden, spatial_out_weight, gain_one)
         )
         arrived = send(mixed[f])
         projected.append(
@@ -547,12 +551,12 @@
 
     late_shape = (rows, late * width)
     own_late = call(
-        functools.partial(late_kernel, early, groups, halves),
-        [smem, smem, smem] + sum_specs + [whole((late,) + edge.shape)] * 2,
+        functools.partial(late_kernel, groups, halves),
+        sum_specs + [whole((late,) + edge.shape)] * 2,
         [whole(late_shape)] * (groups * halves),
         [jax.ShapeDtypeStruct(late_shape, BF)] * (groups * halves),
         [pltpu.VMEM((late, width, tokens), BF), pltpu.VMEM((tokens, late * width), BF)],
-    )(place, counts, lists, *own_sums[1], *halos[1][2:])
+    )(*own_sums[1], *halos[1][2:])
     own_late = [own_late[half * groups:(half + 1) * groups] for half in range(halves)]
     far_late = []
     for half in range(halves):
@@ -609,8 +613,7 @@
         extra = [] if out is None else [out]
         writes = (len(before[0]) if before else 0) + (len(js) if last else 0)
         in_specs = (
-            [smem]
-            + [whole(back_shape)] * len(js)
+            [whole(back_shape)] * len(js)
             + [whole((1, share, model))] * (len(js) * early)
             + [whole((groups, late, share, model)), whole((width, model)), whole((1, model))]
             + ([whole(handed.shape)] if before else [])
@@ -627,7 +630,6 @@
             scratch,
             alias={len(in_specs) - 1: 0} if extra else None,
         )(
-            place,
             *[returned[half][j] for j in js],
             *[mixed[f][j] for j in js for f in range(early)],
             late_mixed,

time: 81.7 us -> 78.6 us (0.962)
  Pallas kernels: 36.2 us -> 32.1 us
  waiting for transfers between devices: 21 us -> 22.1 us
    pallas_call x4, Pallas kernels: 8.23 us -> 5.93 us  [shards(): call(functools.partial(output_kernel, groups, js, early, half, halves, be...]
    pallas_call x7, Pallas kernels: 15.8 us -> 14 us  [the longest x2 4.78 us: shards(): call(functools.partial(local_kernel, some * late), [smem, smem, block] +...]
  transfers between devices with their start and end apart: 25 -> 25, of which waited for: 8 -> 10; matrix products, arithmetic and copies ran while one was open for 0% -> 0% of each run, Pallas kernels for 36% -> 33%
where the time goes in v11:
time: 78.6 us; the launch traced here: 78.3 us
  Pallas kernels  32.1 us (41%)
  starting transfers between devices  23.6 us (30%)
  waiting for transfers between devices  22.1 us (28%)
    ppermute x2, waiting for transfers between devices, shards(): lax.ppermute(a, 'strip', near)  11.1 us
    ppermute x15, waiting for transfers between devices, send(): sent[j] = lax.ppermute(parts[j], 'frame', out_pairs(j))  10.6 us
    ppermute x15, starting transfers between devices, send(): sent[j] = lax.ppermute(parts[j], 'frame', out_pairs(j))  10.1 us
    ppermute x2, starting transfers between devices, shards(): lax.ppermute(a, 'strip', near)  7.54 us
    pallas_call x4, Pallas kernels, shards(): call(functools.partial(output_kernel, groups, js, early, half, halves, be...  5.93 us
    pallas_call x2, Pallas kernels, shards(): call(functools.partial(local_kernel, some * late), [smem, smem, block] +...  4.78 us
    ppermute x6, starting transfers between devices, shards(): home[j] = lax.ppermute(back[j], 'frame', [(b, a) for a, b in out_pairs(j)])  4.39 us
    pallas_call x2, Pallas kernels, shards(): call(functools.partial(late_project_kernel, early, frames), late_specs +...  4.33 us
  transfers between devices with their start and end apart: 25, of which 10 were waited for; matrix products, arithmetic and copies ran while one was open for 0% of the time, Pallas kernels for 33%

profile of v11, /device:TPU:0, one launch (start us, length us, event | category | flops | bytes accessed | tf_op | source)
XLA Modules:
  0.0 78.3 jit_solution(4681549325843797416)
XLA Ops:
  0.0 1.5 %shard_map.109 = (bf16[2,1152,128]{2,1,0:T(8,128)(2,1)S(1)}, bf16[2,1152,128]{2,1,0:T(8,128)(2,1)S(1)}) custom-call(bf16[4,576,256]{2,1,0:T(8,128)(2,1)} %bitcast.16, bf16[4,576,256]{2,1,0:T(8,128)(2,1)} %bitcast.18), custom_call_target="tpu_custom_call" | custom-call | tf_op jit(solution)/shard_map/pallas_call | solution.py:487
  1.5 3.1 %collective-permute-start = (bf16[2,1152,128]{2,1,0:T(8,128)(2,1)S(1)}, bf16[2,1152,128]{2,1,0:T(8,128)(2,1)S(1)}, u32[]{:S(2)}, u32[]{:S(2)}) collective-permute-start(bf16[2,1152,128]{2,1,0:T(8,128)(2,1)S(1)} %get-tuple-element.47.a_ref), channel_id=1, source_target_pairs={{0,1},{1,0},{2,3},{3,2},{4,5},{5,4},{6,7},{7,6},{8,9},{9,8},{10,11... | collective-permute-start | bytes 1769480 | tf_op jit(solution)/shard_map/ppermute | solution.py:498
  4.6 0.8 %collective-permute-start.1 = (bf16[2,1152,128]{2,1,0:T(8,128)(2,1)S(1)}, bf16[2,1152,128]{2,1,0:T(8,128)(2,1)S(1)}, u32[]{:S(2)}, u32[]{:S(2)}) collective-permute-start(bf16[2,1152,128]{2,1,0:T(8,128)(2,1)S(1)} %get-tuple-element.48.b_ref), channel_id=1, source_target_pairs={{1,2},{2,1},{5,6},{6,5},{9,10},{10,9},{13,14},{14,13},{17,18},{18,... | collective-permute-start | bytes 1769480 | tf_op jit(solution)/shard_map/ppermute | solution.py:498
  5.4 0.0 copy-start.2
  5.4 2.7 %shard_map.115 = (bf16[2,1152,128]{2,1,0:T(8,128)(2,1)S(1)}, bf16[2,1152,128]{2,1,0:T(8,128)(2,1)S(1)}, bf16[2,64,1152]{2,1,0:T(8,128)(2,1)S(1)}, bf16[2,64,1152...) custom-call(bf16[4,576,256]{2,1,0:T(8,128)(2,1)} %bitcast.17, ...), custom_call_target="tpu_custom_call" | custom-call | tf_op jit(solution)/shard_map/pallas_call | solution.py:487
  8.1 0.0 copy-start.1
  8.1 4.4 %collective-permute-start.8 = (bf16[2,1152,128]{2,1,0:T(8,128)(2,1)S(1)}, bf16[2,1152,128]{2,1,0:T(8,128)(2,1)S(1)}, u32[]{:S(2)}, u32[]{:S(2)}) collective-permute-start(bf16[2,1152,128]{2,1,0:T(8,128)(2,1)S(1)} %get-tuple-element.60.a_ref), channel_id=1, source_target_pairs={{0,1},{1,0},{2,3},{3,2},{4,5},{5,4},{6,7},{7,6},{8,9},{9,8},{10,11... | collective-permute-start | bytes 1769480 | tf_op jit(solution)/shard_map/ppermute | solution.py:498
  12.5 0.7 collective-permute-start.9
  13.2 0.1 collective-permute-start.13
  13.3 5.5 %collective-permute-done.ra_ref = bf16[2,1152,128]{2,1,0:T(8,128)(2,1)S(1)} collective-permute-done((bf16[2,1152,128]{2,1,0:T(8,128)(2,1)S(1)}, bf16[2,1152,128]{2,1,0:T(8,128)(2,1)S(1)}, u32[]{:S(2)}, u32[]{:S(2)}) %collective-permute-start) | collective-permute-done | bytes 589856 | tf_op jit(solution)/shard_map/ppermute | solution.py:498
  18.8 2.0 %collective-permute-start.14 = (bf16[2,64,1152]{2,1,0:T(8,128)(2,1)S(1)}, bf16[2,64,1152]{2,1,0:T(8,128)(2,1)S(1)}, u32[]{:S(2)}, u32[]{:S(2)}) collective-permute-start(bf16[2,64,1152]{2,1,0:T(8,128)(2,1)S(1)} %get-tuple-element.71.refs_10_), channel_id=1, source_target_pairs={{0,8},{4,12},{8,0},{12,4},{1,9},{5,13},{9,1},{13,5},{2,10},{6,14},... | collective-permute-start | bytes 884744 | tf_op jit(solution)/shard_map/ppermute | solution.py:480
  20.7 0.0 collective-permute-done.1.rb_ref
  20.7 0.0 collective-permute-start.15
  20.8 2.4 %shard_map.110 = (bf16[2,576,256]{2,1,0:T(8,128)(2,1)S(1)}, f32[2,640,256]{2,1,0:T(8,128)S(1)}, bf16[2,2,16,256]{3,2,1,0:T(8,128)(2,1)S(1)}) custom-call(s32[2,4]{1,0:T(2,128)S(1)} %bitcast.12, s32[3,2,4]{2,1,0:T(2,128)S(1)} %bitcast.10, bf16[4,576,256]{2,1,0:T(8,128)(2,1)} %bitcast.14, bf16[2,1152,128]{2,1,0:T(8,128)(2,1)S(1)} %get-tuple-element.47.a_ref, ...), custom_call_target="tpu_custom_call" | custom-call | tf_op jit(solution)/shard_map/pallas_call | solution.py:509
  23.2 1.7 %shard_map.111 = (bf16[1,64,1152]{2,1,0:T(8,128)(2,1)S(1)}, bf16[1,64,1152]{2,1,0:T(8,128)(2,1)S(1)}, bf16[1,64,1152]{2,1,0:T(8,128)(2,1)S(1)}, bf16[1,64,1152]{2,1,0:T(8,128)(2,1)S(1)}) custom-call(bf16[2,576,256]{2,1,0:T(8,128)(2,1)S(1)} %get-tuple-element.49.qn_ref, f32[2,640,256]{2,1,0:T(8,128)S(1)} %get-tuple-element.50.sum_ref, ...), custom_call_target="tpu_custom_call" | custom-call | tf_op jit(solution)/shard_map/pallas_call | solution.py:528
  25.0 5.6 %collective-permute-done.8.ra_ref = bf16[2,1152,128]{2,1,0:T(8,128)(2,1)S(1)} collective-permute-done((bf16[2,1152,128]{2,1,0:T(8,128)(2,1)S(1)}, bf16[2,1152,128]{2,1,0:T(8,128)(2,1)S(1)}, u32[]{:S(2)}, u32[]{:S(2)}) %collective-permute-start.8) | collective-permute-done | bytes 589856 | tf_op jit(solution)/shard_map/ppermute | solution.py:498
  30.6 0.0 collective-permute-start.2
  30.6 2.4 %shard_map.116 = (bf16[2,576,256]{2,1,0:T(8,128)(2,1)S(1)}, f32[2,640,256]{2,1,0:T(8,128)S(1)}, bf16[2,2,16,256]{3,2,1,0:T(8,128)(2,1)S(1)}) custom-call(s32[2,4]{1,0:T(2,128)S(1)} %bitcast.13, s32[3,2,4]{2,1,0:T(2,128)S(1)} %bitcast.11, bf16[4,576,256]{2,1,0:T(8,128)(2,1)} %bitcast.15, bf16[2,1152,128]{2,1,0:T(8,128)(2,1)S(1)} %get-tuple-element.60.a_ref, ...), custom_call_target="tpu_custom_call" | custom-call | tf_op jit(solution)/shard_map/pallas_call | solution.py:509
  33.0 0.0 collective-permute-done.9.rb_ref
  33.0 1.6 %shard_map.117 = (bf16[32,1152]{1,0:T(8,128)(2,1)S(1)}, bf16[32,1152]{1,0:T(8,128)(2,1)S(1)}, bf16[32,1152]{1,0:T(8,128)(2,1)S(1)}, bf16[32,1152]{1,0:T(8,128)(2...) custom-call(bf16[2,576,256]{2,1,0:T(8,128)(2,1)S(1)} %get-tuple-elem, ...), custom_call_target="tpu_custom_call" | custom-call | tf_op jit(solution)/shard_map/pallas_call | solution.py:553
  34.6 0.6 collective-permute-start.19
  35.1 0.0 collective-permute-done.13.refs_5_
  35.1 1.7 %collective-permute-start.20 = (bf16[32,1152]{1,0:T(8,128)(2,1)S(1)}, bf16[32,1152]{1,0:T(8,128)(2,1)S(1)}, u32[]{:S(2)}, u32[]{:S(2)}) collective-permute-start(bf16[32,1152]{1,0:T(8,128)(2,1)S(1)} %get-tuple-element.76.refs_2_), channel_id=1, source_target_pairs={{0,8},{4,12},{8,0},{12,4},{1,9},{5,13},{9,1},{13,5},{2,10},{6,14},... | collective-permute-start | bytes 221192 | tf_op jit(solution)/shard_map/ppermute | solution.py:480
  36.8 0.0 collective-permute-done.14.refs_6_
  36.8 1.7 %shard_map.113 = (bf16[1,64,1152]{2,1,0:T(8,128)(2,1)S(1)}, bf16[1,64,1152]{2,1,0:T(8,128)(2,1)S(1)}, bf16[1,64,1152]{2,1,0:T(8,128)(2,1)S(1)}, bf16[1,64,1152]{2,1,0:T(8,128)(2,1)S(1)}) custom-call(bf16[2,576,256]{2,1,0:T(8,128)(2,1)S(1)} %get-tuple-element.49.qn_ref, f32[2,640,256]{2,1,0:T(8,128)S(1)} %get-tuple-element.50.sum_ref, ...), custom_call_target="tpu_custom_call" | custom-call | tf_op jit(solution)/shard_map/pallas_call | solution.py:528
  38.6 1.5 %collective-permute-start.3 = (bf16[1,64,1152]{2,1,0:T(8,128)(2,1)S(1)}, bf16[1,64,1152]{2,1,0:T(8,128)(2,1)S(1)}, u32[]{:S(2)}, u32[]{:S(2)}) collective-permute-start(bf16[1,64,1152]{2,1,0:T(8,128)(2,1)S(1)} %get-tuple-element.54.refs_8_.refs_1_), channel_id=1, source_target_pairs={{0,8},{4,12},{8,0},{12,4},{1,9},{5,13},{9,1},{13,5},{2,10},{6,14},... | collective-permute-start | bytes 442376 | tf_op jit(solution)/shard_map/ppermute | solution.py:480
  40.1 0.4 collective-permute-start.4
  40.5 0.0 collective-permute-done.20.refs_2_
  40.5 0.3 collective-permute-start.5
  40.8 0.6 collective-permute-done.21.refs_3_
  41.4 0.9 %collective-permute-start.6 = (bf16[1,64,1152]{2,1,0:T(8,128)(2,1)S(1)}, bf16[1,64,1152]{2,1,0:T(8,128)(2,1)S(1)}, u32[]{:S(2)}, u32[]{:S(2)}) collective-permute-start(bf16[1,64,1152]{2,1,0:T(8,128)(2,1)S(1)} %get-tuple-element.58.refs_9_.refs_2_), channel_id=1, source_target_pairs={{0,8},{4,12},{8,0},{12,4},{1,9},{5,13},{9,1},{13,5},{2,10},{6,14},... | collective-permute-start | bytes 442376 | tf_op jit(solution)/shard_map/ppermute | solution.py:480
  42.3 0.6 collective-permute-start.7
  42.8 2.2 %shard_map.121.refs_2_ = bf16[1920,256]{1,0:T(8,128)(2,1)S(1)} custom-call(bf16[32,1152]{1,0:T(8,128)(2,1)S(1)} %get-tuple-element.74.refs_0_, bf16[32,1152]{1,0:T(8,128)(2,1)S(1)} %collective-permute-done.19.refs_1_, bf16[32,1152]{1,0:T(8,128)(2,1)S(1)} %collective-permute-done.20.refs_2_, bf16[32,1152]{1,0:T(8,128)(2,1)S(1)} %collective-permute-done.21.refs_3_, ...), custom_call_target="tpu_custom_call" | custom-call | tf_op jit(solution)/shard_map/pallas_call | solution.py:572
  45.0 0.4 collective-permute-done.3.refs_2_
  45.4 2.1 %collective-permute-done.4.refs_3_ = bf16[1,64,1152]{2,1,0:T(8,128)(2,1)S(1)} collective-permute-done((bf16[1,64,1152]{2,1,0:T(8,128)(2,1)S(1)}, bf16[1,64,1152]{2,1,0:T(8,128)(2,1)S(1)}, u32[]{:S(2)}, u32[]{:S(2)}) %collective-permute-start.4) | collective-permute-done | bytes 147488 | tf_op jit(solution)/shard_map/ppermute | solution.py:480
  47.5 1.4 %shard_map.112.refs_0_ = bf16[1920,256]{1,0:T(8,128)(2,1)S(1)} custom-call(bf16[1,64,1152]{2,1,0:T(8,128)(2,1)S(1)} %get-tuple-element.52.refs_0_.refs_4_.refs_2_, bf16[1,64,1152]{2,1,0:T(8,128)(2,1)S(1)} %collective-permute-done.2.refs_1_, bf16[1,64,1152]{2,1,0:T(8,128)(2,1)S(1)} %collective-permute-done.3.refs_2_, ...), custom_call_target="tpu_custom_call" | custom-call | tf_op jit(solution)/shard_map/pallas_call | solution.py:543
  48.9 2.8 %collective-permute-done.6.refs_2_ = bf16[1,64,1152]{2,1,0:T(8,128)(2,1)S(1)} collective-permute-done((bf16[1,64,1152]{2,1,0:T(8,128)(2,1)S(1)}, bf16[1,64,1152]{2,1,0:T(8,128)(2,1)S(1)}, u32[]{:S(2)}, u32[]{:S(2)}) %collective-permute-start.6) | collective-permute-done | bytes 147488 | tf_op jit(solution)/shard_map/ppermute | solution.py:480
  51.7 2.1 %collective-permute-done.7.refs_3_ = bf16[1,64,1152]{2,1,0:T(8,128)(2,1)S(1)} collective-permute-done((bf16[1,64,1152]{2,1,0:T(8,128)(2,1)S(1)}, bf16[1,64,1152]{2,1,0:T(8,128)(2,1)S(1)}, u32[]{:S(2)}, u32[]{:S(2)}) %collective-permute-start.7) | collective-permute-done | bytes 147488 | tf_op jit(solution)/shard_map/ppermute | solution.py:480
  53.8 1.4 %shard_map.114.refs_1_ = bf16[1920,256]{1,0:T(8,128)(2,1)S(1)} custom-call(bf16[1,64,1152]{2,1,0:T(8,128)(2,1)S(1)} %get-tuple-element.56.refs_0_.refs_5_.refs_3_, bf16[1,64,1152]{2,1,0:T(8,128)(2,1)S(1)} %collective-permute-done.5.refs_1_, bf16[1,64,1152]{2,1,0:T(8,128)(2,1)S(1)} %collective-permute-done.6.refs_2_, ...), custom_call_target="tpu_custom_call" | custom-call | tf_op jit(solution)/shard_map/pallas_call | solution.py:543
  55.2 1.8 %shard_map.122 = (bf16[32,2304]{1,0:T(8,128)(2,1)S(1)}, bf16[32,2304]{1,0:T(8,128)(2,1)S(1)}, bf16[32,2304]{1,0:T(8,128)(2,1)S(1)}, bf16[32,2304]{1,0:T(8,128)(2,1)S(1)}) custom-call(bf16[1920,256]{1,0:T(8,128)(2,1)S(1)} %shard_map.112.refs_0_, bf16[1920,256]{1,0:T(8,128)(2,1)S(1)} %shard_map.114.refs_1_, bf16[1920,256]{1,0:T(8,128)(2,1)S(1)} %shard_map.121.refs_2_), custom_call_target="tpu_custom_call" | custom-call | tf_op jit(solution)/shard_map/pallas_call | solution.py:583
  56.9 0.4 collective-permute-start.22
  57.4 0.3 collective-permute-start.10
  57.6 1.9 %collective-permute-start.11 = (bf16[32,1152]{1,0:T(8,128)(2,1)S(1)}, bf16[32,1152]{1,0:T(8,128)(2,1)S(1)}, u32[]{:S(2)}, u32[]{:S(2)}) collective-permute-start(bf16[32,1152]{1,0:T(8,128)(2,1)S(1)} %get-tuple-element.67.refs_6_), channel_id=1, source_target_pairs={{0,8},{4,12},{8,0},{12,4},{1,9},{5,13},{9,1},{13,5},{2,10},{6,14},... | collective-permute-start | bytes 221192 | tf_op jit(solution)/shard_map/ppermute | solution.py:480
  59.5 0.0 collective-permute-start.12
  59.5 1.6 %collective-permute-start.23 = (bf16[32,2304]{1,0:T(8,128)(2,1)S(1)}, bf16[32,2304]{1,0:T(8,128)(2,1)S(1)}, u32[]{:S(2)}, u32[]{:S(2)}) collective-permute-start(bf16[32,2304]{1,0:T(8,128)(2,1)S(1)} %get-tuple-element.83), channel_id=1, source_target_pairs={{8,0},{12,4},{0,8},{4,12},{9,1},{13,5},{1,9},{5,13},{10,2},{14,6},... | collective-permute-start | bytes 442376 | tf_op jit(solution)/shard_map/ppermute | solution.py:592
  61.1 0.0 collective-permute-done.10.refs_1_
  61.1 0.1 collective-permute-start.24
  61.3 0.9 %collective-permute-done.11.refs_2_ = bf16[32,1152]{1,0:T(8,128)(2,1)S(1)} collective-permute-done((bf16[32,1152]{1,0:T(8,128)(2,1)S(1)}, bf16[32,1152]{1,0:T(8,128)(2,1)S(1)}, u32[]{:S(2)}, u32[]{:S(2)}) %collective-permute-start.11) | collective-permute-done | bytes 73760 | tf_op jit(solution)/shard_map/ppermute | solution.py:480
  62.2 1.7 %collective-permute-done.12.refs_3_ = bf16[32,1152]{1,0:T(8,128)(2,1)S(1)} collective-permute-done((bf16[32,1152]{1,0:T(8,128)(2,1)S(1)}, bf16[32,1152]{1,0:T(8,128)(2,1)S(1)}, u32[]{:S(2)}, u32[]{:S(2)}) %collective-permute-start.12) | collective-permute-done | bytes 73760 | tf_op jit(solution)/shard_map/ppermute | solution.py:480
  63.9 2.2 %shard_map.118.refs_2_ = bf16[1920,256]{1,0:T(8,128)(2,1)S(1)} custom-call(bf16[32,1152]{1,0:T(8,128)(2,1)S(1)} %get-tuple-element.65.refs_0_.refs_4_, bf16[32,1152]{1,0:T(8,128)(2,1)S(1)} %collective-permute-done.10.refs_1_, bf16[32,1152]{1,0:T(8,128)(2,1)S(1)} %collective-permute-done.11.refs_2_, bf16[32,1152]{1,0:T(8,128)(2,1)S(1)} %collective-permute-done.12.refs_3_, ...), custom_call_target="tpu_custom_call" | custom-call | tf_op jit(solution)/shard_map/pallas_call | solution.py:572
  66.1 0.0 copy-start.7
  66.1 1.8 %shard_map.119 = (bf16[32,2304]{1,0:T(8,128)(2,1)S(1)}, bf16[32,2304]{1,0:T(8,128)(2,1)S(1)}, bf16[32,2304]{1,0:T(8,128)(2,1)S(1)}, bf16[32,2304]{1,0:T(8,128)(2,1)S(1)}) custom-call(bf16[1920,256]{1,0:T(8,128)(2,1)S(1)} %shard_map.112.refs_0_, bf16[1920,256]{1,0:T(8,128)(2,1)S(1)} %shard_map.114.refs_1_, bf16[1920,256]{1,0:T(8,128)(2,1)S(1)} %shard_map.118.refs_2_), custom_call_target="tpu_custom_call" | custom-call | tf_op jit(solution)/shard_map/pallas_call | solution.py:583
  67.9 0.2 collective-permute-start.18
  68.1 2.0 %collective-permute-start.17 = (bf16[32,2304]{1,0:T(8,128)(2,1)S(1)}, bf16[32,2304]{1,0:T(8,128)(2,1)S(1)}, u32[]{:S(2)}, u32[]{:S(2)}) collective-permute-start(bf16[32,2304]{1,0:T(8,128)(2,1)S(1)} %get-tuple-element.78), channel_id=1, source_target_pairs={{8,0},{12,4},{0,8},{4,12},{9,1},{13,5},{1,9},{5,13},{10,2},{14,6},... | collective-permute-start | bytes 442376 | tf_op jit(solution)/shard_map/ppermute | solution.py:592
  70.1 0.0 copy-start.3
  70.2 1.5 %shard_map.120.refs_12_.refs_6_.refs_3_ = bf16[4,2,64,1152]{3,2,1,0:T(8,128)(2,1)S(1)} custom-call(bf16[32,1152]{1,0:T(8,128)(2,1)S(1)} %get-tuple-element.74.refs_0_, bf16[32,1152]{1,0:T(8,128)(2,1)S(1)} %get-tuple-element.75.refs_1_, bf16[32,1152]{1,0:T(8,128)(2,1)S(1)} %get-tuple-element.76.refs_2_, bf16[32,1152]{1,0:T(8,128)(2,1)S(1)} %get-tuple-element.77.refs_3_, ...), custom_call_target="tpu_custom_call" | custom-call | tf_op jit(solution)/shard_map/pallas_call | solution.py:595
  71.7 0.0 collective-permute-done.23.refs_2_
  71.7 0.0 collective-permute-done.24.refs_3_
  71.7 1.5 %shard_map.123.refs_9_ = bf16[4,4,32,1152]{3,2,1,0:T(8,128)(2,1)S(1)} custom-call(bf16[32,2304]{1,0:T(8,128)(2,1)S(1)} %get-tuple-element.81.refs_0_, bf16[32,2304]{1,0:T(8,128)(2,1)S(1)} %collective-permute-done.22.refs_1_, bf16[32,2304]{1,0:T(8,128)(2,1)S(1)} %collective-permute-done.23.refs_2_, bf16[32,2304]{1,0:T(8,128)(2,1)S(1)} %collective-permute-done.24.refs_3_, ...), custom_call_target="tpu_custom_call" | custom-call | tf_op jit(solution)/shard_map/pallas_call | solution.py:625
  73.3 0.0 collective-permute-done.18.refs_1_
  73.3 1.8 %shard_map.124 = (bf16[4,256,1152]{2,1,0:T(8,128)(2,1)}, bf16[2,4,32,1152]{3,2,1,0:T(8,128)(2,1)S(1)}) custom-call(bf16[32,2304]{1,0:T(8,128)(2,1)S(1)} %get-tuple-element.79.refs_0_, bf16[32,2304]{1,0:T(8,128)(2,1)S(1)} %collective-permute-done.18.refs_1_, bf16[1,64,1152]{2,1,0:T(8,128)(2,1)S(1)} %get-tuple-element.52.refs_0_.refs_4_.refs_2_, ...), custom_call_target="tpu_custom_call" | custom-call | tf_op jit(solution)/shard_map/pallas_call | solution.py:625
  75.1 1.3 %shard_map.125 = (bf16[4,256,1152]{2,1,0:T(8,128)(2,1)}, bf16[1,4,32,1152]{3,2,1,0:T(8,128)(2,1)S(1)}) custom-call(bf16[32,2304]{1,0:T(8,128)(2,1)S(1)} %collective-permute-done.17.refs_0_, bf16[1,64,1152]{2,1,0:T(8,128)(2,1)S(1)} %get-tuple-element.54.refs_8_.refs_1_, ...), custom_call_target="tpu_custom_call", output_to_operand_aliasing={{0}: (7, {})} | custom-call | tf_op jit(solution)/shard_map/pallas_call | solution.py:625
  76.4 0.4 collective-permute-done.16.refs_0_
  76.8 1.3 %shard_map.126 = bf16[4,256,1152]{2,1,0:T(8,128)(2,1)} custom-call(bf16[32,2304]{1,0:T(8,128)(2,1)S(1)} %collective-permute-done.16.refs_0_, bf16[1,64,1152]{2,1,0:T(8,128)(2,1)S(1)} %get-tuple-element.55.refs_10_.refs_1_, bf16[1,64,1152]{2,1,0:T(8,128)(2,1)S(1)} %get-tuple-element.59.refs_11_.refs_2_, ...), custom_call_target="tpu_custom_call", output_to_operand_aliasing={{}: (7, {})} | custom-call | tf_op jit(solution)/shard_map/pallas_call | solution.py:625
  (22 shorter events, 0.1 us)
Async XLA Ops:
  1.5 17.3 %collective-permute-start = (bf16[2,1152,128]{2,1,0:T(8,128)(2,1)S(1)}, bf16[2,1152,128]{2,1,0:T(8,128)(2,1)S(1)}, u32[]{:S(2)}, u32[]{:S(2)}) collective-permute-start(bf16[2,1152,128]{2,1,0:T(8,128)(2,1)S(1)} %get-tuple-element.47.a_ref), channel_id=1, source_target_pairs={{0,1},{1,0},{2,3},{3,2},{4,5},{5,4},{6,7},{7,6},{8,9},{9,8},{10,11... | collective-permute-start | bytes 1769480 | tf_op jit(solution)/shard_map/ppermute | solution.py:498
  4.6 16.2 %copy-start.6 = (f32[1152]{0:T(1024)S(1)}, f32[1152]{0:T(1024)}, u32[]{:S(2)}) copy-start(f32[1152]{0:T(1024)} %param.16) | copy-start | bytes 13828
  4.6 16.2 %copy-start.4 = (s32[4,2,3]{0,1,2:T(2,128)S(1)}, s32[4,2,3]{0,1,2:T(2,128)}, u32[]{:S(2)}) copy-start(s32[4,2,3]{0,1,2:T(2,128)} %param.20) | copy-start | bytes 292
  4.6 16.2 %copy-start.5 = (s32[4,2]{0,1:T(2,128)S(1)}, s32[4,2]{0,1:T(2,128)}, u32[]{:S(2)}) copy-start(s32[4,2]{0,1:T(2,128)} %param.21) | copy-start | bytes 100
  4.6 16.1 %collective-permute-start.1 = (bf16[2,1152,128]{2,1,0:T(8,128)(2,1)S(1)}, bf16[2,1152,128]{2,1,0:T(8,128)(2,1)S(1)}, u32[]{:S(2)}, u32[]{:S(2)}) collective-permute-start(bf16[2,1152,128]{2,1,0:T(8,128)(2,1)S(1)} %get-tuple-element.48.b_ref), channel_id=1, source_target_pairs={{1,2},{2,1},{5,6},{6,5},{9,10},{10,9},{13,14},{14,13},{17,18},{18,... | collective-permute-start | bytes 1769480 | tf_op jit(solution)/shard_map/ppermute | solution.py:498
  5.4 17.8 %copy-start.2 = (bf16[4,256,1152]{2,1,0:T(8,128)(2,1)S(1)}, bf16[4,256,1152]{2,1,0:T(8,128)(2,1)}, u32[]{:S(2)}) copy-start(bf16[4,256,1152]{2,1,0:T(8,128)(2,1)} %refs_0_.1) | copy-start | bytes 7077892
  8.1 15.1 %copy-start.1 = (bf16[576,1152]{1,0:T(8,128)(2,1)S(1)}, bf16[576,1152]{1,0:T(8,128)(2,1)}, u32[]{:S(2)}) copy-start(bf16[576,1152]{1,0:T(8,128)(2,1)} %refs_8_.3) | copy-start | bytes 3981316
  8.1 22.4 %collective-permute-start.8 = (bf16[2,1152,128]{2,1,0:T(8,128)(2,1)S(1)}, bf16[2,1152,128]{2,1,0:T(8,128)(2,1)S(1)}, u32[]{:S(2)}, u32[]{:S(2)}) collective-permute-start(bf16[2,1152,128]{2,1,0:T(8,128)(2,1)S(1)} %get-tuple-element.60.a_ref), channel_id=1, source_target_pairs={{0,1},{1,0},{2,3},{3,2},{4,5},{5,4},{6,7},{7,6},{8,9},{9,8},{10,11... | collective-permute-start | bytes 1769480 | tf_op jit(solution)/shard_map/ppermute | solution.py:498
  12.5 20.4 %collective-permute-start.9 = (bf16[2,1152,128]{2,1,0:T(8,128)(2,1)S(1)}, bf16[2,1152,128]{2,1,0:T(8,128)(2,1)S(1)}, u32[]{:S(2)}, u32[]{:S(2)}) collective-permute-start(bf16[2,1152,128]{2,1,0:T(8,128)(2,1)S(1)} %get-tuple-element.61.b_ref), channel_id=1, source_target_pairs={{1,2},{2,1},{5,6},{6,5},{9,10},{10,9},{13,14},{14,13},{17,18},{18,... | collective-permute-start | bytes 1769480 | tf_op jit(solution)/shard_map/ppermute | solution.py:498
  13.2 21.9 %collective-permute-start.13 = (bf16[2,64,1152]{2,1,0:T(8,128)(2,1)S(1)}, bf16[2,64,1152]{2,1,0:T(8,128)(2,1)S(1)}, u32[]{:S(2)}, u32[]{:S(2)}) collective-permute-start(bf16[2,64,1152]{2,1,0:T(8,128)(2,1)S(1)} %get-tuple-element.70.refs_9_), channel_id=1, source_target_pairs={{0,4},{4,0},{8,12},{12,8},{1,5},{5,1},{9,13},{13,9},{2,6},{6,2},{1... | collective-permute-start | bytes 884744 | tf_op jit(solution)/shard_map/ppermute | solution.py:480
  18.8 18.1 %collective-permute-start.14 = (bf16[2,64,1152]{2,1,0:T(8,128)(2,1)S(1)}, bf16[2,64,1152]{2,1,0:T(8,128)(2,1)S(1)}, u32[]{:S(2)}, u32[]{:S(2)}) collective-permute-start(bf16[2,64,1152]{2,1,0:T(8,128)(2,1)S(1)} %get-tuple-element.71.refs_10_), channel_id=1, source_target_pairs={{0,8},{4,12},{8,0},{12,4},{1,9},{5,13},{9,1},{13,5},{2,10},{6,14},... | collective-permute-start | bytes 884744 | tf_op jit(solution)/shard_map/ppermute | solution.py:480
  20.7 17.9 %collective-permute-start.15 = (bf16[2,64,1152]{2,1,0:T(8,128)(2,1)S(1)}, bf16[2,64,1152]{2,1,0:T(8,128)(2,1)S(1)}, u32[]{:S(2)}, u32[]{:S(2)}) collective-permute-start(bf16[2,64,1152]{2,1,0:T(8,128)(2,1)S(1)} %get-tuple-element.72.refs_11_), channel_id=1, source_target_pairs={{0,12},{4,8},{8,4},{12,0},{1,13},{5,9},{9,5},{13,1},{2,14},{6,10},... | collective-permute-start | bytes 884744 | tf_op jit(solution)/shard_map/ppermute | solution.py:480
  30.6 11.7 %collective-permute-start.2 = (bf16[1,64,1152]{2,1,0:T(8,128)(2,1)S(1)}, bf16[1,64,1152]{2,1,0:T(8,128)(2,1)S(1)}, u32[]{:S(2)}, u32[]{:S(2)}) collective-permute-start(bf16[1,64,1152]{2,1,0:T(8,128)(2,1)S(1)} %get-tuple-element.53.refs_6_.refs_4_), channel_id=1, source_target_pairs={{0,4},{4,0},{8,12},{12,8},{1,5},{5,1},{9,13},{13,9},{2,6},{6,2},{1... | collective-permute-start | bytes 442376 | tf_op jit(solution)/shard_map/ppermute | solution.py:480
  34.6 5.5 %collective-permute-start.19 = (bf16[32,1152]{1,0:T(8,128)(2,1)S(1)}, bf16[32,1152]{1,0:T(8,128)(2,1)S(1)}, u32[]{:S(2)}, u32[]{:S(2)}) collective-permute-start(bf16[32,1152]{1,0:T(8,128)(2,1)S(1)} %get-tuple-element.75.refs_1_), channel_id=1, source_target_pairs={{0,4},{4,0},{8,12},{12,8},{1,5},{5,1},{9,13},{13,9},{2,6},{6,2},{1... | collective-permute-start | bytes 221192 | tf_op jit(solution)/shard_map/ppermute | solution.py:480
  35.1 5.4 %collective-permute-start.20 = (bf16[32,1152]{1,0:T(8,128)(2,1)S(1)}, bf16[32,1152]{1,0:T(8,128)(2,1)S(1)}, u32[]{:S(2)}, u32[]{:S(2)}) collective-permute-start(bf16[32,1152]{1,0:T(8,128)(2,1)S(1)} %get-tuple-element.76.refs_2_), channel_id=1, source_target_pairs={{0,8},{4,12},{8,0},{12,4},{1,9},{5,13},{9,1},{13,5},{2,10},{6,14},... | collective-permute-start | bytes 221192 | tf_op jit(solution)/shard_map/ppermute | solution.py:480
  36.8 4.6 %collective-permute-start.21 = (bf16[32,1152]{1,0:T(8,128)(2,1)S(1)}, bf16[32,1152]{1,0:T(8,128)(2,1)S(1)}, u32[]{:S(2)}, u32[]{:S(2)}) collective-permute-start(bf16[32,1152]{1,0:T(8,128)(2,1)S(1)} %get-tuple-element.77.refs_3_), channel_id=1, source_target_pairs={{0,12},{4,8},{8,4},{12,0},{1,13},{5,9},{9,5},{13,1},{2,14},{6,10},... | collective-permute-start | bytes 221192 | tf_op jit(solution)/shard_map/ppermute | solution.py:480
  36.8 6.0 %copy-start = (bf16[1152,1728]{0,1:T(8,128)(2,1)S(1)}, bf16[1152,1728]{0,1:T(8,128)(2,1)}, u32[]{:S(2)}) copy-start(bf16[1152,1728]{0,1:T(8,128)(2,1)} %param.17) | copy-start | bytes 11943940
  38.6 6.8 %collective-permute-start.3 = (bf16[1,64,1152]{2,1,0:T(8,128)(2,1)S(1)}, bf16[1,64,1152]{2,1,0:T(8,128)(2,1)S(1)}, u32[]{:S(2)}, u32[]{:S(2)}) collective-permute-start(bf16[1,64,1152]{2,1,0:T(8,128)(2,1)S(1)} %get-tuple-element.54.refs_8_.refs_1_), channel_id=1, source_target_pairs={{0,8},{4,12},{8,0},{12,4},{1,9},{5,13},{9,1},{13,5},{2,10},{6,14},... | collective-permute-start | bytes 442376 | tf_op jit(solution)/shard_map/ppermute | solution.py:480
  40.1 7.4 %collective-permute-start.4 = (bf16[1,64,1152]{2,1,0:T(8,128)(2,1)S(1)}, bf16[1,64,1152]{2,1,0:T(8,128)(2,1)S(1)}, u32[]{:S(2)}, u32[]{:S(2)}) collective-permute-start(bf16[1,64,1152]{2,1,0:T(8,128)(2,1)S(1)} %get-tuple-element.55.refs_10_.refs_1_), channel_id=1, source_target_pairs={{0,12},{4,8},{8,4},{12,0},{1,13},{5,9},{9,5},{13,1},{2,14},{6,10},... | collective-permute-start | bytes 442376 | tf_op jit(solution)/shard_map/ppermute | solution.py:480
  40.5 8.4 %collective-permute-start.5 = (bf16[1,64,1152]{2,1,0:T(8,128)(2,1)S(1)}, bf16[1,64,1152]{2,1,0:T(8,128)(2,1)S(1)}, u32[]{:S(2)}, u32[]{:S(2)}) collective-permute-start(bf16[1,64,1152]{2,1,0:T(8,128)(2,1)S(1)} %get-tuple-element.57.refs_7_.refs_5_), channel_id=1, source_target_pairs={{0,4},{4,0},{8,12},{12,8},{1,5},{5,1},{9,13},{13,9},{2,6},{6,2},{1... | collective-permute-start | bytes 442376 | tf_op jit(solution)/shard_map/ppermute | solution.py:480
  41.4 10.3 %collective-permute-start.6 = (bf16[1,64,1152]{2,1,0:T(8,128)(2,1)S(1)}, bf16[1,64,1152]{2,1,0:T(8,128)(2,1)S(1)}, u32[]{:S(2)}, u32[]{:S(2)}) collective-permute-start(bf16[1,64,1152]{2,1,0:T(8,128)(2,1)S(1)} %get-tuple-element.58.refs_9_.refs_2_), channel_id=1, source_target_pairs={{0,8},{4,12},{8,0},{12,4},{1,9},{5,13},{9,1},{13,5},{2,10},{6,14},... | collective-permute-start | bytes 442376 | tf_op jit(solution)/shard_map/ppermute | solution.py:480
  42.3 11.5 %collective-permute-start.7 = (bf16[1,64,1152]{2,1,0:T(8,128)(2,1)S(1)}, bf16[1,64,1152]{2,1,0:T(8,128)(2,1)S(1)}, u32[]{:S(2)}, u32[]{:S(2)}) collective-permute-start(bf16[1,64,1152]{2,1,0:T(8,128)(2,1)S(1)} %get-tuple-element.59.refs_11_.refs_2_), channel_id=1, source_target_pairs={{0,12},{4,8},{8,4},{12,0},{1,13},{5,9},{9,5},{13,1},{2,14},{6,10},... | collective-permute-start | bytes 442376 | tf_op jit(solution)/shard_map/ppermute | solution.py:480
  56.9 13.2 %collective-permute-start.22 = (bf16[32,2304]{1,0:T(8,128)(2,1)S(1)}, bf16[32,2304]{1,0:T(8,128)(2,1)S(1)}, u32[]{:S(2)}, u32[]{:S(2)}) collective-permute-start(bf16[32,2304]{1,0:T(8,128)(2,1)S(1)} %get-tuple-element.82), channel_id=1, source_target_pairs={{4,0},{0,4},{12,8},{8,12},{5,1},{1,5},{13,9},{9,13},{6,2},{2,6},{1... | collective-permute-start | bytes 442376 | tf_op jit(solution)/shard_map/ppermute | solution.py:592
  57.4 3.8 %collective-permute-start.10 = (bf16[32,1152]{1,0:T(8,128)(2,1)S(1)}, bf16[32,1152]{1,0:T(8,128)(2,1)S(1)}, u32[]{:S(2)}, u32[]{:S(2)}) collective-permute-start(bf16[32,1152]{1,0:T(8,128)(2,1)S(1)} %get-tuple-element.66.refs_5_), channel_id=1, source_target_pairs={{0,4},{4,0},{8,12},{12,8},{1,5},{5,1},{9,13},{13,9},{2,6},{6,2},{1... | collective-permute-start | bytes 221192 | tf_op jit(solution)/shard_map/ppermute | solution.py:480
  57.6 4.6 %collective-permute-start.11 = (bf16[32,1152]{1,0:T(8,128)(2,1)S(1)}, bf16[32,1152]{1,0:T(8,128)(2,1)S(1)}, u32[]{:S(2)}, u32[]{:S(2)}) collective-permute-start(bf16[32,1152]{1,0:T(8,128)(2,1)S(1)} %get-tuple-element.67.refs_6_), channel_id=1, source_target_pairs={{0,8},{4,12},{8,0},{12,4},{1,9},{5,13},{9,1},{13,5},{2,10},{6,14},... | collective-permute-start | bytes 221192 | tf_op jit(solution)/shard_map/ppermute | solution.py:480
  59.5 4.4 %collective-permute-start.12 = (bf16[32,1152]{1,0:T(8,128)(2,1)S(1)}, bf16[32,1152]{1,0:T(8,128)(2,1)S(1)}, u32[]{:S(2)}, u32[]{:S(2)}) collective-permute-start(bf16[32,1152]{1,0:T(8,128)(2,1)S(1)} %get-tuple-element.68.refs_7_), channel_id=1, source_target_pairs={{0,12},{4,8},{8,4},{12,0},{1,13},{5,9},{9,5},{13,1},{2,14},{6,10},... | collective-permute-start | bytes 221192 | tf_op jit(solution)/shard_map/ppermute | solution.py:480
  59.5 12.2 %collective-permute-start.23 = (bf16[32,2304]{1,0:T(8,128)(2,1)S(1)}, bf16[32,2304]{1,0:T(8,128)(2,1)S(1)}, u32[]{:S(2)}, u32[]{:S(2)}) collective-permute-start(bf16[32,2304]{1,0:T(8,128)(2,1)S(1)} %get-tuple-element.83), channel_id=1, source_target_pairs={{8,0},{12,4},{0,8},{4,12},{9,1},{13,5},{1,9},{5,13},{10,2},{14,6},... | collective-permute-start | bytes 442376 | tf_op jit(solution)/shard_map/ppermute | solution.py:592
  61.1 10.6 %collective-permute-start.24 = (bf16[32,2304]{1,0:T(8,128)(2,1)S(1)}, bf16[32,2304]{1,0:T(8,128)(2,1)S(1)}, u32[]{:S(2)}, u32[]{:S(2)}) collective-permute-start(bf16[32,2304]{1,0:T(8,128)(2,1)S(1)} %get-tuple-element.84), channel_id=1, source_target_pairs={{12,0},{8,4},{4,8},{0,12},{13,1},{9,5},{5,9},{1,13},{14,2},{10,6},... | collective-permute-start | bytes 442376 | tf_op jit(solution)/shard_map/ppermute | solution.py:592
  66.1 4.0 %copy-start.7 = (f32[1152]{0:T(1024)S(1)}, f32[1152]{0:T(1024)}, u32[]{:S(2)}) copy-start(f32[1152]{0:T(1024)} %param.19) | copy-start | bytes 13828
  67.9 5.4 %collective-permute-start.18 = (bf16[32,2304]{1,0:T(8,128)(2,1)S(1)}, bf16[32,2304]{1,0:T(8,128)(2,1)S(1)}, u32[]{:S(2)}, u32[]{:S(2)}) collective-permute-start(bf16[32,2304]{1,0:T(8,128)(2,1)S(1)} %get-tuple-element.80), channel_id=1, source_target_pairs={{4,0},{0,4},{12,8},{8,12},{5,1},{1,5},{13,9},{9,13},{6,2},{2,6},{1... | collective-permute-start | bytes 442376 | tf_op jit(solution)/shard_map/ppermute | solution.py:592
  68.1 6.9 %collective-permute-start.17 = (bf16[32,2304]{1,0:T(8,128)(2,1)S(1)}, bf16[32,2304]{1,0:T(8,128)(2,1)S(1)}, u32[]{:S(2)}, u32[]{:S(2)}) collective-permute-start(bf16[32,2304]{1,0:T(8,128)(2,1)S(1)} %get-tuple-element.78), channel_id=1, source_target_pairs={{8,0},{12,4},{0,8},{4,12},{9,1},{13,5},{1,9},{5,13},{10,2},{14,6},... | collective-permute-start | bytes 442376 | tf_op jit(solution)/shard_map/ppermute | solution.py:592
  70.1 6.7 %collective-permute-start.16 = (bf16[32,2304]{1,0:T(8,128)(2,1)S(1)}, bf16[32,2304]{1,0:T(8,128)(2,1)S(1)}, u32[]{:S(2)}, u32[]{:S(2)}) collective-permute-start(bf16[32,2304]{1,0:T(8,128)(2,1)S(1)} %get-tuple-element.73), channel_id=1, source_target_pairs={{12,0},{8,4},{4,8},{0,12},{13,1},{9,5},{5,9},{1,13},{14,2},{10,6},... | collective-permute-start | bytes 442376 | tf_op jit(solution)/shard_map/ppermute | solution.py:592
  70.1 1.6 %copy-start.3 = (bf16[576,1152]{1,0:T(8,128)(2,1)S(1)}, bf16[576,1152]{1,0:T(8,128)(2,1)}, u32[]{:S(2)}) copy-start(bf16[576,1152]{1,0:T(8,128)(2,1)} %refs_4_.3) | copy-start | bytes 3981316
